TPU v7x, 256 devices: a whole 4x4x8 slice. The times are simulated.
256 devices in a mesh: dom: 32 (over z_lo, y, x), ch: 8 (over z_hi, core).
Axes of the slice: x: 4, y: 4, z: 8 (z_hi: 4, z_lo: 2; z = z_hi * 2 + z_lo), core: 2. Of those that a mesh axis runs over, the one named last changes fastest.
Arguments:
- node_feats: bfloat16 [512, 24576], P('ch', 'dom'), may hold values from -6 to 6
- edge_feats: bfloat16 [512, 32768], P('ch', 'dom'), may hold values from -6 to 6
- send_rows: int32 [32768], P('dom'), may hold values from 0 to 767
- edge_src: int32 [32768], P('dom'), may hold values from 0 to 1791
- edge_dst: int32 [32768], P('dom'), may hold values from 0 to 767
- w_edge_in: bfloat16 [2, 3, 512, 512], P(None, None, None, 'ch'), may hold values from -0.15625 to 0.15625
- w_edge_out: bfloat16 [2, 512, 512], P(None, 'ch'), may hold values from -0.25 to 0.25
- w_node_in: bfloat16 [2, 2, 512, 512], P(None, None, None, 'ch'), may hold values from -0.1875 to 0.1875
- w_node_out: bfloat16 [2, 512, 512], P(None, 'ch'), may hold values from -0.25 to 0.25
Outputs:
- nodes_out: bfloat16 [512, 24576], P('ch', 'dom')
- edges_out: bfloat16 [512, 32768], P('ch', 'dom')
All inputs are finite; a program needn't handle non-finite values.
Results may differ from a plain program's by a relative error of at most 0.0085.
Values may be sent and summed in bfloat16 or wider, within the bound.
No kernel may reach another device: no remote copies, remote signals or barrier semaphores. Data moves between devices by JAX's collectives and lax.ppermute only.
A program may use at most 64 MiB of HBM per device.

v0:
```python
import jax
import jax.numpy as jnp
from jax import lax
from jax.experimental import pallas as pl
from jax.experimental.pallas import tpu as pltpu
from jax.sharding import PartitionSpec as P

LATENT = 512
HALF = 256
SLOTS = 32
CHUNK = 256
BF = jnp.bfloat16
F32 = jnp.float32

CORE = [(c, c ^ 1) for c in range(8)]
VMEM = pl.BlockSpec(memory_space=pltpu.VMEM)
SMEM = pl.BlockSpec(memory_space=pltpu.SMEM)


def z_shift(s):
    return [(c, ((c // 2 + s) % 4) * 2 + c % 2) for c in range(8)]


def ring(stage, s):
    pairs = []
    for d in range(32):
        along_x = (d // 4) * 4 + (d + s) % 4
        along_y = (d // 16) * 16 + (d + 4 * s) % 16
        for c in range(8):
            to = along_y if (c % 2 == 0) == (stage == 1) else along_x
            pairs.append((d * 8 + c, to * 8 + c))
    return pairs


def swap(x):
    return lax.ppermute(x, "ch", CORE)


def ring_gather(x, axis, perm):
    half = x.shape[0] // 2
    prev = lax.ppermute(x, axis, perm(1))
    nxt = lax.ppermute(x, axis, perm(3))
    far_a = lax.ppermute(prev[:half], axis, perm(1))
    far_b = lax.ppermute(nxt[half:], axis, perm(3))
    return x, nxt, far_a, far_b, prev


def dot(a, b, ca=1, cb=0):
    return lax.dot_general(a, b, (((ca,), (cb,)), ((), ())), preferred_element_type=F32)


def norm_add(msg, residual):
    mean = jnp.sum(msg, axis=0, keepdims=True) / LATENT
    var = jnp.sum(msg * msg, axis=0, keepdims=True) / LATENT - mean * mean
    return (residual.astype(F32) + (msg - mean) * lax.rsqrt(var + 1e-05)).astype(BF)


def silu(x):
    return (x * jax.nn.sigmoid(x)).astype(BF)


def hot(idx, first, rows):
    where = lax.broadcasted_iota(jnp.int32, (rows, idx.shape[1]), 0) + first == idx
    return jnp.where(where, 1.0, 0.0).astype(BF)


def chunks(n, body):
    def step(i, carry):
        body(pl.ds(pl.multiple_of(i * CHUNK, CHUNK), CHUNK), i * CHUNK)
        return carry

    lax.fori_loop(0, n // CHUNK, step, 0)


def call(kernel, outs, *args, scratch=(), flops=0):
    specs = [SMEM] + [VMEM] * (len(args) - 1)
    moved = sum(a.size * a.dtype.itemsize for a in args)
    return pl.pallas_call(
        kernel,
        out_shape=[jax.ShapeDtypeStruct(s, d) for s, d in outs],
        in_specs=specs,
        out_specs=[VMEM] * len(outs),
        scratch_shapes=list(scratch),
        cost_estimate=pl.CostEstimate(flops=flops, bytes_accessed=moved, transcendentals=0),
    )(*args)


def place_half(meta, parts, out):
    own, nxt, far_a, far_b, prev = parts
    zi = meta[0]
    at = lambda s: pl.multiple_of(((zi + s) & 3) * 64, 64)
    n = out.shape[1]
    out[pl.ds(at(0), 64), :] = own[:, :n]
    out[pl.ds(at(1), 64), :] = nxt[:, :n]
    out[pl.ds(at(2), 32), :] = far_a[:, :n]
    out[pl.ds(at(2) + 32, 32), :] = far_b[:, :n]
    out[pl.ds(at(3), 64), :] = prev[:, :n]


def select_rows(send, x, rows):
    def body(sl, _):
        rows[sl, :] = dot(x, hot(send[:, sl], 0, x.shape[1])).T.astype(BF)

    chunks(rows.shape[0], body)


def send_first(meta, own, nxt, far_a, far_b, prev, send, half, rows):
    place_half(meta, (own, nxt, far_a, far_b, prev), half)
    select_rows(send, half[...], rows)


def gather_edges(meta, own, nxt, far_a, far_b, prev, half):
    place_half(meta, (own, nxt, far_a, far_b, prev), half)


def split_layers(meta, own, nxt, far, prev, one, two):
    for s, part in enumerate((own, nxt, far, prev)):
        a = (meta[1] + s) & 3

        @pl.when(a < 2)
        def _():
            one[a] = part[...]

        @pl.when(a >= 2)
        def _():
            two[a - 2] = part[...]


def unpack(meta, own, nxt, far_a, far_b, prev, mats, outs):
    def rows_of(ref, a, m):
        return ref[a, :, m].astype(F32).reshape(32, LATENT)

    pieces = ((own, own), (nxt, nxt), (far_a, far_b), (prev, prev))
    for m in range(7):
        for s in range(4):
            at = pl.multiple_of(((meta[2] + s) & 3) * 64, 64)
            for a in range(2):
                ref = pieces[s][a]
                rows = rows_of(ref, a if ref.shape[0] == 2 else 0, m)
                mats[m, pl.ds(at + 32 * a, 32), :] = rows.astype(BF)
    outs[0] = mats[3].astype(F32).T.astype(BF)
    outs[1] = mats[6].astype(F32).T.astype(BF)


def interleave(meta, own, other, out):
    for z in range(4):
        out[pl.ds(pl.multiple_of(z * 128 + meta[3] * 64, 64), 64), :] = own[z * 64 : z * 64 + 64]
        out[pl.ds(pl.multiple_of(z * 128 + 64 - meta[3] * 64, 64), 64), :] = other[z * 64 : z * 64 + 64]


def edge_first(meta, v_own, v_other, e_own, e_other, h_own, h_other, mats, src, dst, v_all, e_all, hidden, sender, receiver, halo):
    n = v_all.shape[1]
    interleave(meta, v_own, v_other, v_all)
    interleave(meta, e_own, e_other, e_all)
    swapped = meta[3] == 1
    low = lax.broadcasted_iota(jnp.int32, (halo.shape[0], 128), 1) < 64
    for b in range(2):
        blk = slice(128 * b, 128 * b + 128)
        own, other = h_own[:, blk].astype(F32), h_other[:, blk].astype(F32)
        even = jnp.where(swapped, other, own)
        odd = jnp.where(swapped, own, other)
        halo[:, 256 * b : 256 * b + 128] = jnp.where(low, even, pltpu.roll(odd, 64, 1)).astype(BF)
        halo[:, 256 * b + 128 : 256 * b + 256] = jnp.where(low, pltpu.roll(even, 64, 1), odd).astype(BF)
    sender[:, :n] = dot(mats[1], v_all[...]).astype(BF)
    sender[:, n:] = dot(mats[1], halo[...], 1, 1).astype(BF)
    receiver[...] = dot(mats[2], v_all[...]).astype(BF)

    def body(sl, _):
        pre = dot(mats[0], e_all[:, sl])
        pre += dot(sender[...], hot(src[:, sl], 0, sender.shape[1]))
        pre += dot(receiver[...], hot(dst[:, sl], 0, n))
        hidden[:, sl] = silu(pre)

    chunks(hidden.shape[1], body)


def aggregate(meta, hid, hid_other, turned, turned_other, mats, e_all, v_all, dst, e_new, hidden):
    def edges(sl, _):
        msg = dot(turned[0], hid[:, sl]) + dot(turned_other[0], hid_other[:, sl])
        e_new[:, sl] = norm_add(msg, e_all[:, sl])

    chunks(e_new.shape[1], edges)

    def nodes(sl, first):
        agg = dot(e_new[...], hot(dst[...], first, CHUNK), 1, 1).astype(BF)
        hidden[:, sl] = silu(dot(mats[4], v_all[:, sl]) + dot(mats[5], agg))

    chunks(hidden.shape[1], nodes)


def aggregate_last(meta, hid, hid_other, turned, turned_other, mats, e_all, v_all, dst, e_out, hidden, e_new):
    aggregate(meta, hid, hid_other, turned, turned_other, mats, e_all, v_all, dst, e_new, hidden)
    e_out[...] = e_new[pl.ds(pl.multiple_of(meta[4] * 64, 64), 64), :]


def node_norm(hid, hid_other, turned, turned_other, v_all, v_new):
    def nodes(sl, _):
        msg = dot(turned[1], hid[:, sl]) + dot(turned_other[1], hid_other[:, sl])
        v_new[:, sl] = norm_add(msg, v_all[:, sl])

    chunks(v_new.shape[1], nodes)


def send_next(meta, hid, hid_other, turned, turned_other, v_all, mats, send, v_new, sender, rows):
    node_norm(hid, hid_other, turned, turned_other, v_all, v_new)
    sender[...] = dot(mats[1], v_new[...]).astype(BF)
    select_rows(send, sender[...], rows)


def edge_local(meta, v_all, e_all, sender, mats, src, dst, part, receiver):
    n = v_all.shape[1]
    receiver[...] = dot(mats[2], v_all[...]).astype(BF)

    def body(sl, _):
        pre = dot(mats[0], e_all[:, sl])
        pre += dot(sender[...], hot(src[:, sl], 0, n))
        part[:, sl] = pre + dot(receiver[...], hot(dst[:, sl], 0, n))

    chunks(part.shape[1], body)


def edge_far(n, meta, part, rows, src, hidden, far):
    far[...] = rows[...].astype(F32).T.astype(BF)

    def body(sl, _):
        hidden[:, sl] = silu(part[:, sl] + dot(far[...], hot(src[:, sl], n, far.shape[1])))

    chunks(hidden.shape[1], body)


def finish(meta, hid, hid_other, turned, turned_other, v_all, v_out, v_new):
    node_norm(hid, hid_other, turned, turned_other, v_all, v_new)
    v_out[...] = v_new[pl.ds(pl.multiple_of(meta[4] * 64, 64), 64), :]


def shards(node_feats, edge_feats, send_rows, edge_src, edge_dst, w_edge_in, w_edge_out, w_node_in, w_node_out):
    d = lax.axis_index("dom")
    c = lax.axis_index("ch")
    k = c & 1
    y, x = (d >> 2) & 3, d & 3
    n = node_feats.shape[1]
    m = edge_feats.shape[1]
    first = jnp.where(k == 0, y, x)
    second = jnp.where(k == 0, x, y)
    meta = jnp.stack([c >> 1, first, second, k, c]).astype(jnp.int32)
    send, src, dst = (a.reshape(1, -1) for a in (send_rows, edge_src, edge_dst))

    row = 8 * ((first & 1) * 4 + second)

    def cut(w):
        return lax.dynamic_slice(w, (first >> 1, 0, row, 0), (1, w.shape[1], 8, LATENT)).reshape(-1, LATENT)

    piece = [cut(jnp.swapaxes(w_edge_in, 2, 3)), cut(w_edge_out[:, None]), cut(jnp.swapaxes(w_node_in, 2, 3)), cut(w_node_out[:, None])]
    piece = jnp.concatenate(piece + [piece[-1]])
    v_parts = ring_gather(jnp.concatenate([node_feats, piece], axis=1), "ch", z_shift)
    e_parts = ring_gather(lax.optimization_barrier((edge_feats, v_parts[1], v_parts[4]))[0], "ch", z_shift)

    own, nxt, far_a, far_b, prev = (p[:, n:] for p in v_parts)
    wz = jnp.stack([own, nxt, jnp.concatenate([far_a, far_b]), prev])[:, :56].reshape(4, 7, 8, LATENT)
    w_parts = [wz] + [lax.ppermute(wz, ("dom", "ch"), ring(1, s)) for s in (3, 2, 1)]
    layers = call(split_layers, [((2, 4, 7, 8, LATENT), BF)] * 2, meta, *w_parts)

    v_half, rows = call(
        send_first, [((HALF, n), BF), ((m, HALF), BF)], meta, *v_parts, send, flops=2 * HALF * n * m
    )

    def exchange(rows):
        return lax.all_to_all(rows.reshape(32, SLOTS, HALF), "dom", 0, 0, tiled=True).reshape(-1, HALF)

    halo = exchange(rows)
    v_other = swap(v_half)
    (e_half,) = call(gather_edges, [((HALF, m), BF)], meta, *e_parts)
    e_other = swap(e_half)
    halo_other = swap(halo)

    mats, turned, turned_other = [], [], []
    for layer in range(2):
        parts = ring_gather(layers[layer], ("dom", "ch"), lambda s: ring(2, s))
        w, t = call(unpack_call, [((7, HALF, LATENT), BF), ((2, LATENT, HALF), BF)], meta, *parts)
        mats.append(w)
        turned.append(t)
        turned_other.append(swap(t))

    big = lambda r, q: 2 * r * q * LATENT
    v_all, e_all, hid = call(
        edge_first,
        [((LATENT, n), BF), ((LATENT, m), BF), ((HALF, m), BF)],
        meta, v_half, v_other, e_half, e_other, halo, halo_other, mats[0], src, dst,
        scratch=[pltpu.VMEM((HALF, n + m), BF), pltpu.VMEM((HALF, n), BF), pltpu.VMEM((m, LATENT), BF)],
        flops=4 * big(HALF, n + m),
    )
    e_new, hid_n = call(
        aggregate,
        [((LATENT, m), BF), ((HALF, n), BF)],
        meta, hid, swap(hid), turned[0], turned_other[0], mats[0], e_all, v_all, dst,
        flops=3 * big(LATENT, m),
    )
    v_new, sender, rows = call(
        send_next,
        [((LATENT, n), BF), ((HALF, n), BF), ((m, HALF), BF)],
        meta, hid_n, swap(hid_n), turned[0], turned_other[0], v_all, mats[1], send,
        flops=2 * big(LATENT, n),
    )
    far = exchange(rows)
    (part,) = call(
        edge_local, [((HALF, m), F32)], meta, v_new, e_new, sender, mats[1], src, dst,
        scratch=[pltpu.VMEM((HALF, n), BF)], flops=3 * big(HALF, m),
    )
    (hid,) = call(
        lambda *refs: edge_far(n, *refs), [((HALF, m), BF)], meta, part, far, src,
        scratch=[pltpu.VMEM((HALF, m), BF)], flops=2 * big(HALF, m),
    )
    e_out, hid_n = call(
        aggregate_last,
        [((64, m), BF), ((HALF, n), BF)],
        meta, hid, swap(hid), turned[1], turned_other[1], mats[1], e_new, v_new, dst,
        scratch=[pltpu.VMEM((LATENT, m), BF)], flops=3 * big(LATENT, m),
    )
    (v_out,) = call(
        finish, [((64, n), BF)], meta, hid_n, swap(hid_n), turned[1], turned_other[1], v_new,
        scratch=[pltpu.VMEM((LATENT, n), BF)], flops=big(LATENT, n),
    )
    return v_out, e_out


def unpack_call(meta, own, nxt, far_a, far_b, prev, mats, turned):
    unpack(meta, own, nxt, far_a, far_b, prev, mats, turned)


def solution(mesh):
    in_specs = (
        P("ch", "dom"),
        P("ch", "dom"),
        P("dom"),
        P("dom"),
        P("dom"),
        P(None, None, None, "ch"),
        P(None, "ch", None),
        P(None, None, None, "ch"),
        P(None, "ch", None),
    )
    out_specs = (P("ch", "dom"), P("ch", "dom"))
    return jax.shard_map(shards, mesh=mesh, in_specs=in_specs, out_specs=out_specs, check_vma=False)
```

profile of v0, /device:TPU:1, one launch (start us, length us, event | category | flops | bytes accessed | tf_op | source)
XLA Modules:
  0.0 166.7 jit_solution(8430442642016043724)
XLA Ops:
  5.1 3.9 %collective-permute-start.1 = (bf16[64,1280]{1,0:T(8,128)(2,1)S(1)}, bf16[64,1280]{1,0:T(8,128)(2,1)S(1)}, u32[]{:S(2)}, u32[]{:S(2)}) collective-permute-start(bf16[64,1280]{1,0:T(8,128)(2,1)S(1)} %pad_maximum_fusion.3.own), channel_id=1, source_target_pairs={{0,2},{1,3},{2,4},{3,5},{4,6},{5,7},{6,0},{7,1},{8,10},{9,11},{10,... | collective-permute-start | bytes 491528 | tf_op jit(solution)/shard_map/ppermute | solution.py:41
  9.0 3.1 %collective-permute-start = (bf16[64,1280]{1,0:T(8,128)(2,1)S(1)}, bf16[64,1280]{1,0:T(8,128)(2,1)S(1)}, u32[]{:S(2)}, u32[]{:S(2)}) collective-permute-start(bf16[64,1280]{1,0:T(8,128)(2,1)S(1)} %pad_maximum_fusion.3.own), channel_id=1, source_target_pairs={{0,6},{1,7},{2,0},{3,1},{4,2},{5,3},{6,4},{7,5},{8,14},{9,15},{10,... | collective-permute-start | bytes 491528 | tf_op jit(solution)/shard_map/ppermute | solution.py:42
  12.1 4.4 %collective-permute-done.1.prev = bf16[64,1280]{1,0:T(8,128)(2,1)S(1)} collective-permute-done((bf16[64,1280]{1,0:T(8,128)(2,1)S(1)}, bf16[64,1280]{1,0:T(8,128)(2,1)S(1)}, u32[]{:S(2)}, u32[]{:S(2)}) %collective-permute-start.1) | collective-permute-done | bytes 163872 | tf_op jit(solution)/shard_map/ppermute | solution.py:41
  16.6 3.6 %collective-permute-start.2 = (bf16[32,1280]{1,0:T(8,128)(2,1)S(1)}, bf16[32,1280]{1,0:T(8,128)(2,1)S(1)}, u32[]{:S(2)}, u32[]{:S(2)}) collective-permute-start(bf16[32,1280]{1,0:T(8,128)(2,1)S(1)} %slice.52), channel_id=1, source_target_pairs={{0,2},{1,3},{2,4},{3,5},{4,6},{5,7},{6,0},{7,1},{8,10},{9,11},{10,... | collective-permute-start | bytes 245768 | tf_op jit(solution)/shard_map/ppermute | solution.py:43
  27.2 3.5 %shard_map.104 = (bf16[256,768]{1,0:T(8,128)(2,1)}, bf16[1024,256]{1,0:T(8,128)(2,1)}) custom-call(s32[5]{0:T(128)} %stack.38.meta.refs_0_, bf16[64,1280]{1,0:T(8,128)(2,1)} %copy-done.22, bf16[64,1280]{1,0:T(8,128)(2,1)} %copy-done.24, bf16[32,1280]{1,0:T(8,128)(2,1)} %copy-done.28, bf16[32,1280]{1,0:T(8,128)(2,1)} %copy-done.29, ...), custom_call_target="tpu_custom_call" | custom-call | flops 402653184 | bytes 659476 | tf_op jit(solution)/shard_map/pallas_call | solution.py:78
  30.6 7.0 %all-to-all-start = ((bf16[32,32,256]{2,1,0:T(8,128)(2,1)}), bf16[32,32,256]{2,1,0:T(8,128)(2,1)S(1)}, u32[]{:S(2)}, u32[]{:S(2)}) async-start(bf16[32,32,256]{2,1,0:T(8,128)(2,1)} %bitcast.37), calls=%async_computation | async-start | bytes 1048576 | tf_op jit(solution)/shard_map/all_to_all | solution.py:268
  44.7 3.5 %collective-permute-start.6 = (bf16[64,1024]{1,0:T(8,128)(2,1)S(1)}, bf16[64,1024]{1,0:T(8,128)(2,1)S(1)}, u32[]{:S(2)}, u32[]{:S(2)}) collective-permute-start(bf16[64,1024]{1,0:T(8,128)(2,1)S(1)} %copy-done.25), channel_id=1, source_target_pairs={{0,2},{1,3},{2,4},{3,5},{4,6},{5,7},{6,0},{7,1},{8,10},{9,11},{10,... | collective-permute-start | bytes 393224 | tf_op jit(solution)/shard_map/ppermute | solution.py:41
  50.6 2.7 %collective-permute-done.13.prev = bf16[4,7,8,512]{3,2,1,0:T(8,128)(2,1)S(1)} collective-permute-done((bf16[4,7,8,512]{3,2,1,0:T(8,128)(2,1)S(1)}, bf16[4,7,8,512]{3,2,1,0:T(8,128)(2,1)S(1)}, u32[]{:S(2)}, u32[]{:S(2)}) %collective-permute-start.13) | collective-permute-done | bytes 229408 | tf_op jit(solution)/shard_map/ppermute | solution.py:260
  59.1 3.6 %collective-permute-start.7 = (bf16[32,1024]{1,0:T(8,128)(2,1)S(1)}, bf16[32,1024]{1,0:T(8,128)(2,1)S(1)}, u32[]{:S(2)}, u32[]{:S(2)}) collective-permute-start(bf16[32,1024]{1,0:T(8,128)(2,1)S(1)} %slice.54), channel_id=1, source_target_pairs={{0,2},{1,3},{2,4},{3,5},{4,6},{5,7},{6,0},{7,1},{8,10},{9,11},{10,... | collective-permute-start | bytes 196616 | tf_op jit(solution)/shard_map/ppermute | solution.py:43
  64.7 3.1 %collective-permute-done.8.far_b = bf16[32,1024]{1,0:T(8,128)(2,1)S(1)} collective-permute-done((bf16[32,1024]{1,0:T(8,128)(2,1)S(1)}, bf16[32,1024]{1,0:T(8,128)(2,1)S(1)}, u32[]{:S(2)}, u32[]{:S(2)}) %collective-permute-start.8) | collective-permute-done | bytes 65568 | tf_op jit(solution)/shard_map/ppermute | solution.py:44
  70.4 4.9 %collective-permute-start.9 = (bf16[256,1024]{1,0:T(8,128)(2,1)}, bf16[256,1024]{1,0:T(8,128)(2,1)S(1)}, u32[]{:S(2)}, u32[]{:S(2)}) collective-permute-start(bf16[256,1024]{1,0:T(8,128)(2,1)} %shard_map.105.e_own), channel_id=1, source_target_pairs={{0,1},{1,0},{2,3},{3,2},{4,5},{5,4},{6,7},{7,6},{8,9},{9,8},{10,11... | collective-permute-start | bytes 1572872 | tf_op jit(solution)/shard_map/ppermute | solution.py:36
  78.7 3.6 %collective-permute-done.16.far_a = bf16[1,4,7,8,512]{4,3,2,1,0:T(8,128)(2,1)S(1)} collective-permute-done((bf16[1,4,7,8,512]{4,3,2,1,0:T(8,128)(2,1)S(1)}, bf16[1,4,7,8,512]{4,3,2,1,0:T(8,128)(2,1)S(1)}, u32[]{:S(2)}, u32[]{:S(2)}) %collective-permute-start.16) | collective-permute-done | bytes 229408 | tf_op jit(solution)/shard_map/ppermute | solution.py:43
  83.7 3.2 %shard_map.107 = (bf16[7,256,512]{2,1,0:T(8,128)(2,1)}, bf16[2,512,256]{2,1,0:T(8,128)(2,1)}) custom-call(s32[5]{0:T(128)} %stack.38.meta.refs_0_, bf16[2,4,7,8,512]{4,3,2,1,0:T(8,128)(2,1)} %get-tuple-element.24.own, bf16[2,4,7,8,512]{4,3,2,1,0:T(8,128)(2,1)} %copy-done.2, bf16[1,4,7,8,512]{4,3,2,1,0:T(8,128)(2,1)} %copy-done.18, ...), custom_call_target="tpu_custom_call" | custom-call | bytes 1835028 | tf_op jit(solution)/shard_map/pallas_call | solution.py:78
  88.9 6.7 %shard_map.108 = (bf16[512,768]{1,0:T(8,128)(2,1)}, bf16[512,1024]{1,0:T(8,128)(2,1)}, bf16[256,1024]{1,0:T(8,128)(2,1)}) custom-call(s32[5]{0:T(128)} %stack.38.meta.refs_0_, bf16[256,768]{1,0:T(8,128)(2,1)} %get-tuple-element.21.v_own, bf16[256,768]{1,0:T(8,128)(2,1)} %collective-permute-done.4.v_other, bf16[256,1024]{1,0:T(8,128)(2,1)} %shard_map.105.e_own, ...), custom_call_target="tpu_custom_call" | custom-call | flops 1879048192 | bytes 4726804 | tf_op jit(solution)/shard_map/pallas_call | solution.py:78
  99.3 8.1 %shard_map.109 = (bf16[512,1024]{1,0:T(8,128)(2,1)}, bf16[256,768]{1,0:T(8,128)(2,1)}) custom-call(s32[5]{0:T(128)} %stack.38.meta.refs_0_, bf16[256,1024]{1,0:T(8,128)(2,1)} %get-tuple-element.26.hid, bf16[256,1024]{1,0:T(8,128)(2,1)} %copy-done.32, bf16[2,512,256]{2,1,0:T(8,128)(2,1)} %get-tuple-element.27.turned, bf16[2,512,256]{2,1,0:T(8,128)(2,1)} %copy-done.9, ...), custom_call_target="tpu_custom_call" | custom-call | flops 1610612736 | bytes 5771284 | tf_op jit(solution)/shard_map/pallas_call | solution.py:78
  111.3 3.6 %collective-permute-done.23.far_a = bf16[1,4,7,8,512]{4,3,2,1,0:T(8,128)(2,1)S(1)} collective-permute-done((bf16[1,4,7,8,512]{4,3,2,1,0:T(8,128)(2,1)S(1)}, bf16[1,4,7,8,512]{4,3,2,1,0:T(8,128)(2,1)S(1)}, u32[]{:S(2)}, u32[]{:S(2)}) %collective-permute-start.23) | collective-permute-done | bytes 229408 | tf_op jit(solution)/shard_map/ppermute | solution.py:43
  116.3 3.2 %shard_map.110 = (bf16[7,256,512]{2,1,0:T(8,128)(2,1)}, bf16[2,512,256]{2,1,0:T(8,128)(2,1)}) custom-call(s32[5]{0:T(128)} %stack.38.meta.refs_0_, bf16[2,4,7,8,512]{4,3,2,1,0:T(8,128)(2,1)} %get-tuple-element.31.own, bf16[2,4,7,8,512]{4,3,2,1,0:T(8,128)(2,1)} %copy-done.4, bf16[1,4,7,8,512]{4,3,2,1,0:T(8,128)(2,1)} %copy-done.19, ...), custom_call_target="tpu_custom_call" | custom-call | bytes 1835028 | tf_op jit(solution)/shard_map/pallas_call | solution.py:78
  120.2 6.3 %shard_map.111 = (bf16[512,768]{1,0:T(8,128)(2,1)}, bf16[256,768]{1,0:T(8,128)(2,1)}, bf16[1024,256]{1,0:T(8,128)(2,1)}) custom-call(s32[5]{0:T(128)} %stack.38.meta.refs_0_, bf16[256,768]{1,0:T(8,128)(2,1)} %get-tuple-element.30.hid, bf16[256,768]{1,0:T(8,128)(2,1)} %copy-done.12, bf16[2,512,256]{2,1,0:T(8,128)(2,1)} %get-tuple-element.27.turned, ...), custom_call_target="tpu_custom_call" | custom-call | flops 805306368 | bytes 4460564 | tf_op jit(solution)/shard_map/pallas_call | solution.py:78
  126.5 6.3 %all-to-all-start.1 = ((bf16[32,32,256]{2,1,0:T(8,128)(2,1)}), bf16[32,32,256]{2,1,0:T(8,128)(2,1)S(1)}, u32[]{:S(2)}, u32[]{:S(2)}) async-start(bf16[32,32,256]{2,1,0:T(8,128)(2,1)} %bitcast.38), calls=%async_computation.1 | async-start | bytes 1048576 | tf_op jit(solution)/shard_map/all_to_all | solution.py:268
  133.9 5.3 %shard_map.112.refs_1_ = f32[256,1024]{1,0:T(8,128)} custom-call(s32[5]{0:T(128)} %stack.38.meta.refs_0_, bf16[512,768]{1,0:T(8,128)(2,1)} %get-tuple-element.33.v_all, bf16[512,1024]{1,0:T(8,128)(2,1)} %get-tuple-element.34.e_all, bf16[256,768]{1,0:T(8,128)(2,1)} %get-tuple-element.35.sender, bf16[7,256,512]{2,1,0:T(8,128)(2,1)} %get-tuple-element.32.mats, ...), custom_call_target="tpu_custom_call" | custom-call | flops 805306368 | bytes 4071444 | tf_op jit(solution)/shard_map/pallas_call | solution.py:78
  139.2 4.0 %all-to-all-done.1 = bf16[32,32,256]{2,1,0:T(8,128)(2,1)S(1)} async-done(((bf16[32,32,256]{2,1,0:T(8,128)(2,1)}), bf16[32,32,256]{2,1,0:T(8,128)(2,1)S(1)}, u32[]{:S(2)}, u32[]{:S(2)}) %all-to-all-start.1) | async-done | bytes 524320 | tf_op jit(solution)/shard_map/all_to_all | solution.py:268
  143.9 3.7 %shard_map.113.hid = bf16[256,1024]{1,0:T(8,128)(2,1)} custom-call(s32[5]{0:T(128)} %stack.38.meta.refs_0_, f32[256,1024]{1,0:T(8,128)} %shard_map.112.refs_1_, bf16[1024,256]{1,0:T(8,128)(2,1)} %bitcast.34, s32[1,1024]{1,0:T(1,128)} %bitcast.42), custom_call_target="tpu_custom_call" | custom-call | flops 536870912 | bytes 1576980 | tf_op jit(solution)/shard_map/pallas_call | solution.py:78
  152.3 8.1 %shard_map.114 = (bf16[64,1024]{1,0:T(8,128)(2,1)}, bf16[256,768]{1,0:T(8,128)(2,1)}) custom-call(s32[5]{0:T(128)} %stack.38.meta.refs_0_, bf16[256,1024]{1,0:T(8,128)(2,1)} %shard_map.113.hid, bf16[256,1024]{1,0:T(8,128)(2,1)} %copy-done.33, bf16[2,512,256]{2,1,0:T(8,128)(2,1)} %get-tuple-element.37.turned, bf16[2,512,256]{2,1,0:T(8,128)(2,1)} %copy-done.8, ...), custom_call_target="tpu_custom_call" | custom-call | flops 1610612736 | bytes 5771284 | tf_op jit(solution)/shard_map/pallas_call | solution.py:78
  163.0 3.6 %shard_map.115 = bf16[64,768]{1,0:T(8,128)(2,1)} custom-call(s32[5]{0:T(128)} %stack.38.meta.refs_0_, bf16[256,768]{1,0:T(8,128)(2,1)} %get-tuple-element.38.hid, bf16[256,768]{1,0:T(8,128)(2,1)} %copy-done.11, bf16[2,512,256]{2,1,0:T(8,128)(2,1)} %get-tuple-element.37.turned, bf16[2,512,256]{2,1,0:T(8,128)(2,1)} %copy-done.8, ...), custom_call_target="tpu_custom_call" | custom-call | flops 402653184 | bytes 2621460 | tf_op jit(solution)/shard_map/pallas_call | solution.py:78
  (139 shorter events, 56.8 us)
Async XLA Ops:
  5.1 11.4 %collective-permute-start.1 = (bf16[64,1280]{1,0:T(8,128)(2,1)S(1)}, bf16[64,1280]{1,0:T(8,128)(2,1)S(1)}, u32[]{:S(2)}, u32[]{:S(2)}) collective-permute-start(bf16[64,1280]{1,0:T(8,128)(2,1)S(1)} %pad_maximum_fusion.3.own), channel_id=1, source_target_pairs={{0,2},{1,3},{2,4},{3,5},{4,6},{5,7},{6,0},{7,1},{8,10},{9,11},{10,... | collective-permute-start | bytes 491528 | tf_op jit(solution)/shard_map/ppermute | solution.py:41
  9.0 11.9 %collective-permute-start = (bf16[64,1280]{1,0:T(8,128)(2,1)S(1)}, bf16[64,1280]{1,0:T(8,128)(2,1)S(1)}, u32[]{:S(2)}, u32[]{:S(2)}) collective-permute-start(bf16[64,1280]{1,0:T(8,128)(2,1)S(1)} %pad_maximum_fusion.3.own), channel_id=1, source_target_pairs={{0,6},{1,7},{2,0},{3,1},{4,2},{5,3},{6,4},{7,5},{8,14},{9,15},{10,... | collective-permute-start | bytes 491528 | tf_op jit(solution)/shard_map/ppermute | solution.py:42
  16.6 7.4 %collective-permute-start.2 = (bf16[32,1280]{1,0:T(8,128)(2,1)S(1)}, bf16[32,1280]{1,0:T(8,128)(2,1)S(1)}, u32[]{:S(2)}, u32[]{:S(2)}) collective-permute-start(bf16[32,1280]{1,0:T(8,128)(2,1)S(1)} %slice.52), channel_id=1, source_target_pairs={{0,2},{1,3},{2,4},{3,5},{4,6},{5,7},{6,0},{7,1},{8,10},{9,11},{10,... | collective-permute-start | bytes 245768 | tf_op jit(solution)/shard_map/ppermute | solution.py:43
  30.6 44.7 %all-to-all-start = ((bf16[32,32,256]{2,1,0:T(8,128)(2,1)}), bf16[32,32,256]{2,1,0:T(8,128)(2,1)S(1)}, u32[]{:S(2)}, u32[]{:S(2)}) async-start(bf16[32,32,256]{2,1,0:T(8,128)(2,1)} %bitcast.37), calls=%async_computation | async-start | bytes 1048576 | tf_op jit(solution)/shard_map/all_to_all | solution.py:268
  41.0 8.0 %collective-permute-start.11 = (bf16[4,7,8,512]{3,2,1,0:T(8,128)(2,1)S(1)}, bf16[4,7,8,512]{3,2,1,0:T(8,128)(2,1)S(1)}, u32[]{:S(2)}, u32[]{:S(2)}) collective-permute-start(bf16[4,7,8,512]{3,2,1,0:T(8,128)(2,1)S(1)} %fusion.own), channel_id=1, source_target_pairs={{0,96},{1,25},{2,98},{3,27},{4,100},{5,29},{6,102},{7,31},{8,104},... | collective-permute-start | bytes 688136 | tf_op jit(solution)/shard_map/ppermute | solution.py:260
  43.5 7.1 %collective-permute-start.12 = (bf16[4,7,8,512]{3,2,1,0:T(8,128)(2,1)S(1)}, bf16[4,7,8,512]{3,2,1,0:T(8,128)(2,1)S(1)}, u32[]{:S(2)}, u32[]{:S(2)}) collective-permute-start(bf16[4,7,8,512]{3,2,1,0:T(8,128)(2,1)S(1)} %fusion.own), channel_id=1, source_target_pairs={{0,64},{1,17},{2,66},{3,19},{4,68},{5,21},{6,70},{7,23},{8,72},{9,... | collective-permute-start | bytes 688136 | tf_op jit(solution)/shard_map/ppermute | solution.py:260
  44.1 9.3 %collective-permute-start.13 = (bf16[4,7,8,512]{3,2,1,0:T(8,128)(2,1)S(1)}, bf16[4,7,8,512]{3,2,1,0:T(8,128)(2,1)S(1)}, u32[]{:S(2)}, u32[]{:S(2)}) collective-permute-start(bf16[4,7,8,512]{3,2,1,0:T(8,128)(2,1)S(1)} %fusion.own), channel_id=1, source_target_pairs={{0,32},{1,9},{2,34},{3,11},{4,36},{5,13},{6,38},{7,15},{8,40},{9,1... | collective-permute-start | bytes 688136 | tf_op jit(solution)/shard_map/ppermute | solution.py:260
  44.7 14.4 %collective-permute-start.6 = (bf16[64,1024]{1,0:T(8,128)(2,1)S(1)}, bf16[64,1024]{1,0:T(8,128)(2,1)S(1)}, u32[]{:S(2)}, u32[]{:S(2)}) collective-permute-start(bf16[64,1024]{1,0:T(8,128)(2,1)S(1)} %copy-done.25), channel_id=1, source_target_pairs={{0,2},{1,3},{2,4},{3,5},{4,6},{5,7},{6,0},{7,1},{8,10},{9,11},{10,... | collective-permute-start | bytes 393224 | tf_op jit(solution)/shard_map/ppermute | solution.py:41
  48.1 14.6 %collective-permute-start.5 = (bf16[64,1024]{1,0:T(8,128)(2,1)S(1)}, bf16[64,1024]{1,0:T(8,128)(2,1)S(1)}, u32[]{:S(2)}, u32[]{:S(2)}) collective-permute-start(bf16[64,1024]{1,0:T(8,128)(2,1)S(1)} %copy-done.25), channel_id=1, source_target_pairs={{0,6},{1,7},{2,0},{3,1},{4,2},{5,3},{6,4},{7,5},{8,14},{9,15},{10,... | collective-permute-start | bytes 393224 | tf_op jit(solution)/shard_map/ppermute | solution.py:42
  56.4 19.4 %collective-permute-start.15 = (bf16[2,4,7,8,512]{4,3,2,1,0:T(8,128)(2,1)}, bf16[2,4,7,8,512]{4,3,2,1,0:T(8,128)(2,1)S(1)}, u32[]{:S(2)}, u32[]{:S(2)}) collective-permute-start(bf16[2,4,7,8,512]{4,3,2,1,0:T(8,128)(2,1)} %get-tuple-element.24.own), channel_id=1, source_target_pairs={{0,8},{1,33},{2,10},{3,35},{4,12},{5,37},{6,14},{7,39},{8,16},{9,4... | collective-permute-start | bytes 1376264 | tf_op jit(solution)/shard_map/ppermute | solution.py:41
  57.4 18.5 %collective-permute-start.14 = (bf16[2,4,7,8,512]{4,3,2,1,0:T(8,128)(2,1)}, bf16[2,4,7,8,512]{4,3,2,1,0:T(8,128)(2,1)S(1)}, u32[]{:S(2)}, u32[]{:S(2)}) collective-permute-start(bf16[2,4,7,8,512]{4,3,2,1,0:T(8,128)(2,1)} %get-tuple-element.24.own), channel_id=1, source_target_pairs={{0,24},{1,97},{2,26},{3,99},{4,28},{5,101},{6,30},{7,103},{8,0},{9... | collective-permute-start | bytes 1376264 | tf_op jit(solution)/shard_map/ppermute | solution.py:42
  70.4 17.6 %collective-permute-start.9 = (bf16[256,1024]{1,0:T(8,128)(2,1)}, bf16[256,1024]{1,0:T(8,128)(2,1)S(1)}, u32[]{:S(2)}, u32[]{:S(2)}) collective-permute-start(bf16[256,1024]{1,0:T(8,128)(2,1)} %shard_map.105.e_own), channel_id=1, source_target_pairs={{0,1},{1,0},{2,3},{3,2},{4,5},{5,4},{6,7},{7,6},{8,9},{9,8},{10,11... | collective-permute-start | bytes 1572872 | tf_op jit(solution)/shard_map/ppermute | solution.py:36
  75.3 12.7 %collective-permute-start.10 = (bf16[1024,256]{1,0:T(8,128)(2,1)S(1)}, bf16[1024,256]{1,0:T(8,128)(2,1)S(1)}, u32[]{:S(2)}, u32[]{:S(2)}) collective-permute-start(bf16[1024,256]{1,0:T(8,128)(2,1)S(1)} %bitcast.35), channel_id=1, source_target_pairs={{0,1},{1,0},{2,3},{3,2},{4,5},{5,4},{6,7},{7,6},{8,9},{9,8},{10,11... | collective-permute-start | bytes 1572872 | tf_op jit(solution)/shard_map/ppermute | solution.py:36
  75.6 12.4 %collective-permute-start.4 = (bf16[256,768]{1,0:T(8,128)(2,1)S(1)}, bf16[256,768]{1,0:T(8,128)(2,1)}, u32[]{:S(2)}, u32[]{:S(2)}) collective-permute-start(bf16[256,768]{1,0:T(8,128)(2,1)S(1)} %copy-done.34), channel_id=1, source_target_pairs={{0,1},{1,0},{2,3},{3,2},{4,5},{5,4},{6,7},{7,6},{8,9},{9,8},{10,11... | collective-permute-start | bytes 1179656 | tf_op jit(solution)/shard_map/ppermute | solution.py:36
  75.9 6.5 %collective-permute-start.16 = (bf16[1,4,7,8,512]{4,3,2,1,0:T(8,128)(2,1)S(1)}, bf16[1,4,7,8,512]{4,3,2,1,0:T(8,128)(2,1)S(1)}, u32[]{:S(2)}, u32[]{:S(2)}) collective-permute-start(bf16[1,4,7,8,512]{4,3,2,1,0:T(8,128)(2,1)S(1)} %slice.60), channel_id=1, source_target_pairs={{0,8},{1,33},{2,10},{3,35},{4,12},{5,37},{6,14},{7,39},{8,16},{9,4... | collective-permute-start | bytes 688136 | tf_op jit(solution)/shard_map/ppermute | solution.py:43
  76.0 6.3 %collective-permute-start.17 = (bf16[1,4,7,8,512]{4,3,2,1,0:T(8,128)(2,1)S(1)}, bf16[1,4,7,8,512]{4,3,2,1,0:T(8,128)(2,1)S(1)}, u32[]{:S(2)}, u32[]{:S(2)}) collective-permute-start(bf16[1,4,7,8,512]{4,3,2,1,0:T(8,128)(2,1)S(1)} %slice.61), channel_id=1, source_target_pairs={{0,24},{1,97},{2,26},{3,99},{4,28},{5,101},{6,30},{7,103},{8,0},{9... | collective-permute-start | bytes 688136 | tf_op jit(solution)/shard_map/ppermute | solution.py:44
  86.8 11.5 %collective-permute-start.19 = (bf16[2,512,256]{2,1,0:T(8,128)(2,1)}, bf16[2,512,256]{2,1,0:T(8,128)(2,1)S(1)}, u32[]{:S(2)}, u32[]{:S(2)}) collective-permute-start(bf16[2,512,256]{2,1,0:T(8,128)(2,1)} %get-tuple-element.27.turned), channel_id=1, source_target_pairs={{0,1},{1,0},{2,3},{3,2},{4,5},{5,4},{6,7},{7,6},{8,9},{9,8},{10,11... | collective-permute-start | bytes 1572872 | tf_op jit(solution)/shard_map/ppermute | solution.py:36
  95.6 12.8 %collective-permute-start.22 = (bf16[2,4,7,8,512]{4,3,2,1,0:T(8,128)(2,1)S(1)}, bf16[2,4,7,8,512]{4,3,2,1,0:T(8,128)(2,1)S(1)}, u32[]{:S(2)}, u32[]{:S(2)}) collective-permute-start(bf16[2,4,7,8,512]{4,3,2,1,0:T(8,128)(2,1)S(1)} %copy-done.10), channel_id=1, source_target_pairs={{0,8},{1,33},{2,10},{3,35},{4,12},{5,37},{6,14},{7,39},{8,16},{9,4... | collective-permute-start | bytes 1376264 | tf_op jit(solution)/shard_map/ppermute | solution.py:41
  95.7 12.8 %collective-permute-start.21 = (bf16[2,4,7,8,512]{4,3,2,1,0:T(8,128)(2,1)S(1)}, bf16[2,4,7,8,512]{4,3,2,1,0:T(8,128)(2,1)S(1)}, u32[]{:S(2)}, u32[]{:S(2)}) collective-permute-start(bf16[2,4,7,8,512]{4,3,2,1,0:T(8,128)(2,1)S(1)} %copy-done.10), channel_id=1, source_target_pairs={{0,24},{1,97},{2,26},{3,99},{4,28},{5,101},{6,30},{7,103},{8,0},{9... | collective-permute-start | bytes 1376264 | tf_op jit(solution)/shard_map/ppermute | solution.py:42
  107.4 12.1 %collective-permute-start.20 = (bf16[256,768]{1,0:T(8,128)(2,1)}, bf16[256,768]{1,0:T(8,128)(2,1)S(1)}, u32[]{:S(2)}, u32[]{:S(2)}) collective-permute-start(bf16[256,768]{1,0:T(8,128)(2,1)} %get-tuple-element.30.hid), channel_id=1, source_target_pairs={{0,1},{1,0},{2,3},{3,2},{4,5},{5,4},{6,7},{7,6},{8,9},{9,8},{10,11... | collective-permute-start | bytes 1179656 | tf_op jit(solution)/shard_map/ppermute | solution.py:36
  108.4 6.5 %collective-permute-start.23 = (bf16[1,4,7,8,512]{4,3,2,1,0:T(8,128)(2,1)S(1)}, bf16[1,4,7,8,512]{4,3,2,1,0:T(8,128)(2,1)S(1)}, u32[]{:S(2)}, u32[]{:S(2)}) collective-permute-start(bf16[1,4,7,8,512]{4,3,2,1,0:T(8,128)(2,1)S(1)} %slice.62), channel_id=1, source_target_pairs={{0,8},{1,33},{2,10},{3,35},{4,12},{5,37},{6,14},{7,39},{8,16},{9,4... | collective-permute-start | bytes 688136 | tf_op jit(solution)/shard_map/ppermute | solution.py:43
  108.5 6.3 %collective-permute-start.24 = (bf16[1,4,7,8,512]{4,3,2,1,0:T(8,128)(2,1)S(1)}, bf16[1,4,7,8,512]{4,3,2,1,0:T(8,128)(2,1)S(1)}, u32[]{:S(2)}, u32[]{:S(2)}) collective-permute-start(bf16[1,4,7,8,512]{4,3,2,1,0:T(8,128)(2,1)S(1)} %slice.63), channel_id=1, source_target_pairs={{0,24},{1,97},{2,26},{3,99},{4,28},{5,101},{6,30},{7,103},{8,0},{9... | collective-permute-start | bytes 688136 | tf_op jit(solution)/shard_map/ppermute | solution.py:44
  126.5 16.6 %all-to-all-start.1 = ((bf16[32,32,256]{2,1,0:T(8,128)(2,1)}), bf16[32,32,256]{2,1,0:T(8,128)(2,1)S(1)}, u32[]{:S(2)}, u32[]{:S(2)}) async-start(bf16[32,32,256]{2,1,0:T(8,128)(2,1)} %bitcast.38), calls=%async_computation.1 | async-start | bytes 1048576 | tf_op jit(solution)/shard_map/all_to_all | solution.py:268
  132.8 17.0 %collective-permute-start.26 = (bf16[2,512,256]{2,1,0:T(8,128)(2,1)S(1)}, bf16[2,512,256]{2,1,0:T(8,128)(2,1)S(1)}, u32[]{:S(2)}, u32[]{:S(2)}) collective-permute-start(bf16[2,512,256]{2,1,0:T(8,128)(2,1)S(1)} %copy-done.7), channel_id=1, source_target_pairs={{0,1},{1,0},{2,3},{3,2},{4,5},{5,4},{6,7},{7,6},{8,9},{9,8},{10,11... | collective-permute-start | bytes 1572872 | tf_op jit(solution)/shard_map/ppermute | solution.py:36
  (41 other events, 237.7 us)
where the time goes:
time: 168 us; the launch traced here: 167 us
  starting transfers between devices  60.3 us (36%)
  Pallas kernels  55.8 us (33%)
  waiting for transfers between devices  31.5 us (19%)
  local copies, waits for them, and re-layouts  17.2 us (10%)
    pallas_call x12, Pallas kernels, call(): pl.pallas_call(kernel, out_shape=[jax.ShapeDtypeStruct(s, d) for s, d in...  55.8 us
    all_to_all x2, starting transfers between devices, exchange(): lax.all_to_all(rows.reshape(32, SLOTS, HALF), 'dom', 0, 0, tiled=True)  13.3 us
    unnamed x74, local copies, waits for them, and re-layouts  12.5 us
    ppermute x9, starting transfers between devices, swap(): return lax.ppermute(x, 'ch', CORE)  11.1 us
    ppermute x4, waiting for transfers between devices, ring_gather(): far_a = lax.ppermute(prev[:half], axis, perm(1))  8.83 us
    ppermute x4, starting transfers between devices, ring_gather(): prev = lax.ppermute(x, axis, perm(1))  8.48 us
    ppermute x4, starting transfers between devices, ring_gather(): far_b = lax.ppermute(nxt[half:], axis, perm(3))  8.24 us
    ppermute x4, starting transfers between devices, ring_gather(): nxt = lax.ppermute(x, axis, perm(3))  8.06 us
  transfers between devices with their start and end apart: 30, of which 13 were waited for; matrix products, arithmetic and copies ran while one was open for 2% of the time, Pallas kernels for 21%

commit v1 on v0

--- a/solution.py
+++ b/solution.py
@@ -1,3 +1,5 @@
+import functools
+
 import jax
 import jax.numpy as jnp
 from jax import lax
@@ -72,8 +74,8 @@
     lax.fori_loop(0, n // CHUNK, step, 0)
 
 
-def call(kernel, outs, *args, scratch=(), flops=0):
-    specs = [SMEM] + [VMEM] * (len(args) - 1)
+def call(kernel, outs, *args, scratch=(), flops=0, space=VMEM):
+    specs = [SMEM] + [space] * (len(args) - 1)
     moved = sum(a.size * a.dtype.itemsize for a in args)
     return pl.pallas_call(
         kernel,
@@ -81,20 +83,21 @@
         in_specs=specs,
         out_specs=[VMEM] * len(outs),
         scratch_shapes=list(scratch),
+        compiler_params=pltpu.CompilerParams(vmem_limit_bytes=6 << 20),
         cost_estimate=pl.CostEstimate(flops=flops, bytes_accessed=moved, transcendentals=0),
     )(*args)
 
 
-def place_half(meta, parts, out):
+def place_half(meta, parts, out, col):
     own, nxt, far_a, far_b, prev = parts
     zi = meta[0]
     at = lambda s: pl.multiple_of(((zi + s) & 3) * 64, 64)
-    n = out.shape[1]
-    out[pl.ds(at(0), 64), :] = own[:, :n]
-    out[pl.ds(at(1), 64), :] = nxt[:, :n]
-    out[pl.ds(at(2), 32), :] = far_a[:, :n]
-    out[pl.ds(at(2) + 32, 32), :] = far_b[:, :n]
-    out[pl.ds(at(3), 64), :] = prev[:, :n]
+    cols = slice(col, col + out.shape[1])
+    out[pl.ds(at(0), 64), :] = own[:, cols]
+    out[pl.ds(at(1), 64), :] = nxt[:, cols]
+    out[pl.ds(at(2), 32), :] = far_a[:, cols]
+    out[pl.ds(at(2) + 32, 32), :] = far_b[:, cols]
+    out[pl.ds(at(3), 64), :] = prev[:, cols]
 
 
 def select_rows(send, x, rows):
@@ -105,41 +108,53 @@
 
 
 def send_first(meta, own, nxt, far_a, far_b, prev, send, half, rows):
-    place_half(meta, (own, nxt, far_a, far_b, prev), half)
+    place_half(meta, (own, nxt, far_a, far_b, prev), half, 0)
     select_rows(send, half[...], rows)
 
 
 def gather_edges(meta, own, nxt, far_a, far_b, prev, half):
-    place_half(meta, (own, nxt, far_a, far_b, prev), half)
-
-
-def split_layers(meta, own, nxt, far, prev, one, two):
-    for s, part in enumerate((own, nxt, far, prev)):
-        a = (meta[1] + s) & 3
-
-        @pl.when(a < 2)
-        def _():
-            one[a] = part[...]
-
-        @pl.when(a >= 2)
-        def _():
-            two[a - 2] = part[...]
-
-
-def unpack(meta, own, nxt, far_a, far_b, prev, mats, outs):
-    def rows_of(ref, a, m):
-        return ref[a, :, m].astype(F32).reshape(32, LATENT)
-
-    pieces = ((own, own), (nxt, nxt), (far_a, far_b), (prev, prev))
-    for m in range(7):
-        for s in range(4):
-            at = pl.multiple_of(((meta[2] + s) & 3) * 64, 64)
-            for a in range(2):
-                ref = pieces[s][a]
-                rows = rows_of(ref, a if ref.shape[0] == 2 else 0, m)
-                mats[m, pl.ds(at + 32 * a, 32), :] = rows.astype(BF)
-    outs[0] = mats[3].astype(F32).T.astype(BF)
-    outs[1] = mats[6].astype(F32).T.astype(BF)
+    place_half(meta, (own, nxt, far_a, far_b, prev), half, own.shape[1] - half.shape[1])
+
+
+def copy_all(copies, sem):
+    copies = [pltpu.make_async_copy(a, b, sem.at[i]) for i, (a, b) in enumerate(copies)]
+    for copy in copies:
+        copy.start()
+    for copy in copies:
+        copy.wait()
+
+
+def cut_weights(meta, w_e, w_eo, w_n, w_no, piece, sem):
+    lay = meta[1] >> 1
+    rows = pl.ds(pl.multiple_of(8 * ((meta[1] & 1) * 4 + meta[2]), 8), 8)
+    copies = [
+        (w_e.at[lay, :, rows], piece.at[0:3]),
+        (w_eo.at[lay, rows], piece.at[3]),
+        (w_n.at[lay, :, rows], piece.at[4:6]),
+        (w_no.at[lay, rows], piece.at[6]),
+    ]
+    copy_all(copies, sem)
+
+
+def beside(meta, v, e, piece, both, sem):
+    n = v.shape[1]
+    copy_all([(v, both.at[:, :n]), (e, both.at[:, n:])], sem)
+
+
+def unpack(layer, meta, own, nxt, far_a, far_b, prev, mats, turned):
+    for s in range(4):
+        for r in range(4):
+            a = (meta[1] + r) & 3
+            at = pl.multiple_of((((meta[2] + s) & 3) * 2 + (a & 1)) * 32, 32)
+            ref, row = ((own, r), (nxt, r), (far_a, r) if r < 2 else (far_b, r - 2), (prev, r))[s]
+
+            @pl.when((a >> 1) == layer)
+            def _():
+                for m in range(7):
+                    mats[m, pl.ds(at, 32), :] = ref[row, :, m].astype(F32).reshape(32, LATENT).astype(BF)
+
+    turned[0] = mats[3].astype(F32).T.astype(BF)
+    turned[1] = mats[6].astype(F32).T.astype(BF)
 
 
 def interleave(meta, own, other, out):
@@ -245,23 +260,24 @@
     meta = jnp.stack([c >> 1, first, second, k, c]).astype(jnp.int32)
     send, src, dst = (a.reshape(1, -1) for a in (send_rows, edge_src, edge_dst))
 
-    row = 8 * ((first & 1) * 4 + second)
-
-    def cut(w):
-        return lax.dynamic_slice(w, (first >> 1, 0, row, 0), (1, w.shape[1], 8, LATENT)).reshape(-1, LATENT)
-
-    piece = [cut(jnp.swapaxes(w_edge_in, 2, 3)), cut(w_edge_out[:, None]), cut(jnp.swapaxes(w_node_in, 2, 3)), cut(w_node_out[:, None])]
-    piece = jnp.concatenate(piece + [piece[-1]])
-    v_parts = ring_gather(jnp.concatenate([node_feats, piece], axis=1), "ch", z_shift)
-    e_parts = ring_gather(lax.optimization_barrier((edge_feats, v_parts[1], v_parts[4]))[0], "ch", z_shift)
-
-    own, nxt, far_a, far_b, prev = (p[:, n:] for p in v_parts)
-    wz = jnp.stack([own, nxt, jnp.concatenate([far_a, far_b]), prev])[:, :56].reshape(4, 7, 8, LATENT)
-    w_parts = [wz] + [lax.ppermute(wz, ("dom", "ch"), ring(1, s)) for s in (3, 2, 1)]
-    layers = call(split_layers, [((2, 4, 7, 8, LATENT), BF)] * 2, meta, *w_parts)
+    in_hbm = lambda a: pltpu.with_memory_space_constraint(a, pltpu.HBM)
+    weights = (jnp.swapaxes(w_edge_in, 2, 3), w_edge_out, jnp.swapaxes(w_node_in, 2, 3), w_node_out)
+    anywhere = pl.BlockSpec(memory_space=pl.ANY)
+    (piece,) = call(
+        cut_weights, [((7, 8, LATENT), BF)], meta, *map(in_hbm, weights),
+        scratch=[pltpu.SemaphoreType.DMA((4,))], space=pl.BlockSpec(memory_space=pltpu.HBM),
+    )
+    (both,) = call(
+        beside, [((64, n + m), BF)], meta, in_hbm(node_feats), in_hbm(edge_feats), piece,
+        scratch=[pltpu.SemaphoreType.DMA((2,))], space=anywhere,
+    )
+    wz = jnp.stack([piece] + [lax.ppermute(piece, "ch", z_shift(s)) for s in (1, 3, 2)])
+    parts = ring_gather(both, "ch", z_shift)
+    one = jnp.stack([wz] + [lax.ppermute(wz, ("dom", "ch"), ring(1, s)) for s in (3, 2, 1)])
+    w_parts = ring_gather(one, ("dom", "ch"), lambda s: ring(2, s))
 
     v_half, rows = call(
-        send_first, [((HALF, n), BF), ((m, HALF), BF)], meta, *v_parts, send, flops=2 * HALF * n * m
+        send_first, [((HALF, n), BF), ((m, HALF), BF)], meta, *parts, send, flops=2 * HALF * n * m
     )
 
     def exchange(rows):
@@ -269,14 +285,14 @@
 
     halo = exchange(rows)
     v_other = swap(v_half)
-    (e_half,) = call(gather_edges, [((HALF, m), BF)], meta, *e_parts)
+    (e_half,) = call(gather_edges, [((HALF, m), BF)], meta, *parts)
     e_other = swap(e_half)
     halo_other = swap(halo)
 
     mats, turned, turned_other = [], [], []
     for layer in range(2):
-        parts = ring_gather(layers[layer], ("dom", "ch"), lambda s: ring(2, s))
-        w, t = call(unpack_call, [((7, HALF, LATENT), BF), ((2, LATENT, HALF), BF)], meta, *parts)
+        unpack_layer = functools.partial(unpack, layer)
+        w, t = call(unpack_layer, [((7, HALF, LATENT), BF), ((2, LATENT, HALF), BF)], meta, *w_parts)
         mats.append(w)
         turned.append(t)
         turned_other.append(swap(t))
@@ -321,10 +337,6 @@
         scratch=[pltpu.VMEM((LATENT, n), BF)], flops=big(LATENT, n),
     )
     return v_out, e_out
-
-
-def unpack_call(meta, own, nxt, far_a, far_b, prev, mats, turned):
-    unpack(meta, own, nxt, far_a, far_b, prev, mats, turned)
 
 
 def solution(mesh):

time: 168 us -> 139 us (0.83)
  Pallas kernels: 55.8 us -> 36.6 us
  local copies, waits for them, and re-layouts: 17.2 us -> 8.79 us
  waiting for transfers between devices: 31.5 us -> 34.8 us
  starting transfers between devices: 60.3 us -> 57.2 us
    pallas_call x12 -> x13, Pallas kernels: 55.8 us -> 36.6 us  [call(): pl.pallas_call(kernel, out_shape=[jax.ShapeDtypeStruct(s, d) for s, d in...]
    ppermute x0 -> x3, starting transfers between devices: none -> 7.95 us  [shards(): lax.ppermute(piece, 'ch', z_shift(s))]
    ppermute x0 -> x3, waiting for transfers between devices: none -> 7.77 us  [shards(): lax.ppermute(piece, 'ch', z_shift(s))]
    ppermute x4 -> x2, starting transfers between devices: 8.24 us -> 3.61 us  [ring_gather(): far_b = lax.ppermute(nxt[half:], axis, perm(3))]
    ppermute x3, waiting for transfers between devices: 4.57 us -> 0.01 us  [shards(): lax.ppermute(wz, ('dom', 'ch'), ring(1, s))]
    ppermute x4 -> x2, starting transfers between devices: 7.41 us -> 3.11 us  [ring_gather(): far_a = lax.ppermute(prev[:half], axis, perm(1))]
    unnamed x74 -> x54, local copies, waits for them, and re-layouts: 12.5 us -> 8.63 us
    ppermute x4 -> x2, starting transfers between devices: 8.06 us -> 4.56 us  [ring_gather(): nxt = lax.ppermute(x, axis, perm(3))]
  transfers between devices with their start and end apart: 30 -> 25, of which waited for: 13 -> 11; matrix products, arithmetic and copies ran while one was open for 2% -> 0% of each run, Pallas kernels for 21% -> 11%
where the time goes in v1:
time: 139 us; the launch traced here: 138 us
  starting transfers between devices  57.2 us (41%)
  Pallas kernels  36.6 us (26%)
  waiting for transfers between devices  34.8 us (25%)
  local copies, waits for them, and re-layouts  8.79 us (6%)
    pallas_call x13, Pallas kernels, call(): pl.pallas_call(kernel, out_shape=[jax.ShapeDtypeStruct(s, d) for s, d in...  36.6 us
    all_to_all x2, starting transfers between devices, exchange(): lax.all_to_all(rows.reshape(32, SLOTS, HALF), 'dom', 0, 0, tiled=True)  16 us
    ppermute x9, starting transfers between devices, swap(): return lax.ppermute(x, 'ch', CORE)  13.1 us
    unnamed x54, local copies, waits for them, and re-layouts  8.63 us
    ppermute x3, starting transfers between devices, shards(): lax.ppermute(piece, 'ch', z_shift(s))  7.95 us
    ppermute x3, waiting for transfers between devices, shards(): lax.ppermute(piece, 'ch', z_shift(s))  7.77 us
    ppermute x2, waiting for transfers between devices, ring_gather(): far_a = lax.ppermute(prev[:half], axis, perm(1))  6.8 us
    ppermute x2, waiting for transfers between devices, ring_gather(): prev = lax.ppermute(x, axis, perm(1))  6.75 us
  transfers between devices with their start and end apart: 25, of which 11 were waited for; matrix products, arithmetic and copies ran while one was open for 0% of the time, Pallas kernels for 11%

profile of v1, /device:TPU:1, one launch (start us, length us, event | category | flops | bytes accessed | tf_op | source)
XLA Modules:
  0.0 138.5 jit_solution(4588372480742237245)
XLA Ops:
  3.6 3.9 %collective-permute-start.1 = (bf16[64,1792]{1,0:T(8,128)(2,1)S(1)}, bf16[64,1792]{1,0:T(8,128)(2,1)S(1)}, u32[]{:S(2)}, u32[]{:S(2)}) collective-permute-start(bf16[64,1792]{1,0:T(8,128)(2,1)S(1)} %shard_map.105.own), channel_id=1, source_target_pairs={{0,2},{1,3},{2,4},{3,5},{4,6},{5,7},{6,0},{7,1},{8,10},{9,11},{10,... | collective-permute-start | bytes 688136 | tf_op jit(solution)/shard_map/ppermute | solution.py:43
  7.5 3.1 %collective-permute-start = (bf16[64,1792]{1,0:T(8,128)(2,1)S(1)}, bf16[64,1792]{1,0:T(8,128)(2,1)S(1)}, u32[]{:S(2)}, u32[]{:S(2)}) collective-permute-start(bf16[64,1792]{1,0:T(8,128)(2,1)S(1)} %shard_map.105.own), channel_id=1, source_target_pairs={{0,6},{1,7},{2,0},{3,1},{4,2},{5,3},{6,4},{7,5},{8,14},{9,15},{10,... | collective-permute-start | bytes 688136 | tf_op jit(solution)/shard_map/ppermute | solution.py:44
  11.7 2.5 %collective-permute-start.8 = (bf16[7,8,512]{2,1,0:T(8,128)(2,1)S(1)}, bf16[7,8,512]{2,1,0:T(8,128)(2,1)S(1)}, u32[]{:S(2)}, u32[]{:S(2)}) collective-permute-start(bf16[7,8,512]{2,1,0:T(8,128)(2,1)S(1)} %shard_map.104.piece), channel_id=1, source_target_pairs={{0,6},{1,7},{2,0},{3,1},{4,2},{5,3},{6,4},{7,5},{8,14},{9,15},{10,... | collective-permute-start | bytes 172040 | tf_op jit(solution)/shard_map/ppermute | solution.py:274
  14.2 4.4 %collective-permute-start.9 = (bf16[7,8,512]{2,1,0:T(8,128)(2,1)S(1)}, bf16[7,8,512]{2,1,0:T(8,128)(2,1)S(1)}, u32[]{:S(2)}, u32[]{:S(2)}) collective-permute-start(bf16[7,8,512]{2,1,0:T(8,128)(2,1)S(1)} %shard_map.104.piece), channel_id=1, source_target_pairs={{0,4},{1,5},{2,6},{3,7},{4,0},{5,1},{6,2},{7,3},{8,12},{9,13},{10,... | collective-permute-start | bytes 172040 | tf_op jit(solution)/shard_map/ppermute | solution.py:274
  19.1 7.3 %collective-permute-done.8 = bf16[7,8,512]{2,1,0:T(8,128)(2,1)S(1)} collective-permute-done((bf16[7,8,512]{2,1,0:T(8,128)(2,1)S(1)}, bf16[7,8,512]{2,1,0:T(8,128)(2,1)S(1)}, u32[]{:S(2)}, u32[]{:S(2)}) %collective-permute-start.8) | collective-permute-done | bytes 57376 | tf_op jit(solution)/shard_map/ppermute | solution.py:274
  26.4 2.5 %collective-permute-start.10 = (bf16[4,7,8,512]{3,2,1,0:T(8,128)(2,1)S(1)}, bf16[4,7,8,512]{3,2,1,0:T(8,128)(2,1)S(1)}, u32[]{:S(2)}, u32[]{:S(2)}) collective-permute-start(bf16[4,7,8,512]{3,2,1,0:T(8,128)(2,1)S(1)} %get-tuple-element.35), channel_id=1, source_target_pairs={{0,96},{1,25},{2,98},{3,27},{4,100},{5,29},{6,102},{7,31},{8,104},... | collective-permute-start | bytes 688136 | tf_op jit(solution)/shard_map/ppermute | solution.py:276
  30.1 3.0 %collective-permute-start.2 = (bf16[32,1792]{1,0:T(8,128)(2,1)S(1)}, bf16[32,1792]{1,0:T(8,128)(2,1)S(1)}, u32[]{:S(2)}, u32[]{:S(2)}) collective-permute-start(bf16[32,1792]{1,0:T(8,128)(2,1)S(1)} %slice.16), channel_id=1, source_target_pairs={{0,2},{1,3},{2,4},{3,5},{4,6},{5,7},{6,0},{7,1},{8,10},{9,11},{10,... | collective-permute-start | bytes 344072 | tf_op jit(solution)/shard_map/ppermute | solution.py:45
  33.8 2.4 %collective-permute-done.2.far_a = bf16[32,1792]{1,0:T(8,128)(2,1)S(1)} collective-permute-done((bf16[32,1792]{1,0:T(8,128)(2,1)S(1)}, bf16[32,1792]{1,0:T(8,128)(2,1)S(1)}, u32[]{:S(2)}, u32[]{:S(2)}) %collective-permute-start.2) | collective-permute-done | bytes 114720 | tf_op jit(solution)/shard_map/ppermute | solution.py:45
  36.2 3.0 %collective-permute-done.3.far_b = bf16[32,1792]{1,0:T(8,128)(2,1)S(1)} collective-permute-done((bf16[32,1792]{1,0:T(8,128)(2,1)S(1)}, bf16[32,1792]{1,0:T(8,128)(2,1)S(1)}, u32[]{:S(2)}, u32[]{:S(2)}) %collective-permute-start.3) | collective-permute-done | bytes 114720 | tf_op jit(solution)/shard_map/ppermute | solution.py:46
  39.3 2.8 %shard_map.106 = (bf16[256,768]{1,0:T(8,128)(2,1)S(1)}, bf16[1024,256]{1,0:T(8,128)(2,1)}) custom-call(s32[5]{0:T(128)S(1)} %stack.53.meta.refs_0_, bf16[64,1792]{1,0:T(8,128)(2,1)S(1)} %shard_map.105.own, bf16[64,1792]{1,0:T(8,128)(2,1)S(1)} %collective-permute-done.nxt, bf16[32,1792]{1,0:T(8,128)(2,1)S(1)} %collective-permute-done.2.far_a, ...), custom_call_target="tpu_custom_call" | custom-call | flops 402653184 | bytes 921620 | tf_op jit(solution)/shard_map/pallas_call | solution.py:80
  42.9 8.2 %all-to-all-start = ((bf16[32,32,256]{2,1,0:T(8,128)(2,1)}), bf16[32,32,256]{2,1,0:T(8,128)(2,1)S(1)}, u32[]{:S(2)}, u32[]{:S(2)}) async-start(bf16[32,32,256]{2,1,0:T(8,128)(2,1)} %bitcast.8), calls=%async_computation | async-start | bytes 1048576 | tf_op jit(solution)/shard_map/all_to_all | solution.py:284
  55.4 2.8 %collective-permute-start.5 = (bf16[256,1024]{1,0:T(8,128)(2,1)}, bf16[256,1024]{1,0:T(8,128)(2,1)}, u32[]{:S(2)}, u32[]{:S(2)}) collective-permute-start(bf16[256,1024]{1,0:T(8,128)(2,1)} %shard_map.107.e_own), channel_id=1, source_target_pairs={{0,1},{1,0},{2,3},{3,2},{4,5},{5,4},{6,7},{7,6},{8,9},{9,8},{10,11... | collective-permute-start | bytes 1572872 | tf_op jit(solution)/shard_map/ppermute | solution.py:38
  60.3 3.3 %collective-permute-start.6 = (bf16[1024,256]{1,0:T(8,128)(2,1)S(1)}, bf16[1024,256]{1,0:T(8,128)(2,1)S(1)}, u32[]{:S(2)}, u32[]{:S(2)}) collective-permute-start(bf16[1024,256]{1,0:T(8,128)(2,1)S(1)} %bitcast.24), channel_id=1, source_target_pairs={{0,1},{1,0},{2,3},{3,2},{4,5},{5,4},{6,7},{7,6},{8,9},{9,8},{10,11... | collective-permute-start | bytes 1572872 | tf_op jit(solution)/shard_map/ppermute | solution.py:38
  63.7 6.7 %collective-permute-done.14.prev = bf16[4,4,7,8,512]{4,3,2,1,0:T(8,128)(2,1)S(1)} collective-permute-done((bf16[4,4,7,8,512]{4,3,2,1,0:T(8,128)(2,1)S(1)}, bf16[4,4,7,8,512]{4,3,2,1,0:T(8,128)(2,1)S(1)}, u32[]{:S(2)}, u32[]{:S(2)}) %collective-permute-start.14) | collective-permute-done | bytes 917536 | tf_op jit(solution)/shard_map/ppermute | solution.py:43
  70.6 2.9 %collective-permute-start.16 = (bf16[2,4,7,8,512]{4,3,2,1,0:T(8,128)(2,1)S(1)}, bf16[2,4,7,8,512]{4,3,2,1,0:T(8,128)(2,1)S(1)}, u32[]{:S(2)}, u32[]{:S(2)}) collective-permute-start(bf16[2,4,7,8,512]{4,3,2,1,0:T(8,128)(2,1)S(1)} %slice.19), channel_id=1, source_target_pairs={{0,24},{1,97},{2,26},{3,99},{4,28},{5,101},{6,30},{7,103},{8,0},{9... | collective-permute-start | bytes 1376264 | tf_op jit(solution)/shard_map/ppermute | solution.py:46
  74.9 4.4 %collective-permute-done.15.far_a = bf16[2,4,7,8,512]{4,3,2,1,0:T(8,128)(2,1)S(1)} collective-permute-done((bf16[2,4,7,8,512]{4,3,2,1,0:T(8,128)(2,1)S(1)}, bf16[2,4,7,8,512]{4,3,2,1,0:T(8,128)(2,1)S(1)}, u32[]{:S(2)}, u32[]{:S(2)}) %collective-permute-start.15) | collective-permute-done | bytes 458784 | tf_op jit(solution)/shard_map/ppermute | solution.py:45
  82.2 4.7 %shard_map.109 = (bf16[512,768]{1,0:T(8,128)(2,1)S(1)}, bf16[512,1024]{1,0:T(8,128)(2,1)S(1)}, bf16[256,1024]{1,0:T(8,128)(2,1)S(1)}) custom-call(s32[5]{0:T(128)S(1)} %stack.53.meta.refs_0_, bf16[256,768]{1,0:T(8,128)(2,1)S(1)} %copy-done.26, bf16[256,768]{1,0:T(8,128)(2,1)S(1)} %collective-permute-done.4.v_other, bf16[256,1024]{1,0:T(8,128)(2,1)} %shard_map.107.e_own, ...), custom_call_target="tpu_custom_call" | custom-call | flops 1879048192 | bytes 4726804 | tf_op jit(solution)/shard_map/pallas_call | solution.py:80
  88.9 5.2 %shard_map.110 = (bf16[512,1024]{1,0:T(8,128)(2,1)S(1)}, bf16[256,768]{1,0:T(8,128)(2,1)S(1)}) custom-call(s32[5]{0:T(128)S(1)} %stack.53.meta.refs_0_, bf16[256,1024]{1,0:T(8,128)(2,1)S(1)} %get-tuple-element.21.hid, bf16[256,1024]{1,0:T(8,128)(2,1)S(1)} %collective-permute-done.17.hid_other, bf16[2,512,256]{2,1,0:T(8,128)(2,1)S(1)} %get-tuple-element.22.turned, ...), custom_call_target="tpu_custom_call" | custom-call | flops 1610612736 | bytes 5771284 | tf_op jit(solution)/shard_map/pallas_call | solution.py:80
  97.1 3.6 %shard_map.112 = (bf16[512,768]{1,0:T(8,128)(2,1)S(1)}, bf16[256,768]{1,0:T(8,128)(2,1)S(1)}, bf16[1024,256]{1,0:T(8,128)(2,1)S(1)}) custom-call(s32[5]{0:T(128)S(1)} %stack.53.meta.refs_0_, bf16[256,768]{1,0:T(8,128)(2,1)S(1)} %get-tuple-element.25.hid, bf16[256,768]{1,0:T(8,128)(2,1)S(1)} %collective-permute-done.19.hid_other, ...), custom_call_target="tpu_custom_call" | custom-call | flops 805306368 | bytes 4460564 | tf_op jit(solution)/shard_map/pallas_call | solution.py:80
  102.2 7.8 %all-to-all-start.1 = ((bf16[32,32,256]{2,1,0:T(8,128)(2,1)}), bf16[32,32,256]{2,1,0:T(8,128)(2,1)S(1)}, u32[]{:S(2)}, u32[]{:S(2)}) async-start(bf16[32,32,256]{2,1,0:T(8,128)(2,1)} %bitcast.26), calls=%async_computation.1 | async-start | bytes 1048576 | tf_op jit(solution)/shard_map/all_to_all | solution.py:284
  113.0 2.7 %shard_map.113.refs_1_ = f32[256,1024]{1,0:T(8,128)S(1)} custom-call(s32[5]{0:T(128)S(1)} %stack.53.meta.refs_0_, bf16[512,768]{1,0:T(8,128)(2,1)S(1)} %get-tuple-element.27.v_all, bf16[512,1024]{1,0:T(8,128)(2,1)S(1)} %copy-done.7, bf16[256,768]{1,0:T(8,128)(2,1)S(1)} %copy-done.17, bf16[7,256,512]{2,1,0:T(8,128)(2,1)S(1)} %get-tuple-element.26.mats, ...), custom_call_target="tpu_custom_call" | custom-call | flops 805306368 | bytes 4071444 | tf_op jit(solution)/shard_map/pallas_call | solution.py:80
  116.8 3.6 %all-to-all-done.1 = bf16[32,32,256]{2,1,0:T(8,128)(2,1)S(1)} async-done(((bf16[32,32,256]{2,1,0:T(8,128)(2,1)}), bf16[32,32,256]{2,1,0:T(8,128)(2,1)S(1)}, u32[]{:S(2)}, u32[]{:S(2)}) %all-to-all-start.1) | async-done | bytes 524320 | tf_op jit(solution)/shard_map/all_to_all | solution.py:284
  127.5 6.3 %shard_map.115 = (bf16[64,1024]{1,0:T(8,128)(2,1)}, bf16[256,768]{1,0:T(8,128)(2,1)S(1)}) custom-call(s32[5]{0:T(128)S(1)} %stack.53.meta.refs_0_, bf16[256,1024]{1,0:T(8,128)(2,1)S(1)} %shard_map.114.hid, bf16[256,1024]{1,0:T(8,128)(2,1)S(1)} %collective-permute-done.20.hid_other, bf16[2,512,256]{2,1,0:T(8,128)(2,1)S(1)} %copy-done.11, ...), custom_call_target="tpu_custom_call" | custom-call | flops 1610612736 | bytes 5771284 | tf_op jit(solution)/shard_map/pallas_call | solution.py:80
  135.5 3.0 %shard_map.116 = bf16[64,768]{1,0:T(8,128)(2,1)} custom-call(s32[5]{0:T(128)S(1)} %stack.53.meta.refs_0_, bf16[256,768]{1,0:T(8,128)(2,1)S(1)} %get-tuple-element.32.hid, bf16[256,768]{1,0:T(8,128)(2,1)S(1)} %collective-permute-done.22.hid_other, bf16[2,512,256]{2,1,0:T(8,128)(2,1)S(1)} %copy-done.11, ...), custom_call_target="tpu_custom_call" | custom-call | flops 402653184 | bytes 2621460 | tf_op jit(solution)/shard_map/pallas_call | solution.py:80
  (100 shorter events, 37.3 us)
Async XLA Ops:
  3.6 26.5 %collective-permute-start.1 = (bf16[64,1792]{1,0:T(8,128)(2,1)S(1)}, bf16[64,1792]{1,0:T(8,128)(2,1)S(1)}, u32[]{:S(2)}, u32[]{:S(2)}) collective-permute-start(bf16[64,1792]{1,0:T(8,128)(2,1)S(1)} %shard_map.105.own), channel_id=1, source_target_pairs={{0,2},{1,3},{2,4},{3,5},{4,6},{5,7},{6,0},{7,1},{8,10},{9,11},{10,... | collective-permute-start | bytes 688136 | tf_op jit(solution)/shard_map/ppermute | solution.py:43
  7.5 25.6 %collective-permute-start = (bf16[64,1792]{1,0:T(8,128)(2,1)S(1)}, bf16[64,1792]{1,0:T(8,128)(2,1)S(1)}, u32[]{:S(2)}, u32[]{:S(2)}) collective-permute-start(bf16[64,1792]{1,0:T(8,128)(2,1)S(1)} %shard_map.105.own), channel_id=1, source_target_pairs={{0,6},{1,7},{2,0},{3,1},{4,2},{5,3},{6,4},{7,5},{8,14},{9,15},{10,... | collective-permute-start | bytes 688136 | tf_op jit(solution)/shard_map/ppermute | solution.py:44
  10.6 8.5 %collective-permute-start.7 = (bf16[7,8,512]{2,1,0:T(8,128)(2,1)S(1)}, bf16[7,8,512]{2,1,0:T(8,128)(2,1)S(1)}, u32[]{:S(2)}, u32[]{:S(2)}) collective-permute-start(bf16[7,8,512]{2,1,0:T(8,128)(2,1)S(1)} %shard_map.104.piece), channel_id=1, source_target_pairs={{0,2},{1,3},{2,4},{3,5},{4,6},{5,7},{6,0},{7,1},{8,10},{9,11},{10,... | collective-permute-start | bytes 172040 | tf_op jit(solution)/shard_map/ppermute | solution.py:274
  11.7 14.6 %collective-permute-start.8 = (bf16[7,8,512]{2,1,0:T(8,128)(2,1)S(1)}, bf16[7,8,512]{2,1,0:T(8,128)(2,1)S(1)}, u32[]{:S(2)}, u32[]{:S(2)}) collective-permute-start(bf16[7,8,512]{2,1,0:T(8,128)(2,1)S(1)} %shard_map.104.piece), channel_id=1, source_target_pairs={{0,6},{1,7},{2,0},{3,1},{4,2},{5,3},{6,4},{7,5},{8,14},{9,15},{10,... | collective-permute-start | bytes 172040 | tf_op jit(solution)/shard_map/ppermute | solution.py:274
  14.2 12.1 %collective-permute-start.9 = (bf16[7,8,512]{2,1,0:T(8,128)(2,1)S(1)}, bf16[7,8,512]{2,1,0:T(8,128)(2,1)S(1)}, u32[]{:S(2)}, u32[]{:S(2)}) collective-permute-start(bf16[7,8,512]{2,1,0:T(8,128)(2,1)S(1)} %shard_map.104.piece), channel_id=1, source_target_pairs={{0,4},{1,5},{2,6},{3,7},{4,0},{5,1},{6,2},{7,3},{8,12},{9,13},{10,... | collective-permute-start | bytes 172040 | tf_op jit(solution)/shard_map/ppermute | solution.py:274
  26.4 24.7 %collective-permute-start.10 = (bf16[4,7,8,512]{3,2,1,0:T(8,128)(2,1)S(1)}, bf16[4,7,8,512]{3,2,1,0:T(8,128)(2,1)S(1)}, u32[]{:S(2)}, u32[]{:S(2)}) collective-permute-start(bf16[4,7,8,512]{3,2,1,0:T(8,128)(2,1)S(1)} %get-tuple-element.35), channel_id=1, source_target_pairs={{0,96},{1,25},{2,98},{3,27},{4,100},{5,29},{6,102},{7,31},{8,104},... | collective-permute-start | bytes 688136 | tf_op jit(solution)/shard_map/ppermute | solution.py:276
  28.9 22.2 %collective-permute-start.11 = (bf16[4,7,8,512]{3,2,1,0:T(8,128)(2,1)S(1)}, bf16[4,7,8,512]{3,2,1,0:T(8,128)(2,1)S(1)}, u32[]{:S(2)}, u32[]{:S(2)}) collective-permute-start(bf16[4,7,8,512]{3,2,1,0:T(8,128)(2,1)S(1)} %get-tuple-element.35), channel_id=1, source_target_pairs={{0,64},{1,17},{2,66},{3,19},{4,68},{5,21},{6,70},{7,23},{8,72},{9,... | collective-permute-start | bytes 688136 | tf_op jit(solution)/shard_map/ppermute | solution.py:276
  29.5 21.7 %collective-permute-start.12 = (bf16[4,7,8,512]{3,2,1,0:T(8,128)(2,1)S(1)}, bf16[4,7,8,512]{3,2,1,0:T(8,128)(2,1)S(1)}, u32[]{:S(2)}, u32[]{:S(2)}) collective-permute-start(bf16[4,7,8,512]{3,2,1,0:T(8,128)(2,1)S(1)} %get-tuple-element.35), channel_id=1, source_target_pairs={{0,32},{1,9},{2,34},{3,11},{4,36},{5,13},{6,38},{7,15},{8,40},{9,1... | collective-permute-start | bytes 688136 | tf_op jit(solution)/shard_map/ppermute | solution.py:276
  30.1 6.1 %collective-permute-start.2 = (bf16[32,1792]{1,0:T(8,128)(2,1)S(1)}, bf16[32,1792]{1,0:T(8,128)(2,1)S(1)}, u32[]{:S(2)}, u32[]{:S(2)}) collective-permute-start(bf16[32,1792]{1,0:T(8,128)(2,1)S(1)} %slice.16), channel_id=1, source_target_pairs={{0,2},{1,3},{2,4},{3,5},{4,6},{5,7},{6,0},{7,1},{8,10},{9,11},{10,... | collective-permute-start | bytes 344072 | tf_op jit(solution)/shard_map/ppermute | solution.py:45
  33.1 6.1 %collective-permute-start.3 = (bf16[32,1792]{1,0:T(8,128)(2,1)S(1)}, bf16[32,1792]{1,0:T(8,128)(2,1)S(1)}, u32[]{:S(2)}, u32[]{:S(2)}) collective-permute-start(bf16[32,1792]{1,0:T(8,128)(2,1)S(1)} %slice.17), channel_id=1, source_target_pairs={{0,6},{1,7},{2,0},{3,1},{4,2},{5,3},{6,4},{7,5},{8,14},{9,15},{10,... | collective-permute-start | bytes 344072 | tf_op jit(solution)/shard_map/ppermute | solution.py:46
  42.9 17.4 %all-to-all-start = ((bf16[32,32,256]{2,1,0:T(8,128)(2,1)}), bf16[32,32,256]{2,1,0:T(8,128)(2,1)S(1)}, u32[]{:S(2)}, u32[]{:S(2)}) async-start(bf16[32,32,256]{2,1,0:T(8,128)(2,1)} %bitcast.8), calls=%async_computation | async-start | bytes 1048576 | tf_op jit(solution)/shard_map/all_to_all | solution.py:284
  51.3 19.1 %collective-permute-start.14 = (bf16[4,4,7,8,512]{4,3,2,1,0:T(8,128)(2,1)S(1)}, bf16[4,4,7,8,512]{4,3,2,1,0:T(8,128)(2,1)S(1)}, u32[]{:S(2)}, u32[]{:S(2)}) collective-permute-start(bf16[4,4,7,8,512]{4,3,2,1,0:T(8,128)(2,1)S(1)} %pad_maximum_fusion.own), channel_id=1, source_target_pairs={{0,8},{1,33},{2,10},{3,35},{4,12},{5,37},{6,14},{7,39},{8,16},{9,4... | collective-permute-start | bytes 2752520 | tf_op jit(solution)/shard_map/ppermute | solution.py:43
  52.6 18.0 %collective-permute-start.13 = (bf16[4,4,7,8,512]{4,3,2,1,0:T(8,128)(2,1)S(1)}, bf16[4,4,7,8,512]{4,3,2,1,0:T(8,128)(2,1)S(1)}, u32[]{:S(2)}, u32[]{:S(2)}) collective-permute-start(bf16[4,4,7,8,512]{4,3,2,1,0:T(8,128)(2,1)S(1)} %pad_maximum_fusion.own), channel_id=1, source_target_pairs={{0,24},{1,97},{2,26},{3,99},{4,28},{5,101},{6,30},{7,103},{8,0},{9... | collective-permute-start | bytes 2752520 | tf_op jit(solution)/shard_map/ppermute | solution.py:44
  55.4 26.8 %collective-permute-start.5 = (bf16[256,1024]{1,0:T(8,128)(2,1)}, bf16[256,1024]{1,0:T(8,128)(2,1)}, u32[]{:S(2)}, u32[]{:S(2)}) collective-permute-start(bf16[256,1024]{1,0:T(8,128)(2,1)} %shard_map.107.e_own), channel_id=1, source_target_pairs={{0,1},{1,0},{2,3},{3,2},{4,5},{5,4},{6,7},{7,6},{8,9},{9,8},{10,11... | collective-permute-start | bytes 1572872 | tf_op jit(solution)/shard_map/ppermute | solution.py:38
  60.3 21.9 %collective-permute-start.6 = (bf16[1024,256]{1,0:T(8,128)(2,1)S(1)}, bf16[1024,256]{1,0:T(8,128)(2,1)S(1)}, u32[]{:S(2)}, u32[]{:S(2)}) collective-permute-start(bf16[1024,256]{1,0:T(8,128)(2,1)S(1)} %bitcast.24), channel_id=1, source_target_pairs={{0,1},{1,0},{2,3},{3,2},{4,5},{5,4},{6,7},{7,6},{8,9},{9,8},{10,11... | collective-permute-start | bytes 1572872 | tf_op jit(solution)/shard_map/ppermute | solution.py:38
  70.4 8.9 %collective-permute-start.15 = (bf16[2,4,7,8,512]{4,3,2,1,0:T(8,128)(2,1)S(1)}, bf16[2,4,7,8,512]{4,3,2,1,0:T(8,128)(2,1)S(1)}, u32[]{:S(2)}, u32[]{:S(2)}) collective-permute-start(bf16[2,4,7,8,512]{4,3,2,1,0:T(8,128)(2,1)S(1)} %slice.18), channel_id=1, source_target_pairs={{0,8},{1,33},{2,10},{3,35},{4,12},{5,37},{6,14},{7,39},{8,16},{9,4... | collective-permute-start | bytes 1376264 | tf_op jit(solution)/shard_map/ppermute | solution.py:45
  70.6 8.8 %collective-permute-start.16 = (bf16[2,4,7,8,512]{4,3,2,1,0:T(8,128)(2,1)S(1)}, bf16[2,4,7,8,512]{4,3,2,1,0:T(8,128)(2,1)S(1)}, u32[]{:S(2)}, u32[]{:S(2)}) collective-permute-start(bf16[2,4,7,8,512]{4,3,2,1,0:T(8,128)(2,1)S(1)} %slice.19), channel_id=1, source_target_pairs={{0,24},{1,97},{2,26},{3,99},{4,28},{5,101},{6,30},{7,103},{8,0},{9... | collective-permute-start | bytes 1376264 | tf_op jit(solution)/shard_map/ppermute | solution.py:46
  73.5 8.7 %collective-permute-start.4 = (bf16[256,768]{1,0:T(8,128)(2,1)S(1)}, bf16[256,768]{1,0:T(8,128)(2,1)S(1)}, u32[]{:S(2)}, u32[]{:S(2)}) collective-permute-start(bf16[256,768]{1,0:T(8,128)(2,1)S(1)} %copy-done.26), channel_id=1, source_target_pairs={{0,1},{1,0},{2,3},{3,2},{4,5},{5,4},{6,7},{7,6},{8,9},{9,8},{10,11... | collective-permute-start | bytes 1179656 | tf_op jit(solution)/shard_map/ppermute | solution.py:38
  80.4 6.6 %collective-permute-start.18 = (bf16[2,512,256]{2,1,0:T(8,128)(2,1)S(1)}, bf16[2,512,256]{2,1,0:T(8,128)(2,1)S(1)}, u32[]{:S(2)}, u32[]{:S(2)}) collective-permute-start(bf16[2,512,256]{2,1,0:T(8,128)(2,1)S(1)} %get-tuple-element.22.turned), channel_id=1, source_target_pairs={{0,1},{1,0},{2,3},{3,2},{4,5},{5,4},{6,7},{7,6},{8,9},{9,8},{10,11... | collective-permute-start | bytes 1572872 | tf_op jit(solution)/shard_map/ppermute | solution.py:38
  86.9 2.0 %collective-permute-start.17 = (bf16[256,1024]{1,0:T(8,128)(2,1)S(1)}, bf16[256,1024]{1,0:T(8,128)(2,1)S(1)}, u32[]{:S(2)}, u32[]{:S(2)}) collective-permute-start(bf16[256,1024]{1,0:T(8,128)(2,1)S(1)} %get-tuple-element.21.hid), channel_id=1, source_target_pairs={{0,1},{1,0},{2,3},{3,2},{4,5},{5,4},{6,7},{7,6},{8,9},{9,8},{10,11... | collective-permute-start | bytes 1572872 | tf_op jit(solution)/shard_map/ppermute | solution.py:38
  95.1 1.9 %collective-permute-start.19 = (bf16[256,768]{1,0:T(8,128)(2,1)S(1)}, bf16[256,768]{1,0:T(8,128)(2,1)S(1)}, u32[]{:S(2)}, u32[]{:S(2)}) collective-permute-start(bf16[256,768]{1,0:T(8,128)(2,1)S(1)} %get-tuple-element.25.hid), channel_id=1, source_target_pairs={{0,1},{1,0},{2,3},{3,2},{4,5},{5,4},{6,7},{7,6},{8,9},{9,8},{10,11... | collective-permute-start | bytes 1179656 | tf_op jit(solution)/shard_map/ppermute | solution.py:38
  102.2 18.1 %all-to-all-start.1 = ((bf16[32,32,256]{2,1,0:T(8,128)(2,1)}), bf16[32,32,256]{2,1,0:T(8,128)(2,1)S(1)}, u32[]{:S(2)}, u32[]{:S(2)}) async-start(bf16[32,32,256]{2,1,0:T(8,128)(2,1)} %bitcast.26), calls=%async_computation.1 | async-start | bytes 1048576 | tf_op jit(solution)/shard_map/all_to_all | solution.py:284
  110.0 15.9 %collective-permute-start.21 = (bf16[2,512,256]{2,1,0:T(8,128)(2,1)}, bf16[2,512,256]{2,1,0:T(8,128)(2,1)}, u32[]{:S(2)}, u32[]{:S(2)}) collective-permute-start(bf16[2,512,256]{2,1,0:T(8,128)(2,1)} %copy-done.10), channel_id=1, source_target_pairs={{0,1},{1,0},{2,3},{3,2},{4,5},{5,4},{6,7},{7,6},{8,9},{9,8},{10,11... | collective-permute-start | bytes 1572872 | tf_op jit(solution)/shard_map/ppermute | solution.py:38
  123.6 3.8 %collective-permute-start.20 = (bf16[256,1024]{1,0:T(8,128)(2,1)S(1)}, bf16[256,1024]{1,0:T(8,128)(2,1)S(1)}, u32[]{:S(2)}, u32[]{:S(2)}) collective-permute-start(bf16[256,1024]{1,0:T(8,128)(2,1)S(1)} %shard_map.114.hid), channel_id=1, source_target_pairs={{0,1},{1,0},{2,3},{3,2},{4,5},{5,4},{6,7},{7,6},{8,9},{9,8},{10,11... | collective-permute-start | bytes 1572872 | tf_op jit(solution)/shard_map/ppermute | solution.py:38
  (28 other events, 164.1 us)

commit v2 on v1

--- a/solution.py
+++ b/solution.py
@@ -74,18 +74,23 @@
     lax.fori_loop(0, n // CHUNK, step, 0)
 
 
-def call(kernel, outs, *args, scratch=(), flops=0, space=VMEM):
-    specs = [SMEM] + [space] * (len(args) - 1)
+def call(kernel, outs, *args, scratch=(), flops=0, space=VMEM, after=()):
+    specs = [SMEM] + [space] * (len(args) - 1) + [pl.BlockSpec(memory_space=pl.ANY)] * len(after)
     moved = sum(a.size * a.dtype.itemsize for a in args)
+    inputs = len(args)
+
+    def body(*refs):
+        kernel(*refs[:inputs], *refs[inputs + len(after) :])
+
     return pl.pallas_call(
-        kernel,
+        body,
         out_shape=[jax.ShapeDtypeStruct(s, d) for s, d in outs],
         in_specs=specs,
         out_specs=[VMEM] * len(outs),
         scratch_shapes=list(scratch),
         compiler_params=pltpu.CompilerParams(vmem_limit_bytes=6 << 20),
         cost_estimate=pl.CostEstimate(flops=flops, bytes_accessed=moved, transcendentals=0),
-    )(*args)
+    )(*args, *after)
 
 
 def place_half(meta, parts, out, col):
@@ -136,7 +141,7 @@
     copy_all(copies, sem)
 
 
-def beside(meta, v, e, piece, both, sem):
+def beside(meta, v, e, both, sem):
     n = v.shape[1]
     copy_all([(v, both.at[:, :n]), (e, both.at[:, n:])], sem)
 
@@ -262,22 +267,25 @@
 
     in_hbm = lambda a: pltpu.with_memory_space_constraint(a, pltpu.HBM)
     weights = (jnp.swapaxes(w_edge_in, 2, 3), w_edge_out, jnp.swapaxes(w_node_in, 2, 3), w_node_out)
-    anywhere = pl.BlockSpec(memory_space=pl.ANY)
+    hbm = pl.BlockSpec(memory_space=pltpu.HBM)
     (piece,) = call(
         cut_weights, [((7, 8, LATENT), BF)], meta, *map(in_hbm, weights),
-        scratch=[pltpu.SemaphoreType.DMA((4,))], space=pl.BlockSpec(memory_space=pltpu.HBM),
-    )
+        scratch=[pltpu.SemaphoreType.DMA((4,))], space=hbm,
+    )
+    pieces = [piece] + [lax.ppermute(piece, "ch", z_shift(s)) for s in (1, 3, 2)]
     (both,) = call(
-        beside, [((64, n + m), BF)], meta, in_hbm(node_feats), in_hbm(edge_feats), piece,
-        scratch=[pltpu.SemaphoreType.DMA((2,))], space=anywhere,
-    )
-    wz = jnp.stack([piece] + [lax.ppermute(piece, "ch", z_shift(s)) for s in (1, 3, 2)])
+        beside, [((64, n + m), BF)], meta, in_hbm(node_feats), in_hbm(edge_feats),
+        scratch=[pltpu.SemaphoreType.DMA((2,))], space=hbm, after=pieces[1:2],
+    )
+    wz = jnp.stack(pieces)
     parts = ring_gather(both, "ch", z_shift)
-    one = jnp.stack([wz] + [lax.ppermute(wz, ("dom", "ch"), ring(1, s)) for s in (3, 2, 1)])
+    quarters = [wz] + [lax.ppermute(wz, ("dom", "ch"), ring(1, s)) for s in (3, 2, 1)]
+    quarters[0] = lax.optimization_barrier((wz, parts[1], parts[4]))[0]
+    one = jnp.stack(quarters)
     w_parts = ring_gather(one, ("dom", "ch"), lambda s: ring(2, s))
 
     v_half, rows = call(
-        send_first, [((HALF, n), BF), ((m, HALF), BF)], meta, *parts, send, flops=2 * HALF * n * m
+        send_first, [((HALF, n), BF), ((m, HALF), BF)], meta, *parts, send, flops=2 * HALF * n * m, after=(w_parts[1], w_parts[4])
     )
 
     def exchange(rows):

time: 139 us -> 135 us (0.971)
  starting transfers between devices: 57.2 us -> 52.7 us
  waiting for transfers between devices: 34.8 us -> 33.1 us
    ppermute x3, waiting for transfers between devices: 7.77 us -> 0.01 us  [shards(): lax.ppermute(piece, 'ch', z_shift(s))]
    ppermute x2, waiting for transfers between devices: 0.01 us -> 6.74 us  [ring_gather(): nxt = lax.ppermute(x, axis, perm(3))]
    ppermute x3, starting transfers between devices: 7.95 us -> 11.4 us  [shards(): lax.ppermute(piece, 'ch', z_shift(s))]
    ppermute x2, waiting for transfers between devices: 6.75 us -> 3.52 us  [ring_gather(): prev = lax.ppermute(x, axis, perm(1))]
    ppermute x2, starting transfers between devices: 4.56 us -> 1.62 us  [ring_gather(): nxt = lax.ppermute(x, axis, perm(3))]
    all_to_all x2, starting transfers between devices: 16 us -> 13.9 us  [exchange(): lax.all_to_all(rows.reshape(32, SLOTS, HALF), 'dom', 0, 0, tiled=True)]
    all_to_all x2, waiting for transfers between devices: 5.67 us -> 7.67 us  [exchange(): lax.all_to_all(rows.reshape(32, SLOTS, HALF), 'dom', 0, 0, tiled=True)]
    ppermute x2, starting transfers between devices: 5.21 us -> 3.57 us  [ring_gather(): prev = lax.ppermute(x, axis, perm(1))]
where the time goes in v2:
time: 135 us; the launch traced here: 134 us
  starting transfers between devices  52.7 us (39%)
  Pallas kernels  37.7 us (28%)
  waiting for transfers between devices  33.1 us (25%)
  local copies, waits for them, and re-layouts  9.89 us (7%)
    pallas_call x13, Pallas kernels, call(): pl.pallas_call(body, out_shape=[jax.ShapeDtypeStruct(s, d) for s, d in ou...  37.7 us
    all_to_all x2, starting transfers between devices, exchange(): lax.all_to_all(rows.reshape(32, SLOTS, HALF), 'dom', 0, 0, tiled=True)  13.9 us
    ppermute x9, starting transfers between devices, swap(): return lax.ppermute(x, 'ch', CORE)  11.8 us
    ppermute x3, starting transfers between devices, shards(): lax.ppermute(piece, 'ch', z_shift(s))  11.4 us
    unnamed x46, local copies, waits for them, and re-layouts  9.73 us
    all_to_all x2, waiting for transfers between devices, exchange(): lax.all_to_all(rows.reshape(32, SLOTS, HALF), 'dom', 0, 0, tiled=True)  7.67 us
    ppermute x2, waiting for transfers between devices, ring_gather(): far_a = lax.ppermute(prev[:half], axis, perm(1))  7.5 us
    ppermute x2, waiting for transfers between devices, ring_gather(): nxt = lax.ppermute(x, axis, perm(3))  6.74 us
  transfers between devices with their start and end apart: 25, of which 11 were waited for; matrix products, arithmetic and copies ran while one was open for 0% of the time, Pallas kernels for 11%

profile of v2, /device:TPU:1, one launch (start us, length us, event | category | flops | bytes accessed | tf_op | source)
XLA Modules:
  0.0 134.3 jit_solution(4756724595703175909)
XLA Ops:
  2.1 3.9 %collective-permute-start = (bf16[7,8,512]{2,1,0:T(8,128)(2,1)S(1)}, bf16[7,8,512]{2,1,0:T(8,128)(2,1)S(1)}, u32[]{:S(2)}, u32[]{:S(2)}) collective-permute-start(bf16[7,8,512]{2,1,0:T(8,128)(2,1)S(1)} %shard_map.104), channel_id=1, source_target_pairs={{0,2},{1,3},{2,4},{3,5},{4,6},{5,7},{6,0},{7,1},{8,10},{9,11},{10,... | collective-permute-start | bytes 172040 | tf_op jit(solution)/shard_map/ppermute | solution.py:275
  6.0 3.1 %collective-permute-start.5 = (bf16[7,8,512]{2,1,0:T(8,128)(2,1)S(1)}, bf16[7,8,512]{2,1,0:T(8,128)(2,1)S(1)}, u32[]{:S(2)}, u32[]{:S(2)}) collective-permute-start(bf16[7,8,512]{2,1,0:T(8,128)(2,1)S(1)} %shard_map.104), channel_id=1, source_target_pairs={{0,6},{1,7},{2,0},{3,1},{4,2},{5,3},{6,4},{7,5},{8,14},{9,15},{10,... | collective-permute-start | bytes 172040 | tf_op jit(solution)/shard_map/ppermute | solution.py:275
  9.1 4.4 %collective-permute-start.6 = (bf16[7,8,512]{2,1,0:T(8,128)(2,1)S(1)}, bf16[7,8,512]{2,1,0:T(8,128)(2,1)S(1)}, u32[]{:S(2)}, u32[]{:S(2)}) collective-permute-start(bf16[7,8,512]{2,1,0:T(8,128)(2,1)S(1)} %shard_map.104), channel_id=1, source_target_pairs={{0,4},{1,5},{2,6},{3,7},{4,0},{5,1},{6,2},{7,3},{8,12},{9,13},{10,... | collective-permute-start | bytes 172040 | tf_op jit(solution)/shard_map/ppermute | solution.py:275
  15.1 2.4 %collective-permute-start.2 = (bf16[64,1792]{1,0:T(8,128)(2,1)S(1)}, bf16[64,1792]{1,0:T(8,128)(2,1)S(1)}, u32[]{:S(2)}, u32[]{:S(2)}) collective-permute-start(bf16[64,1792]{1,0:T(8,128)(2,1)S(1)} %shard_map.105.refs_1_), channel_id=1, source_target_pairs={{0,2},{1,3},{2,4},{3,5},{4,6},{5,7},{6,0},{7,1},{8,10},{9,11},{10,... | collective-permute-start | bytes 688136 | tf_op jit(solution)/shard_map/ppermute | solution.py:43
  17.5 2.6 %collective-permute-start.7 = (bf16[4,7,8,512]{3,2,1,0:T(8,128)(2,1)S(1)}, bf16[4,7,8,512]{3,2,1,0:T(8,128)(2,1)S(1)}, u32[]{:S(2)}, u32[]{:S(2)}) collective-permute-start(bf16[4,7,8,512]{3,2,1,0:T(8,128)(2,1)S(1)} %pad_maximum_fusion.1), channel_id=1, source_target_pairs={{0,96},{1,25},{2,98},{3,27},{4,100},{5,29},{6,102},{7,31},{8,104},... | collective-permute-start | bytes 688136 | tf_op jit(solution)/shard_map/ppermute | solution.py:282
  21.2 6.7 %collective-permute-done.1.refs_2_ = bf16[64,1792]{1,0:T(8,128)(2,1)S(1)} collective-permute-done((bf16[64,1792]{1,0:T(8,128)(2,1)S(1)}, bf16[64,1792]{1,0:T(8,128)(2,1)S(1)}, u32[]{:S(2)}, u32[]{:S(2)}) %collective-permute-start.1) | collective-permute-done | bytes 229408 | tf_op jit(solution)/shard_map/ppermute | solution.py:44
  33.3 2.5 %collective-permute-start.4 = (bf16[32,1792]{1,0:T(8,128)(2,1)S(1)}, bf16[32,1792]{1,0:T(8,128)(2,1)S(1)}, u32[]{:S(2)}, u32[]{:S(2)}) collective-permute-start(bf16[32,1792]{1,0:T(8,128)(2,1)S(1)} %slice.17), channel_id=1, source_target_pairs={{0,6},{1,7},{2,0},{3,1},{4,2},{5,3},{6,4},{7,5},{8,14},{9,15},{10,... | collective-permute-start | bytes 344072 | tf_op jit(solution)/shard_map/ppermute | solution.py:46
  35.8 2.2 %collective-permute-done.3.refs_3_ = bf16[32,1792]{1,0:T(8,128)(2,1)S(1)} collective-permute-done((bf16[32,1792]{1,0:T(8,128)(2,1)S(1)}, bf16[32,1792]{1,0:T(8,128)(2,1)S(1)}, u32[]{:S(2)}, u32[]{:S(2)}) %collective-permute-start.3) | collective-permute-done | bytes 114720 | tf_op jit(solution)/shard_map/ppermute | solution.py:45
  39.6 3.5 %collective-permute-done.11.refs_8_.refs_5_ = bf16[4,4,7,8,512]{4,3,2,1,0:T(8,128)(2,1)S(1)} collective-permute-done((bf16[4,4,7,8,512]{4,3,2,1,0:T(8,128)(2,1)S(1)}, bf16[4,4,7,8,512]{4,3,2,1,0:T(8,128)(2,1)S(1)}, u32[]{:S(2)}, u32[]{:S(2)}) %collective-permute-start.11) | collective-permute-done | bytes 917536 | tf_op jit(solution)/shard_map/ppermute | solution.py:43
  46.7 7.6 %all-to-all-start = ((bf16[32,32,256]{2,1,0:T(8,128)(2,1)}), bf16[32,32,256]{2,1,0:T(8,128)(2,1)}, u32[]{:S(2)}, u32[]{:S(2)}) async-start(bf16[32,32,256]{2,1,0:T(8,128)(2,1)} %bitcast.23), calls=%async_computation | async-start | bytes 1048576 | tf_op jit(solution)/shard_map/all_to_all | solution.py:292
  57.2 2.8 %collective-permute-start.13 = (bf16[256,1024]{1,0:T(8,128)(2,1)}, bf16[256,1024]{1,0:T(8,128)(2,1)S(1)}, u32[]{:S(2)}, u32[]{:S(2)}) collective-permute-start(bf16[256,1024]{1,0:T(8,128)(2,1)} %shard_map.107.refs_3_), channel_id=1, source_target_pairs={{0,1},{1,0},{2,3},{3,2},{4,5},{5,4},{6,7},{7,6},{8,9},{9,8},{10,11... | collective-permute-start | bytes 1572872 | tf_op jit(solution)/shard_map/ppermute | solution.py:38
  60.0 3.4 %all-to-all-done = bf16[32,32,256]{2,1,0:T(8,128)(2,1)} async-done(((bf16[32,32,256]{2,1,0:T(8,128)(2,1)}), bf16[32,32,256]{2,1,0:T(8,128)(2,1)}, u32[]{:S(2)}, u32[]{:S(2)}) %all-to-all-start) | async-done | bytes 524320 | tf_op jit(solution)/shard_map/all_to_all | solution.py:292
  63.4 3.8 %collective-permute-start.14 = (bf16[1024,256]{1,0:T(8,128)(2,1)}, bf16[1024,256]{1,0:T(8,128)(2,1)S(1)}, u32[]{:S(2)}, u32[]{:S(2)}) collective-permute-start(bf16[1024,256]{1,0:T(8,128)(2,1)} %bitcast.17.refs_5_), channel_id=1, source_target_pairs={{0,1},{1,0},{2,3},{3,2},{4,5},{5,4},{6,7},{7,6},{8,9},{9,8},{10,11... | collective-permute-start | bytes 1572872 | tf_op jit(solution)/shard_map/ppermute | solution.py:38
  67.7 2.6 %collective-permute-start.16 = (bf16[2,4,7,8,512]{4,3,2,1,0:T(8,128)(2,1)S(1)}, bf16[2,4,7,8,512]{4,3,2,1,0:T(8,128)(2,1)S(1)}, u32[]{:S(2)}, u32[]{:S(2)}) collective-permute-start(bf16[2,4,7,8,512]{4,3,2,1,0:T(8,128)(2,1)S(1)} %slice.19), channel_id=1, source_target_pairs={{0,24},{1,97},{2,26},{3,99},{4,28},{5,101},{6,30},{7,103},{8,0},{9... | collective-permute-start | bytes 1376264 | tf_op jit(solution)/shard_map/ppermute | solution.py:46
  70.9 5.3 %collective-permute-done.15.refs_3_ = bf16[2,4,7,8,512]{4,3,2,1,0:T(8,128)(2,1)S(1)} collective-permute-done((bf16[2,4,7,8,512]{4,3,2,1,0:T(8,128)(2,1)S(1)}, bf16[2,4,7,8,512]{4,3,2,1,0:T(8,128)(2,1)S(1)}, u32[]{:S(2)}, u32[]{:S(2)}) %collective-permute-start.15) | collective-permute-done | bytes 458784 | tf_op jit(solution)/shard_map/ppermute | solution.py:45
  78.2 4.7 %shard_map.109 = (bf16[512,768]{1,0:T(8,128)(2,1)S(1)}, bf16[512,1024]{1,0:T(8,128)(2,1)S(1)}, bf16[256,1024]{1,0:T(8,128)(2,1)S(1)}) custom-call(s32[5]{0:T(128)S(1)} %copy-done.16, bf16[256,768]{1,0:T(8,128)(2,1)S(1)} %copy-done.22, bf16[256,768]{1,0:T(8,128)(2,1)S(1)} %collective-permute-done.12.refs_2_, bf16[256,1024]{1,0:T(8,128)(2,1)} %shard_map.107.refs_3_, ...), custom_call_target="tpu_custom_call" | custom-call | flops 1879048192 | bytes 4726804 | tf_op jit(solution)/shard_map/pallas_call | solution.py:85
  84.9 5.2 %shard_map.110 = (bf16[512,1024]{1,0:T(8,128)(2,1)S(1)}, bf16[256,768]{1,0:T(8,128)(2,1)S(1)}) custom-call(s32[5]{0:T(128)S(1)} %copy-done.16, bf16[256,1024]{1,0:T(8,128)(2,1)S(1)} %get-tuple-element.23.refs_1_, bf16[256,1024]{1,0:T(8,128)(2,1)S(1)} %collective-permute-done.17.refs_2_, bf16[2,512,256]{2,1,0:T(8,128)(2,1)S(1)} %get-tuple-element.24.refs_3_, ...), custom_call_target="tpu_custom_call" | custom-call | flops 1610612736 | bytes 5771284 | tf_op jit(solution)/shard_map/pallas_call | solution.py:85
  93.0 4.4 %shard_map.112 = (bf16[512,768]{1,0:T(8,128)(2,1)S(1)}, bf16[256,768]{1,0:T(8,128)(2,1)S(1)}, bf16[1024,256]{1,0:T(8,128)(2,1)}) custom-call(s32[5]{0:T(128)S(1)} %copy-done.16, bf16[256,768]{1,0:T(8,128)(2,1)S(1)} %get-tuple-element.27.refs_1_, bf16[256,768]{1,0:T(8,128)(2,1)S(1)} %collective-permute-done.19.refs_2_, ...), custom_call_target="tpu_custom_call" | custom-call | flops 805306368 | bytes 4460564 | tf_op jit(solution)/shard_map/pallas_call | solution.py:85
  98.2 6.3 %all-to-all-start.1 = ((bf16[32,32,256]{2,1,0:T(8,128)(2,1)}), bf16[32,32,256]{2,1,0:T(8,128)(2,1)S(1)}, u32[]{:S(2)}, u32[]{:S(2)}) async-start(bf16[32,32,256]{2,1,0:T(8,128)(2,1)} %bitcast.20), calls=%async_computation.1 | async-start | bytes 1048576 | tf_op jit(solution)/shard_map/all_to_all | solution.py:292
  107.7 2.7 %shard_map.113.refs_1_ = f32[256,1024]{1,0:T(8,128)S(1)} custom-call(s32[5]{0:T(128)S(1)} %copy-done.16, bf16[512,768]{1,0:T(8,128)(2,1)S(1)} %get-tuple-element.29.refs_1_.refs_7_.refs_5_, bf16[512,1024]{1,0:T(8,128)(2,1)S(1)} %copy-done.6, bf16[256,768]{1,0:T(8,128)(2,1)S(1)} %copy-done.12, bf16[7,256,512]{2,1,0:T(8,128)(2,1)S(1)} %copy-done.1, ...), custom_call_target="tpu_custom_call" | custom-call | flops 805306368 | bytes 4071444 | tf_op jit(solution)/shard_map/pallas_call | solution.py:85
  110.4 4.3 %all-to-all-done.1 = bf16[32,32,256]{2,1,0:T(8,128)(2,1)S(1)} async-done(((bf16[32,32,256]{2,1,0:T(8,128)(2,1)}), bf16[32,32,256]{2,1,0:T(8,128)(2,1)S(1)}, u32[]{:S(2)}, u32[]{:S(2)}) %all-to-all-start.1) | async-done | bytes 524320 | tf_op jit(solution)/shard_map/all_to_all | solution.py:292
  116.8 2.3 %collective-permute-start.20 = (bf16[256,1024]{1,0:T(8,128)(2,1)S(1)}, bf16[256,1024]{1,0:T(8,128)(2,1)S(1)}, u32[]{:S(2)}, u32[]{:S(2)}) collective-permute-start(bf16[256,1024]{1,0:T(8,128)(2,1)S(1)} %shard_map.114.refs_1_), channel_id=1, source_target_pairs={{0,1},{1,0},{2,3},{3,2},{4,5},{5,4},{6,7},{7,6},{8,9},{9,8},{10,11... | collective-permute-start | bytes 1572872 | tf_op jit(solution)/shard_map/ppermute | solution.py:38
  123.0 6.5 %shard_map.115 = (bf16[64,1024]{1,0:T(8,128)(2,1)}, bf16[256,768]{1,0:T(8,128)(2,1)S(1)}) custom-call(s32[5]{0:T(128)S(1)} %copy-done.16, bf16[256,1024]{1,0:T(8,128)(2,1)S(1)} %shard_map.114.refs_1_, bf16[256,1024]{1,0:T(8,128)(2,1)S(1)} %collective-permute-done.20.refs_2_, bf16[2,512,256]{2,1,0:T(8,128)(2,1)} %get-tuple-element.33.refs_3_, ...), custom_call_target="tpu_custom_call" | custom-call | flops 1610612736 | bytes 5771284 | tf_op jit(solution)/shard_map/pallas_call | solution.py:85
  131.2 3.1 %shard_map.116 = bf16[64,768]{1,0:T(8,128)(2,1)} custom-call(s32[5]{0:T(128)S(1)} %copy-done.16, bf16[256,768]{1,0:T(8,128)(2,1)S(1)} %get-tuple-element.34.refs_1_, bf16[256,768]{1,0:T(8,128)(2,1)S(1)} %collective-permute-done.22.refs_2_, bf16[2,512,256]{2,1,0:T(8,128)(2,1)} %get-tuple-element.33.refs_3_, ...), custom_call_target="tpu_custom_call" | custom-call | flops 402653184 | bytes 2621460 | tf_op jit(solution)/shard_map/pallas_call | solution.py:85
  (92 shorter events, 37.2 us)
Async XLA Ops:
  2.1 11.4 %collective-permute-start = (bf16[7,8,512]{2,1,0:T(8,128)(2,1)S(1)}, bf16[7,8,512]{2,1,0:T(8,128)(2,1)S(1)}, u32[]{:S(2)}, u32[]{:S(2)}) collective-permute-start(bf16[7,8,512]{2,1,0:T(8,128)(2,1)S(1)} %shard_map.104), channel_id=1, source_target_pairs={{0,2},{1,3},{2,4},{3,5},{4,6},{5,7},{6,0},{7,1},{8,10},{9,11},{10,... | collective-permute-start | bytes 172040 | tf_op jit(solution)/shard_map/ppermute | solution.py:275
  6.0 11.5 %collective-permute-start.5 = (bf16[7,8,512]{2,1,0:T(8,128)(2,1)S(1)}, bf16[7,8,512]{2,1,0:T(8,128)(2,1)S(1)}, u32[]{:S(2)}, u32[]{:S(2)}) collective-permute-start(bf16[7,8,512]{2,1,0:T(8,128)(2,1)S(1)} %shard_map.104), channel_id=1, source_target_pairs={{0,6},{1,7},{2,0},{3,1},{4,2},{5,3},{6,4},{7,5},{8,14},{9,15},{10,... | collective-permute-start | bytes 172040 | tf_op jit(solution)/shard_map/ppermute | solution.py:275
  9.1 8.3 %collective-permute-start.6 = (bf16[7,8,512]{2,1,0:T(8,128)(2,1)S(1)}, bf16[7,8,512]{2,1,0:T(8,128)(2,1)S(1)}, u32[]{:S(2)}, u32[]{:S(2)}) collective-permute-start(bf16[7,8,512]{2,1,0:T(8,128)(2,1)S(1)} %shard_map.104), channel_id=1, source_target_pairs={{0,4},{1,5},{2,6},{3,7},{4,0},{5,1},{6,2},{7,3},{8,12},{9,13},{10,... | collective-permute-start | bytes 172040 | tf_op jit(solution)/shard_map/ppermute | solution.py:275
  15.0 12.9 %collective-permute-start.1 = (bf16[64,1792]{1,0:T(8,128)(2,1)S(1)}, bf16[64,1792]{1,0:T(8,128)(2,1)S(1)}, u32[]{:S(2)}, u32[]{:S(2)}) collective-permute-start(bf16[64,1792]{1,0:T(8,128)(2,1)S(1)} %shard_map.105.refs_1_), channel_id=1, source_target_pairs={{0,6},{1,7},{2,0},{3,1},{4,2},{5,3},{6,4},{7,5},{8,14},{9,15},{10,... | collective-permute-start | bytes 688136 | tf_op jit(solution)/shard_map/ppermute | solution.py:44
  15.1 12.8 %collective-permute-start.2 = (bf16[64,1792]{1,0:T(8,128)(2,1)S(1)}, bf16[64,1792]{1,0:T(8,128)(2,1)S(1)}, u32[]{:S(2)}, u32[]{:S(2)}) collective-permute-start(bf16[64,1792]{1,0:T(8,128)(2,1)S(1)} %shard_map.105.refs_1_), channel_id=1, source_target_pairs={{0,2},{1,3},{2,4},{3,5},{4,6},{5,7},{6,0},{7,1},{8,10},{9,11},{10,... | collective-permute-start | bytes 688136 | tf_op jit(solution)/shard_map/ppermute | solution.py:43
  17.5 10.4 %collective-permute-start.7 = (bf16[4,7,8,512]{3,2,1,0:T(8,128)(2,1)S(1)}, bf16[4,7,8,512]{3,2,1,0:T(8,128)(2,1)S(1)}, u32[]{:S(2)}, u32[]{:S(2)}) collective-permute-start(bf16[4,7,8,512]{3,2,1,0:T(8,128)(2,1)S(1)} %pad_maximum_fusion.1), channel_id=1, source_target_pairs={{0,96},{1,25},{2,98},{3,27},{4,100},{5,29},{6,102},{7,31},{8,104},... | collective-permute-start | bytes 688136 | tf_op jit(solution)/shard_map/ppermute | solution.py:282
  20.0 7.9 %collective-permute-start.8 = (bf16[4,7,8,512]{3,2,1,0:T(8,128)(2,1)S(1)}, bf16[4,7,8,512]{3,2,1,0:T(8,128)(2,1)S(1)}, u32[]{:S(2)}, u32[]{:S(2)}) collective-permute-start(bf16[4,7,8,512]{3,2,1,0:T(8,128)(2,1)S(1)} %pad_maximum_fusion.1), channel_id=1, source_target_pairs={{0,64},{1,17},{2,66},{3,19},{4,68},{5,21},{6,70},{7,23},{8,72},{9,... | collective-permute-start | bytes 688136 | tf_op jit(solution)/shard_map/ppermute | solution.py:282
  20.6 8.6 %collective-permute-start.9 = (bf16[4,7,8,512]{3,2,1,0:T(8,128)(2,1)S(1)}, bf16[4,7,8,512]{3,2,1,0:T(8,128)(2,1)S(1)}, u32[]{:S(2)}, u32[]{:S(2)}) collective-permute-start(bf16[4,7,8,512]{3,2,1,0:T(8,128)(2,1)S(1)} %pad_maximum_fusion.1), channel_id=1, source_target_pairs={{0,32},{1,9},{2,34},{3,11},{4,36},{5,13},{6,38},{7,15},{8,40},{9,1... | collective-permute-start | bytes 688136 | tf_op jit(solution)/shard_map/ppermute | solution.py:282
  29.3 13.8 %collective-permute-start.11 = (bf16[4,4,7,8,512]{4,3,2,1,0:T(8,128)(2,1)S(1)}, bf16[4,4,7,8,512]{4,3,2,1,0:T(8,128)(2,1)S(1)}, u32[]{:S(2)}, u32[]{:S(2)}) collective-permute-start(bf16[4,4,7,8,512]{4,3,2,1,0:T(8,128)(2,1)S(1)} %pad_maximum_fusion.refs_1_), channel_id=1, source_target_pairs={{0,8},{1,33},{2,10},{3,35},{4,12},{5,37},{6,14},{7,39},{8,16},{9,4... | collective-permute-start | bytes 2752520 | tf_op jit(solution)/shard_map/ppermute | solution.py:43
  30.5 12.6 %collective-permute-start.10 = (bf16[4,4,7,8,512]{4,3,2,1,0:T(8,128)(2,1)S(1)}, bf16[4,4,7,8,512]{4,3,2,1,0:T(8,128)(2,1)S(1)}, u32[]{:S(2)}, u32[]{:S(2)}) collective-permute-start(bf16[4,4,7,8,512]{4,3,2,1,0:T(8,128)(2,1)S(1)} %pad_maximum_fusion.refs_1_), channel_id=1, source_target_pairs={{0,24},{1,97},{2,26},{3,99},{4,28},{5,101},{6,30},{7,103},{8,0},{9... | collective-permute-start | bytes 2752520 | tf_op jit(solution)/shard_map/ppermute | solution.py:44
  32.1 5.9 %collective-permute-start.3 = (bf16[32,1792]{1,0:T(8,128)(2,1)S(1)}, bf16[32,1792]{1,0:T(8,128)(2,1)S(1)}, u32[]{:S(2)}, u32[]{:S(2)}) collective-permute-start(bf16[32,1792]{1,0:T(8,128)(2,1)S(1)} %slice.16), channel_id=1, source_target_pairs={{0,2},{1,3},{2,4},{3,5},{4,6},{5,7},{6,0},{7,1},{8,10},{9,11},{10,... | collective-permute-start | bytes 344072 | tf_op jit(solution)/shard_map/ppermute | solution.py:45
  33.3 6.3 %collective-permute-start.4 = (bf16[32,1792]{1,0:T(8,128)(2,1)S(1)}, bf16[32,1792]{1,0:T(8,128)(2,1)S(1)}, u32[]{:S(2)}, u32[]{:S(2)}) collective-permute-start(bf16[32,1792]{1,0:T(8,128)(2,1)S(1)} %slice.17), channel_id=1, source_target_pairs={{0,6},{1,7},{2,0},{3,1},{4,2},{5,3},{6,4},{7,5},{8,14},{9,15},{10,... | collective-permute-start | bytes 344072 | tf_op jit(solution)/shard_map/ppermute | solution.py:46
  46.7 16.7 %all-to-all-start = ((bf16[32,32,256]{2,1,0:T(8,128)(2,1)}), bf16[32,32,256]{2,1,0:T(8,128)(2,1)}, u32[]{:S(2)}, u32[]{:S(2)}) async-start(bf16[32,32,256]{2,1,0:T(8,128)(2,1)} %bitcast.23), calls=%async_computation | async-start | bytes 1048576 | tf_op jit(solution)/shard_map/all_to_all | solution.py:292
  57.2 20.9 %collective-permute-start.13 = (bf16[256,1024]{1,0:T(8,128)(2,1)}, bf16[256,1024]{1,0:T(8,128)(2,1)S(1)}, u32[]{:S(2)}, u32[]{:S(2)}) collective-permute-start(bf16[256,1024]{1,0:T(8,128)(2,1)} %shard_map.107.refs_3_), channel_id=1, source_target_pairs={{0,1},{1,0},{2,3},{3,2},{4,5},{5,4},{6,7},{7,6},{8,9},{9,8},{10,11... | collective-permute-start | bytes 1572872 | tf_op jit(solution)/shard_map/ppermute | solution.py:38
  63.4 14.8 %collective-permute-start.14 = (bf16[1024,256]{1,0:T(8,128)(2,1)}, bf16[1024,256]{1,0:T(8,128)(2,1)S(1)}, u32[]{:S(2)}, u32[]{:S(2)}) collective-permute-start(bf16[1024,256]{1,0:T(8,128)(2,1)} %bitcast.17.refs_5_), channel_id=1, source_target_pairs={{0,1},{1,0},{2,3},{3,2},{4,5},{5,4},{6,7},{7,6},{8,9},{9,8},{10,11... | collective-permute-start | bytes 1572872 | tf_op jit(solution)/shard_map/ppermute | solution.py:38
  67.3 8.9 %collective-permute-start.15 = (bf16[2,4,7,8,512]{4,3,2,1,0:T(8,128)(2,1)S(1)}, bf16[2,4,7,8,512]{4,3,2,1,0:T(8,128)(2,1)S(1)}, u32[]{:S(2)}, u32[]{:S(2)}) collective-permute-start(bf16[2,4,7,8,512]{4,3,2,1,0:T(8,128)(2,1)S(1)} %slice.18), channel_id=1, source_target_pairs={{0,8},{1,33},{2,10},{3,35},{4,12},{5,37},{6,14},{7,39},{8,16},{9,4... | collective-permute-start | bytes 1376264 | tf_op jit(solution)/shard_map/ppermute | solution.py:45
  67.7 8.5 %collective-permute-start.16 = (bf16[2,4,7,8,512]{4,3,2,1,0:T(8,128)(2,1)S(1)}, bf16[2,4,7,8,512]{4,3,2,1,0:T(8,128)(2,1)S(1)}, u32[]{:S(2)}, u32[]{:S(2)}) collective-permute-start(bf16[2,4,7,8,512]{4,3,2,1,0:T(8,128)(2,1)S(1)} %slice.19), channel_id=1, source_target_pairs={{0,24},{1,97},{2,26},{3,99},{4,28},{5,101},{6,30},{7,103},{8,0},{9... | collective-permute-start | bytes 1376264 | tf_op jit(solution)/shard_map/ppermute | solution.py:46
  70.3 7.8 %collective-permute-start.12 = (bf16[256,768]{1,0:T(8,128)(2,1)S(1)}, bf16[256,768]{1,0:T(8,128)(2,1)S(1)}, u32[]{:S(2)}, u32[]{:S(2)}) collective-permute-start(bf16[256,768]{1,0:T(8,128)(2,1)S(1)} %copy-done.22), channel_id=1, source_target_pairs={{0,1},{1,0},{2,3},{3,2},{4,5},{5,4},{6,7},{7,6},{8,9},{9,8},{10,11... | collective-permute-start | bytes 1179656 | tf_op jit(solution)/shard_map/ppermute | solution.py:38
  77.2 5.8 %collective-permute-start.18 = (bf16[2,512,256]{2,1,0:T(8,128)(2,1)S(1)}, bf16[2,512,256]{2,1,0:T(8,128)(2,1)S(1)}, u32[]{:S(2)}, u32[]{:S(2)}) collective-permute-start(bf16[2,512,256]{2,1,0:T(8,128)(2,1)S(1)} %get-tuple-element.24.refs_3_), channel_id=1, source_target_pairs={{0,1},{1,0},{2,3},{3,2},{4,5},{5,4},{6,7},{7,6},{8,9},{9,8},{10,11... | collective-permute-start | bytes 1572872 | tf_op jit(solution)/shard_map/ppermute | solution.py:38
  82.9 2.0 %collective-permute-start.17 = (bf16[256,1024]{1,0:T(8,128)(2,1)S(1)}, bf16[256,1024]{1,0:T(8,128)(2,1)S(1)}, u32[]{:S(2)}, u32[]{:S(2)}) collective-permute-start(bf16[256,1024]{1,0:T(8,128)(2,1)S(1)} %get-tuple-element.23.refs_1_), channel_id=1, source_target_pairs={{0,1},{1,0},{2,3},{3,2},{4,5},{5,4},{6,7},{7,6},{8,9},{9,8},{10,11... | collective-permute-start | bytes 1572872 | tf_op jit(solution)/shard_map/ppermute | solution.py:38
  91.0 1.9 %collective-permute-start.19 = (bf16[256,768]{1,0:T(8,128)(2,1)S(1)}, bf16[256,768]{1,0:T(8,128)(2,1)S(1)}, u32[]{:S(2)}, u32[]{:S(2)}) collective-permute-start(bf16[256,768]{1,0:T(8,128)(2,1)S(1)} %get-tuple-element.27.refs_1_), channel_id=1, source_target_pairs={{0,1},{1,0},{2,3},{3,2},{4,5},{5,4},{6,7},{7,6},{8,9},{9,8},{10,11... | collective-permute-start | bytes 1179656 | tf_op jit(solution)/shard_map/ppermute | solution.py:38
  98.2 16.6 %all-to-all-start.1 = ((bf16[32,32,256]{2,1,0:T(8,128)(2,1)}), bf16[32,32,256]{2,1,0:T(8,128)(2,1)S(1)}, u32[]{:S(2)}, u32[]{:S(2)}) async-start(bf16[32,32,256]{2,1,0:T(8,128)(2,1)} %bitcast.20), calls=%async_computation.1 | async-start | bytes 1048576 | tf_op jit(solution)/shard_map/all_to_all | solution.py:292
  104.5 14.6 %collective-permute-start.21 = (bf16[2,512,256]{2,1,0:T(8,128)(2,1)}, bf16[2,512,256]{2,1,0:T(8,128)(2,1)}, u32[]{:S(2)}, u32[]{:S(2)}) collective-permute-start(bf16[2,512,256]{2,1,0:T(8,128)(2,1)} %get-tuple-element.33.refs_3_), channel_id=1, source_target_pairs={{0,1},{1,0},{2,3},{3,2},{4,5},{5,4},{6,7},{7,6},{8,9},{9,8},{10,11... | collective-permute-start | bytes 1572872 | tf_op jit(solution)/shard_map/ppermute | solution.py:38
  116.8 3.9 %collective-permute-start.20 = (bf16[256,1024]{1,0:T(8,128)(2,1)S(1)}, bf16[256,1024]{1,0:T(8,128)(2,1)S(1)}, u32[]{:S(2)}, u32[]{:S(2)}) collective-permute-start(bf16[256,1024]{1,0:T(8,128)(2,1)S(1)} %shard_map.114.refs_1_), channel_id=1, source_target_pairs={{0,1},{1,0},{2,3},{3,2},{4,5},{5,4},{6,7},{7,6},{8,9},{9,8},{10,11... | collective-permute-start | bytes 1572872 | tf_op jit(solution)/shard_map/ppermute | solution.py:38
  (24 other events, 177.9 us)

commit v3 on v2

--- a/solution.py
+++ b/solution.py
@@ -121,29 +121,23 @@
     place_half(meta, (own, nxt, far_a, far_b, prev), half, own.shape[1] - half.shape[1])
 
 
-def copy_all(copies, sem):
+def prepare(meta, w_e, w_eo, w_n, w_no, v, e, piece, both, sem):
+    lay = meta[1] >> 1
+    rows = pl.ds(pl.multiple_of(8 * ((meta[1] & 1) * 4 + meta[2]), 8), 8)
+    n = v.shape[1]
+    copies = [
+        (w_e.at[lay, :, rows], piece.at[0:3]),
+        (w_eo.at[lay, rows], piece.at[3]),
+        (w_n.at[lay, :, rows], piece.at[4:6]),
+        (w_no.at[lay, rows], piece.at[6]),
+        (v, both.at[:, :n]),
+        (e, both.at[:, n:]),
+    ]
     copies = [pltpu.make_async_copy(a, b, sem.at[i]) for i, (a, b) in enumerate(copies)]
     for copy in copies:
         copy.start()
     for copy in copies:
         copy.wait()
-
-
-def cut_weights(meta, w_e, w_eo, w_n, w_no, piece, sem):
-    lay = meta[1] >> 1
-    rows = pl.ds(pl.multiple_of(8 * ((meta[1] & 1) * 4 + meta[2]), 8), 8)
-    copies = [
-        (w_e.at[lay, :, rows], piece.at[0:3]),
-        (w_eo.at[lay, rows], piece.at[3]),
-        (w_n.at[lay, :, rows], piece.at[4:6]),
-        (w_no.at[lay, rows], piece.at[6]),
-    ]
-    copy_all(copies, sem)
-
-
-def beside(meta, v, e, both, sem):
-    n = v.shape[1]
-    copy_all([(v, both.at[:, :n]), (e, both.at[:, n:])], sem)
 
 
 def unpack(layer, meta, own, nxt, far_a, far_b, prev, mats, turned):
@@ -265,18 +259,15 @@
     meta = jnp.stack([c >> 1, first, second, k, c]).astype(jnp.int32)
     send, src, dst = (a.reshape(1, -1) for a in (send_rows, edge_src, edge_dst))
 
-    in_hbm = lambda a: pltpu.with_memory_space_constraint(a, pltpu.HBM)
-    weights = (jnp.swapaxes(w_edge_in, 2, 3), w_edge_out, jnp.swapaxes(w_node_in, 2, 3), w_node_out)
-    hbm = pl.BlockSpec(memory_space=pltpu.HBM)
-    (piece,) = call(
-        cut_weights, [((7, 8, LATENT), BF)], meta, *map(in_hbm, weights),
-        scratch=[pltpu.SemaphoreType.DMA((4,))], space=hbm,
+    shared = (jnp.swapaxes(w_edge_in, 2, 3), w_edge_out, jnp.swapaxes(w_node_in, 2, 3), w_node_out, node_feats, edge_feats)
+    piece, both = call(
+        prepare,
+        [((7, 8, LATENT), BF), ((64, n + m), BF)],
+        meta, *(pltpu.with_memory_space_constraint(a, pltpu.HBM) for a in shared),
+        scratch=[pltpu.SemaphoreType.DMA((6,))], space=pl.BlockSpec(memory_space=pltpu.HBM),
     )
     pieces = [piece] + [lax.ppermute(piece, "ch", z_shift(s)) for s in (1, 3, 2)]
-    (both,) = call(
-        beside, [((64, n + m), BF)], meta, in_hbm(node_feats), in_hbm(edge_feats),
-        scratch=[pltpu.SemaphoreType.DMA((2,))], space=hbm, after=pieces[1:2],
-    )
+    both = lax.optimization_barrier((both, pieces[1]))[0]
     wz = jnp.stack(pieces)
     parts = ring_gather(both, "ch", z_shift)
     quarters = [wz] + [lax.ppermute(wz, ("dom", "ch"), ring(1, s)) for s in (3, 2, 1)]
@@ -285,15 +276,15 @@
     w_parts = ring_gather(one, ("dom", "ch"), lambda s: ring(2, s))
 
     v_half, rows = call(
-        send_first, [((HALF, n), BF), ((m, HALF), BF)], meta, *parts, send, flops=2 * HALF * n * m, after=(w_parts[1], w_parts[4])
+        send_first, [((HALF, n), BF), ((m, HALF), BF)], meta, *parts, send, flops=2 * HALF * n * m
     )
 
     def exchange(rows):
         return lax.all_to_all(rows.reshape(32, SLOTS, HALF), "dom", 0, 0, tiled=True).reshape(-1, HALF)
 
-    halo = exchange(rows)
+    halo = exchange(lax.optimization_barrier((rows, w_parts[1], w_parts[4]))[0])
     v_other = swap(v_half)
-    (e_half,) = call(gather_edges, [((HALF, m), BF)], meta, *parts)
+    (e_half,) = call(gather_edges, [((HALF, m), BF)], meta, *parts, flops=8 * HALF * n * m, after=w_parts[2:4])
     e_other = swap(e_half)
     halo_other = swap(halo)
 

time: 135 us -> 132 us (0.978); the launches traced: 134 us -> 130 us
  waiting for transfers between devices: 33.1 us -> 30.1 us
  starting transfers between devices: 52.7 us -> 55 us
  Pallas kernels: 37.7 us -> 35.5 us
  local copies, waits for them, and re-layouts: 9.89 us -> 8.27 us
    all_to_all x2, waiting for transfers between devices: 7.67 us -> 3.57 us  [exchange(): lax.all_to_all(rows.reshape(32, SLOTS, HALF), 'dom', 0, 0, tiled=True)]
    ppermute x2, waiting for transfers between devices: 3.52 us -> 0.01 us  [ring_gather(): prev = lax.ppermute(x, axis, perm(1))]
    ppermute x9, starting transfers between devices: 11.8 us -> 15.4 us  [swap(): return lax.ppermute(x, 'ch', CORE)]
    ppermute x2, waiting for transfers between devices: 7.5 us -> 10.8 us  [ring_gather(): far_a = lax.ppermute(prev[:half], axis, perm(1))]
    pallas_call x13 -> x12, Pallas kernels: 37.7 us -> 35.5 us  [call(): pl.pallas_call(body, out_shape=[jax.ShapeDtypeStruct(s, d) for s, d in ou...]
    unnamed x46 -> x60, local copies, waits for them, and re-layouts: 9.73 us -> 8.1 us
    ppermute x2, starting transfers between devices: 5.09 us -> 3.72 us  [ring_gather(): far_b = lax.ppermute(nxt[half:], axis, perm(3))]
  transfers between devices with their start and end apart: 25 -> 25, of which waited for: 11 -> 11; matrix products, arithmetic and copies ran while one was open for 0% -> 0% of each run, Pallas kernels for 11% -> 12%
where the time goes in v3:
time: 132 us; the launch traced here: 130 us
  starting transfers between devices  55 us (42%)
  Pallas kernels  35.5 us (27%)
  waiting for transfers between devices  30.1 us (23%)
  local copies, waits for them, and re-layouts  8.27 us (6%)
    pallas_call x12, Pallas kernels, call(): pl.pallas_call(body, out_shape=[jax.ShapeDtypeStruct(s, d) for s, d in ou...  35.5 us
    ppermute x9, starting transfers between devices, swap(): return lax.ppermute(x, 'ch', CORE)  15.4 us
    all_to_all x2, starting transfers between devices, exchange(): lax.all_to_all(rows.reshape(32, SLOTS, HALF), 'dom', 0, 0, tiled=True)  12.8 us
    ppermute x3, starting transfers between devices, shards(): lax.ppermute(piece, 'ch', z_shift(s))  11.4 us
    ppermute x2, waiting for transfers between devices, ring_gather(): far_a = lax.ppermute(prev[:half], axis, perm(1))  10.8 us
    unnamed x60, local copies, waits for them, and re-layouts  8.1 us
    ppermute x2, waiting for transfers between devices, ring_gather(): nxt = lax.ppermute(x, axis, perm(3))  7.93 us
    ppermute x9, waiting for transfers between devices, swap(): return lax.ppermute(x, 'ch', CORE)  4.89 us
  transfers between devices with their start and end apart: 25, of which 11 were waited for; matrix products, arithmetic and copies ran while one was open for 0% of the time, Pallas kernels for 12%

profile of v3, /device:TPU:1, one launch (start us, length us, event | category | flops | bytes accessed | tf_op | source)
XLA Modules:
  0.0 129.9 jit_solution(18431164102508094435)
XLA Ops:
  0.7 1.6 %shard_map.104 = (bf16[7,8,512]{2,1,0:T(8,128)(2,1)S(1)}, bf16[64,1792]{1,0:T(8,128)(2,1)S(1)}) custom-call(s32[5]{0:T(128)S(1)} %stack.53.refs_0_, bf16[2,3,64,512]{3,2,1,0:T(8,128)(2,1)} %bitcast.35, bf16[2,64,512]{2,1,0:T(8,128)(2,1)} %refs_2_.1, bf16[2,2,64,512]{3,2,1,0:T(8,128)(2,1)} %bitcast.36, bf16[2,64,512]{2,1,0:T(8,128)(2,1)} %refs_4_.1, ...), custom_call_target="tpu_custom_call" | custom-call | bytes 1146900 | tf_op jit(solution)/shard_map/pallas_call | solution.py:85
  2.4 3.9 %collective-permute-start = (bf16[7,8,512]{2,1,0:T(8,128)(2,1)S(1)}, bf16[7,8,512]{2,1,0:T(8,128)(2,1)S(1)}, u32[]{:S(2)}, u32[]{:S(2)}) collective-permute-start(bf16[7,8,512]{2,1,0:T(8,128)(2,1)S(1)} %get-tuple-element.24), channel_id=1, source_target_pairs={{0,2},{1,3},{2,4},{3,5},{4,6},{5,7},{6,0},{7,1},{8,10},{9,11},{10,... | collective-permute-start | bytes 172040 | tf_op jit(solution)/shard_map/ppermute | solution.py:269
  6.3 3.1 %collective-permute-start.6 = (bf16[7,8,512]{2,1,0:T(8,128)(2,1)S(1)}, bf16[7,8,512]{2,1,0:T(8,128)(2,1)S(1)}, u32[]{:S(2)}, u32[]{:S(2)}) collective-permute-start(bf16[7,8,512]{2,1,0:T(8,128)(2,1)S(1)} %get-tuple-element.24), channel_id=1, source_target_pairs={{0,6},{1,7},{2,0},{3,1},{4,2},{5,3},{6,4},{7,5},{8,14},{9,15},{10,... | collective-permute-start | bytes 172040 | tf_op jit(solution)/shard_map/ppermute | solution.py:269
  9.4 4.4 %collective-permute-start.7 = (bf16[7,8,512]{2,1,0:T(8,128)(2,1)S(1)}, bf16[7,8,512]{2,1,0:T(8,128)(2,1)S(1)}, u32[]{:S(2)}, u32[]{:S(2)}) collective-permute-start(bf16[7,8,512]{2,1,0:T(8,128)(2,1)S(1)} %get-tuple-element.24), channel_id=1, source_target_pairs={{0,4},{1,5},{2,6},{3,7},{4,0},{5,1},{6,2},{7,3},{8,12},{9,13},{10,... | collective-permute-start | bytes 172040 | tf_op jit(solution)/shard_map/ppermute | solution.py:269
  13.8 2.4 %collective-permute-start.2 = (bf16[64,1792]{1,0:T(8,128)(2,1)S(1)}, bf16[64,1792]{1,0:T(8,128)(2,1)S(1)}, u32[]{:S(2)}, u32[]{:S(2)}) collective-permute-start(bf16[64,1792]{1,0:T(8,128)(2,1)S(1)} %get-tuple-element.25.refs_1_), channel_id=1, source_target_pairs={{0,2},{1,3},{2,4},{3,5},{4,6},{5,7},{6,0},{7,1},{8,10},{9,11},{10,... | collective-permute-start | bytes 688136 | tf_op jit(solution)/shard_map/ppermute | solution.py:43
  16.8 2.6 %collective-permute-start.8 = (bf16[4,7,8,512]{3,2,1,0:T(8,128)(2,1)S(1)}, bf16[4,7,8,512]{3,2,1,0:T(8,128)(2,1)S(1)}, u32[]{:S(2)}, u32[]{:S(2)}) collective-permute-start(bf16[4,7,8,512]{3,2,1,0:T(8,128)(2,1)S(1)} %pad_maximum_fusion.1), channel_id=1, source_target_pairs={{0,96},{1,25},{2,98},{3,27},{4,100},{5,29},{6,102},{7,31},{8,104},... | collective-permute-start | bytes 688136 | tf_op jit(solution)/shard_map/ppermute | solution.py:273
  20.5 7.9 %collective-permute-done.1.refs_2_ = bf16[64,1792]{1,0:T(8,128)(2,1)S(1)} collective-permute-done((bf16[64,1792]{1,0:T(8,128)(2,1)S(1)}, bf16[64,1792]{1,0:T(8,128)(2,1)S(1)}, u32[]{:S(2)}, u32[]{:S(2)}) %collective-permute-start.1) | collective-permute-done | bytes 229408 | tf_op jit(solution)/shard_map/ppermute | solution.py:44
  33.1 2.1 %collective-permute-start.4 = (bf16[32,1792]{1,0:T(8,128)(2,1)S(1)}, bf16[32,1792]{1,0:T(8,128)(2,1)S(1)}, u32[]{:S(2)}, u32[]{:S(2)}) collective-permute-start(bf16[32,1792]{1,0:T(8,128)(2,1)S(1)} %slice.17), channel_id=1, source_target_pairs={{0,6},{1,7},{2,0},{3,1},{4,2},{5,3},{6,4},{7,5},{8,14},{9,15},{10,... | collective-permute-start | bytes 344072 | tf_op jit(solution)/shard_map/ppermute | solution.py:46
  35.2 2.5 %collective-permute-done.3.refs_3_ = bf16[32,1792]{1,0:T(8,128)(2,1)S(1)} collective-permute-done((bf16[32,1792]{1,0:T(8,128)(2,1)S(1)}, bf16[32,1792]{1,0:T(8,128)(2,1)S(1)}, u32[]{:S(2)}, u32[]{:S(2)}) %collective-permute-start.3) | collective-permute-done | bytes 114720 | tf_op jit(solution)/shard_map/ppermute | solution.py:45
  37.7 2.2 %collective-permute-done.4.refs_4_ = bf16[32,1792]{1,0:T(8,128)(2,1)S(1)} collective-permute-done((bf16[32,1792]{1,0:T(8,128)(2,1)S(1)}, bf16[32,1792]{1,0:T(8,128)(2,1)S(1)}, u32[]{:S(2)}, u32[]{:S(2)}) %collective-permute-start.4) | collective-permute-done | bytes 114720 | tf_op jit(solution)/shard_map/ppermute | solution.py:46
  39.9 2.8 %shard_map.105 = (bf16[256,768]{1,0:T(8,128)(2,1)S(1)}, bf16[1024,256]{1,0:T(8,128)(2,1)}) custom-call(s32[5]{0:T(128)S(1)} %stack.53.refs_0_, bf16[64,1792]{1,0:T(8,128)(2,1)S(1)} %get-tuple-element.25.refs_1_, bf16[64,1792]{1,0:T(8,128)(2,1)S(1)} %collective-permute-done.1.refs_2_, bf16[32,1792]{1,0:T(8,128)(2,1)S(1)} %collective-permute-done.3.refs_3_, ...), custom_call_target="tpu_custom_call" | custom-call | flops 402653184 | bytes 921620 | tf_op jit(solution)/shard_map/pallas_call | solution.py:85
  42.8 6.6 %all-to-all-start = ((bf16[32,32,256]{2,1,0:T(8,128)(2,1)}), bf16[32,32,256]{2,1,0:T(8,128)(2,1)}, u32[]{:S(2)}, u32[]{:S(2)}) async-start(bf16[32,32,256]{2,1,0:T(8,128)(2,1)} %bitcast.16), calls=%async_computation | async-start | bytes 1048576 | tf_op jit(solution)/shard_map/all_to_all | solution.py:283
  52.4 8.2 %collective-permute-done.12.refs_6_.refs_3_ = bf16[2,4,7,8,512]{4,3,2,1,0:T(8,128)(2,1)S(1)} collective-permute-done((bf16[2,4,7,8,512]{4,3,2,1,0:T(8,128)(2,1)S(1)}, bf16[2,4,7,8,512]{4,3,2,1,0:T(8,128)(2,1)S(1)}, u32[]{:S(2)}, u32[]{:S(2)}) %collective-permute-start.12) | collective-permute-done | bytes 458784 | tf_op jit(solution)/shard_map/ppermute | solution.py:45
  62.0 10.2 %collective-permute-start.15 = (bf16[256,1024]{1,0:T(8,128)(2,1)}, bf16[256,1024]{1,0:T(8,128)(2,1)}, u32[]{:S(2)}, u32[]{:S(2)}) collective-permute-start(bf16[256,1024]{1,0:T(8,128)(2,1)} %shard_map.106.refs_3_), channel_id=1, source_target_pairs={{0,1},{1,0},{2,3},{3,2},{4,5},{5,4},{6,7},{7,6},{8,9},{9,8},{10,11... | collective-permute-start | bytes 1572872 | tf_op jit(solution)/shard_map/ppermute | solution.py:38
  75.3 4.8 %shard_map.108 = (bf16[512,768]{1,0:T(8,128)(2,1)S(1)}, bf16[512,1024]{1,0:T(8,128)(2,1)S(1)}, bf16[256,1024]{1,0:T(8,128)(2,1)S(1)}) custom-call(s32[5]{0:T(128)S(1)} %stack.53.refs_0_, bf16[256,768]{1,0:T(8,128)(2,1)S(1)} %copy-done.23, bf16[256,768]{1,0:T(8,128)(2,1)S(1)} %collective-permute-done.5.refs_2_, bf16[256,1024]{1,0:T(8,128)(2,1)} %shard_map.106.refs_3_, ...), custom_call_target="tpu_custom_call" | custom-call | flops 1879048192 | bytes 4726804 | tf_op jit(solution)/shard_map/pallas_call | solution.py:85
  82.2 5.2 %shard_map.109 = (bf16[512,1024]{1,0:T(8,128)(2,1)S(1)}, bf16[256,768]{1,0:T(8,128)(2,1)S(1)}) custom-call(s32[5]{0:T(128)S(1)} %stack.53.refs_0_, bf16[256,1024]{1,0:T(8,128)(2,1)S(1)} %get-tuple-element.31.refs_1_, bf16[256,1024]{1,0:T(8,128)(2,1)S(1)} %collective-permute-done.17.refs_2_, bf16[2,512,256]{2,1,0:T(8,128)(2,1)S(1)} %get-tuple-element.32.refs_3_, ...), custom_call_target="tpu_custom_call" | custom-call | flops 1610612736 | bytes 5771284 | tf_op jit(solution)/shard_map/pallas_call | solution.py:85
  90.1 3.6 %shard_map.111 = (bf16[512,768]{1,0:T(8,128)(2,1)S(1)}, bf16[256,768]{1,0:T(8,128)(2,1)S(1)}, bf16[1024,256]{1,0:T(8,128)(2,1)S(1)}) custom-call(s32[5]{0:T(128)S(1)} %stack.53.refs_0_, bf16[256,768]{1,0:T(8,128)(2,1)S(1)} %get-tuple-element.35.refs_1_, bf16[256,768]{1,0:T(8,128)(2,1)S(1)} %collective-permute-done.19.refs_2_, ...), custom_call_target="tpu_custom_call" | custom-call | flops 805306368 | bytes 4460564 | tf_op jit(solution)/shard_map/pallas_call | solution.py:85
  95.3 6.2 %all-to-all-start.1 = ((bf16[32,32,256]{2,1,0:T(8,128)(2,1)}), bf16[32,32,256]{2,1,0:T(8,128)(2,1)S(1)}, u32[]{:S(2)}, u32[]{:S(2)}) async-start(bf16[32,32,256]{2,1,0:T(8,128)(2,1)} %bitcast.23), calls=%async_computation.1 | async-start | bytes 1048576 | tf_op jit(solution)/shard_map/all_to_all | solution.py:283
  104.4 2.7 %shard_map.112.refs_1_ = f32[256,1024]{1,0:T(8,128)S(1)} custom-call(s32[5]{0:T(128)S(1)} %stack.53.refs_0_, bf16[512,768]{1,0:T(8,128)(2,1)S(1)} %get-tuple-element.37.refs_1_.refs_7_.refs_5_, bf16[512,1024]{1,0:T(8,128)(2,1)S(1)} %copy-done.10, bf16[256,768]{1,0:T(8,128)(2,1)S(1)} %copy-done.16, ...), custom_call_target="tpu_custom_call" | custom-call | flops 805306368 | bytes 4071444 | tf_op jit(solution)/shard_map/pallas_call | solution.py:85
  108.2 3.6 %all-to-all-done.1 = bf16[32,32,256]{2,1,0:T(8,128)(2,1)S(1)} async-done(((bf16[32,32,256]{2,1,0:T(8,128)(2,1)}), bf16[32,32,256]{2,1,0:T(8,128)(2,1)S(1)}, u32[]{:S(2)}, u32[]{:S(2)}) %all-to-all-start.1) | async-done | bytes 524320 | tf_op jit(solution)/shard_map/all_to_all | solution.py:283
  113.0 2.0 %shard_map.113.refs_1_ = bf16[256,1024]{1,0:T(8,128)(2,1)S(1)} custom-call(s32[5]{0:T(128)S(1)} %stack.53.refs_0_, f32[256,1024]{1,0:T(8,128)S(1)} %copy-done.5, bf16[1024,256]{1,0:T(8,128)(2,1)S(1)} %bitcast.22, s32[1,1024]{1,0:T(1,128)S(1)} %bitcast.27), custom_call_target="tpu_custom_call" | custom-call | flops 536870912 | bytes 1576980 | tf_op jit(solution)/shard_map/pallas_call | solution.py:85
  115.0 2.3 %collective-permute-start.20 = (bf16[256,1024]{1,0:T(8,128)(2,1)S(1)}, bf16[256,1024]{1,0:T(8,128)(2,1)S(1)}, u32[]{:S(2)}, u32[]{:S(2)}) collective-permute-start(bf16[256,1024]{1,0:T(8,128)(2,1)S(1)} %shard_map.113.refs_1_), channel_id=1, source_target_pairs={{0,1},{1,0},{2,3},{3,2},{4,5},{5,4},{6,7},{7,6},{8,9},{9,8},{10,11... | collective-permute-start | bytes 1572872 | tf_op jit(solution)/shard_map/ppermute | solution.py:38
  118.9 6.3 %shard_map.114 = (bf16[64,1024]{1,0:T(8,128)(2,1)}, bf16[256,768]{1,0:T(8,128)(2,1)S(1)}) custom-call(s32[5]{0:T(128)S(1)} %stack.53.refs_0_, bf16[256,1024]{1,0:T(8,128)(2,1)S(1)} %shard_map.113.refs_1_, bf16[256,1024]{1,0:T(8,128)(2,1)S(1)} %collective-permute-done.20.refs_2_, bf16[2,512,256]{2,1,0:T(8,128)(2,1)S(1)} %copy-done.14, ...), custom_call_target="tpu_custom_call" | custom-call | flops 1610612736 | bytes 5771284 | tf_op jit(solution)/shard_map/pallas_call | solution.py:85
  126.9 3.0 %shard_map.115 = bf16[64,768]{1,0:T(8,128)(2,1)} custom-call(s32[5]{0:T(128)S(1)} %stack.53.refs_0_, bf16[256,768]{1,0:T(8,128)(2,1)S(1)} %get-tuple-element.42.refs_1_, bf16[256,768]{1,0:T(8,128)(2,1)S(1)} %collective-permute-done.22.refs_2_, bf16[2,512,256]{2,1,0:T(8,128)(2,1)S(1)} %copy-done.14, bf16[2,512,256]{2,1,0:T(8,128)(2,1)} %collective-permute-done.21.refs_4_, ...), custom_call_target="tpu_custom_call" | custom-call | flops 402653184 | bytes 2621460 | tf_op jit(solution)/shard_map/pallas_call | solution.py:85
  (105 shorter events, 28.7 us)
Async XLA Ops:
  2.4 11.4 %collective-permute-start = (bf16[7,8,512]{2,1,0:T(8,128)(2,1)S(1)}, bf16[7,8,512]{2,1,0:T(8,128)(2,1)S(1)}, u32[]{:S(2)}, u32[]{:S(2)}) collective-permute-start(bf16[7,8,512]{2,1,0:T(8,128)(2,1)S(1)} %get-tuple-element.24), channel_id=1, source_target_pairs={{0,2},{1,3},{2,4},{3,5},{4,6},{5,7},{6,0},{7,1},{8,10},{9,11},{10,... | collective-permute-start | bytes 172040 | tf_op jit(solution)/shard_map/ppermute | solution.py:269
  6.3 9.9 %collective-permute-start.6 = (bf16[7,8,512]{2,1,0:T(8,128)(2,1)S(1)}, bf16[7,8,512]{2,1,0:T(8,128)(2,1)S(1)}, u32[]{:S(2)}, u32[]{:S(2)}) collective-permute-start(bf16[7,8,512]{2,1,0:T(8,128)(2,1)S(1)} %get-tuple-element.24), channel_id=1, source_target_pairs={{0,6},{1,7},{2,0},{3,1},{4,2},{5,3},{6,4},{7,5},{8,14},{9,15},{10,... | collective-permute-start | bytes 172040 | tf_op jit(solution)/shard_map/ppermute | solution.py:269
  9.4 7.4 %collective-permute-start.7 = (bf16[7,8,512]{2,1,0:T(8,128)(2,1)S(1)}, bf16[7,8,512]{2,1,0:T(8,128)(2,1)S(1)}, u32[]{:S(2)}, u32[]{:S(2)}) collective-permute-start(bf16[7,8,512]{2,1,0:T(8,128)(2,1)S(1)} %get-tuple-element.24), channel_id=1, source_target_pairs={{0,4},{1,5},{2,6},{3,7},{4,0},{5,1},{6,2},{7,3},{8,12},{9,13},{10,... | collective-permute-start | bytes 172040 | tf_op jit(solution)/shard_map/ppermute | solution.py:269
  13.8 14.6 %collective-permute-start.1 = (bf16[64,1792]{1,0:T(8,128)(2,1)S(1)}, bf16[64,1792]{1,0:T(8,128)(2,1)S(1)}, u32[]{:S(2)}, u32[]{:S(2)}) collective-permute-start(bf16[64,1792]{1,0:T(8,128)(2,1)S(1)} %get-tuple-element.25.refs_1_), channel_id=1, source_target_pairs={{0,6},{1,7},{2,0},{3,1},{4,2},{5,3},{6,4},{7,5},{8,14},{9,15},{10,... | collective-permute-start | bytes 688136 | tf_op jit(solution)/shard_map/ppermute | solution.py:44
  13.8 14.6 %collective-permute-start.2 = (bf16[64,1792]{1,0:T(8,128)(2,1)S(1)}, bf16[64,1792]{1,0:T(8,128)(2,1)S(1)}, u32[]{:S(2)}, u32[]{:S(2)}) collective-permute-start(bf16[64,1792]{1,0:T(8,128)(2,1)S(1)} %get-tuple-element.25.refs_1_), channel_id=1, source_target_pairs={{0,2},{1,3},{2,4},{3,5},{4,6},{5,7},{6,0},{7,1},{8,10},{9,11},{10,... | collective-permute-start | bytes 688136 | tf_op jit(solution)/shard_map/ppermute | solution.py:43
  16.8 11.6 %collective-permute-start.8 = (bf16[4,7,8,512]{3,2,1,0:T(8,128)(2,1)S(1)}, bf16[4,7,8,512]{3,2,1,0:T(8,128)(2,1)S(1)}, u32[]{:S(2)}, u32[]{:S(2)}) collective-permute-start(bf16[4,7,8,512]{3,2,1,0:T(8,128)(2,1)S(1)} %pad_maximum_fusion.1), channel_id=1, source_target_pairs={{0,96},{1,25},{2,98},{3,27},{4,100},{5,29},{6,102},{7,31},{8,104},... | collective-permute-start | bytes 688136 | tf_op jit(solution)/shard_map/ppermute | solution.py:273
  19.3 9.1 %collective-permute-start.9 = (bf16[4,7,8,512]{3,2,1,0:T(8,128)(2,1)S(1)}, bf16[4,7,8,512]{3,2,1,0:T(8,128)(2,1)S(1)}, u32[]{:S(2)}, u32[]{:S(2)}) collective-permute-start(bf16[4,7,8,512]{3,2,1,0:T(8,128)(2,1)S(1)} %pad_maximum_fusion.1), channel_id=1, source_target_pairs={{0,64},{1,17},{2,66},{3,19},{4,68},{5,21},{6,70},{7,23},{8,72},{9,... | collective-permute-start | bytes 688136 | tf_op jit(solution)/shard_map/ppermute | solution.py:273
  19.9 8.6 %collective-permute-start.10 = (bf16[4,7,8,512]{3,2,1,0:T(8,128)(2,1)S(1)}, bf16[4,7,8,512]{3,2,1,0:T(8,128)(2,1)S(1)}, u32[]{:S(2)}, u32[]{:S(2)}) collective-permute-start(bf16[4,7,8,512]{3,2,1,0:T(8,128)(2,1)S(1)} %pad_maximum_fusion.1), channel_id=1, source_target_pairs={{0,32},{1,9},{2,34},{3,11},{4,36},{5,13},{6,38},{7,15},{8,40},{9,1... | collective-permute-start | bytes 688136 | tf_op jit(solution)/shard_map/ppermute | solution.py:273
  28.6 14.2 %collective-permute-start.11 = (bf16[4,4,7,8,512]{4,3,2,1,0:T(8,128)(2,1)S(1)}, bf16[4,4,7,8,512]{4,3,2,1,0:T(8,128)(2,1)S(1)}, u32[]{:S(2)}, u32[]{:S(2)}) collective-permute-start(bf16[4,4,7,8,512]{4,3,2,1,0:T(8,128)(2,1)S(1)} %pad_maximum_fusion.refs_1_), channel_id=1, source_target_pairs={{0,8},{1,33},{2,10},{3,35},{4,12},{5,37},{6,14},{7,39},{8,16},{9,4... | collective-permute-start | bytes 2752520 | tf_op jit(solution)/shard_map/ppermute | solution.py:43
  29.9 12.9 %collective-permute-start.13 = (bf16[4,4,7,8,512]{4,3,2,1,0:T(8,128)(2,1)S(1)}, bf16[4,4,7,8,512]{4,3,2,1,0:T(8,128)(2,1)S(1)}, u32[]{:S(2)}, u32[]{:S(2)}) collective-permute-start(bf16[4,4,7,8,512]{4,3,2,1,0:T(8,128)(2,1)S(1)} %pad_maximum_fusion.refs_1_), channel_id=1, source_target_pairs={{0,24},{1,97},{2,26},{3,99},{4,28},{5,101},{6,30},{7,103},{8,0},{9... | collective-permute-start | bytes 2752520 | tf_op jit(solution)/shard_map/ppermute | solution.py:44
  31.5 6.3 %collective-permute-start.3 = (bf16[32,1792]{1,0:T(8,128)(2,1)S(1)}, bf16[32,1792]{1,0:T(8,128)(2,1)S(1)}, u32[]{:S(2)}, u32[]{:S(2)}) collective-permute-start(bf16[32,1792]{1,0:T(8,128)(2,1)S(1)} %slice.16), channel_id=1, source_target_pairs={{0,2},{1,3},{2,4},{3,5},{4,6},{5,7},{6,0},{7,1},{8,10},{9,11},{10,... | collective-permute-start | bytes 344072 | tf_op jit(solution)/shard_map/ppermute | solution.py:45
  33.1 6.9 %collective-permute-start.4 = (bf16[32,1792]{1,0:T(8,128)(2,1)S(1)}, bf16[32,1792]{1,0:T(8,128)(2,1)S(1)}, u32[]{:S(2)}, u32[]{:S(2)}) collective-permute-start(bf16[32,1792]{1,0:T(8,128)(2,1)S(1)} %slice.17), channel_id=1, source_target_pairs={{0,6},{1,7},{2,0},{3,1},{4,2},{5,3},{6,4},{7,5},{8,14},{9,15},{10,... | collective-permute-start | bytes 344072 | tf_op jit(solution)/shard_map/ppermute | solution.py:46
  42.8 29.4 %all-to-all-start = ((bf16[32,32,256]{2,1,0:T(8,128)(2,1)}), bf16[32,32,256]{2,1,0:T(8,128)(2,1)}, u32[]{:S(2)}, u32[]{:S(2)}) async-start(bf16[32,32,256]{2,1,0:T(8,128)(2,1)} %bitcast.16), calls=%async_computation | async-start | bytes 1048576 | tf_op jit(solution)/shard_map/all_to_all | solution.py:283
  49.5 11.1 %collective-permute-start.12 = (bf16[2,4,7,8,512]{4,3,2,1,0:T(8,128)(2,1)S(1)}, bf16[2,4,7,8,512]{4,3,2,1,0:T(8,128)(2,1)S(1)}, u32[]{:S(2)}, u32[]{:S(2)}) collective-permute-start(bf16[2,4,7,8,512]{4,3,2,1,0:T(8,128)(2,1)S(1)} %slice.18), channel_id=1, source_target_pairs={{0,8},{1,33},{2,10},{3,35},{4,12},{5,37},{6,14},{7,39},{8,16},{9,4... | collective-permute-start | bytes 1376264 | tf_op jit(solution)/shard_map/ppermute | solution.py:45
  50.8 9.8 %collective-permute-start.14 = (bf16[2,4,7,8,512]{4,3,2,1,0:T(8,128)(2,1)S(1)}, bf16[2,4,7,8,512]{4,3,2,1,0:T(8,128)(2,1)S(1)}, u32[]{:S(2)}, u32[]{:S(2)}) collective-permute-start(bf16[2,4,7,8,512]{4,3,2,1,0:T(8,128)(2,1)S(1)} %slice.19), channel_id=1, source_target_pairs={{0,24},{1,97},{2,26},{3,99},{4,28},{5,101},{6,30},{7,103},{8,0},{9... | collective-permute-start | bytes 1376264 | tf_op jit(solution)/shard_map/ppermute | solution.py:46
  62.0 13.3 %collective-permute-start.15 = (bf16[256,1024]{1,0:T(8,128)(2,1)}, bf16[256,1024]{1,0:T(8,128)(2,1)}, u32[]{:S(2)}, u32[]{:S(2)}) collective-permute-start(bf16[256,1024]{1,0:T(8,128)(2,1)} %shard_map.106.refs_3_), channel_id=1, source_target_pairs={{0,1},{1,0},{2,3},{3,2},{4,5},{5,4},{6,7},{7,6},{8,9},{9,8},{10,11... | collective-permute-start | bytes 1572872 | tf_op jit(solution)/shard_map/ppermute | solution.py:38
  72.3 3.1 %collective-permute-start.16 = (bf16[1024,256]{1,0:T(8,128)(2,1)}, bf16[1024,256]{1,0:T(8,128)(2,1)S(1)}, u32[]{:S(2)}, u32[]{:S(2)}) collective-permute-start(bf16[1024,256]{1,0:T(8,128)(2,1)} %bitcast.17.refs_5_), channel_id=1, source_target_pairs={{0,1},{1,0},{2,3},{3,2},{4,5},{5,4},{6,7},{7,6},{8,9},{9,8},{10,11... | collective-permute-start | bytes 1572872 | tf_op jit(solution)/shard_map/ppermute | solution.py:38
  72.5 2.8 %collective-permute-start.5 = (bf16[256,768]{1,0:T(8,128)(2,1)}, bf16[256,768]{1,0:T(8,128)(2,1)S(1)}, u32[]{:S(2)}, u32[]{:S(2)}) collective-permute-start(bf16[256,768]{1,0:T(8,128)(2,1)} %copy-done.22), channel_id=1, source_target_pairs={{0,1},{1,0},{2,3},{3,2},{4,5},{5,4},{6,7},{7,6},{8,9},{9,8},{10,11... | collective-permute-start | bytes 1179656 | tf_op jit(solution)/shard_map/ppermute | solution.py:38
  74.8 5.8 %collective-permute-start.18 = (bf16[2,512,256]{2,1,0:T(8,128)(2,1)S(1)}, bf16[2,512,256]{2,1,0:T(8,128)(2,1)S(1)}, u32[]{:S(2)}, u32[]{:S(2)}) collective-permute-start(bf16[2,512,256]{2,1,0:T(8,128)(2,1)S(1)} %get-tuple-element.32.refs_3_), channel_id=1, source_target_pairs={{0,1},{1,0},{2,3},{3,2},{4,5},{5,4},{6,7},{7,6},{8,9},{9,8},{10,11... | collective-permute-start | bytes 1572872 | tf_op jit(solution)/shard_map/ppermute | solution.py:38
  80.1 2.0 %collective-permute-start.17 = (bf16[256,1024]{1,0:T(8,128)(2,1)S(1)}, bf16[256,1024]{1,0:T(8,128)(2,1)S(1)}, u32[]{:S(2)}, u32[]{:S(2)}) collective-permute-start(bf16[256,1024]{1,0:T(8,128)(2,1)S(1)} %get-tuple-element.31.refs_1_), channel_id=1, source_target_pairs={{0,1},{1,0},{2,3},{3,2},{4,5},{5,4},{6,7},{7,6},{8,9},{9,8},{10,11... | collective-permute-start | bytes 1572872 | tf_op jit(solution)/shard_map/ppermute | solution.py:38
  88.3 1.7 %collective-permute-start.19 = (bf16[256,768]{1,0:T(8,128)(2,1)S(1)}, bf16[256,768]{1,0:T(8,128)(2,1)S(1)}, u32[]{:S(2)}, u32[]{:S(2)}) collective-permute-start(bf16[256,768]{1,0:T(8,128)(2,1)S(1)} %get-tuple-element.35.refs_1_), channel_id=1, source_target_pairs={{0,1},{1,0},{2,3},{3,2},{4,5},{5,4},{6,7},{7,6},{8,9},{9,8},{10,11... | collective-permute-start | bytes 1179656 | tf_op jit(solution)/shard_map/ppermute | solution.py:38
  95.3 16.5 %all-to-all-start.1 = ((bf16[32,32,256]{2,1,0:T(8,128)(2,1)}), bf16[32,32,256]{2,1,0:T(8,128)(2,1)S(1)}, u32[]{:S(2)}, u32[]{:S(2)}) async-start(bf16[32,32,256]{2,1,0:T(8,128)(2,1)} %bitcast.23), calls=%async_computation.1 | async-start | bytes 1048576 | tf_op jit(solution)/shard_map/all_to_all | solution.py:283
  101.5 15.9 %collective-permute-start.21 = (bf16[2,512,256]{2,1,0:T(8,128)(2,1)}, bf16[2,512,256]{2,1,0:T(8,128)(2,1)}, u32[]{:S(2)}, u32[]{:S(2)}) collective-permute-start(bf16[2,512,256]{2,1,0:T(8,128)(2,1)} %copy-done.13), channel_id=1, source_target_pairs={{0,1},{1,0},{2,3},{3,2},{4,5},{5,4},{6,7},{7,6},{8,9},{9,8},{10,11... | collective-permute-start | bytes 1572872 | tf_op jit(solution)/shard_map/ppermute | solution.py:38
  115.0 3.9 %collective-permute-start.20 = (bf16[256,1024]{1,0:T(8,128)(2,1)S(1)}, bf16[256,1024]{1,0:T(8,128)(2,1)S(1)}, u32[]{:S(2)}, u32[]{:S(2)}) collective-permute-start(bf16[256,1024]{1,0:T(8,128)(2,1)S(1)} %shard_map.113.refs_1_), channel_id=1, source_target_pairs={{0,1},{1,0},{2,3},{3,2},{4,5},{5,4},{6,7},{7,6},{8,9},{9,8},{10,11... | collective-permute-start | bytes 1572872 | tf_op jit(solution)/shard_map/ppermute | solution.py:38
  (31 other events, 264.5 us)

commit v4 on v3

--- a/solution.py
+++ b/solution.py
@@ -10,7 +10,7 @@
 LATENT = 512
 HALF = 256
 SLOTS = 32
-CHUNK = 256
+CHUNK = 512
 BF = jnp.bfloat16
 F32 = jnp.float32
 
@@ -51,10 +51,11 @@
     return lax.dot_general(a, b, (((ca,), (cb,)), ((), ())), preferred_element_type=F32)
 
 
-def norm_add(msg, residual):
+def norm_add(msg, residual, part=None):
     mean = jnp.sum(msg, axis=0, keepdims=True) / LATENT
     var = jnp.sum(msg * msg, axis=0, keepdims=True) / LATENT - mean * mean
-    return (residual.astype(F32) + (msg - mean) * lax.rsqrt(var + 1e-05)).astype(BF)
+    part = msg if part is None else part
+    return (residual.astype(F32) + (part - mean) * lax.rsqrt(var + 1e-05)).astype(BF)
 
 
 def silu(x):
@@ -63,15 +64,13 @@
 
 def hot(idx, first, rows):
     where = lax.broadcasted_iota(jnp.int32, (rows, idx.shape[1]), 0) + first == idx
-    return jnp.where(where, 1.0, 0.0).astype(BF)
+    return where.astype(BF)
 
 
 def chunks(n, body):
-    def step(i, carry):
-        body(pl.ds(pl.multiple_of(i * CHUNK, CHUNK), CHUNK), i * CHUNK)
-        return carry
-
-    lax.fori_loop(0, n // CHUNK, step, 0)
+    size = CHUNK if n % CHUNK == 0 else n // 2
+    for first in range(0, n, size):
+        body(slice(first, first + size), first)
 
 
 def call(kernel, outs, *args, scratch=(), flops=0, space=VMEM, after=()):
@@ -140,7 +139,8 @@
         copy.wait()
 
 
-def unpack(layer, meta, own, nxt, far_a, far_b, prev, mats, turned):
+def unpack(layer, meta, own, nxt, far_a, far_b, prev, mats, nodes, turned, outs):
+    where = [mats.at[0], mats.at[1], mats.at[2], outs.at[0], nodes.at[0], nodes.at[1], outs.at[1]]
     for s in range(4):
         for r in range(4):
             a = (meta[1] + r) & 3
@@ -150,10 +150,10 @@
             @pl.when((a >> 1) == layer)
             def _():
                 for m in range(7):
-                    mats[m, pl.ds(at, 32), :] = ref[row, :, m].astype(F32).reshape(32, LATENT).astype(BF)
-
-    turned[0] = mats[3].astype(F32).T.astype(BF)
-    turned[1] = mats[6].astype(F32).T.astype(BF)
+                    where[m][pl.ds(at, 32), :] = ref[row, :, m].astype(F32).reshape(32, LATENT).astype(BF)
+
+    turned[0] = outs[0].astype(F32).T.astype(BF)
+    turned[1] = outs[1].astype(F32).T.astype(BF)
 
 
 def interleave(meta, own, other, out):
@@ -188,37 +188,49 @@
     chunks(hidden.shape[1], body)
 
 
-def aggregate(meta, hid, hid_other, turned, turned_other, mats, e_all, v_all, dst, e_new, hidden):
+def new_edges(hid, hid_other, turned, turned_other, e_all, e_new):
     def edges(sl, _):
         msg = dot(turned[0], hid[:, sl]) + dot(turned_other[0], hid_other[:, sl])
         e_new[:, sl] = norm_add(msg, e_all[:, sl])
 
     chunks(e_new.shape[1], edges)
 
-    def nodes(sl, first):
-        agg = dot(e_new[...], hot(dst[...], first, CHUNK), 1, 1).astype(BF)
-        hidden[:, sl] = silu(dot(mats[4], v_all[:, sl]) + dot(mats[5], agg))
-
-    chunks(hidden.shape[1], nodes)
-
-
-def aggregate_last(meta, hid, hid_other, turned, turned_other, mats, e_all, v_all, dst, e_out, hidden, e_new):
-    aggregate(meta, hid, hid_other, turned, turned_other, mats, e_all, v_all, dst, e_new, hidden)
-    e_out[...] = e_new[pl.ds(pl.multiple_of(meta[4] * 64, 64), 64), :]
-
-
-def node_norm(hid, hid_other, turned, turned_other, v_all, v_new):
-    def nodes(sl, _):
-        msg = dot(turned[1], hid[:, sl]) + dot(turned_other[1], hid_other[:, sl])
+
+def node_message(first, sl, turned, turned_other, nodes, nodes_other, e_new, v_all, dst):
+    agg = dot(e_new[...], hot(dst[...], first, sl.stop - sl.start), 1, 1).astype(BF)
+    msg = dot(turned[1], silu(dot(nodes[0], v_all[:, sl]) + dot(nodes[1], agg)))
+    return msg + dot(turned_other[1], silu(dot(nodes_other[0], v_all[:, sl]) + dot(nodes_other[1], agg)))
+
+
+def tail_first(
+    meta, hid, hid_other, turned, turned_other, nodes, nodes_other, e_all, v_all, dst, mats_next, send,
+    e_new, v_new, sender, rows,
+):
+    new_edges(hid, hid_other, turned, turned_other, e_all, e_new)
+
+    def body(sl, first):
+        msg = node_message(first, sl, turned, turned_other, nodes, nodes_other, e_new, v_all, dst)
         v_new[:, sl] = norm_add(msg, v_all[:, sl])
 
-    chunks(v_new.shape[1], nodes)
-
-
-def send_next(meta, hid, hid_other, turned, turned_other, v_all, mats, send, v_new, sender, rows):
-    node_norm(hid, hid_other, turned, turned_other, v_all, v_new)
-    sender[...] = dot(mats[1], v_new[...]).astype(BF)
+    chunks(v_new.shape[1], body)
+    sender[...] = dot(mats_next[1], v_new[...]).astype(BF)
     select_rows(send, sender[...], rows)
+
+
+def tail_last(
+    meta, hid, hid_other, turned, turned_other, nodes, nodes_other, e_all, v_all, dst,
+    e_out, v_out, e_new, sums,
+):
+    new_edges(hid, hid_other, turned, turned_other, e_all, e_new)
+    mine = pl.ds(pl.multiple_of(meta[4] * 64, 64), 64)
+    e_out[...] = e_new[mine, :]
+
+    def body(sl, first):
+        msg = node_message(first, sl, turned, turned_other, nodes, nodes_other, e_new, v_all, dst)
+        sums[...] = msg
+        v_out[:, sl] = norm_add(msg, v_all[mine, sl], sums[mine, :])
+
+    chunks(v_out.shape[1], body)
 
 
 def edge_local(meta, v_all, e_all, sender, mats, src, dst, part, receiver):
@@ -240,11 +252,6 @@
         hidden[:, sl] = silu(part[:, sl] + dot(far[...], hot(src[:, sl], n, far.shape[1])))
 
     chunks(hidden.shape[1], body)
-
-
-def finish(meta, hid, hid_other, turned, turned_other, v_all, v_out, v_new):
-    node_norm(hid, hid_other, turned, turned_other, v_all, v_new)
-    v_out[...] = v_new[pl.ds(pl.multiple_of(meta[4] * 64, 64), 64), :]
 
 
 def shards(node_feats, edge_feats, send_rows, edge_src, edge_dst, w_edge_in, w_edge_out, w_node_in, w_node_out):
@@ -284,17 +291,19 @@
 
     halo = exchange(lax.optimization_barrier((rows, w_parts[1], w_parts[4]))[0])
     v_other = swap(v_half)
-    (e_half,) = call(gather_edges, [((HALF, m), BF)], meta, *parts, flops=8 * HALF * n * m, after=w_parts[2:4])
+    (e_half,) = call(gather_edges, [((HALF, m), BF)], meta, *parts)
     e_other = swap(e_half)
     halo_other = swap(halo)
 
-    mats, turned, turned_other = [], [], []
+    mats, tails = [], []
     for layer in range(2):
-        unpack_layer = functools.partial(unpack, layer)
-        w, t = call(unpack_layer, [((7, HALF, LATENT), BF), ((2, LATENT, HALF), BF)], meta, *w_parts)
+        w, nodes, turned = call(
+            functools.partial(unpack, layer),
+            [((3, HALF, LATENT), BF), ((2, HALF, LATENT), BF), ((2, LATENT, HALF), BF)],
+            meta, *w_parts, scratch=[pltpu.VMEM((2, HALF, LATENT), BF)], flops=8 * HALF * n * m * (1 - layer),
+        )
         mats.append(w)
-        turned.append(t)
-        turned_other.append(swap(t))
+        tails.append((turned, swap(turned), nodes, swap(nodes)))
 
     big = lambda r, q: 2 * r * q * LATENT
     v_all, e_all, hid = call(
@@ -304,17 +313,11 @@
         scratch=[pltpu.VMEM((HALF, n + m), BF), pltpu.VMEM((HALF, n), BF), pltpu.VMEM((m, LATENT), BF)],
         flops=4 * big(HALF, n + m),
     )
-    e_new, hid_n = call(
-        aggregate,
-        [((LATENT, m), BF), ((HALF, n), BF)],
-        meta, hid, swap(hid), turned[0], turned_other[0], mats[0], e_all, v_all, dst,
-        flops=3 * big(LATENT, m),
-    )
-    v_new, sender, rows = call(
-        send_next,
-        [((LATENT, n), BF), ((HALF, n), BF), ((m, HALF), BF)],
-        meta, hid_n, swap(hid_n), turned[0], turned_other[0], v_all, mats[1], send,
-        flops=2 * big(LATENT, n),
+    e_new, v_new, sender, rows = call(
+        tail_first,
+        [((LATENT, m), BF), ((LATENT, n), BF), ((HALF, n), BF), ((m, HALF), BF)],
+        meta, hid, swap(hid), *tails[0], e_all, v_all, dst, mats[1], send,
+        flops=6 * big(LATENT, m),
     )
     far = exchange(rows)
     (part,) = call(
@@ -325,15 +328,11 @@
         lambda *refs: edge_far(n, *refs), [((HALF, m), BF)], meta, part, far, src,
         scratch=[pltpu.VMEM((HALF, m), BF)], flops=2 * big(HALF, m),
     )
-    e_out, hid_n = call(
-        aggregate_last,
-        [((64, m), BF), ((HALF, n), BF)],
-        meta, hid, swap(hid), turned[1], turned_other[1], mats[1], e_new, v_new, dst,
-        scratch=[pltpu.VMEM((LATENT, m), BF)], flops=3 * big(LATENT, m),
-    )
-    (v_out,) = call(
-        finish, [((64, n), BF)], meta, hid_n, swap(hid_n), turned[1], turned_other[1], v_new,
-        scratch=[pltpu.VMEM((LATENT, n), BF)], flops=big(LATENT, n),
+    e_out, v_out = call(
+        tail_last,
+        [((64, m), BF), ((64, n), BF)],
+        meta, hid, swap(hid), *tails[1], e_new, v_new, dst,
+        scratch=[pltpu.VMEM((LATENT, m), BF), pltpu.VMEM((LATENT, n // 2), F32)], flops=5 * big(LATENT, m),
     )
     return v_out, e_out
 

time: 132 us -> 120 us (0.909)
  the two profiles are of different devices: /device:TPU:1 before, /device:TPU:65 now
where the time goes in v4:
time: 120 us; the launch traced here: 119 us
  starting transfers between devices  57 us (48%)
  Pallas kernels  29.4 us (24%)
  waiting for transfers between devices  26.2 us (22%)
  local copies, waits for them, and re-layouts  5.48 us (5%)
    pallas_call x10, Pallas kernels, call(): pl.pallas_call(body, out_shape=[jax.ShapeDtypeStruct(s, d) for s, d in ou...  29.4 us
    ppermute x9, starting transfers between devices, swap(): return lax.ppermute(x, 'ch', CORE)  21.3 us
    all_to_all x2, starting transfers between devices, exchange(): lax.all_to_all(rows.reshape(32, SLOTS, HALF), 'dom', 0, 0, tiled=True)  12 us
    ppermute x2, waiting for transfers between devices, ring_gather(): nxt = lax.ppermute(x, axis, perm(3))  8.77 us
    ppermute x3, starting transfers between devices, shards(): lax.ppermute(piece, 'ch', z_shift(s))  7.55 us
    all_to_all x2, waiting for transfers between devices, exchange(): lax.all_to_all(rows.reshape(32, SLOTS, HALF), 'dom', 0, 0, tiled=True)  5.48 us
    ppermute x2, waiting for transfers between devices, ring_gather(): far_b = lax.ppermute(nxt[half:], axis, perm(3))  5.03 us
    ppermute x2, starting transfers between devices, ring_gather(): far_a = lax.ppermute(prev[:half], axis, perm(1))  4.45 us
  transfers between devices with their start and end apart: 25, of which 7 were waited for; matrix products, arithmetic and copies ran while one was open for 1% of the time, Pallas kernels for 12%

profile of v4, /device:TPU:65, one launch (start us, length us, event | category | flops | bytes accessed | tf_op | source)
XLA Modules:
  0.0 119.1 jit_solution(1237360616197826675)
XLA Ops:
  0.7 1.6 %shard_map.104 = (bf16[7,8,512]{2,1,0:T(8,128)(2,1)S(1)}, bf16[64,1792]{1,0:T(8,128)(2,1)S(1)}) custom-call(s32[5]{0:T(128)S(1)} %stack.53.refs_0_, bf16[2,3,64,512]{3,2,1,0:T(8,128)(2,1)} %bitcast.37, bf16[2,64,512]{2,1,0:T(8,128)(2,1)} %refs_2_.1, bf16[2,2,64,512]{3,2,1,0:T(8,128)(2,1)} %bitcast.38, bf16[2,64,512]{2,1,0:T(8,128)(2,1)} %refs_4_.1, ...), custom_call_target="tpu_custom_call" | custom-call | bytes 1146900 | tf_op jit(solution)/shard_map/pallas_call | solution.py:84
  2.4 4.3 %collective-permute-start = (bf16[7,8,512]{2,1,0:T(8,128)(2,1)S(1)}, bf16[7,8,512]{2,1,0:T(8,128)(2,1)S(1)}, u32[]{:S(2)}, u32[]{:S(2)}) collective-permute-start(bf16[7,8,512]{2,1,0:T(8,128)(2,1)S(1)} %get-tuple-element.25), channel_id=1, source_target_pairs={{0,2},{1,3},{2,4},{3,5},{4,6},{5,7},{6,0},{7,1},{8,10},{9,11},{10,... | collective-permute-start | bytes 172040 | tf_op jit(solution)/shard_map/ppermute | solution.py:276
  6.6 3.3 %collective-permute-start.8 = (bf16[7,8,512]{2,1,0:T(8,128)(2,1)S(1)}, bf16[7,8,512]{2,1,0:T(8,128)(2,1)S(1)}, u32[]{:S(2)}, u32[]{:S(2)}) collective-permute-start(bf16[7,8,512]{2,1,0:T(8,128)(2,1)S(1)} %get-tuple-element.25), channel_id=1, source_target_pairs={{0,4},{1,5},{2,6},{3,7},{4,0},{5,1},{6,2},{7,3},{8,12},{9,13},{10,... | collective-permute-start | bytes 172040 | tf_op jit(solution)/shard_map/ppermute | solution.py:276
  9.9 2.4 %collective-permute-start.1 = (bf16[64,1792]{1,0:T(8,128)(2,1)S(1)}, bf16[64,1792]{1,0:T(8,128)(2,1)S(1)}, u32[]{:S(2)}, u32[]{:S(2)}) collective-permute-start(bf16[64,1792]{1,0:T(8,128)(2,1)S(1)} %get-tuple-element.26.refs_1_), channel_id=1, source_target_pairs={{0,6},{1,7},{2,0},{3,1},{4,2},{5,3},{6,4},{7,5},{8,14},{9,15},{10,... | collective-permute-start | bytes 688136 | tf_op jit(solution)/shard_map/ppermute | solution.py:44
  13.7 2.6 %collective-permute-start.9 = (bf16[4,7,8,512]{3,2,1,0:T(8,128)(2,1)S(1)}, bf16[4,7,8,512]{3,2,1,0:T(8,128)(2,1)S(1)}, u32[]{:S(2)}, u32[]{:S(2)}) collective-permute-start(bf16[4,7,8,512]{3,2,1,0:T(8,128)(2,1)S(1)} %pad_maximum_fusion.1), channel_id=1, source_target_pairs={{0,96},{1,25},{2,98},{3,27},{4,100},{5,29},{6,102},{7,31},{8,104},... | collective-permute-start | bytes 688136 | tf_op jit(solution)/shard_map/ppermute | solution.py:280
  17.3 8.8 %collective-permute-done.1.refs_2_ = bf16[64,1792]{1,0:T(8,128)(2,1)S(1)} collective-permute-done((bf16[64,1792]{1,0:T(8,128)(2,1)S(1)}, bf16[64,1792]{1,0:T(8,128)(2,1)S(1)}, u32[]{:S(2)}, u32[]{:S(2)}) %collective-permute-start.1) | collective-permute-done | bytes 229408 | tf_op jit(solution)/shard_map/ppermute | solution.py:44
  29.2 3.1 %collective-permute-start.3 = (bf16[32,1792]{1,0:T(8,128)(2,1)S(1)}, bf16[32,1792]{1,0:T(8,128)(2,1)S(1)}, u32[]{:S(2)}, u32[]{:S(2)}) collective-permute-start(bf16[32,1792]{1,0:T(8,128)(2,1)S(1)} %slice.16), channel_id=1, source_target_pairs={{0,2},{1,3},{2,4},{3,5},{4,6},{5,7},{6,0},{7,1},{8,10},{9,11},{10,... | collective-permute-start | bytes 344072 | tf_op jit(solution)/shard_map/ppermute | solution.py:45
  32.4 1.9 %collective-permute-done.3.refs_3_ = bf16[32,1792]{1,0:T(8,128)(2,1)S(1)} collective-permute-done((bf16[32,1792]{1,0:T(8,128)(2,1)S(1)}, bf16[32,1792]{1,0:T(8,128)(2,1)S(1)}, u32[]{:S(2)}, u32[]{:S(2)}) %collective-permute-start.3) | collective-permute-done | bytes 114720 | tf_op jit(solution)/shard_map/ppermute | solution.py:45
  34.4 5.0 %collective-permute-done.4.refs_4_ = bf16[32,1792]{1,0:T(8,128)(2,1)S(1)} collective-permute-done((bf16[32,1792]{1,0:T(8,128)(2,1)S(1)}, bf16[32,1792]{1,0:T(8,128)(2,1)S(1)}, u32[]{:S(2)}, u32[]{:S(2)}) %collective-permute-start.4) | collective-permute-done | bytes 114720 | tf_op jit(solution)/shard_map/ppermute | solution.py:46
  41.5 3.3 %collective-permute-done.13.refs_5_ = bf16[4,4,7,8,512]{4,3,2,1,0:T(8,128)(2,1)S(1)} collective-permute-done((bf16[4,4,7,8,512]{4,3,2,1,0:T(8,128)(2,1)S(1)}, bf16[4,4,7,8,512]{4,3,2,1,0:T(8,128)(2,1)S(1)}, u32[]{:S(2)}, u32[]{:S(2)}) %collective-permute-start.13) | collective-permute-done | bytes 917536 | tf_op jit(solution)/shard_map/ppermute | solution.py:43
  44.7 4.5 %all-to-all-start = ((bf16[32,32,256]{2,1,0:T(8,128)(2,1)}), bf16[32,32,256]{2,1,0:T(8,128)(2,1)S(1)}, u32[]{:S(2)}, u32[]{:S(2)}) async-start(bf16[32,32,256]{2,1,0:T(8,128)(2,1)} %bitcast.25), calls=%async_computation | async-start | bytes 1048576 | tf_op jit(solution)/shard_map/all_to_all | solution.py:290
  55.0 11.6 %collective-permute-start.6 = (bf16[256,1024]{1,0:T(8,128)(2,1)}, bf16[256,1024]{1,0:T(8,128)(2,1)}, u32[]{:S(2)}, u32[]{:S(2)}) collective-permute-start(bf16[256,1024]{1,0:T(8,128)(2,1)} %shard_map.106.refs_3_), channel_id=1, source_target_pairs={{0,1},{1,0},{2,3},{3,2},{4,5},{5,4},{6,7},{7,6},{8,9},{9,8},{10,11... | collective-permute-start | bytes 1572872 | tf_op jit(solution)/shard_map/ppermute | solution.py:38
  66.6 3.8 %collective-permute-start.14 = (bf16[1024,256]{1,0:T(8,128)(2,1)S(1)}, bf16[1024,256]{1,0:T(8,128)(2,1)S(1)}, u32[]{:S(2)}, u32[]{:S(2)}) collective-permute-start(bf16[1024,256]{1,0:T(8,128)(2,1)S(1)} %bitcast.23), channel_id=1, source_target_pairs={{0,1},{1,0},{2,3},{3,2},{4,5},{5,4},{6,7},{7,6},{8,9},{9,8},{10,11... | collective-permute-start | bytes 1572872 | tf_op jit(solution)/shard_map/ppermute | solution.py:38
  70.4 1.7 %shard_map.107 = (bf16[3,256,512]{2,1,0:T(8,128)(2,1)S(1)}, bf16[2,256,512]{2,1,0:T(8,128)(2,1)S(1)}, bf16[2,512,256]{2,1,0:T(8,128)(2,1)S(1)}) custom-call(s32[5]{0:T(128)S(1)} %stack.53.refs_0_, bf16[4,4,7,8,512]{4,3,2,1,0:T(8,128)(2,1)S(1)} %pad_maximum_fusion.refs_1_, bf16[4,4,7,8,512]{4,3,2,1,0:T(8,128)(2,1)S(1)} %collective-permute-done.12.refs_2_, ...), custom_call_target="tpu_custom_call" | custom-call | flops 1610612736 | bytes 3670036 | tf_op jit(solution)/shard_map/pallas_call | solution.py:84
  72.1 2.3 %collective-permute-start.18 = (bf16[2,512,256]{2,1,0:T(8,128)(2,1)S(1)}, bf16[2,512,256]{2,1,0:T(8,128)(2,1)S(1)}, u32[]{:S(2)}, u32[]{:S(2)}) collective-permute-start(bf16[2,512,256]{2,1,0:T(8,128)(2,1)S(1)} %get-tuple-element.33.refs_3_), channel_id=1, source_target_pairs={{0,1},{1,0},{2,3},{3,2},{4,5},{5,4},{6,7},{7,6},{8,9},{9,8},{10,11... | collective-permute-start | bytes 1572872 | tf_op jit(solution)/shard_map/ppermute | solution.py:38
  74.6 4.0 %shard_map.108 = (bf16[512,768]{1,0:T(8,128)(2,1)S(1)}, bf16[512,1024]{1,0:T(8,128)(2,1)S(1)}, bf16[256,1024]{1,0:T(8,128)(2,1)S(1)}) custom-call(s32[5]{0:T(128)S(1)} %stack.53.refs_0_, bf16[256,768]{1,0:T(8,128)(2,1)S(1)} %copy-done.16, bf16[256,768]{1,0:T(8,128)(2,1)S(1)} %collective-permute-done.5.refs_2_, bf16[256,1024]{1,0:T(8,128)(2,1)} %shard_map.106.refs_3_, ...), custom_call_target="tpu_custom_call" | custom-call | flops 1879048192 | bytes 3678228 | tf_op jit(solution)/shard_map/pallas_call | solution.py:84
  79.2 2.4 %shard_map.109 = (bf16[3,256,512]{2,1,0:T(8,128)(2,1)S(1)}, bf16[2,256,512]{2,1,0:T(8,128)(2,1)}, bf16[2,512,256]{2,1,0:T(8,128)(2,1)}) custom-call(s32[5]{0:T(128)S(1)} %stack.53.refs_0_, bf16[4,4,7,8,512]{4,3,2,1,0:T(8,128)(2,1)S(1)} %pad_maximum_fusion.refs_1_, bf16[4,4,7,8,512]{4,3,2,1,0:T(8,128)(2,1)S(1)} %collective-permute-done.12.refs_2_, ...), custom_call_target="tpu_custom_call" | custom-call | bytes 3670036 | tf_op jit(solution)/shard_map/pallas_call | solution.py:84
  81.6 7.0 %shard_map.110 = (bf16[512,1024]{1,0:T(8,128)(2,1)S(1)}, bf16[512,768]{1,0:T(8,128)(2,1)S(1)}, bf16[256,768]{1,0:T(8,128)(2,1)S(1)}, bf16[1024,256]{1,0:T(8,128)(2,1)}) custom-call(s32[5]{0:T(128)S(1)} %stack.53.refs_0_, bf16[256,1024]{1,0:T(8,128)(2,1)S(1)} %get-tuple-element.32.refs_1_, bf16[256,1024]{1,0:T(8,128)(2,1)S(1)} %collective-permute-done.17.refs_2_, ...), custom_call_target="tpu_custom_call" | custom-call | flops 3221225472 | bytes 5775380 | tf_op jit(solution)/shard_map/pallas_call | solution.py:84
  89.4 7.6 %all-to-all-start.1 = ((bf16[32,32,256]{2,1,0:T(8,128)(2,1)}), bf16[32,32,256]{2,1,0:T(8,128)(2,1)S(1)}, u32[]{:S(2)}, u32[]{:S(2)}) async-start(bf16[32,32,256]{2,1,0:T(8,128)(2,1)} %bitcast.20), calls=%async_computation.1 | async-start | bytes 1048576 | tf_op jit(solution)/shard_map/all_to_all | solution.py:290
  99.9 2.1 %shard_map.111.refs_1_ = f32[256,1024]{1,0:T(8,128)S(1)} custom-call(s32[5]{0:T(128)S(1)} %stack.53.refs_0_, bf16[512,768]{1,0:T(8,128)(2,1)S(1)} %get-tuple-element.38.refs_1_.refs_8_, bf16[512,1024]{1,0:T(8,128)(2,1)S(1)} %get-tuple-element.39.refs_2_.refs_7_, bf16[256,768]{1,0:T(8,128)(2,1)S(1)} %copy-done.6, bf16[3,256,512]{2,1,0:T(8,128)(2,1)S(1)} %copy-done.1, ...), custom_call_target="tpu_custom_call" | custom-call | flops 805306368 | bytes 3022868 | tf_op jit(solution)/shard_map/pallas_call | solution.py:84
  102.0 5.5 %all-to-all-done.1 = bf16[32,32,256]{2,1,0:T(8,128)(2,1)S(1)} async-done(((bf16[32,32,256]{2,1,0:T(8,128)(2,1)}), bf16[32,32,256]{2,1,0:T(8,128)(2,1)S(1)}, u32[]{:S(2)}, u32[]{:S(2)}) %all-to-all-start.1) | async-done | bytes 524320 | tf_op jit(solution)/shard_map/all_to_all | solution.py:290
  108.8 2.1 %collective-permute-start.20 = (bf16[256,1024]{1,0:T(8,128)(2,1)S(1)}, bf16[256,1024]{1,0:T(8,128)(2,1)S(1)}, u32[]{:S(2)}, u32[]{:S(2)}) collective-permute-start(bf16[256,1024]{1,0:T(8,128)(2,1)S(1)} %shard_map.112.refs_1_), channel_id=1, source_target_pairs={{0,1},{1,0},{2,3},{3,2},{4,5},{5,4},{6,7},{7,6},{8,9},{9,8},{10,11... | collective-permute-start | bytes 1572872 | tf_op jit(solution)/shard_map/ppermute | solution.py:38
  110.9 1.5 %collective-permute-done.20.refs_2_ = bf16[256,1024]{1,0:T(8,128)(2,1)S(1)} collective-permute-done((bf16[256,1024]{1,0:T(8,128)(2,1)S(1)}, bf16[256,1024]{1,0:T(8,128)(2,1)S(1)}, u32[]{:S(2)}, u32[]{:S(2)}) %collective-permute-start.20) | collective-permute-done | bytes 524320 | tf_op jit(solution)/shard_map/ppermute | solution.py:38
  112.4 6.8 %shard_map.113 = (bf16[64,1024]{1,0:T(8,128)(2,1)}, bf16[64,768]{1,0:T(8,128)(2,1)}) custom-call(s32[5]{0:T(128)S(1)} %stack.53.refs_0_, bf16[256,1024]{1,0:T(8,128)(2,1)S(1)} %shard_map.112.refs_1_, bf16[256,1024]{1,0:T(8,128)(2,1)S(1)} %collective-permute-done.20.refs_2_, bf16[2,512,256]{2,1,0:T(8,128)(2,1)} %get-tuple-element.42.refs_3_, ...), custom_call_target="tpu_custom_call" | custom-call | flops 2684354560 | bytes 4984852 | tf_op jit(solution)/shard_map/pallas_call | solution.py:84
  (79 shorter events, 19.2 us)
Async XLA Ops:
  2.4 7.6 %collective-permute-start = (bf16[7,8,512]{2,1,0:T(8,128)(2,1)S(1)}, bf16[7,8,512]{2,1,0:T(8,128)(2,1)S(1)}, u32[]{:S(2)}, u32[]{:S(2)}) collective-permute-start(bf16[7,8,512]{2,1,0:T(8,128)(2,1)S(1)} %get-tuple-element.25), channel_id=1, source_target_pairs={{0,2},{1,3},{2,4},{3,5},{4,6},{5,7},{6,0},{7,1},{8,10},{9,11},{10,... | collective-permute-start | bytes 172040 | tf_op jit(solution)/shard_map/ppermute | solution.py:276
  6.6 6.9 %collective-permute-start.7 = (bf16[7,8,512]{2,1,0:T(8,128)(2,1)S(1)}, bf16[7,8,512]{2,1,0:T(8,128)(2,1)S(1)}, u32[]{:S(2)}, u32[]{:S(2)}) collective-permute-start(bf16[7,8,512]{2,1,0:T(8,128)(2,1)S(1)} %get-tuple-element.25), channel_id=1, source_target_pairs={{0,6},{1,7},{2,0},{3,1},{4,2},{5,3},{6,4},{7,5},{8,14},{9,15},{10,... | collective-permute-start | bytes 172040 | tf_op jit(solution)/shard_map/ppermute | solution.py:276
  6.6 7.0 %collective-permute-start.8 = (bf16[7,8,512]{2,1,0:T(8,128)(2,1)S(1)}, bf16[7,8,512]{2,1,0:T(8,128)(2,1)S(1)}, u32[]{:S(2)}, u32[]{:S(2)}) collective-permute-start(bf16[7,8,512]{2,1,0:T(8,128)(2,1)S(1)} %get-tuple-element.25), channel_id=1, source_target_pairs={{0,4},{1,5},{2,6},{3,7},{4,0},{5,1},{6,2},{7,3},{8,12},{9,13},{10,... | collective-permute-start | bytes 172040 | tf_op jit(solution)/shard_map/ppermute | solution.py:276
  9.9 16.2 %collective-permute-start.1 = (bf16[64,1792]{1,0:T(8,128)(2,1)S(1)}, bf16[64,1792]{1,0:T(8,128)(2,1)S(1)}, u32[]{:S(2)}, u32[]{:S(2)}) collective-permute-start(bf16[64,1792]{1,0:T(8,128)(2,1)S(1)} %get-tuple-element.26.refs_1_), channel_id=1, source_target_pairs={{0,6},{1,7},{2,0},{3,1},{4,2},{5,3},{6,4},{7,5},{8,14},{9,15},{10,... | collective-permute-start | bytes 688136 | tf_op jit(solution)/shard_map/ppermute | solution.py:44
  12.3 13.8 %collective-permute-start.2 = (bf16[64,1792]{1,0:T(8,128)(2,1)S(1)}, bf16[64,1792]{1,0:T(8,128)(2,1)S(1)}, u32[]{:S(2)}, u32[]{:S(2)}) collective-permute-start(bf16[64,1792]{1,0:T(8,128)(2,1)S(1)} %get-tuple-element.26.refs_1_), channel_id=1, source_target_pairs={{0,2},{1,3},{2,4},{3,5},{4,6},{5,7},{6,0},{7,1},{8,10},{9,11},{10,... | collective-permute-start | bytes 688136 | tf_op jit(solution)/shard_map/ppermute | solution.py:43
  13.7 12.5 %collective-permute-start.9 = (bf16[4,7,8,512]{3,2,1,0:T(8,128)(2,1)S(1)}, bf16[4,7,8,512]{3,2,1,0:T(8,128)(2,1)S(1)}, u32[]{:S(2)}, u32[]{:S(2)}) collective-permute-start(bf16[4,7,8,512]{3,2,1,0:T(8,128)(2,1)S(1)} %pad_maximum_fusion.1), channel_id=1, source_target_pairs={{0,96},{1,25},{2,98},{3,27},{4,100},{5,29},{6,102},{7,31},{8,104},... | collective-permute-start | bytes 688136 | tf_op jit(solution)/shard_map/ppermute | solution.py:280
  16.2 9.9 %collective-permute-start.10 = (bf16[4,7,8,512]{3,2,1,0:T(8,128)(2,1)S(1)}, bf16[4,7,8,512]{3,2,1,0:T(8,128)(2,1)S(1)}, u32[]{:S(2)}, u32[]{:S(2)}) collective-permute-start(bf16[4,7,8,512]{3,2,1,0:T(8,128)(2,1)S(1)} %pad_maximum_fusion.1), channel_id=1, source_target_pairs={{0,64},{1,17},{2,66},{3,19},{4,68},{5,21},{6,70},{7,23},{8,72},{9,... | collective-permute-start | bytes 688136 | tf_op jit(solution)/shard_map/ppermute | solution.py:280
  16.7 9.4 %collective-permute-start.11 = (bf16[4,7,8,512]{3,2,1,0:T(8,128)(2,1)S(1)}, bf16[4,7,8,512]{3,2,1,0:T(8,128)(2,1)S(1)}, u32[]{:S(2)}, u32[]{:S(2)}) collective-permute-start(bf16[4,7,8,512]{3,2,1,0:T(8,128)(2,1)S(1)} %pad_maximum_fusion.1), channel_id=1, source_target_pairs={{0,32},{1,9},{2,34},{3,11},{4,36},{5,13},{6,38},{7,15},{8,40},{9,1... | collective-permute-start | bytes 688136 | tf_op jit(solution)/shard_map/ppermute | solution.py:280
  26.3 18.5 %collective-permute-start.13 = (bf16[4,4,7,8,512]{4,3,2,1,0:T(8,128)(2,1)S(1)}, bf16[4,4,7,8,512]{4,3,2,1,0:T(8,128)(2,1)S(1)}, u32[]{:S(2)}, u32[]{:S(2)}) collective-permute-start(bf16[4,4,7,8,512]{4,3,2,1,0:T(8,128)(2,1)S(1)} %pad_maximum_fusion.refs_1_), channel_id=1, source_target_pairs={{0,8},{1,33},{2,10},{3,35},{4,12},{5,37},{6,14},{7,39},{8,16},{9,4... | collective-permute-start | bytes 2752520 | tf_op jit(solution)/shard_map/ppermute | solution.py:43
  27.6 17.1 %collective-permute-start.12 = (bf16[4,4,7,8,512]{4,3,2,1,0:T(8,128)(2,1)S(1)}, bf16[4,4,7,8,512]{4,3,2,1,0:T(8,128)(2,1)S(1)}, u32[]{:S(2)}, u32[]{:S(2)}) collective-permute-start(bf16[4,4,7,8,512]{4,3,2,1,0:T(8,128)(2,1)S(1)} %pad_maximum_fusion.refs_1_), channel_id=1, source_target_pairs={{0,24},{1,97},{2,26},{3,99},{4,28},{5,101},{6,30},{7,103},{8,0},{9... | collective-permute-start | bytes 2752520 | tf_op jit(solution)/shard_map/ppermute | solution.py:44
  29.2 5.2 %collective-permute-start.3 = (bf16[32,1792]{1,0:T(8,128)(2,1)S(1)}, bf16[32,1792]{1,0:T(8,128)(2,1)S(1)}, u32[]{:S(2)}, u32[]{:S(2)}) collective-permute-start(bf16[32,1792]{1,0:T(8,128)(2,1)S(1)} %slice.16), channel_id=1, source_target_pairs={{0,2},{1,3},{2,4},{3,5},{4,6},{5,7},{6,0},{7,1},{8,10},{9,11},{10,... | collective-permute-start | bytes 344072 | tf_op jit(solution)/shard_map/ppermute | solution.py:45
  32.3 7.1 %collective-permute-start.4 = (bf16[32,1792]{1,0:T(8,128)(2,1)S(1)}, bf16[32,1792]{1,0:T(8,128)(2,1)S(1)}, u32[]{:S(2)}, u32[]{:S(2)}) collective-permute-start(bf16[32,1792]{1,0:T(8,128)(2,1)S(1)} %slice.17), channel_id=1, source_target_pairs={{0,6},{1,7},{2,0},{3,1},{4,2},{5,3},{6,4},{7,5},{8,14},{9,15},{10,... | collective-permute-start | bytes 344072 | tf_op jit(solution)/shard_map/ppermute | solution.py:46
  44.7 21.9 %all-to-all-start = ((bf16[32,32,256]{2,1,0:T(8,128)(2,1)}), bf16[32,32,256]{2,1,0:T(8,128)(2,1)S(1)}, u32[]{:S(2)}, u32[]{:S(2)}) async-start(bf16[32,32,256]{2,1,0:T(8,128)(2,1)} %bitcast.25), calls=%async_computation | async-start | bytes 1048576 | tf_op jit(solution)/shard_map/all_to_all | solution.py:290
  50.1 20.4 %collective-permute-start.15 = (bf16[2,4,7,8,512]{4,3,2,1,0:T(8,128)(2,1)}, bf16[2,4,7,8,512]{4,3,2,1,0:T(8,128)(2,1)}, u32[]{:S(2)}, u32[]{:S(2)}) collective-permute-start(bf16[2,4,7,8,512]{4,3,2,1,0:T(8,128)(2,1)} %slice.18), channel_id=1, source_target_pairs={{0,8},{1,33},{2,10},{3,35},{4,12},{5,37},{6,14},{7,39},{8,16},{9,4... | collective-permute-start | bytes 1376264 | tf_op jit(solution)/shard_map/ppermute | solution.py:45
  52.2 18.2 %collective-permute-start.16 = (bf16[2,4,7,8,512]{4,3,2,1,0:T(8,128)(2,1)}, bf16[2,4,7,8,512]{4,3,2,1,0:T(8,128)(2,1)}, u32[]{:S(2)}, u32[]{:S(2)}) collective-permute-start(bf16[2,4,7,8,512]{4,3,2,1,0:T(8,128)(2,1)} %slice.19), channel_id=1, source_target_pairs={{0,24},{1,97},{2,26},{3,99},{4,28},{5,101},{6,30},{7,103},{8,0},{9... | collective-permute-start | bytes 1376264 | tf_op jit(solution)/shard_map/ppermute | solution.py:46
  55.0 19.6 %collective-permute-start.6 = (bf16[256,1024]{1,0:T(8,128)(2,1)}, bf16[256,1024]{1,0:T(8,128)(2,1)}, u32[]{:S(2)}, u32[]{:S(2)}) collective-permute-start(bf16[256,1024]{1,0:T(8,128)(2,1)} %shard_map.106.refs_3_), channel_id=1, source_target_pairs={{0,1},{1,0},{2,3},{3,2},{4,5},{5,4},{6,7},{7,6},{8,9},{9,8},{10,11... | collective-permute-start | bytes 1572872 | tf_op jit(solution)/shard_map/ppermute | solution.py:38
  66.6 8.0 %collective-permute-start.14 = (bf16[1024,256]{1,0:T(8,128)(2,1)S(1)}, bf16[1024,256]{1,0:T(8,128)(2,1)S(1)}, u32[]{:S(2)}, u32[]{:S(2)}) collective-permute-start(bf16[1024,256]{1,0:T(8,128)(2,1)S(1)} %bitcast.23), channel_id=1, source_target_pairs={{0,1},{1,0},{2,3},{3,2},{4,5},{5,4},{6,7},{7,6},{8,9},{9,8},{10,11... | collective-permute-start | bytes 1572872 | tf_op jit(solution)/shard_map/ppermute | solution.py:38
  70.4 4.2 %collective-permute-start.5 = (bf16[256,768]{1,0:T(8,128)(2,1)}, bf16[256,768]{1,0:T(8,128)(2,1)S(1)}, u32[]{:S(2)}, u32[]{:S(2)}) collective-permute-start(bf16[256,768]{1,0:T(8,128)(2,1)} %copy-done.15), channel_id=1, source_target_pairs={{0,1},{1,0},{2,3},{3,2},{4,5},{5,4},{6,7},{7,6},{8,9},{9,8},{10,11... | collective-permute-start | bytes 1179656 | tf_op jit(solution)/shard_map/ppermute | solution.py:38
  72.1 9.4 %collective-permute-start.18 = (bf16[2,512,256]{2,1,0:T(8,128)(2,1)S(1)}, bf16[2,512,256]{2,1,0:T(8,128)(2,1)S(1)}, u32[]{:S(2)}, u32[]{:S(2)}) collective-permute-start(bf16[2,512,256]{2,1,0:T(8,128)(2,1)S(1)} %get-tuple-element.33.refs_3_), channel_id=1, source_target_pairs={{0,1},{1,0},{2,3},{3,2},{4,5},{5,4},{6,7},{7,6},{8,9},{9,8},{10,11... | collective-permute-start | bytes 1572872 | tf_op jit(solution)/shard_map/ppermute | solution.py:38
  74.5 7.1 %collective-permute-start.19 = (bf16[2,256,512]{2,1,0:T(8,128)(2,1)S(1)}, bf16[2,256,512]{2,1,0:T(8,128)(2,1)S(1)}, u32[]{:S(2)}, u32[]{:S(2)}) collective-permute-start(bf16[2,256,512]{2,1,0:T(8,128)(2,1)S(1)} %get-tuple-element.34.refs_5_), channel_id=1, source_target_pairs={{0,1},{1,0},{2,3},{3,2},{4,5},{5,4},{6,7},{7,6},{8,9},{9,8},{10,11... | collective-permute-start | bytes 1572872 | tf_op jit(solution)/shard_map/ppermute | solution.py:38
  89.4 18.1 %all-to-all-start.1 = ((bf16[32,32,256]{2,1,0:T(8,128)(2,1)}), bf16[32,32,256]{2,1,0:T(8,128)(2,1)S(1)}, u32[]{:S(2)}, u32[]{:S(2)}) async-start(bf16[32,32,256]{2,1,0:T(8,128)(2,1)} %bitcast.20), calls=%async_computation.1 | async-start | bytes 1048576 | tf_op jit(solution)/shard_map/all_to_all | solution.py:290
  96.9 13.9 %collective-permute-start.21 = (bf16[2,512,256]{2,1,0:T(8,128)(2,1)}, bf16[2,512,256]{2,1,0:T(8,128)(2,1)}, u32[]{:S(2)}, u32[]{:S(2)}) collective-permute-start(bf16[2,512,256]{2,1,0:T(8,128)(2,1)} %get-tuple-element.42.refs_3_), channel_id=1, source_target_pairs={{0,1},{1,0},{2,3},{3,2},{4,5},{5,4},{6,7},{7,6},{8,9},{9,8},{10,11... | collective-permute-start | bytes 1572872 | tf_op jit(solution)/shard_map/ppermute | solution.py:38
  97.6 13.3 %collective-permute-start.22 = (bf16[2,256,512]{2,1,0:T(8,128)(2,1)}, bf16[2,256,512]{2,1,0:T(8,128)(2,1)}, u32[]{:S(2)}, u32[]{:S(2)}) collective-permute-start(bf16[2,256,512]{2,1,0:T(8,128)(2,1)} %get-tuple-element.43.refs_5_), channel_id=1, source_target_pairs={{0,1},{1,0},{2,3},{3,2},{4,5},{5,4},{6,7},{7,6},{8,9},{9,8},{10,11... | collective-permute-start | bytes 1572872 | tf_op jit(solution)/shard_map/ppermute | solution.py:38
  108.8 3.6 %collective-permute-start.20 = (bf16[256,1024]{1,0:T(8,128)(2,1)S(1)}, bf16[256,1024]{1,0:T(8,128)(2,1)S(1)}, u32[]{:S(2)}, u32[]{:S(2)}) collective-permute-start(bf16[256,1024]{1,0:T(8,128)(2,1)S(1)} %shard_map.112.refs_1_), channel_id=1, source_target_pairs={{0,1},{1,0},{2,3},{3,2},{4,5},{5,4},{6,7},{7,6},{8,9},{9,8},{10,11... | collective-permute-start | bytes 1572872 | tf_op jit(solution)/shard_map/ppermute | solution.py:38
  (19 other events, 108.6 us)

commit v5 on v4

--- a/solution.py
+++ b/solution.py
@@ -196,10 +196,15 @@
     chunks(e_new.shape[1], edges)
 
 
-def node_message(first, sl, turned, turned_other, nodes, nodes_other, e_new, v_all, dst):
+def node_message(first, sl, turned, turned_other, nodes, nodes_other, e_new, dst, local):
     agg = dot(e_new[...], hot(dst[...], first, sl.stop - sl.start), 1, 1).astype(BF)
-    msg = dot(turned[1], silu(dot(nodes[0], v_all[:, sl]) + dot(nodes[1], agg)))
-    return msg + dot(turned_other[1], silu(dot(nodes_other[0], v_all[:, sl]) + dot(nodes_other[1], agg)))
+    msg = dot(turned[1], silu(local(0) + dot(nodes[1], agg)))
+    return msg + dot(turned_other[1], silu(local(1) + dot(nodes_other[1], agg)))
+
+
+def node_local(meta, nodes, nodes_other, v_all, out):
+    out[0] = dot(nodes[0], v_all[...])
+    out[1] = dot(nodes_other[0], v_all[...])
 
 
 def tail_first(
@@ -209,7 +214,8 @@
     new_edges(hid, hid_other, turned, turned_other, e_all, e_new)
 
     def body(sl, first):
-        msg = node_message(first, sl, turned, turned_other, nodes, nodes_other, e_new, v_all, dst)
+        local = lambda i: dot((nodes, nodes_other)[i][0], v_all[:, sl])
+        msg = node_message(first, sl, turned, turned_other, nodes, nodes_other, e_new, dst, local)
         v_new[:, sl] = norm_add(msg, v_all[:, sl])
 
     chunks(v_new.shape[1], body)
@@ -218,7 +224,7 @@
 
 
 def tail_last(
-    meta, hid, hid_other, turned, turned_other, nodes, nodes_other, e_all, v_all, dst,
+    meta, hid, hid_other, turned, turned_other, nodes, nodes_other, e_all, v_all, dst, local,
     e_out, v_out, e_new, sums,
 ):
     new_edges(hid, hid_other, turned, turned_other, e_all, e_new)
@@ -226,7 +232,7 @@
     e_out[...] = e_new[mine, :]
 
     def body(sl, first):
-        msg = node_message(first, sl, turned, turned_other, nodes, nodes_other, e_new, v_all, dst)
+        msg = node_message(first, sl, turned, turned_other, nodes, nodes_other, e_new, dst, lambda i: local[i, :, sl])
         sums[...] = msg
         v_out[:, sl] = norm_add(msg, v_all[mine, sl], sums[mine, :])
 
@@ -273,11 +279,12 @@
         meta, *(pltpu.with_memory_space_constraint(a, pltpu.HBM) for a in shared),
         scratch=[pltpu.SemaphoreType.DMA((6,))], space=pl.BlockSpec(memory_space=pltpu.HBM),
     )
-    pieces = [piece] + [lax.ppermute(piece, "ch", z_shift(s)) for s in (1, 3, 2)]
+    pieces = [piece] + [lax.ppermute(piece, "ch", z_shift(s)) for s in (2, 1, 3)]
     both = lax.optimization_barrier((both, pieces[1]))[0]
     wz = jnp.stack(pieces)
     parts = ring_gather(both, "ch", z_shift)
-    quarters = [wz] + [lax.ppermute(wz, ("dom", "ch"), ring(1, s)) for s in (3, 2, 1)]
+    far, nxt, prev = (lax.ppermute(wz, ("dom", "ch"), ring(1, s)) for s in (2, 3, 1))
+    quarters = [wz, nxt, far, prev]
     quarters[0] = lax.optimization_barrier((wz, parts[1], parts[4]))[0]
     one = jnp.stack(quarters)
     w_parts = ring_gather(one, ("dom", "ch"), lambda s: ring(2, s))
@@ -324,6 +331,7 @@
         edge_local, [((HALF, m), F32)], meta, v_new, e_new, sender, mats[1], src, dst,
         scratch=[pltpu.VMEM((HALF, n), BF)], flops=3 * big(HALF, m),
     )
+    (local,) = call(node_local, [((2, HALF, n), F32)], meta, tails[1][2], tails[1][3], v_new, flops=2 * big(HALF, n))
     (hid,) = call(
         lambda *refs: edge_far(n, *refs), [((HALF, m), BF)], meta, part, far, src,
         scratch=[pltpu.VMEM((HALF, m), BF)], flops=2 * big(HALF, m),
@@ -331,7 +339,7 @@
     e_out, v_out = call(
         tail_last,
         [((64, m), BF), ((64, n), BF)],
-        meta, hid, swap(hid), *tails[1], e_new, v_new, dst,
+        meta, hid, swap(hid), *tails[1], e_new, v_new, dst, local,
         scratch=[pltpu.VMEM((LATENT, m), BF), pltpu.VMEM((LATENT, n // 2), F32)], flops=5 * big(LATENT, m),
     )
     return v_out, e_out

time: 120 us -> 114 us (0.950)
  the two profiles are of different devices: /device:TPU:65 before, /device:TPU:1 now
where the time goes in v5:
time: 114 us; the launch traced here: 113 us
  starting transfers between devices  56 us (49%)
  Pallas kernels  30.6 us (27%)
  waiting for transfers between devices  20.1 us (18%)
  local copies, waits for them, and re-layouts  5.48 us (5%)
    pallas_call x11, Pallas kernels, call(): pl.pallas_call(body, out_shape=[jax.ShapeDtypeStruct(s, d) for s, d in ou...  30.6 us
    all_to_all x2, starting transfers between devices, exchange(): lax.all_to_all(rows.reshape(32, SLOTS, HALF), 'dom', 0, 0, tiled=True)  16.3 us
    ppermute x9, starting transfers between devices, swap(): return lax.ppermute(x, 'ch', CORE)  12.9 us
    ppermute x3, starting transfers between devices, shards(): lax.ppermute(piece, 'ch', z_shift(s))  11.4 us
    ppermute x2, waiting for transfers between devices, ring_gather(): nxt = lax.ppermute(x, axis, perm(3))  7.2 us
    all_to_all x2, waiting for transfers between devices, exchange(): lax.all_to_all(rows.reshape(32, SLOTS, HALF), 'dom', 0, 0, tiled=True)  5.48 us
    ppermute x2, starting transfers between devices, ring_gather(): nxt = lax.ppermute(x, axis, perm(3))  4.1 us
    ppermute x2, starting transfers between devices, ring_gather(): far_b = lax.ppermute(nxt[half:], axis, perm(3))  3.74 us
  transfers between devices with their start and end apart: 25, of which 7 were waited for; matrix products, arithmetic and copies ran while one was open for 1% of the time, Pallas kernels for 14%

profile of v5, /device:TPU:1, one launch (start us, length us, event | category | flops | bytes accessed | tf_op | source)
XLA Modules:
  0.0 113.3 jit_solution(12629867946884073380)
XLA Ops:
  0.7 1.6 %shard_map.104 = (bf16[7,8,512]{2,1,0:T(8,128)(2,1)S(1)}, bf16[64,1792]{1,0:T(8,128)(2,1)S(1)}) custom-call(s32[5]{0:T(128)S(1)} %stack.53.refs_0_, bf16[2,3,64,512]{3,2,1,0:T(8,128)(2,1)} %bitcast.37, bf16[2,64,512]{2,1,0:T(8,128)(2,1)} %refs_2_.1, bf16[2,2,64,512]{3,2,1,0:T(8,128)(2,1)} %bitcast.38, bf16[2,64,512]{2,1,0:T(8,128)(2,1)} %refs_4_.1, ...), custom_call_target="tpu_custom_call" | custom-call | bytes 1146900 | tf_op jit(solution)/shard_map/pallas_call | solution.py:84
  2.4 7.8 %collective-permute-start = (bf16[7,8,512]{2,1,0:T(8,128)(2,1)S(1)}, bf16[7,8,512]{2,1,0:T(8,128)(2,1)S(1)}, u32[]{:S(2)}, u32[]{:S(2)}) collective-permute-start(bf16[7,8,512]{2,1,0:T(8,128)(2,1)S(1)} %get-tuple-element.25), channel_id=1, source_target_pairs={{0,4},{1,5},{2,6},{3,7},{4,0},{5,1},{6,2},{7,3},{8,12},{9,13},{10,... | collective-permute-start | bytes 172040 | tf_op jit(solution)/shard_map/ppermute | solution.py:282
  11.4 2.4 %collective-permute-start.8 = (bf16[7,8,512]{2,1,0:T(8,128)(2,1)S(1)}, bf16[7,8,512]{2,1,0:T(8,128)(2,1)S(1)}, u32[]{:S(2)}, u32[]{:S(2)}) collective-permute-start(bf16[7,8,512]{2,1,0:T(8,128)(2,1)S(1)} %get-tuple-element.25), channel_id=1, source_target_pairs={{0,6},{1,7},{2,0},{3,1},{4,2},{5,3},{6,4},{7,5},{8,14},{9,15},{10,... | collective-permute-start | bytes 172040 | tf_op jit(solution)/shard_map/ppermute | solution.py:282
  13.8 2.6 %collective-permute-start.1 = (bf16[64,1792]{1,0:T(8,128)(2,1)S(1)}, bf16[64,1792]{1,0:T(8,128)(2,1)S(1)}, u32[]{:S(2)}, u32[]{:S(2)}) collective-permute-start(bf16[64,1792]{1,0:T(8,128)(2,1)S(1)} %get-tuple-element.26.refs_1_), channel_id=1, source_target_pairs={{0,6},{1,7},{2,0},{3,1},{4,2},{5,3},{6,4},{7,5},{8,14},{9,15},{10,... | collective-permute-start | bytes 688136 | tf_op jit(solution)/shard_map/ppermute | solution.py:44
  16.4 2.6 %collective-permute-start.9 = (bf16[4,7,8,512]{3,2,1,0:T(8,128)(2,1)S(1)}, bf16[4,7,8,512]{3,2,1,0:T(8,128)(2,1)S(1)}, u32[]{:S(2)}, u32[]{:S(2)}) collective-permute-start(bf16[4,7,8,512]{3,2,1,0:T(8,128)(2,1)S(1)} %pad_maximum_fusion.1), channel_id=1, source_target_pairs={{0,96},{1,25},{2,98},{3,27},{4,100},{5,29},{6,102},{7,31},{8,104},... | collective-permute-start | bytes 688136 | tf_op jit(solution)/shard_map/ppermute | solution.py:286
  20.1 7.2 %collective-permute-done.1.refs_2_ = bf16[64,1792]{1,0:T(8,128)(2,1)S(1)} collective-permute-done((bf16[64,1792]{1,0:T(8,128)(2,1)S(1)}, bf16[64,1792]{1,0:T(8,128)(2,1)S(1)}, u32[]{:S(2)}, u32[]{:S(2)}) %collective-permute-start.1) | collective-permute-done | bytes 229408 | tf_op jit(solution)/shard_map/ppermute | solution.py:44
  29.6 1.5 %collective-permute-start.12 = (bf16[4,4,7,8,512]{4,3,2,1,0:T(8,128)(2,1)S(1)}, bf16[4,4,7,8,512]{4,3,2,1,0:T(8,128)(2,1)S(1)}, u32[]{:S(2)}, u32[]{:S(2)}) collective-permute-start(bf16[4,4,7,8,512]{4,3,2,1,0:T(8,128)(2,1)S(1)} %pad_maximum_fusion.refs_1_), channel_id=1, source_target_pairs={{0,24},{1,97},{2,26},{3,99},{4,28},{5,101},{6,30},{7,103},{8,0},{9... | collective-permute-start | bytes 2752520 | tf_op jit(solution)/shard_map/ppermute | solution.py:44
  32.6 2.3 %collective-permute-start.4 = (bf16[32,1792]{1,0:T(8,128)(2,1)S(1)}, bf16[32,1792]{1,0:T(8,128)(2,1)S(1)}, u32[]{:S(2)}, u32[]{:S(2)}) collective-permute-start(bf16[32,1792]{1,0:T(8,128)(2,1)S(1)} %slice.17), channel_id=1, source_target_pairs={{0,6},{1,7},{2,0},{3,1},{4,2},{5,3},{6,4},{7,5},{8,14},{9,15},{10,... | collective-permute-start | bytes 344072 | tf_op jit(solution)/shard_map/ppermute | solution.py:46
  34.9 2.1 %collective-permute-done.3.refs_3_ = bf16[32,1792]{1,0:T(8,128)(2,1)S(1)} collective-permute-done((bf16[32,1792]{1,0:T(8,128)(2,1)S(1)}, bf16[32,1792]{1,0:T(8,128)(2,1)S(1)}, u32[]{:S(2)}, u32[]{:S(2)}) %collective-permute-start.3) | collective-permute-done | bytes 114720 | tf_op jit(solution)/shard_map/ppermute | solution.py:45
  37.0 2.1 %collective-permute-done.4.refs_4_ = bf16[32,1792]{1,0:T(8,128)(2,1)S(1)} collective-permute-done((bf16[32,1792]{1,0:T(8,128)(2,1)S(1)}, bf16[32,1792]{1,0:T(8,128)(2,1)S(1)}, u32[]{:S(2)}, u32[]{:S(2)}) %collective-permute-start.4) | collective-permute-done | bytes 114720 | tf_op jit(solution)/shard_map/ppermute | solution.py:46
  42.4 8.7 %all-to-all-start = ((bf16[32,32,256]{2,1,0:T(8,128)(2,1)}), bf16[32,32,256]{2,1,0:T(8,128)(2,1)S(1)}, u32[]{:S(2)}, u32[]{:S(2)}) async-start(bf16[32,32,256]{2,1,0:T(8,128)(2,1)} %bitcast.25), calls=%async_computation | async-start | bytes 1048576 | tf_op jit(solution)/shard_map/all_to_all | solution.py:297
  54.1 1.4 %collective-permute-start.16 = (bf16[2,4,7,8,512]{4,3,2,1,0:T(8,128)(2,1)}, bf16[2,4,7,8,512]{4,3,2,1,0:T(8,128)(2,1)}, u32[]{:S(2)}, u32[]{:S(2)}) collective-permute-start(bf16[2,4,7,8,512]{4,3,2,1,0:T(8,128)(2,1)} %slice.19), channel_id=1, source_target_pairs={{0,24},{1,97},{2,26},{3,99},{4,28},{5,101},{6,30},{7,103},{8,0},{9... | collective-permute-start | bytes 1376264 | tf_op jit(solution)/shard_map/ppermute | solution.py:46
  56.9 4.2 %collective-permute-start.6 = (bf16[256,1024]{1,0:T(8,128)(2,1)}, bf16[256,1024]{1,0:T(8,128)(2,1)}, u32[]{:S(2)}, u32[]{:S(2)}) collective-permute-start(bf16[256,1024]{1,0:T(8,128)(2,1)} %shard_map.106.refs_3_), channel_id=1, source_target_pairs={{0,1},{1,0},{2,3},{3,2},{4,5},{5,4},{6,7},{7,6},{8,9},{9,8},{10,11... | collective-permute-start | bytes 1572872 | tf_op jit(solution)/shard_map/ppermute | solution.py:38
  61.1 3.9 %collective-permute-start.14 = (bf16[1024,256]{1,0:T(8,128)(2,1)S(1)}, bf16[1024,256]{1,0:T(8,128)(2,1)S(1)}, u32[]{:S(2)}, u32[]{:S(2)}) collective-permute-start(bf16[1024,256]{1,0:T(8,128)(2,1)S(1)} %bitcast.23), channel_id=1, source_target_pairs={{0,1},{1,0},{2,3},{3,2},{4,5},{5,4},{6,7},{7,6},{8,9},{9,8},{10,11... | collective-permute-start | bytes 1572872 | tf_op jit(solution)/shard_map/ppermute | solution.py:38
  66.3 1.6 %shard_map.107 = (bf16[3,256,512]{2,1,0:T(8,128)(2,1)S(1)}, bf16[2,256,512]{2,1,0:T(8,128)(2,1)S(1)}, bf16[2,512,256]{2,1,0:T(8,128)(2,1)S(1)}) custom-call(s32[5]{0:T(128)S(1)} %stack.53.refs_0_, bf16[4,4,7,8,512]{4,3,2,1,0:T(8,128)(2,1)S(1)} %pad_maximum_fusion.refs_1_, bf16[4,4,7,8,512]{4,3,2,1,0:T(8,128)(2,1)S(1)} %collective-permute-done.12.refs_2_, ...), custom_call_target="tpu_custom_call" | custom-call | flops 1610612736 | bytes 3670036 | tf_op jit(solution)/shard_map/pallas_call | solution.py:84
  69.2 4.0 %shard_map.108 = (bf16[512,768]{1,0:T(8,128)(2,1)S(1)}, bf16[512,1024]{1,0:T(8,128)(2,1)S(1)}, bf16[256,1024]{1,0:T(8,128)(2,1)S(1)}) custom-call(s32[5]{0:T(128)S(1)} %stack.53.refs_0_, bf16[256,768]{1,0:T(8,128)(2,1)S(1)} %copy-done.16, bf16[256,768]{1,0:T(8,128)(2,1)S(1)} %collective-permute-done.5.refs_2_, bf16[256,1024]{1,0:T(8,128)(2,1)} %shard_map.106.refs_3_, ...), custom_call_target="tpu_custom_call" | custom-call | flops 1879048192 | bytes 3678228 | tf_op jit(solution)/shard_map/pallas_call | solution.py:84
  73.6 2.4 %shard_map.109 = (bf16[3,256,512]{2,1,0:T(8,128)(2,1)S(1)}, bf16[2,256,512]{2,1,0:T(8,128)(2,1)}, bf16[2,512,256]{2,1,0:T(8,128)(2,1)}) custom-call(s32[5]{0:T(128)S(1)} %stack.53.refs_0_, bf16[4,4,7,8,512]{4,3,2,1,0:T(8,128)(2,1)S(1)} %pad_maximum_fusion.refs_1_, bf16[4,4,7,8,512]{4,3,2,1,0:T(8,128)(2,1)S(1)} %collective-permute-done.12.refs_2_, ...), custom_call_target="tpu_custom_call" | custom-call | bytes 3670036 | tf_op jit(solution)/shard_map/pallas_call | solution.py:84
  76.1 7.0 %shard_map.110 = (bf16[512,1024]{1,0:T(8,128)(2,1)S(1)}, bf16[512,768]{1,0:T(8,128)(2,1)S(1)}, bf16[256,768]{1,0:T(8,128)(2,1)S(1)}, bf16[1024,256]{1,0:T(8,128)(2,1)}) custom-call(s32[5]{0:T(128)S(1)} %stack.53.refs_0_, bf16[256,1024]{1,0:T(8,128)(2,1)S(1)} %get-tuple-element.32.refs_1_, bf16[256,1024]{1,0:T(8,128)(2,1)S(1)} %collective-permute-done.17.refs_2_, ...), custom_call_target="tpu_custom_call" | custom-call | flops 3221225472 | bytes 5775380 | tf_op jit(solution)/shard_map/pallas_call | solution.py:84
  83.9 7.5 %all-to-all-start.1 = ((bf16[32,32,256]{2,1,0:T(8,128)(2,1)}), bf16[32,32,256]{2,1,0:T(8,128)(2,1)S(1)}, u32[]{:S(2)}, u32[]{:S(2)}) async-start(bf16[32,32,256]{2,1,0:T(8,128)(2,1)} %bitcast.20), calls=%async_computation.1 | async-start | bytes 1048576 | tf_op jit(solution)/shard_map/all_to_all | solution.py:297
  94.3 2.1 %shard_map.111.refs_1_ = f32[256,1024]{1,0:T(8,128)S(1)} custom-call(s32[5]{0:T(128)S(1)} %stack.53.refs_0_, bf16[512,768]{1,0:T(8,128)(2,1)S(1)} %get-tuple-element.38.refs_1_.refs_3_.refs_8_, bf16[512,1024]{1,0:T(8,128)(2,1)S(1)} %get-tuple-element.39.refs_2_.refs_7_, bf16[256,768]{1,0:T(8,128)(2,1)S(1)} %copy-done.6, bf16[3,256,512]{2,1,0:T(8,128)(2,1)S(1)} %copy-done.1, ...), custom_call_target="tpu_custom_call" | custom-call | flops 805306368 | bytes 3022868 | tf_op jit(solution)/shard_map/pallas_call | solution.py:84
  96.4 5.5 %all-to-all-done.1 = bf16[32,32,256]{2,1,0:T(8,128)(2,1)S(1)} async-done(((bf16[32,32,256]{2,1,0:T(8,128)(2,1)}), bf16[32,32,256]{2,1,0:T(8,128)(2,1)S(1)}, u32[]{:S(2)}, u32[]{:S(2)}) %all-to-all-start.1) | async-done | bytes 524320 | tf_op jit(solution)/shard_map/all_to_all | solution.py:297
  103.2 2.1 %collective-permute-start.20 = (bf16[256,1024]{1,0:T(8,128)(2,1)S(1)}, bf16[256,1024]{1,0:T(8,128)(2,1)S(1)}, u32[]{:S(2)}, u32[]{:S(2)}) collective-permute-start(bf16[256,1024]{1,0:T(8,128)(2,1)S(1)} %shard_map.112.refs_1_), channel_id=1, source_target_pairs={{0,1},{1,0},{2,3},{3,2},{4,5},{5,4},{6,7},{7,6},{8,9},{9,8},{10,11... | collective-permute-start | bytes 1572872 | tf_op jit(solution)/shard_map/ppermute | solution.py:38
  105.3 1.8 %shard_map.113.refs_10_ = f32[2,256,768]{2,1,0:T(8,128)S(1)} custom-call(s32[5]{0:T(128)S(1)} %stack.53.refs_0_, bf16[2,256,512]{2,1,0:T(8,128)(2,1)} %get-tuple-element.43.refs_1_.refs_5_, bf16[2,256,512]{2,1,0:T(8,128)(2,1)} %collective-permute-done.22.refs_2_.refs_6_, bf16[512,768]{1,0:T(8,128)(2,1)S(1)} %get-tuple-element.38.refs_1_.refs_3_.refs_8_), custom_call_target="tpu_custom_call" | custom-call | flops 402653184 | bytes 1835028 | tf_op jit(solution)/shard_map/pallas_call | solution.py:84
  107.1 6.2 %shard_map.114 = (bf16[64,1024]{1,0:T(8,128)(2,1)}, bf16[64,768]{1,0:T(8,128)(2,1)}) custom-call(s32[5]{0:T(128)S(1)} %stack.53.refs_0_, bf16[256,1024]{1,0:T(8,128)(2,1)S(1)} %shard_map.112.refs_1_, bf16[256,1024]{1,0:T(8,128)(2,1)S(1)} %collective-permute-done.20.refs_2_, bf16[2,512,256]{2,1,0:T(8,128)(2,1)} %get-tuple-element.42.refs_3_, ...), custom_call_target="tpu_custom_call" | custom-call | flops 2684354560 | bytes 6557716 | tf_op jit(solution)/shard_map/pallas_call | solution.py:84
  (80 shorter events, 21.7 us)
Async XLA Ops:
  2.4 11.4 %collective-permute-start = (bf16[7,8,512]{2,1,0:T(8,128)(2,1)S(1)}, bf16[7,8,512]{2,1,0:T(8,128)(2,1)S(1)}, u32[]{:S(2)}, u32[]{:S(2)}) collective-permute-start(bf16[7,8,512]{2,1,0:T(8,128)(2,1)S(1)} %get-tuple-element.25), channel_id=1, source_target_pairs={{0,4},{1,5},{2,6},{3,7},{4,0},{5,1},{6,2},{7,3},{8,12},{9,13},{10,... | collective-permute-start | bytes 172040 | tf_op jit(solution)/shard_map/ppermute | solution.py:282
  10.2 6.2 %collective-permute-start.7 = (bf16[7,8,512]{2,1,0:T(8,128)(2,1)S(1)}, bf16[7,8,512]{2,1,0:T(8,128)(2,1)S(1)}, u32[]{:S(2)}, u32[]{:S(2)}) collective-permute-start(bf16[7,8,512]{2,1,0:T(8,128)(2,1)S(1)} %get-tuple-element.25), channel_id=1, source_target_pairs={{0,2},{1,3},{2,4},{3,5},{4,6},{5,7},{6,0},{7,1},{8,10},{9,11},{10,... | collective-permute-start | bytes 172040 | tf_op jit(solution)/shard_map/ppermute | solution.py:282
  11.4 5.0 %collective-permute-start.8 = (bf16[7,8,512]{2,1,0:T(8,128)(2,1)S(1)}, bf16[7,8,512]{2,1,0:T(8,128)(2,1)S(1)}, u32[]{:S(2)}, u32[]{:S(2)}) collective-permute-start(bf16[7,8,512]{2,1,0:T(8,128)(2,1)S(1)} %get-tuple-element.25), channel_id=1, source_target_pairs={{0,6},{1,7},{2,0},{3,1},{4,2},{5,3},{6,4},{7,5},{8,14},{9,15},{10,... | collective-permute-start | bytes 172040 | tf_op jit(solution)/shard_map/ppermute | solution.py:282
  13.8 13.5 %collective-permute-start.1 = (bf16[64,1792]{1,0:T(8,128)(2,1)S(1)}, bf16[64,1792]{1,0:T(8,128)(2,1)S(1)}, u32[]{:S(2)}, u32[]{:S(2)}) collective-permute-start(bf16[64,1792]{1,0:T(8,128)(2,1)S(1)} %get-tuple-element.26.refs_1_), channel_id=1, source_target_pairs={{0,6},{1,7},{2,0},{3,1},{4,2},{5,3},{6,4},{7,5},{8,14},{9,15},{10,... | collective-permute-start | bytes 688136 | tf_op jit(solution)/shard_map/ppermute | solution.py:44
  16.4 11.8 %collective-permute-start.2 = (bf16[64,1792]{1,0:T(8,128)(2,1)S(1)}, bf16[64,1792]{1,0:T(8,128)(2,1)S(1)}, u32[]{:S(2)}, u32[]{:S(2)}) collective-permute-start(bf16[64,1792]{1,0:T(8,128)(2,1)S(1)} %get-tuple-element.26.refs_1_), channel_id=1, source_target_pairs={{0,2},{1,3},{2,4},{3,5},{4,6},{5,7},{6,0},{7,1},{8,10},{9,11},{10,... | collective-permute-start | bytes 688136 | tf_op jit(solution)/shard_map/ppermute | solution.py:43
  16.4 11.7 %collective-permute-start.9 = (bf16[4,7,8,512]{3,2,1,0:T(8,128)(2,1)S(1)}, bf16[4,7,8,512]{3,2,1,0:T(8,128)(2,1)S(1)}, u32[]{:S(2)}, u32[]{:S(2)}) collective-permute-start(bf16[4,7,8,512]{3,2,1,0:T(8,128)(2,1)S(1)} %pad_maximum_fusion.1), channel_id=1, source_target_pairs={{0,96},{1,25},{2,98},{3,27},{4,100},{5,29},{6,102},{7,31},{8,104},... | collective-permute-start | bytes 688136 | tf_op jit(solution)/shard_map/ppermute | solution.py:286
  19.0 9.2 %collective-permute-start.10 = (bf16[4,7,8,512]{3,2,1,0:T(8,128)(2,1)S(1)}, bf16[4,7,8,512]{3,2,1,0:T(8,128)(2,1)S(1)}, u32[]{:S(2)}, u32[]{:S(2)}) collective-permute-start(bf16[4,7,8,512]{3,2,1,0:T(8,128)(2,1)S(1)} %pad_maximum_fusion.1), channel_id=1, source_target_pairs={{0,64},{1,17},{2,66},{3,19},{4,68},{5,21},{6,70},{7,23},{8,72},{9,... | collective-permute-start | bytes 688136 | tf_op jit(solution)/shard_map/ppermute | solution.py:286
  19.5 8.7 %collective-permute-start.11 = (bf16[4,7,8,512]{3,2,1,0:T(8,128)(2,1)S(1)}, bf16[4,7,8,512]{3,2,1,0:T(8,128)(2,1)S(1)}, u32[]{:S(2)}, u32[]{:S(2)}) collective-permute-start(bf16[4,7,8,512]{3,2,1,0:T(8,128)(2,1)S(1)} %pad_maximum_fusion.1), channel_id=1, source_target_pairs={{0,32},{1,9},{2,34},{3,11},{4,36},{5,13},{6,38},{7,15},{8,40},{9,1... | collective-permute-start | bytes 688136 | tf_op jit(solution)/shard_map/ppermute | solution.py:286
  28.3 14.1 %collective-permute-start.13 = (bf16[4,4,7,8,512]{4,3,2,1,0:T(8,128)(2,1)S(1)}, bf16[4,4,7,8,512]{4,3,2,1,0:T(8,128)(2,1)S(1)}, u32[]{:S(2)}, u32[]{:S(2)}) collective-permute-start(bf16[4,4,7,8,512]{4,3,2,1,0:T(8,128)(2,1)S(1)} %pad_maximum_fusion.refs_1_), channel_id=1, source_target_pairs={{0,8},{1,33},{2,10},{3,35},{4,12},{5,37},{6,14},{7,39},{8,16},{9,4... | collective-permute-start | bytes 2752520 | tf_op jit(solution)/shard_map/ppermute | solution.py:43
  29.6 12.8 %collective-permute-start.12 = (bf16[4,4,7,8,512]{4,3,2,1,0:T(8,128)(2,1)S(1)}, bf16[4,4,7,8,512]{4,3,2,1,0:T(8,128)(2,1)S(1)}, u32[]{:S(2)}, u32[]{:S(2)}) collective-permute-start(bf16[4,4,7,8,512]{4,3,2,1,0:T(8,128)(2,1)S(1)} %pad_maximum_fusion.refs_1_), channel_id=1, source_target_pairs={{0,24},{1,97},{2,26},{3,99},{4,28},{5,101},{6,30},{7,103},{8,0},{9... | collective-permute-start | bytes 2752520 | tf_op jit(solution)/shard_map/ppermute | solution.py:44
  31.1 5.8 %collective-permute-start.3 = (bf16[32,1792]{1,0:T(8,128)(2,1)S(1)}, bf16[32,1792]{1,0:T(8,128)(2,1)S(1)}, u32[]{:S(2)}, u32[]{:S(2)}) collective-permute-start(bf16[32,1792]{1,0:T(8,128)(2,1)S(1)} %slice.16), channel_id=1, source_target_pairs={{0,2},{1,3},{2,4},{3,5},{4,6},{5,7},{6,0},{7,1},{8,10},{9,11},{10,... | collective-permute-start | bytes 344072 | tf_op jit(solution)/shard_map/ppermute | solution.py:45
  32.6 6.5 %collective-permute-start.4 = (bf16[32,1792]{1,0:T(8,128)(2,1)S(1)}, bf16[32,1792]{1,0:T(8,128)(2,1)S(1)}, u32[]{:S(2)}, u32[]{:S(2)}) collective-permute-start(bf16[32,1792]{1,0:T(8,128)(2,1)S(1)} %slice.17), channel_id=1, source_target_pairs={{0,6},{1,7},{2,0},{3,1},{4,2},{5,3},{6,4},{7,5},{8,14},{9,15},{10,... | collective-permute-start | bytes 344072 | tf_op jit(solution)/shard_map/ppermute | solution.py:46
  42.4 18.7 %all-to-all-start = ((bf16[32,32,256]{2,1,0:T(8,128)(2,1)}), bf16[32,32,256]{2,1,0:T(8,128)(2,1)S(1)}, u32[]{:S(2)}, u32[]{:S(2)}) async-start(bf16[32,32,256]{2,1,0:T(8,128)(2,1)} %bitcast.25), calls=%async_computation | async-start | bytes 1048576 | tf_op jit(solution)/shard_map/all_to_all | solution.py:297
  52.0 14.2 %collective-permute-start.15 = (bf16[2,4,7,8,512]{4,3,2,1,0:T(8,128)(2,1)}, bf16[2,4,7,8,512]{4,3,2,1,0:T(8,128)(2,1)}, u32[]{:S(2)}, u32[]{:S(2)}) collective-permute-start(bf16[2,4,7,8,512]{4,3,2,1,0:T(8,128)(2,1)} %slice.18), channel_id=1, source_target_pairs={{0,8},{1,33},{2,10},{3,35},{4,12},{5,37},{6,14},{7,39},{8,16},{9,4... | collective-permute-start | bytes 1376264 | tf_op jit(solution)/shard_map/ppermute | solution.py:45
  54.1 12.2 %collective-permute-start.16 = (bf16[2,4,7,8,512]{4,3,2,1,0:T(8,128)(2,1)}, bf16[2,4,7,8,512]{4,3,2,1,0:T(8,128)(2,1)}, u32[]{:S(2)}, u32[]{:S(2)}) collective-permute-start(bf16[2,4,7,8,512]{4,3,2,1,0:T(8,128)(2,1)} %slice.19), channel_id=1, source_target_pairs={{0,24},{1,97},{2,26},{3,99},{4,28},{5,101},{6,30},{7,103},{8,0},{9... | collective-permute-start | bytes 1376264 | tf_op jit(solution)/shard_map/ppermute | solution.py:46
  56.9 12.2 %collective-permute-start.6 = (bf16[256,1024]{1,0:T(8,128)(2,1)}, bf16[256,1024]{1,0:T(8,128)(2,1)}, u32[]{:S(2)}, u32[]{:S(2)}) collective-permute-start(bf16[256,1024]{1,0:T(8,128)(2,1)} %shard_map.106.refs_3_), channel_id=1, source_target_pairs={{0,1},{1,0},{2,3},{3,2},{4,5},{5,4},{6,7},{7,6},{8,9},{9,8},{10,11... | collective-permute-start | bytes 1572872 | tf_op jit(solution)/shard_map/ppermute | solution.py:38
  61.1 8.0 %collective-permute-start.14 = (bf16[1024,256]{1,0:T(8,128)(2,1)S(1)}, bf16[1024,256]{1,0:T(8,128)(2,1)S(1)}, u32[]{:S(2)}, u32[]{:S(2)}) collective-permute-start(bf16[1024,256]{1,0:T(8,128)(2,1)S(1)} %bitcast.23), channel_id=1, source_target_pairs={{0,1},{1,0},{2,3},{3,2},{4,5},{5,4},{6,7},{7,6},{8,9},{9,8},{10,11... | collective-permute-start | bytes 1572872 | tf_op jit(solution)/shard_map/ppermute | solution.py:38
  65.1 4.1 %collective-permute-start.5 = (bf16[256,768]{1,0:T(8,128)(2,1)}, bf16[256,768]{1,0:T(8,128)(2,1)S(1)}, u32[]{:S(2)}, u32[]{:S(2)}) collective-permute-start(bf16[256,768]{1,0:T(8,128)(2,1)} %copy-done.15), channel_id=1, source_target_pairs={{0,1},{1,0},{2,3},{3,2},{4,5},{5,4},{6,7},{7,6},{8,9},{9,8},{10,11... | collective-permute-start | bytes 1179656 | tf_op jit(solution)/shard_map/ppermute | solution.py:38
  67.9 8.2 %collective-permute-start.18 = (bf16[2,512,256]{2,1,0:T(8,128)(2,1)S(1)}, bf16[2,512,256]{2,1,0:T(8,128)(2,1)S(1)}, u32[]{:S(2)}, u32[]{:S(2)}) collective-permute-start(bf16[2,512,256]{2,1,0:T(8,128)(2,1)S(1)} %get-tuple-element.33.refs_3_), channel_id=1, source_target_pairs={{0,1},{1,0},{2,3},{3,2},{4,5},{5,4},{6,7},{7,6},{8,9},{9,8},{10,11... | collective-permute-start | bytes 1572872 | tf_op jit(solution)/shard_map/ppermute | solution.py:38
  69.0 7.1 %collective-permute-start.19 = (bf16[2,256,512]{2,1,0:T(8,128)(2,1)S(1)}, bf16[2,256,512]{2,1,0:T(8,128)(2,1)S(1)}, u32[]{:S(2)}, u32[]{:S(2)}) collective-permute-start(bf16[2,256,512]{2,1,0:T(8,128)(2,1)S(1)} %get-tuple-element.34.refs_5_), channel_id=1, source_target_pairs={{0,1},{1,0},{2,3},{3,2},{4,5},{5,4},{6,7},{7,6},{8,9},{9,8},{10,11... | collective-permute-start | bytes 1572872 | tf_op jit(solution)/shard_map/ppermute | solution.py:38
  83.9 18.0 %all-to-all-start.1 = ((bf16[32,32,256]{2,1,0:T(8,128)(2,1)}), bf16[32,32,256]{2,1,0:T(8,128)(2,1)S(1)}, u32[]{:S(2)}, u32[]{:S(2)}) async-start(bf16[32,32,256]{2,1,0:T(8,128)(2,1)} %bitcast.20), calls=%async_computation.1 | async-start | bytes 1048576 | tf_op jit(solution)/shard_map/all_to_all | solution.py:297
  91.4 13.9 %collective-permute-start.22 = (bf16[2,256,512]{2,1,0:T(8,128)(2,1)}, bf16[2,256,512]{2,1,0:T(8,128)(2,1)}, u32[]{:S(2)}, u32[]{:S(2)}) collective-permute-start(bf16[2,256,512]{2,1,0:T(8,128)(2,1)} %get-tuple-element.43.refs_1_.refs_5_), channel_id=1, source_target_pairs={{0,1},{1,0},{2,3},{3,2},{4,5},{5,4},{6,7},{7,6},{8,9},{9,8},{10,11... | collective-permute-start | bytes 1572872 | tf_op jit(solution)/shard_map/ppermute | solution.py:38
  92.1 15.0 %collective-permute-start.21 = (bf16[2,512,256]{2,1,0:T(8,128)(2,1)}, bf16[2,512,256]{2,1,0:T(8,128)(2,1)}, u32[]{:S(2)}, u32[]{:S(2)}) collective-permute-start(bf16[2,512,256]{2,1,0:T(8,128)(2,1)} %get-tuple-element.42.refs_3_), channel_id=1, source_target_pairs={{0,1},{1,0},{2,3},{3,2},{4,5},{5,4},{6,7},{7,6},{8,9},{9,8},{10,11... | collective-permute-start | bytes 1572872 | tf_op jit(solution)/shard_map/ppermute | solution.py:38
  103.2 3.9 %collective-permute-start.20 = (bf16[256,1024]{1,0:T(8,128)(2,1)S(1)}, bf16[256,1024]{1,0:T(8,128)(2,1)S(1)}, u32[]{:S(2)}, u32[]{:S(2)}) collective-permute-start(bf16[256,1024]{1,0:T(8,128)(2,1)S(1)} %shard_map.112.refs_1_), channel_id=1, source_target_pairs={{0,1},{1,0},{2,3},{3,2},{4,5},{5,4},{6,7},{7,6},{8,9},{9,8},{10,11... | collective-permute-start | bytes 1572872 | tf_op jit(solution)/shard_map/ppermute | solution.py:38
  (19 other events, 140.2 us)

commit v6 on v5

--- a/solution.py
+++ b/solution.py
@@ -17,6 +17,7 @@
 CORE = [(c, c ^ 1) for c in range(8)]
 VMEM = pl.BlockSpec(memory_space=pltpu.VMEM)
 SMEM = pl.BlockSpec(memory_space=pltpu.SMEM)
+HBM = pl.BlockSpec(memory_space=pltpu.HBM)
 
 
 def z_shift(s):
@@ -83,9 +84,9 @@
 
     return pl.pallas_call(
         body,
-        out_shape=[jax.ShapeDtypeStruct(s, d) for s, d in outs],
+        out_shape=[o if isinstance(o, pl.MemoryRef) else jax.ShapeDtypeStruct(*o) for o in outs],
         in_specs=specs,
-        out_specs=[VMEM] * len(outs),
+        out_specs=[HBM if isinstance(o, pl.MemoryRef) else VMEM for o in outs],
         scratch_shapes=list(scratch),
         compiler_params=pltpu.CompilerParams(vmem_limit_bytes=6 << 20),
         cost_estimate=pl.CostEstimate(flops=flops, bytes_accessed=moved, transcendentals=0),
@@ -104,16 +105,21 @@
     out[pl.ds(at(3), 64), :] = prev[:, cols]
 
 
-def select_rows(send, x, rows):
-    def body(sl, _):
-        rows[sl, :] = dot(x, hot(send[:, sl], 0, x.shape[1])).T.astype(BF)
-
-    chunks(rows.shape[0], body)
-
-
-def send_first(meta, own, nxt, far_a, far_b, prev, send, half, rows):
+def select_rows(send, x, rows, held, sem):
+    size = rows.shape[0] // 4
+    copies = []
+    for i in range(4):
+        sl = slice(i * size, i * size + size)
+        held[sl, :] = dot(x, hot(send[:, sl], 0, x.shape[1])).T.astype(BF)
+        copies.append(pltpu.make_async_copy(held.at[sl], rows.at[sl], sem.at[i]))
+        copies[-1].start()
+    for copy in copies:
+        copy.wait()
+
+
+def send_first(meta, own, nxt, far_a, far_b, prev, send, half, rows, held, sem):
     place_half(meta, (own, nxt, far_a, far_b, prev), half, 0)
-    select_rows(send, half[...], rows)
+    select_rows(send, half[...], rows, held, sem)
 
 
 def gather_edges(meta, own, nxt, far_a, far_b, prev, half):
@@ -209,7 +215,7 @@
 
 def tail_first(
     meta, hid, hid_other, turned, turned_other, nodes, nodes_other, e_all, v_all, dst, mats_next, send,
-    e_new, v_new, sender, rows,
+    e_new, v_new, rows, sender, held, sem,
 ):
     new_edges(hid, hid_other, turned, turned_other, e_all, e_new)
 
@@ -220,7 +226,7 @@
 
     chunks(v_new.shape[1], body)
     sender[...] = dot(mats_next[1], v_new[...]).astype(BF)
-    select_rows(send, sender[...], rows)
+    select_rows(send, sender[...], rows, held, sem)
 
 
 def tail_last(
@@ -239,8 +245,9 @@
     chunks(v_out.shape[1], body)
 
 
-def edge_local(meta, v_all, e_all, sender, mats, src, dst, part, receiver):
+def edge_local(meta, v_all, e_all, mats, src, dst, part, sender, receiver):
     n = v_all.shape[1]
+    sender[...] = dot(mats[1], v_all[...]).astype(BF)
     receiver[...] = dot(mats[2], v_all[...]).astype(BF)
 
     def body(sl, _):
@@ -277,7 +284,7 @@
         prepare,
         [((7, 8, LATENT), BF), ((64, n + m), BF)],
         meta, *(pltpu.with_memory_space_constraint(a, pltpu.HBM) for a in shared),
-        scratch=[pltpu.SemaphoreType.DMA((6,))], space=pl.BlockSpec(memory_space=pltpu.HBM),
+        scratch=[pltpu.SemaphoreType.DMA((6,))], space=HBM,
     )
     pieces = [piece] + [lax.ppermute(piece, "ch", z_shift(s)) for s in (2, 1, 3)]
     both = lax.optimization_barrier((both, pieces[1]))[0]
@@ -290,7 +297,8 @@
     w_parts = ring_gather(one, ("dom", "ch"), lambda s: ring(2, s))
 
     v_half, rows = call(
-        send_first, [((HALF, n), BF), ((m, HALF), BF)], meta, *parts, send, flops=2 * HALF * n * m
+        send_first, [((HALF, n), BF), pltpu.HBM((m, HALF), BF)], meta, *parts, send,
+        scratch=[pltpu.VMEM((m, HALF), BF), pltpu.SemaphoreType.DMA((4,))], flops=2 * HALF * n * m,
     )
 
     def exchange(rows):
@@ -320,16 +328,16 @@
         scratch=[pltpu.VMEM((HALF, n + m), BF), pltpu.VMEM((HALF, n), BF), pltpu.VMEM((m, LATENT), BF)],
         flops=4 * big(HALF, n + m),
     )
-    e_new, v_new, sender, rows = call(
+    e_new, v_new, rows = call(
         tail_first,
-        [((LATENT, m), BF), ((LATENT, n), BF), ((HALF, n), BF), ((m, HALF), BF)],
+        [((LATENT, m), BF), ((LATENT, n), BF), pltpu.HBM((m, HALF), BF)],
         meta, hid, swap(hid), *tails[0], e_all, v_all, dst, mats[1], send,
-        flops=6 * big(LATENT, m),
+        scratch=[pltpu.VMEM((HALF, n), BF), pltpu.VMEM((m, HALF), BF), pltpu.SemaphoreType.DMA((4,))], flops=6 * big(LATENT, m),
     )
     far = exchange(rows)
     (part,) = call(
-        edge_local, [((HALF, m), F32)], meta, v_new, e_new, sender, mats[1], src, dst,
-        scratch=[pltpu.VMEM((HALF, n), BF)], flops=3 * big(HALF, m),
+        edge_local, [((HALF, m), F32)], meta, v_new, e_new, mats[1], src, dst,
+        scratch=[pltpu.VMEM((HALF, n), BF)] * 2, flops=3 * big(HALF, m),
     )
     (local,) = call(node_local, [((2, HALF, n), F32)], meta, tails[1][2], tails[1][3], v_new, flops=2 * big(HALF, n))
     (hid,) = call(

time: 114 us -> 113 us (level)
  local copies, waits for them, and re-layouts: 5.48 us -> 2.93 us
    unnamed x36 -> x30, local copies, waits for them, and re-layouts: 3.74 us -> 1.19 us
  transfers between devices with their start and end apart: 25 -> 25, of which waited for: 7 -> 7; matrix products, arithmetic and copies ran while one was open for 1% -> 1% of each run, Pallas kernels for 14% -> 15%
where the time goes in v6:
time: 113 us
  starting transfers between devices  56 us (50%)
  Pallas kernels  31.5 us (28%)
  waiting for transfers between devices  20.9 us (18%)
  local copies, waits for them, and re-layouts  2.93 us (3%)
    pallas_call x11, Pallas kernels, call(): pl.pallas_call(body, out_shape=[o if isinstance(o, pl.MemoryRef) else jax...  31.5 us
    all_to_all x2, starting transfers between devices, exchange(): lax.all_to_all(rows.reshape(32, SLOTS, HALF), 'dom', 0, 0, tiled=True)  16.3 us
    ppermute x9, starting transfers between devices, swap(): return lax.ppermute(x, 'ch', CORE)  12.8 us
    ppermute x3, starting transfers between devices, shards(): lax.ppermute(piece, 'ch', z_shift(s))  11.4 us
    ppermute x2, waiting for transfers between devices, ring_gather(): nxt = lax.ppermute(x, axis, perm(3))  7.2 us
    all_to_all x2, waiting for transfers between devices, exchange(): lax.all_to_all(rows.reshape(32, SLOTS, HALF), 'dom', 0, 0, tiled=True)  6.25 us
    ppermute x2, starting transfers between devices, ring_gather(): nxt = lax.ppermute(x, axis, perm(3))  4.1 us
    ppermute x2, starting transfers between devices, ring_gather(): far_b = lax.ppermute(nxt[half:], axis, perm(3))  3.74 us
  transfers between devices with their start and end apart: 25, of which 7 were waited for; matrix products, arithmetic and copies ran while one was open for 1% of the time, Pallas kernels for 15%

profile of v6, /device:TPU:1, one launch (start us, length us, event | category | flops | bytes accessed | tf_op | source)
XLA Modules:
  0.0 112.5 jit_solution(11299937778553537633)
XLA Ops:
  0.7 1.6 %shard_map.104 = (bf16[7,8,512]{2,1,0:T(8,128)(2,1)S(1)}, bf16[64,1792]{1,0:T(8,128)(2,1)S(1)}) custom-call(s32[5]{0:T(128)S(1)} %stack.53.refs_0_, bf16[2,3,64,512]{3,2,1,0:T(8,128)(2,1)} %bitcast.38, bf16[2,64,512]{2,1,0:T(8,128)(2,1)} %refs_2_.1, bf16[2,2,64,512]{3,2,1,0:T(8,128)(2,1)} %bitcast.39, bf16[2,64,512]{2,1,0:T(8,128)(2,1)} %refs_4_.1, ...), custom_call_target="tpu_custom_call" | custom-call | bytes 1146900 | tf_op jit(solution)/shard_map/pallas_call | solution.py:85
  2.4 7.8 %collective-permute-start = (bf16[7,8,512]{2,1,0:T(8,128)(2,1)S(1)}, bf16[7,8,512]{2,1,0:T(8,128)(2,1)S(1)}, u32[]{:S(2)}, u32[]{:S(2)}) collective-permute-start(bf16[7,8,512]{2,1,0:T(8,128)(2,1)S(1)} %get-tuple-element.24), channel_id=1, source_target_pairs={{0,4},{1,5},{2,6},{3,7},{4,0},{5,1},{6,2},{7,3},{8,12},{9,13},{10,... | collective-permute-start | bytes 172040 | tf_op jit(solution)/shard_map/ppermute | solution.py:289
  11.4 2.4 %collective-permute-start.8 = (bf16[7,8,512]{2,1,0:T(8,128)(2,1)S(1)}, bf16[7,8,512]{2,1,0:T(8,128)(2,1)S(1)}, u32[]{:S(2)}, u32[]{:S(2)}) collective-permute-start(bf16[7,8,512]{2,1,0:T(8,128)(2,1)S(1)} %get-tuple-element.24), channel_id=1, source_target_pairs={{0,6},{1,7},{2,0},{3,1},{4,2},{5,3},{6,4},{7,5},{8,14},{9,15},{10,... | collective-permute-start | bytes 172040 | tf_op jit(solution)/shard_map/ppermute | solution.py:289
  13.8 2.6 %collective-permute-start.1 = (bf16[64,1792]{1,0:T(8,128)(2,1)S(1)}, bf16[64,1792]{1,0:T(8,128)(2,1)S(1)}, u32[]{:S(2)}, u32[]{:S(2)}) collective-permute-start(bf16[64,1792]{1,0:T(8,128)(2,1)S(1)} %get-tuple-element.25.refs_1_), channel_id=1, source_target_pairs={{0,6},{1,7},{2,0},{3,1},{4,2},{5,3},{6,4},{7,5},{8,14},{9,15},{10,... | collective-permute-start | bytes 688136 | tf_op jit(solution)/shard_map/ppermute | solution.py:45
  16.4 2.6 %collective-permute-start.9 = (bf16[4,7,8,512]{3,2,1,0:T(8,128)(2,1)S(1)}, bf16[4,7,8,512]{3,2,1,0:T(8,128)(2,1)S(1)}, u32[]{:S(2)}, u32[]{:S(2)}) collective-permute-start(bf16[4,7,8,512]{3,2,1,0:T(8,128)(2,1)S(1)} %pad_maximum_fusion.1), channel_id=1, source_target_pairs={{0,96},{1,25},{2,98},{3,27},{4,100},{5,29},{6,102},{7,31},{8,104},... | collective-permute-start | bytes 688136 | tf_op jit(solution)/shard_map/ppermute | solution.py:293
  20.1 7.2 %collective-permute-done.1.refs_2_ = bf16[64,1792]{1,0:T(8,128)(2,1)S(1)} collective-permute-done((bf16[64,1792]{1,0:T(8,128)(2,1)S(1)}, bf16[64,1792]{1,0:T(8,128)(2,1)S(1)}, u32[]{:S(2)}, u32[]{:S(2)}) %collective-permute-start.1) | collective-permute-done | bytes 229408 | tf_op jit(solution)/shard_map/ppermute | solution.py:45
  29.6 1.5 %collective-permute-start.12 = (bf16[4,4,7,8,512]{4,3,2,1,0:T(8,128)(2,1)S(1)}, bf16[4,4,7,8,512]{4,3,2,1,0:T(8,128)(2,1)S(1)}, u32[]{:S(2)}, u32[]{:S(2)}) collective-permute-start(bf16[4,4,7,8,512]{4,3,2,1,0:T(8,128)(2,1)S(1)} %pad_maximum_fusion.refs_1_), channel_id=1, source_target_pairs={{0,24},{1,97},{2,26},{3,99},{4,28},{5,101},{6,30},{7,103},{8,0},{9... | collective-permute-start | bytes 2752520 | tf_op jit(solution)/shard_map/ppermute | solution.py:45
  32.6 2.3 %collective-permute-start.4 = (bf16[32,1792]{1,0:T(8,128)(2,1)S(1)}, bf16[32,1792]{1,0:T(8,128)(2,1)S(1)}, u32[]{:S(2)}, u32[]{:S(2)}) collective-permute-start(bf16[32,1792]{1,0:T(8,128)(2,1)S(1)} %slice.17), channel_id=1, source_target_pairs={{0,6},{1,7},{2,0},{3,1},{4,2},{5,3},{6,4},{7,5},{8,14},{9,15},{10,... | collective-permute-start | bytes 344072 | tf_op jit(solution)/shard_map/ppermute | solution.py:47
  34.9 2.1 %collective-permute-done.3.refs_3_ = bf16[32,1792]{1,0:T(8,128)(2,1)S(1)} collective-permute-done((bf16[32,1792]{1,0:T(8,128)(2,1)S(1)}, bf16[32,1792]{1,0:T(8,128)(2,1)S(1)}, u32[]{:S(2)}, u32[]{:S(2)}) %collective-permute-start.3) | collective-permute-done | bytes 114720 | tf_op jit(solution)/shard_map/ppermute | solution.py:46
  37.0 2.1 %collective-permute-done.4.refs_4_ = bf16[32,1792]{1,0:T(8,128)(2,1)S(1)} collective-permute-done((bf16[32,1792]{1,0:T(8,128)(2,1)S(1)}, bf16[32,1792]{1,0:T(8,128)(2,1)S(1)}, u32[]{:S(2)}, u32[]{:S(2)}) %collective-permute-start.4) | collective-permute-done | bytes 114720 | tf_op jit(solution)/shard_map/ppermute | solution.py:47
  39.1 2.0 %shard_map.105 = (bf16[256,768]{1,0:T(8,128)(2,1)S(1)}, bf16[1024,256]{1,0:T(8,128)(2,1)}) custom-call(s32[5]{0:T(128)S(1)} %stack.53.refs_0_, bf16[64,1792]{1,0:T(8,128)(2,1)S(1)} %get-tuple-element.25.refs_1_, bf16[64,1792]{1,0:T(8,128)(2,1)S(1)} %collective-permute-done.1.refs_2_, bf16[32,1792]{1,0:T(8,128)(2,1)S(1)} %collective-permute-done.3.refs_3_, ...), custom_call_target="tpu_custom_call" | custom-call | flops 402653184 | bytes 921620 | tf_op jit(solution)/shard_map/pallas_call | solution.py:85
  42.4 8.7 %all-to-all-start = ((bf16[32,32,256]{2,1,0:T(8,128)(2,1)}), bf16[32,32,256]{2,1,0:T(8,128)(2,1)S(1)}, u32[]{:S(2)}, u32[]{:S(2)}) async-start(bf16[32,32,256]{2,1,0:T(8,128)(2,1)} %bitcast.36), calls=%async_computation | async-start | bytes 1048576 | tf_op jit(solution)/shard_map/all_to_all | solution.py:305
  56.9 4.2 %collective-permute-start.6 = (bf16[256,1024]{1,0:T(8,128)(2,1)}, bf16[256,1024]{1,0:T(8,128)(2,1)}, u32[]{:S(2)}, u32[]{:S(2)}) collective-permute-start(bf16[256,1024]{1,0:T(8,128)(2,1)} %shard_map.106.refs_3_), channel_id=1, source_target_pairs={{0,1},{1,0},{2,3},{3,2},{4,5},{5,4},{6,7},{7,6},{8,9},{9,8},{10,11... | collective-permute-start | bytes 1572872 | tf_op jit(solution)/shard_map/ppermute | solution.py:39
  61.1 3.9 %collective-permute-start.14 = (bf16[1024,256]{1,0:T(8,128)(2,1)S(1)}, bf16[1024,256]{1,0:T(8,128)(2,1)S(1)}, u32[]{:S(2)}, u32[]{:S(2)}) collective-permute-start(bf16[1024,256]{1,0:T(8,128)(2,1)S(1)} %bitcast.23), channel_id=1, source_target_pairs={{0,1},{1,0},{2,3},{3,2},{4,5},{5,4},{6,7},{7,6},{8,9},{9,8},{10,11... | collective-permute-start | bytes 1572872 | tf_op jit(solution)/shard_map/ppermute | solution.py:39
  66.3 1.6 %shard_map.107 = (bf16[3,256,512]{2,1,0:T(8,128)(2,1)S(1)}, bf16[2,256,512]{2,1,0:T(8,128)(2,1)S(1)}, bf16[2,512,256]{2,1,0:T(8,128)(2,1)S(1)}) custom-call(s32[5]{0:T(128)S(1)} %stack.53.refs_0_, bf16[4,4,7,8,512]{4,3,2,1,0:T(8,128)(2,1)S(1)} %pad_maximum_fusion.refs_1_, bf16[4,4,7,8,512]{4,3,2,1,0:T(8,128)(2,1)S(1)} %collective-permute-done.12.refs_2_, ...), custom_call_target="tpu_custom_call" | custom-call | flops 1610612736 | bytes 3670036 | tf_op jit(solution)/shard_map/pallas_call | solution.py:85
  69.2 4.0 %shard_map.108 = (bf16[512,768]{1,0:T(8,128)(2,1)S(1)}, bf16[512,1024]{1,0:T(8,128)(2,1)S(1)}, bf16[256,1024]{1,0:T(8,128)(2,1)S(1)}) custom-call(s32[5]{0:T(128)S(1)} %stack.53.refs_0_, bf16[256,768]{1,0:T(8,128)(2,1)S(1)} %copy-done.13, bf16[256,768]{1,0:T(8,128)(2,1)S(1)} %collective-permute-done.5.refs_2_, bf16[256,1024]{1,0:T(8,128)(2,1)} %shard_map.106.refs_3_, ...), custom_call_target="tpu_custom_call" | custom-call | flops 1879048192 | bytes 3678228 | tf_op jit(solution)/shard_map/pallas_call | solution.py:85
  73.7 2.4 %shard_map.109 = (bf16[3,256,512]{2,1,0:T(8,128)(2,1)S(1)}, bf16[2,256,512]{2,1,0:T(8,128)(2,1)}, bf16[2,512,256]{2,1,0:T(8,128)(2,1)}) custom-call(s32[5]{0:T(128)S(1)} %stack.53.refs_0_, bf16[4,4,7,8,512]{4,3,2,1,0:T(8,128)(2,1)S(1)} %pad_maximum_fusion.refs_1_, bf16[4,4,7,8,512]{4,3,2,1,0:T(8,128)(2,1)S(1)} %collective-permute-done.12.refs_2_, ...), custom_call_target="tpu_custom_call" | custom-call | bytes 3670036 | tf_op jit(solution)/shard_map/pallas_call | solution.py:85
  76.1 6.9 %shard_map.110 = (bf16[512,1024]{1,0:T(8,128)(2,1)S(1)}, bf16[512,768]{1,0:T(8,128)(2,1)S(1)}, bf16[1024,256]{1,0:T(8,128)(2,1)}) custom-call(s32[5]{0:T(128)S(1)} %stack.53.refs_0_, bf16[256,1024]{1,0:T(8,128)(2,1)S(1)} %get-tuple-element.31.refs_1_, bf16[256,1024]{1,0:T(8,128)(2,1)S(1)} %collective-permute-done.17.refs_2_, ...), custom_call_target="tpu_custom_call" | custom-call | flops 3221225472 | bytes 5775380 | tf_op jit(solution)/shard_map/pallas_call | solution.py:85
  83.0 7.5 %all-to-all-start.1 = ((bf16[32,32,256]{2,1,0:T(8,128)(2,1)}), bf16[32,32,256]{2,1,0:T(8,128)(2,1)S(1)}, u32[]{:S(2)}, u32[]{:S(2)}) async-start(bf16[32,32,256]{2,1,0:T(8,128)(2,1)} %bitcast.37), calls=%async_computation.1 | async-start | bytes 1048576 | tf_op jit(solution)/shard_map/all_to_all | solution.py:305
  92.5 2.3 %shard_map.111.refs_1_ = f32[256,1024]{1,0:T(8,128)S(1)} custom-call(s32[5]{0:T(128)S(1)} %stack.53.refs_0_, bf16[512,768]{1,0:T(8,128)(2,1)S(1)} %get-tuple-element.37.refs_1_.refs_3_.refs_8_, bf16[512,1024]{1,0:T(8,128)(2,1)S(1)} %get-tuple-element.38.refs_2_.refs_7_, bf16[3,256,512]{2,1,0:T(8,128)(2,1)S(1)} %copy-done.1, s32[1,1024]{1,0:T(1,128)S(1)} %bitcast.27, ...), custom_call_target="tpu_custom_call" | custom-call | flops 805306368 | bytes 2629652 | tf_op jit(solution)/shard_map/pallas_call | solution.py:85
  94.8 6.2 %all-to-all-done.1 = bf16[32,32,256]{2,1,0:T(8,128)(2,1)S(1)} async-done(((bf16[32,32,256]{2,1,0:T(8,128)(2,1)}), bf16[32,32,256]{2,1,0:T(8,128)(2,1)S(1)}, u32[]{:S(2)}, u32[]{:S(2)}) %all-to-all-start.1) | async-done | bytes 524320 | tf_op jit(solution)/shard_map/all_to_all | solution.py:305
  102.4 2.1 %collective-permute-start.20 = (bf16[256,1024]{1,0:T(8,128)(2,1)S(1)}, bf16[256,1024]{1,0:T(8,128)(2,1)S(1)}, u32[]{:S(2)}, u32[]{:S(2)}) collective-permute-start(bf16[256,1024]{1,0:T(8,128)(2,1)S(1)} %shard_map.112.refs_1_), channel_id=1, source_target_pairs={{0,1},{1,0},{2,3},{3,2},{4,5},{5,4},{6,7},{7,6},{8,9},{9,8},{10,11... | collective-permute-start | bytes 1572872 | tf_op jit(solution)/shard_map/ppermute | solution.py:39
  104.5 1.8 %shard_map.113.refs_10_ = f32[2,256,768]{2,1,0:T(8,128)S(1)} custom-call(s32[5]{0:T(128)S(1)} %stack.53.refs_0_, bf16[2,256,512]{2,1,0:T(8,128)(2,1)} %get-tuple-element.41.refs_1_.refs_5_, bf16[2,256,512]{2,1,0:T(8,128)(2,1)} %collective-permute-done.22.refs_2_.refs_6_, bf16[512,768]{1,0:T(8,128)(2,1)S(1)} %get-tuple-element.37.refs_1_.refs_3_.refs_8_), custom_call_target="tpu_custom_call" | custom-call | flops 402653184 | bytes 1835028 | tf_op jit(solution)/shard_map/pallas_call | solution.py:85
  106.3 6.2 %shard_map.114 = (bf16[64,1024]{1,0:T(8,128)(2,1)}, bf16[64,768]{1,0:T(8,128)(2,1)}) custom-call(s32[5]{0:T(128)S(1)} %stack.53.refs_0_, bf16[256,1024]{1,0:T(8,128)(2,1)S(1)} %shard_map.112.refs_1_, bf16[256,1024]{1,0:T(8,128)(2,1)S(1)} %collective-permute-done.20.refs_2_, bf16[2,512,256]{2,1,0:T(8,128)(2,1)} %get-tuple-element.40.refs_3_, ...), custom_call_target="tpu_custom_call" | custom-call | flops 2684354560 | bytes 6557716 | tf_op jit(solution)/shard_map/pallas_call | solution.py:85
  (74 shorter events, 19.4 us)
Async XLA Ops:
  2.4 11.4 %collective-permute-start = (bf16[7,8,512]{2,1,0:T(8,128)(2,1)S(1)}, bf16[7,8,512]{2,1,0:T(8,128)(2,1)S(1)}, u32[]{:S(2)}, u32[]{:S(2)}) collective-permute-start(bf16[7,8,512]{2,1,0:T(8,128)(2,1)S(1)} %get-tuple-element.24), channel_id=1, source_target_pairs={{0,4},{1,5},{2,6},{3,7},{4,0},{5,1},{6,2},{7,3},{8,12},{9,13},{10,... | collective-permute-start | bytes 172040 | tf_op jit(solution)/shard_map/ppermute | solution.py:289
  10.2 6.2 %collective-permute-start.7 = (bf16[7,8,512]{2,1,0:T(8,128)(2,1)S(1)}, bf16[7,8,512]{2,1,0:T(8,128)(2,1)S(1)}, u32[]{:S(2)}, u32[]{:S(2)}) collective-permute-start(bf16[7,8,512]{2,1,0:T(8,128)(2,1)S(1)} %get-tuple-element.24), channel_id=1, source_target_pairs={{0,2},{1,3},{2,4},{3,5},{4,6},{5,7},{6,0},{7,1},{8,10},{9,11},{10,... | collective-permute-start | bytes 172040 | tf_op jit(solution)/shard_map/ppermute | solution.py:289
  11.4 5.0 %collective-permute-start.8 = (bf16[7,8,512]{2,1,0:T(8,128)(2,1)S(1)}, bf16[7,8,512]{2,1,0:T(8,128)(2,1)S(1)}, u32[]{:S(2)}, u32[]{:S(2)}) collective-permute-start(bf16[7,8,512]{2,1,0:T(8,128)(2,1)S(1)} %get-tuple-element.24), channel_id=1, source_target_pairs={{0,6},{1,7},{2,0},{3,1},{4,2},{5,3},{6,4},{7,5},{8,14},{9,15},{10,... | collective-permute-start | bytes 172040 | tf_op jit(solution)/shard_map/ppermute | solution.py:289
  13.8 13.5 %collective-permute-start.1 = (bf16[64,1792]{1,0:T(8,128)(2,1)S(1)}, bf16[64,1792]{1,0:T(8,128)(2,1)S(1)}, u32[]{:S(2)}, u32[]{:S(2)}) collective-permute-start(bf16[64,1792]{1,0:T(8,128)(2,1)S(1)} %get-tuple-element.25.refs_1_), channel_id=1, source_target_pairs={{0,6},{1,7},{2,0},{3,1},{4,2},{5,3},{6,4},{7,5},{8,14},{9,15},{10,... | collective-permute-start | bytes 688136 | tf_op jit(solution)/shard_map/ppermute | solution.py:45
  16.4 11.8 %collective-permute-start.2 = (bf16[64,1792]{1,0:T(8,128)(2,1)S(1)}, bf16[64,1792]{1,0:T(8,128)(2,1)S(1)}, u32[]{:S(2)}, u32[]{:S(2)}) collective-permute-start(bf16[64,1792]{1,0:T(8,128)(2,1)S(1)} %get-tuple-element.25.refs_1_), channel_id=1, source_target_pairs={{0,2},{1,3},{2,4},{3,5},{4,6},{5,7},{6,0},{7,1},{8,10},{9,11},{10,... | collective-permute-start | bytes 688136 | tf_op jit(solution)/shard_map/ppermute | solution.py:44
  16.4 11.7 %collective-permute-start.9 = (bf16[4,7,8,512]{3,2,1,0:T(8,128)(2,1)S(1)}, bf16[4,7,8,512]{3,2,1,0:T(8,128)(2,1)S(1)}, u32[]{:S(2)}, u32[]{:S(2)}) collective-permute-start(bf16[4,7,8,512]{3,2,1,0:T(8,128)(2,1)S(1)} %pad_maximum_fusion.1), channel_id=1, source_target_pairs={{0,96},{1,25},{2,98},{3,27},{4,100},{5,29},{6,102},{7,31},{8,104},... | collective-permute-start | bytes 688136 | tf_op jit(solution)/shard_map/ppermute | solution.py:293
  19.0 9.2 %collective-permute-start.10 = (bf16[4,7,8,512]{3,2,1,0:T(8,128)(2,1)S(1)}, bf16[4,7,8,512]{3,2,1,0:T(8,128)(2,1)S(1)}, u32[]{:S(2)}, u32[]{:S(2)}) collective-permute-start(bf16[4,7,8,512]{3,2,1,0:T(8,128)(2,1)S(1)} %pad_maximum_fusion.1), channel_id=1, source_target_pairs={{0,64},{1,17},{2,66},{3,19},{4,68},{5,21},{6,70},{7,23},{8,72},{9,... | collective-permute-start | bytes 688136 | tf_op jit(solution)/shard_map/ppermute | solution.py:293
  19.5 8.7 %collective-permute-start.11 = (bf16[4,7,8,512]{3,2,1,0:T(8,128)(2,1)S(1)}, bf16[4,7,8,512]{3,2,1,0:T(8,128)(2,1)S(1)}, u32[]{:S(2)}, u32[]{:S(2)}) collective-permute-start(bf16[4,7,8,512]{3,2,1,0:T(8,128)(2,1)S(1)} %pad_maximum_fusion.1), channel_id=1, source_target_pairs={{0,32},{1,9},{2,34},{3,11},{4,36},{5,13},{6,38},{7,15},{8,40},{9,1... | collective-permute-start | bytes 688136 | tf_op jit(solution)/shard_map/ppermute | solution.py:293
  28.3 14.1 %collective-permute-start.13 = (bf16[4,4,7,8,512]{4,3,2,1,0:T(8,128)(2,1)S(1)}, bf16[4,4,7,8,512]{4,3,2,1,0:T(8,128)(2,1)S(1)}, u32[]{:S(2)}, u32[]{:S(2)}) collective-permute-start(bf16[4,4,7,8,512]{4,3,2,1,0:T(8,128)(2,1)S(1)} %pad_maximum_fusion.refs_1_), channel_id=1, source_target_pairs={{0,8},{1,33},{2,10},{3,35},{4,12},{5,37},{6,14},{7,39},{8,16},{9,4... | collective-permute-start | bytes 2752520 | tf_op jit(solution)/shard_map/ppermute | solution.py:44
  29.6 12.8 %collective-permute-start.12 = (bf16[4,4,7,8,512]{4,3,2,1,0:T(8,128)(2,1)S(1)}, bf16[4,4,7,8,512]{4,3,2,1,0:T(8,128)(2,1)S(1)}, u32[]{:S(2)}, u32[]{:S(2)}) collective-permute-start(bf16[4,4,7,8,512]{4,3,2,1,0:T(8,128)(2,1)S(1)} %pad_maximum_fusion.refs_1_), channel_id=1, source_target_pairs={{0,24},{1,97},{2,26},{3,99},{4,28},{5,101},{6,30},{7,103},{8,0},{9... | collective-permute-start | bytes 2752520 | tf_op jit(solution)/shard_map/ppermute | solution.py:45
  31.1 5.8 %collective-permute-start.3 = (bf16[32,1792]{1,0:T(8,128)(2,1)S(1)}, bf16[32,1792]{1,0:T(8,128)(2,1)S(1)}, u32[]{:S(2)}, u32[]{:S(2)}) collective-permute-start(bf16[32,1792]{1,0:T(8,128)(2,1)S(1)} %slice.16), channel_id=1, source_target_pairs={{0,2},{1,3},{2,4},{3,5},{4,6},{5,7},{6,0},{7,1},{8,10},{9,11},{10,... | collective-permute-start | bytes 344072 | tf_op jit(solution)/shard_map/ppermute | solution.py:46
  32.6 6.5 %collective-permute-start.4 = (bf16[32,1792]{1,0:T(8,128)(2,1)S(1)}, bf16[32,1792]{1,0:T(8,128)(2,1)S(1)}, u32[]{:S(2)}, u32[]{:S(2)}) collective-permute-start(bf16[32,1792]{1,0:T(8,128)(2,1)S(1)} %slice.17), channel_id=1, source_target_pairs={{0,6},{1,7},{2,0},{3,1},{4,2},{5,3},{6,4},{7,5},{8,14},{9,15},{10,... | collective-permute-start | bytes 344072 | tf_op jit(solution)/shard_map/ppermute | solution.py:47
  42.4 18.7 %all-to-all-start = ((bf16[32,32,256]{2,1,0:T(8,128)(2,1)}), bf16[32,32,256]{2,1,0:T(8,128)(2,1)S(1)}, u32[]{:S(2)}, u32[]{:S(2)}) async-start(bf16[32,32,256]{2,1,0:T(8,128)(2,1)} %bitcast.36), calls=%async_computation | async-start | bytes 1048576 | tf_op jit(solution)/shard_map/all_to_all | solution.py:305
  52.0 14.2 %collective-permute-start.15 = (bf16[2,4,7,8,512]{4,3,2,1,0:T(8,128)(2,1)}, bf16[2,4,7,8,512]{4,3,2,1,0:T(8,128)(2,1)}, u32[]{:S(2)}, u32[]{:S(2)}) collective-permute-start(bf16[2,4,7,8,512]{4,3,2,1,0:T(8,128)(2,1)} %slice.18), channel_id=1, source_target_pairs={{0,8},{1,33},{2,10},{3,35},{4,12},{5,37},{6,14},{7,39},{8,16},{9,4... | collective-permute-start | bytes 1376264 | tf_op jit(solution)/shard_map/ppermute | solution.py:46
  54.1 12.2 %collective-permute-start.16 = (bf16[2,4,7,8,512]{4,3,2,1,0:T(8,128)(2,1)}, bf16[2,4,7,8,512]{4,3,2,1,0:T(8,128)(2,1)}, u32[]{:S(2)}, u32[]{:S(2)}) collective-permute-start(bf16[2,4,7,8,512]{4,3,2,1,0:T(8,128)(2,1)} %slice.19), channel_id=1, source_target_pairs={{0,24},{1,97},{2,26},{3,99},{4,28},{5,101},{6,30},{7,103},{8,0},{9... | collective-permute-start | bytes 1376264 | tf_op jit(solution)/shard_map/ppermute | solution.py:47
  56.9 12.2 %collective-permute-start.6 = (bf16[256,1024]{1,0:T(8,128)(2,1)}, bf16[256,1024]{1,0:T(8,128)(2,1)}, u32[]{:S(2)}, u32[]{:S(2)}) collective-permute-start(bf16[256,1024]{1,0:T(8,128)(2,1)} %shard_map.106.refs_3_), channel_id=1, source_target_pairs={{0,1},{1,0},{2,3},{3,2},{4,5},{5,4},{6,7},{7,6},{8,9},{9,8},{10,11... | collective-permute-start | bytes 1572872 | tf_op jit(solution)/shard_map/ppermute | solution.py:39
  61.1 8.0 %collective-permute-start.14 = (bf16[1024,256]{1,0:T(8,128)(2,1)S(1)}, bf16[1024,256]{1,0:T(8,128)(2,1)S(1)}, u32[]{:S(2)}, u32[]{:S(2)}) collective-permute-start(bf16[1024,256]{1,0:T(8,128)(2,1)S(1)} %bitcast.23), channel_id=1, source_target_pairs={{0,1},{1,0},{2,3},{3,2},{4,5},{5,4},{6,7},{7,6},{8,9},{9,8},{10,11... | collective-permute-start | bytes 1572872 | tf_op jit(solution)/shard_map/ppermute | solution.py:39
  65.1 4.1 %collective-permute-start.5 = (bf16[256,768]{1,0:T(8,128)(2,1)}, bf16[256,768]{1,0:T(8,128)(2,1)S(1)}, u32[]{:S(2)}, u32[]{:S(2)}) collective-permute-start(bf16[256,768]{1,0:T(8,128)(2,1)} %copy-done.12), channel_id=1, source_target_pairs={{0,1},{1,0},{2,3},{3,2},{4,5},{5,4},{6,7},{7,6},{8,9},{9,8},{10,11... | collective-permute-start | bytes 1179656 | tf_op jit(solution)/shard_map/ppermute | solution.py:39
  67.9 8.2 %collective-permute-start.18 = (bf16[2,512,256]{2,1,0:T(8,128)(2,1)S(1)}, bf16[2,512,256]{2,1,0:T(8,128)(2,1)S(1)}, u32[]{:S(2)}, u32[]{:S(2)}) collective-permute-start(bf16[2,512,256]{2,1,0:T(8,128)(2,1)S(1)} %get-tuple-element.32.refs_3_), channel_id=1, source_target_pairs={{0,1},{1,0},{2,3},{3,2},{4,5},{5,4},{6,7},{7,6},{8,9},{9,8},{10,11... | collective-permute-start | bytes 1572872 | tf_op jit(solution)/shard_map/ppermute | solution.py:39
  69.0 7.1 %collective-permute-start.19 = (bf16[2,256,512]{2,1,0:T(8,128)(2,1)S(1)}, bf16[2,256,512]{2,1,0:T(8,128)(2,1)S(1)}, u32[]{:S(2)}, u32[]{:S(2)}) collective-permute-start(bf16[2,256,512]{2,1,0:T(8,128)(2,1)S(1)} %get-tuple-element.33.refs_5_), channel_id=1, source_target_pairs={{0,1},{1,0},{2,3},{3,2},{4,5},{5,4},{6,7},{7,6},{8,9},{9,8},{10,11... | collective-permute-start | bytes 1572872 | tf_op jit(solution)/shard_map/ppermute | solution.py:39
  83.0 18.0 %all-to-all-start.1 = ((bf16[32,32,256]{2,1,0:T(8,128)(2,1)}), bf16[32,32,256]{2,1,0:T(8,128)(2,1)S(1)}, u32[]{:S(2)}, u32[]{:S(2)}) async-start(bf16[32,32,256]{2,1,0:T(8,128)(2,1)} %bitcast.37), calls=%async_computation.1 | async-start | bytes 1048576 | tf_op jit(solution)/shard_map/all_to_all | solution.py:305
  90.6 13.9 %collective-permute-start.22 = (bf16[2,256,512]{2,1,0:T(8,128)(2,1)}, bf16[2,256,512]{2,1,0:T(8,128)(2,1)}, u32[]{:S(2)}, u32[]{:S(2)}) collective-permute-start(bf16[2,256,512]{2,1,0:T(8,128)(2,1)} %get-tuple-element.41.refs_1_.refs_5_), channel_id=1, source_target_pairs={{0,1},{1,0},{2,3},{3,2},{4,5},{5,4},{6,7},{7,6},{8,9},{9,8},{10,11... | collective-permute-start | bytes 1572872 | tf_op jit(solution)/shard_map/ppermute | solution.py:39
  91.2 15.0 %collective-permute-start.21 = (bf16[2,512,256]{2,1,0:T(8,128)(2,1)}, bf16[2,512,256]{2,1,0:T(8,128)(2,1)}, u32[]{:S(2)}, u32[]{:S(2)}) collective-permute-start(bf16[2,512,256]{2,1,0:T(8,128)(2,1)} %get-tuple-element.40.refs_3_), channel_id=1, source_target_pairs={{0,1},{1,0},{2,3},{3,2},{4,5},{5,4},{6,7},{7,6},{8,9},{9,8},{10,11... | collective-permute-start | bytes 1572872 | tf_op jit(solution)/shard_map/ppermute | solution.py:39
  102.4 3.9 %collective-permute-start.20 = (bf16[256,1024]{1,0:T(8,128)(2,1)S(1)}, bf16[256,1024]{1,0:T(8,128)(2,1)S(1)}, u32[]{:S(2)}, u32[]{:S(2)}) collective-permute-start(bf16[256,1024]{1,0:T(8,128)(2,1)S(1)} %shard_map.112.refs_1_), channel_id=1, source_target_pairs={{0,1},{1,0},{2,3},{3,2},{4,5},{5,4},{6,7},{7,6},{8,9},{9,8},{10,11... | collective-permute-start | bytes 1572872 | tf_op jit(solution)/shard_map/ppermute | solution.py:39
  (16 other events, 139.1 us)

commit v7 on v6

--- a/solution.py
+++ b/solution.py
@@ -145,8 +145,8 @@
         copy.wait()
 
 
-def unpack(layer, meta, own, nxt, far_a, far_b, prev, mats, nodes, turned, outs):
-    where = [mats.at[0], mats.at[1], mats.at[2], outs.at[0], nodes.at[0], nodes.at[1], outs.at[1]]
+def place_rows(layer, meta, parts, where):
+    own, nxt, far_a, far_b, prev = parts
     for s in range(4):
         for r in range(4):
             a = (meta[1] + r) & 3
@@ -155,9 +155,24 @@
 
             @pl.when((a >> 1) == layer)
             def _():
-                for m in range(7):
-                    where[m][pl.ds(at, 32), :] = ref[row, :, m].astype(F32).reshape(32, LATENT).astype(BF)
-
+                for m, out in where:
+                    out[pl.ds(at, 32), :] = ref[row, :, m].astype(F32).reshape(32, LATENT).astype(BF)
+
+
+def unpack(layer, meta, own, nxt, far_a, far_b, prev, mats, nodes, turned, outs):
+    tail = [(3, outs.at[0]), (4, nodes.at[0]), (5, nodes.at[1]), (6, outs.at[1])]
+    place_rows(layer, meta, (own, nxt, far_a, far_b, prev), [(i, mats.at[i]) for i in range(3)] + tail)
+    turned[0] = outs[0].astype(F32).T.astype(BF)
+    turned[1] = outs[1].astype(F32).T.astype(BF)
+
+
+def unpack_edges(layer, meta, own, nxt, far_a, far_b, prev, mats):
+    place_rows(layer, meta, (own, nxt, far_a, far_b, prev), [(i, mats.at[i]) for i in range(3)])
+
+
+def unpack_tail(layer, meta, own, nxt, far_a, far_b, prev, nodes, turned, outs):
+    tail = [(3, outs.at[0]), (4, nodes.at[0]), (5, nodes.at[1]), (6, outs.at[1])]
+    place_rows(layer, meta, (own, nxt, far_a, far_b, prev), tail)
     turned[0] = outs[0].astype(F32).T.astype(BF)
     turned[1] = outs[1].astype(F32).T.astype(BF)
 
@@ -215,9 +230,11 @@
 
 def tail_first(
     meta, hid, hid_other, turned, turned_other, nodes, nodes_other, e_all, v_all, dst, mats_next, send,
-    e_new, v_new, rows, sender, held, sem,
+    e_out, v_out, rows, e_new, v_new, sender, held, sem,
 ):
     new_edges(hid, hid_other, turned, turned_other, e_all, e_new)
+    copies = [pltpu.make_async_copy(e_new, e_out, sem.at[4])]
+    copies[0].start()
 
     def body(sl, first):
         local = lambda i: dot((nodes, nodes_other)[i][0], v_all[:, sl])
@@ -225,24 +242,33 @@
         v_new[:, sl] = norm_add(msg, v_all[:, sl])
 
     chunks(v_new.shape[1], body)
+    copies.append(pltpu.make_async_copy(v_new, v_out, sem.at[5]))
+    copies[1].start()
     sender[...] = dot(mats_next[1], v_new[...]).astype(BF)
     select_rows(send, sender[...], rows, held, sem)
+    for copy in copies:
+        copy.wait()
 
 
 def tail_last(
     meta, hid, hid_other, turned, turned_other, nodes, nodes_other, e_all, v_all, dst, local,
-    e_out, v_out, e_new, sums,
+    e_out, v_out, e_new, sums, held, sem,
 ):
     new_edges(hid, hid_other, turned, turned_other, e_all, e_new)
     mine = pl.ds(pl.multiple_of(meta[4] * 64, 64), 64)
-    e_out[...] = e_new[mine, :]
+    copies = [pltpu.make_async_copy(e_new.at[mine, :], e_out, sem.at[0])]
+    copies[0].start()
 
     def body(sl, first):
         msg = node_message(first, sl, turned, turned_other, nodes, nodes_other, e_new, dst, lambda i: local[i, :, sl])
         sums[...] = msg
-        v_out[:, sl] = norm_add(msg, v_all[mine, sl], sums[mine, :])
+        held[:, sl] = norm_add(msg, v_all[mine, sl], sums[mine, :])
+        copies.append(pltpu.make_async_copy(held.at[:, sl], v_out.at[:, sl], sem.at[len(copies)]))
+        copies[-1].start()
 
     chunks(v_out.shape[1], body)
+    for copy in copies:
+        copy.wait()
 
 
 def edge_local(meta, v_all, e_all, mats, src, dst, part, sender, receiver):
@@ -310,15 +336,18 @@
     e_other = swap(e_half)
     halo_other = swap(halo)
 
-    mats, tails = [], []
-    for layer in range(2):
-        w, nodes, turned = call(
-            functools.partial(unpack, layer),
-            [((3, HALF, LATENT), BF), ((2, HALF, LATENT), BF), ((2, LATENT, HALF), BF)],
-            meta, *w_parts, scratch=[pltpu.VMEM((2, HALF, LATENT), BF)], flops=8 * HALF * n * m * (1 - layer),
-        )
-        mats.append(w)
-        tails.append((turned, swap(turned), nodes, swap(nodes)))
+    turning = [pltpu.VMEM((2, HALF, LATENT), BF)]
+    for_nodes = [((2, HALF, LATENT), BF), ((2, LATENT, HALF), BF)]
+    for_edges = [((3, HALF, LATENT), BF)]
+    w, nodes, turned = call(
+        functools.partial(unpack, 0), for_edges + for_nodes, meta, *w_parts, scratch=turning, flops=8 * HALF * n * m
+    )
+    tails = [(turned, swap(turned), nodes, swap(nodes))]
+    mats = [w, call(functools.partial(unpack_edges, 1), for_edges, meta, *w_parts)[0]]
+    nodes, turned = call(
+        functools.partial(unpack_tail, 1), for_nodes, meta, *w_parts, scratch=turning, flops=4 * HALF * n * m
+    )
+    tails.append((turned, swap(turned), nodes, swap(nodes)))
 
     big = lambda r, q: 2 * r * q * LATENT
     v_all, e_all, hid = call(
@@ -330,9 +359,13 @@
     )
     e_new, v_new, rows = call(
         tail_first,
-        [((LATENT, m), BF), ((LATENT, n), BF), pltpu.HBM((m, HALF), BF)],
+        [pltpu.HBM((LATENT, m), BF), pltpu.HBM((LATENT, n), BF), pltpu.HBM((m, HALF), BF)],
         meta, hid, swap(hid), *tails[0], e_all, v_all, dst, mats[1], send,
-        scratch=[pltpu.VMEM((HALF, n), BF), pltpu.VMEM((m, HALF), BF), pltpu.SemaphoreType.DMA((4,))], flops=6 * big(LATENT, m),
+        scratch=[
+            pltpu.VMEM((LATENT, m), BF), pltpu.VMEM((LATENT, n), BF), pltpu.VMEM((HALF, n), BF),
+            pltpu.VMEM((m, HALF), BF), pltpu.SemaphoreType.DMA((6,)),
+        ],
+        flops=6 * big(LATENT, m),
     )
     far = exchange(rows)
     (part,) = call(
@@ -346,9 +379,9 @@
     )
     e_out, v_out = call(
         tail_last,
-        [((64, m), BF), ((64, n), BF)],
+        [pltpu.HBM((64, m), BF), pltpu.HBM((64, n), BF)],
         meta, hid, swap(hid), *tails[1], e_new, v_new, dst, local,
-        scratch=[pltpu.VMEM((LATENT, m), BF), pltpu.VMEM((LATENT, n // 2), F32)], flops=5 * big(LATENT, m),
+        scratch=[pltpu.VMEM((LATENT, m), BF), pltpu.VMEM((LATENT, n // 2), F32), pltpu.VMEM((64, n), BF), pltpu.SemaphoreType.DMA((3,))], flops=5 * big(LATENT, m),
     )
     return v_out, e_out
 

time: 113 us -> 114 us (level)
  waiting for transfers between devices: 20.9 us -> 18.8 us
  Pallas kernels: 31.5 us -> 33.5 us
  local copies, waits for them, and re-layouts: 2.93 us -> 4.15 us
    all_to_all x2, waiting for transfers between devices: 6.25 us -> 3.9 us  [exchange(): lax.all_to_all(rows.reshape(32, SLOTS, HALF), 'dom', 0, 0, tiled=True)]
    pallas_call x11 -> x12, Pallas kernels: 31.5 us -> 33.5 us  [call(): pl.pallas_call(body, out_shape=[o if isinstance(o, pl.MemoryRef) else jax...]
    unnamed x30 -> x48, local copies, waits for them, and re-layouts: 1.19 us -> 2.43 us
  transfers between devices with their start and end apart: 25 -> 25, of which waited for: 7 -> 8; matrix products, arithmetic and copies ran while one was open for 1% -> 1% of each run, Pallas kernels for 15% -> 16%
where the time goes in v7:
time: 114 us
  starting transfers between devices  55.7 us (49%)
  Pallas kernels  33.5 us (29%)
  waiting for transfers between devices  18.8 us (16%)
  local copies, waits for them, and re-layouts  4.15 us (4%)
  between operations  1.2 us (1%)
    pallas_call x12, Pallas kernels, call(): pl.pallas_call(body, out_shape=[o if isinstance(o, pl.MemoryRef) else jax...  33.5 us
    all_to_all x2, starting transfers between devices, exchange(): lax.all_to_all(rows.reshape(32, SLOTS, HALF), 'dom', 0, 0, tiled=True)  16.7 us
    ppermute x9, starting transfers between devices, swap(): return lax.ppermute(x, 'ch', CORE)  12.1 us
    ppermute x3, starting transfers between devices, shards(): lax.ppermute(piece, 'ch', z_shift(s))  11.4 us
    ppermute x2, waiting for transfers between devices, ring_gather(): nxt = lax.ppermute(x, axis, perm(3))  7.2 us
    ppermute x2, starting transfers between devices, ring_gather(): nxt = lax.ppermute(x, axis, perm(3))  4.1 us
    all_to_all x2, waiting for transfers between devices, exchange(): lax.all_to_all(rows.reshape(32, SLOTS, HALF), 'dom', 0, 0, tiled=True)  3.9 us
    ppermute x2, starting transfers between devices, ring_gather(): far_b = lax.ppermute(nxt[half:], axis, perm(3))  3.82 us
  transfers between devices with their start and end apart: 25, of which 8 were waited for; matrix products, arithmetic and copies ran while one was open for 1% of the time, Pallas kernels for 16%

profile of v7, /device:TPU:1, one launch (start us, length us, event | category | flops | bytes accessed | tf_op | source)
XLA Modules:
  0.0 113.5 jit_solution(2813700690728982958)
XLA Ops:
  0.7 1.6 %shard_map.104 = (bf16[7,8,512]{2,1,0:T(8,128)(2,1)S(1)}, bf16[64,1792]{1,0:T(8,128)(2,1)S(1)}) custom-call(s32[5]{0:T(128)S(1)} %stack.53.refs_0_, bf16[2,3,64,512]{3,2,1,0:T(8,128)(2,1)} %bitcast.35, bf16[2,64,512]{2,1,0:T(8,128)(2,1)} %refs_2_.1, bf16[2,2,64,512]{3,2,1,0:T(8,128)(2,1)} %bitcast.36, bf16[2,64,512]{2,1,0:T(8,128)(2,1)} %refs_4_.1, ...), custom_call_target="tpu_custom_call" | custom-call | bytes 1146900 | tf_op jit(solution)/shard_map/pallas_call | solution.py:85
  2.4 7.8 %collective-permute-start = (bf16[7,8,512]{2,1,0:T(8,128)(2,1)S(1)}, bf16[7,8,512]{2,1,0:T(8,128)(2,1)S(1)}, u32[]{:S(2)}, u32[]{:S(2)}) collective-permute-start(bf16[7,8,512]{2,1,0:T(8,128)(2,1)S(1)} %get-tuple-element.23), channel_id=1, source_target_pairs={{0,4},{1,5},{2,6},{3,7},{4,0},{5,1},{6,2},{7,3},{8,12},{9,13},{10,... | collective-permute-start | bytes 172040 | tf_op jit(solution)/shard_map/ppermute | solution.py:315
  11.4 2.4 %collective-permute-start.8 = (bf16[7,8,512]{2,1,0:T(8,128)(2,1)S(1)}, bf16[7,8,512]{2,1,0:T(8,128)(2,1)S(1)}, u32[]{:S(2)}, u32[]{:S(2)}) collective-permute-start(bf16[7,8,512]{2,1,0:T(8,128)(2,1)S(1)} %get-tuple-element.23), channel_id=1, source_target_pairs={{0,6},{1,7},{2,0},{3,1},{4,2},{5,3},{6,4},{7,5},{8,14},{9,15},{10,... | collective-permute-start | bytes 172040 | tf_op jit(solution)/shard_map/ppermute | solution.py:315
  13.8 2.6 %collective-permute-start.1 = (bf16[64,1792]{1,0:T(8,128)(2,1)S(1)}, bf16[64,1792]{1,0:T(8,128)(2,1)S(1)}, u32[]{:S(2)}, u32[]{:S(2)}) collective-permute-start(bf16[64,1792]{1,0:T(8,128)(2,1)S(1)} %get-tuple-element.24.refs_1_), channel_id=1, source_target_pairs={{0,6},{1,7},{2,0},{3,1},{4,2},{5,3},{6,4},{7,5},{8,14},{9,15},{10,... | collective-permute-start | bytes 688136 | tf_op jit(solution)/shard_map/ppermute | solution.py:45
  16.4 2.6 %collective-permute-start.9 = (bf16[4,7,8,512]{3,2,1,0:T(8,128)(2,1)S(1)}, bf16[4,7,8,512]{3,2,1,0:T(8,128)(2,1)S(1)}, u32[]{:S(2)}, u32[]{:S(2)}) collective-permute-start(bf16[4,7,8,512]{3,2,1,0:T(8,128)(2,1)S(1)} %pad_maximum_fusion.1), channel_id=1, source_target_pairs={{0,96},{1,25},{2,98},{3,27},{4,100},{5,29},{6,102},{7,31},{8,104},... | collective-permute-start | bytes 688136 | tf_op jit(solution)/shard_map/ppermute | solution.py:319
  20.1 7.2 %collective-permute-done.1.refs_2_ = bf16[64,1792]{1,0:T(8,128)(2,1)S(1)} collective-permute-done((bf16[64,1792]{1,0:T(8,128)(2,1)S(1)}, bf16[64,1792]{1,0:T(8,128)(2,1)S(1)}, u32[]{:S(2)}, u32[]{:S(2)}) %collective-permute-start.1) | collective-permute-done | bytes 229408 | tf_op jit(solution)/shard_map/ppermute | solution.py:45
  32.6 2.3 %collective-permute-start.4 = (bf16[32,1792]{1,0:T(8,128)(2,1)S(1)}, bf16[32,1792]{1,0:T(8,128)(2,1)S(1)}, u32[]{:S(2)}, u32[]{:S(2)}) collective-permute-start(bf16[32,1792]{1,0:T(8,128)(2,1)S(1)} %slice.17), channel_id=1, source_target_pairs={{0,6},{1,7},{2,0},{3,1},{4,2},{5,3},{6,4},{7,5},{8,14},{9,15},{10,... | collective-permute-start | bytes 344072 | tf_op jit(solution)/shard_map/ppermute | solution.py:47
  34.9 2.1 %collective-permute-done.3.refs_3_ = bf16[32,1792]{1,0:T(8,128)(2,1)S(1)} collective-permute-done((bf16[32,1792]{1,0:T(8,128)(2,1)S(1)}, bf16[32,1792]{1,0:T(8,128)(2,1)S(1)}, u32[]{:S(2)}, u32[]{:S(2)}) %collective-permute-start.3) | collective-permute-done | bytes 114720 | tf_op jit(solution)/shard_map/ppermute | solution.py:46
  37.0 2.1 %collective-permute-done.4.refs_4_ = bf16[32,1792]{1,0:T(8,128)(2,1)S(1)} collective-permute-done((bf16[32,1792]{1,0:T(8,128)(2,1)S(1)}, bf16[32,1792]{1,0:T(8,128)(2,1)S(1)}, u32[]{:S(2)}, u32[]{:S(2)}) %collective-permute-start.4) | collective-permute-done | bytes 114720 | tf_op jit(solution)/shard_map/ppermute | solution.py:47
  39.1 1.9 %shard_map.105 = (bf16[256,768]{1,0:T(8,128)(2,1)S(1)}, bf16[1024,256]{1,0:T(8,128)(2,1)}) custom-call(s32[5]{0:T(128)S(1)} %copy-done.14, bf16[64,1792]{1,0:T(8,128)(2,1)S(1)} %get-tuple-element.24.refs_1_, bf16[64,1792]{1,0:T(8,128)(2,1)S(1)} %collective-permute-done.1.refs_2_, bf16[32,1792]{1,0:T(8,128)(2,1)S(1)} %collective-permute-done.3.refs_3_, ...), custom_call_target="tpu_custom_call" | custom-call | flops 402653184 | bytes 921620 | tf_op jit(solution)/shard_map/pallas_call | solution.py:85
  42.4 8.9 %all-to-all-start = ((bf16[32,32,256]{2,1,0:T(8,128)(2,1)}), bf16[32,32,256]{2,1,0:T(8,128)(2,1)}, u32[]{:S(2)}, u32[]{:S(2)}) async-start(bf16[32,32,256]{2,1,0:T(8,128)(2,1)} %bitcast.34), calls=%async_computation | async-start | bytes 1048576 | tf_op jit(solution)/shard_map/all_to_all | solution.py:331
  57.7 4.3 %collective-permute-start.6 = (bf16[256,1024]{1,0:T(8,128)(2,1)}, bf16[256,1024]{1,0:T(8,128)(2,1)}, u32[]{:S(2)}, u32[]{:S(2)}) collective-permute-start(bf16[256,1024]{1,0:T(8,128)(2,1)} %shard_map.106.refs_3_), channel_id=1, source_target_pairs={{0,1},{1,0},{2,3},{3,2},{4,5},{5,4},{6,7},{7,6},{8,9},{9,8},{10,11... | collective-permute-start | bytes 1572872 | tf_op jit(solution)/shard_map/ppermute | solution.py:39
  62.0 3.3 %collective-permute-start.14 = (bf16[1024,256]{1,0:T(8,128)(2,1)}, bf16[1024,256]{1,0:T(8,128)(2,1)S(1)}, u32[]{:S(2)}, u32[]{:S(2)}) collective-permute-start(bf16[1024,256]{1,0:T(8,128)(2,1)} %bitcast.17.refs_5_), channel_id=1, source_target_pairs={{0,1},{1,0},{2,3},{3,2},{4,5},{5,4},{6,7},{7,6},{8,9},{9,8},{10,11... | collective-permute-start | bytes 1572872 | tf_op jit(solution)/shard_map/ppermute | solution.py:39
  67.0 1.5 %shard_map.107 = (bf16[3,256,512]{2,1,0:T(8,128)(2,1)S(1)}, bf16[2,256,512]{2,1,0:T(8,128)(2,1)S(1)}, bf16[2,512,256]{2,1,0:T(8,128)(2,1)S(1)}) custom-call(s32[5]{0:T(128)S(1)} %copy-done.16, bf16[4,4,7,8,512]{4,3,2,1,0:T(8,128)(2,1)S(1)} %pad_maximum_fusion.refs_1_, bf16[4,4,7,8,512]{4,3,2,1,0:T(8,128)(2,1)S(1)} %collective-permute-done.12.refs_2_, ...), custom_call_target="tpu_custom_call" | custom-call | flops 1610612736 | bytes 3670036 | tf_op jit(solution)/shard_map/pallas_call | solution.py:85
  69.7 4.2 %shard_map.108 = (bf16[512,768]{1,0:T(8,128)(2,1)S(1)}, bf16[512,1024]{1,0:T(8,128)(2,1)S(1)}, bf16[256,1024]{1,0:T(8,128)(2,1)S(1)}) custom-call(s32[5]{0:T(128)S(1)} %copy-done.17, bf16[256,768]{1,0:T(8,128)(2,1)S(1)} %copy-done.21, bf16[256,768]{1,0:T(8,128)(2,1)S(1)} %collective-permute-done.5.refs_2_, bf16[256,1024]{1,0:T(8,128)(2,1)} %shard_map.106.refs_3_, ...), custom_call_target="tpu_custom_call" | custom-call | flops 1879048192 | bytes 3678228 | tf_op jit(solution)/shard_map/pallas_call | solution.py:85
  76.0 7.3 %shard_map.110 = (bf16[512,1024]{1,0:T(8,128)(2,1)}, bf16[512,768]{1,0:T(8,128)(2,1)}, bf16[1024,256]{1,0:T(8,128)(2,1)}) custom-call(s32[5]{0:T(128)S(1)} %copy-done.17, bf16[256,1024]{1,0:T(8,128)(2,1)S(1)} %get-tuple-element.30.refs_1_, bf16[256,1024]{1,0:T(8,128)(2,1)S(1)} %collective-permute-done.17.refs_2_, ...), custom_call_target="tpu_custom_call" | custom-call | flops 3221225472 | bytes 5775380 | tf_op jit(solution)/shard_map/pallas_call | solution.py:85
  83.3 7.8 %all-to-all-start.1 = ((bf16[32,32,256]{2,1,0:T(8,128)(2,1)}), bf16[32,32,256]{2,1,0:T(8,128)(2,1)}, u32[]{:S(2)}, u32[]{:S(2)}) async-start(bf16[32,32,256]{2,1,0:T(8,128)(2,1)} %bitcast.33), calls=%async_computation.1 | async-start | bytes 1048576 | tf_op jit(solution)/shard_map/all_to_all | solution.py:331
  92.2 2.4 %shard_map.113 = (bf16[2,256,512]{2,1,0:T(8,128)(2,1)}, bf16[2,512,256]{2,1,0:T(8,128)(2,1)}) custom-call(s32[5]{0:T(128)S(1)} %copy-done.17, bf16[4,4,7,8,512]{4,3,2,1,0:T(8,128)(2,1)S(1)} %pad_maximum_fusion.refs_1_, bf16[4,4,7,8,512]{4,3,2,1,0:T(8,128)(2,1)S(1)} %collective-permute-done.12.refs_2_, bf16[2,4,7,8,512]{4,3,2,1,0:T(8,128)(2,1)S(1)} %copy-done.4, ...), custom_call_target="tpu_custom_call" | custom-call | flops 805306368 | bytes 3670036 | tf_op jit(solution)/shard_map/pallas_call | solution.py:85
  95.2 2.3 %shard_map.111.refs_1_ = f32[256,1024]{1,0:T(8,128)S(1)} custom-call(s32[5]{0:T(128)S(1)} %copy-done.17, bf16[512,768]{1,0:T(8,128)(2,1)S(1)} %copy-done, bf16[512,1024]{1,0:T(8,128)(2,1)S(1)} %copy-done.5, bf16[3,256,512]{2,1,0:T(8,128)(2,1)S(1)} %shard_map.109.refs_10_.refs_3_, s32[1,1024]{1,0:T(1,128)S(1)} %bitcast.24, s32[1,1024]{1,0:T(1,128)S(1)} %bitcast.28), custom_call_target="tpu_custom_call" | custom-call | flops 805306368 | bytes 2629652 | tf_op jit(solution)/shard_map/pallas_call | solution.py:85
  97.5 3.9 %all-to-all-done.1 = bf16[32,32,256]{2,1,0:T(8,128)(2,1)} async-done(((bf16[32,32,256]{2,1,0:T(8,128)(2,1)}), bf16[32,32,256]{2,1,0:T(8,128)(2,1)}, u32[]{:S(2)}, u32[]{:S(2)}) %all-to-all-start.1) | async-done | bytes 524320 | tf_op jit(solution)/shard_map/all_to_all | solution.py:331
  101.4 1.8 %shard_map.112.refs_1_ = bf16[256,1024]{1,0:T(8,128)(2,1)S(1)} custom-call(s32[5]{0:T(128)S(1)} %copy-done.17, f32[256,1024]{1,0:T(8,128)S(1)} %shard_map.111.refs_1_, bf16[1024,256]{1,0:T(8,128)(2,1)} %bitcast.21.refs_2_, s32[1,1024]{1,0:T(1,128)S(1)} %bitcast.25), custom_call_target="tpu_custom_call" | custom-call | flops 536870912 | bytes 1576980 | tf_op jit(solution)/shard_map/pallas_call | solution.py:85
  103.3 2.3 %collective-permute-start.20 = (bf16[256,1024]{1,0:T(8,128)(2,1)S(1)}, bf16[256,1024]{1,0:T(8,128)(2,1)S(1)}, u32[]{:S(2)}, u32[]{:S(2)}) collective-permute-start(bf16[256,1024]{1,0:T(8,128)(2,1)S(1)} %shard_map.112.refs_1_), channel_id=1, source_target_pairs={{0,1},{1,0},{2,3},{3,2},{4,5},{5,4},{6,7},{7,6},{8,9},{9,8},{10,11... | collective-permute-start | bytes 1572872 | tf_op jit(solution)/shard_map/ppermute | solution.py:39
  105.6 1.6 %shard_map.114.refs_10_ = f32[2,256,768]{2,1,0:T(8,128)S(1)} custom-call(s32[5]{0:T(128)S(1)} %copy-done.17, bf16[2,256,512]{2,1,0:T(8,128)(2,1)} %get-tuple-element.39.refs_1_.refs_5_, bf16[2,256,512]{2,1,0:T(8,128)(2,1)S(1)} %collective-permute-done.22.refs_2_.refs_6_, bf16[512,768]{1,0:T(8,128)(2,1)S(1)} %copy-done.1), custom_call_target="tpu_custom_call" | custom-call | flops 402653184 | bytes 1835028 | tf_op jit(solution)/shard_map/pallas_call | solution.py:85
  107.2 6.1 %shard_map.115 = (bf16[64,1024]{1,0:T(8,128)(2,1)}, bf16[64,768]{1,0:T(8,128)(2,1)}) custom-call(s32[5]{0:T(128)S(1)} %copy-done.17, bf16[256,1024]{1,0:T(8,128)(2,1)S(1)} %shard_map.112.refs_1_, bf16[256,1024]{1,0:T(8,128)(2,1)S(1)} %collective-permute-done.20.refs_2_, bf16[2,512,256]{2,1,0:T(8,128)(2,1)} %get-tuple-element.38.refs_3_, ...), custom_call_target="tpu_custom_call" | custom-call | flops 2684354560 | bytes 6557716 | tf_op jit(solution)/shard_map/pallas_call | solution.py:85
  (93 shorter events, 21.9 us)
Async XLA Ops:
  2.4 11.4 %collective-permute-start = (bf16[7,8,512]{2,1,0:T(8,128)(2,1)S(1)}, bf16[7,8,512]{2,1,0:T(8,128)(2,1)S(1)}, u32[]{:S(2)}, u32[]{:S(2)}) collective-permute-start(bf16[7,8,512]{2,1,0:T(8,128)(2,1)S(1)} %get-tuple-element.23), channel_id=1, source_target_pairs={{0,4},{1,5},{2,6},{3,7},{4,0},{5,1},{6,2},{7,3},{8,12},{9,13},{10,... | collective-permute-start | bytes 172040 | tf_op jit(solution)/shard_map/ppermute | solution.py:315
  10.2 6.2 %collective-permute-start.7 = (bf16[7,8,512]{2,1,0:T(8,128)(2,1)S(1)}, bf16[7,8,512]{2,1,0:T(8,128)(2,1)S(1)}, u32[]{:S(2)}, u32[]{:S(2)}) collective-permute-start(bf16[7,8,512]{2,1,0:T(8,128)(2,1)S(1)} %get-tuple-element.23), channel_id=1, source_target_pairs={{0,2},{1,3},{2,4},{3,5},{4,6},{5,7},{6,0},{7,1},{8,10},{9,11},{10,... | collective-permute-start | bytes 172040 | tf_op jit(solution)/shard_map/ppermute | solution.py:315
  11.4 5.0 %collective-permute-start.8 = (bf16[7,8,512]{2,1,0:T(8,128)(2,1)S(1)}, bf16[7,8,512]{2,1,0:T(8,128)(2,1)S(1)}, u32[]{:S(2)}, u32[]{:S(2)}) collective-permute-start(bf16[7,8,512]{2,1,0:T(8,128)(2,1)S(1)} %get-tuple-element.23), channel_id=1, source_target_pairs={{0,6},{1,7},{2,0},{3,1},{4,2},{5,3},{6,4},{7,5},{8,14},{9,15},{10,... | collective-permute-start | bytes 172040 | tf_op jit(solution)/shard_map/ppermute | solution.py:315
  13.8 13.5 %collective-permute-start.1 = (bf16[64,1792]{1,0:T(8,128)(2,1)S(1)}, bf16[64,1792]{1,0:T(8,128)(2,1)S(1)}, u32[]{:S(2)}, u32[]{:S(2)}) collective-permute-start(bf16[64,1792]{1,0:T(8,128)(2,1)S(1)} %get-tuple-element.24.refs_1_), channel_id=1, source_target_pairs={{0,6},{1,7},{2,0},{3,1},{4,2},{5,3},{6,4},{7,5},{8,14},{9,15},{10,... | collective-permute-start | bytes 688136 | tf_op jit(solution)/shard_map/ppermute | solution.py:45
  16.4 11.8 %collective-permute-start.2 = (bf16[64,1792]{1,0:T(8,128)(2,1)S(1)}, bf16[64,1792]{1,0:T(8,128)(2,1)S(1)}, u32[]{:S(2)}, u32[]{:S(2)}) collective-permute-start(bf16[64,1792]{1,0:T(8,128)(2,1)S(1)} %get-tuple-element.24.refs_1_), channel_id=1, source_target_pairs={{0,2},{1,3},{2,4},{3,5},{4,6},{5,7},{6,0},{7,1},{8,10},{9,11},{10,... | collective-permute-start | bytes 688136 | tf_op jit(solution)/shard_map/ppermute | solution.py:44
  16.4 11.7 %collective-permute-start.9 = (bf16[4,7,8,512]{3,2,1,0:T(8,128)(2,1)S(1)}, bf16[4,7,8,512]{3,2,1,0:T(8,128)(2,1)S(1)}, u32[]{:S(2)}, u32[]{:S(2)}) collective-permute-start(bf16[4,7,8,512]{3,2,1,0:T(8,128)(2,1)S(1)} %pad_maximum_fusion.1), channel_id=1, source_target_pairs={{0,96},{1,25},{2,98},{3,27},{4,100},{5,29},{6,102},{7,31},{8,104},... | collective-permute-start | bytes 688136 | tf_op jit(solution)/shard_map/ppermute | solution.py:319
  19.0 9.2 %collective-permute-start.10 = (bf16[4,7,8,512]{3,2,1,0:T(8,128)(2,1)S(1)}, bf16[4,7,8,512]{3,2,1,0:T(8,128)(2,1)S(1)}, u32[]{:S(2)}, u32[]{:S(2)}) collective-permute-start(bf16[4,7,8,512]{3,2,1,0:T(8,128)(2,1)S(1)} %pad_maximum_fusion.1), channel_id=1, source_target_pairs={{0,64},{1,17},{2,66},{3,19},{4,68},{5,21},{6,70},{7,23},{8,72},{9,... | collective-permute-start | bytes 688136 | tf_op jit(solution)/shard_map/ppermute | solution.py:319
  19.5 8.7 %collective-permute-start.11 = (bf16[4,7,8,512]{3,2,1,0:T(8,128)(2,1)S(1)}, bf16[4,7,8,512]{3,2,1,0:T(8,128)(2,1)S(1)}, u32[]{:S(2)}, u32[]{:S(2)}) collective-permute-start(bf16[4,7,8,512]{3,2,1,0:T(8,128)(2,1)S(1)} %pad_maximum_fusion.1), channel_id=1, source_target_pairs={{0,32},{1,9},{2,34},{3,11},{4,36},{5,13},{6,38},{7,15},{8,40},{9,1... | collective-permute-start | bytes 688136 | tf_op jit(solution)/shard_map/ppermute | solution.py:319
  28.3 14.1 %collective-permute-start.13 = (bf16[4,4,7,8,512]{4,3,2,1,0:T(8,128)(2,1)S(1)}, bf16[4,4,7,8,512]{4,3,2,1,0:T(8,128)(2,1)S(1)}, u32[]{:S(2)}, u32[]{:S(2)}) collective-permute-start(bf16[4,4,7,8,512]{4,3,2,1,0:T(8,128)(2,1)S(1)} %pad_maximum_fusion.refs_1_), channel_id=1, source_target_pairs={{0,8},{1,33},{2,10},{3,35},{4,12},{5,37},{6,14},{7,39},{8,16},{9,4... | collective-permute-start | bytes 2752520 | tf_op jit(solution)/shard_map/ppermute | solution.py:44
  29.6 12.8 %collective-permute-start.12 = (bf16[4,4,7,8,512]{4,3,2,1,0:T(8,128)(2,1)S(1)}, bf16[4,4,7,8,512]{4,3,2,1,0:T(8,128)(2,1)S(1)}, u32[]{:S(2)}, u32[]{:S(2)}) collective-permute-start(bf16[4,4,7,8,512]{4,3,2,1,0:T(8,128)(2,1)S(1)} %pad_maximum_fusion.refs_1_), channel_id=1, source_target_pairs={{0,24},{1,97},{2,26},{3,99},{4,28},{5,101},{6,30},{7,103},{8,0},{9... | collective-permute-start | bytes 2752520 | tf_op jit(solution)/shard_map/ppermute | solution.py:45
  31.1 5.8 %collective-permute-start.3 = (bf16[32,1792]{1,0:T(8,128)(2,1)S(1)}, bf16[32,1792]{1,0:T(8,128)(2,1)S(1)}, u32[]{:S(2)}, u32[]{:S(2)}) collective-permute-start(bf16[32,1792]{1,0:T(8,128)(2,1)S(1)} %slice.16), channel_id=1, source_target_pairs={{0,2},{1,3},{2,4},{3,5},{4,6},{5,7},{6,0},{7,1},{8,10},{9,11},{10,... | collective-permute-start | bytes 344072 | tf_op jit(solution)/shard_map/ppermute | solution.py:46
  32.6 6.5 %collective-permute-start.4 = (bf16[32,1792]{1,0:T(8,128)(2,1)S(1)}, bf16[32,1792]{1,0:T(8,128)(2,1)S(1)}, u32[]{:S(2)}, u32[]{:S(2)}) collective-permute-start(bf16[32,1792]{1,0:T(8,128)(2,1)S(1)} %slice.17), channel_id=1, source_target_pairs={{0,6},{1,7},{2,0},{3,1},{4,2},{5,3},{6,4},{7,5},{8,14},{9,15},{10,... | collective-permute-start | bytes 344072 | tf_op jit(solution)/shard_map/ppermute | solution.py:47
  42.4 19.6 %all-to-all-start = ((bf16[32,32,256]{2,1,0:T(8,128)(2,1)}), bf16[32,32,256]{2,1,0:T(8,128)(2,1)}, u32[]{:S(2)}, u32[]{:S(2)}) async-start(bf16[32,32,256]{2,1,0:T(8,128)(2,1)} %bitcast.34), calls=%async_computation | async-start | bytes 1048576 | tf_op jit(solution)/shard_map/all_to_all | solution.py:331
  52.1 14.1 %collective-permute-start.15 = (bf16[2,4,7,8,512]{4,3,2,1,0:T(8,128)(2,1)}, bf16[2,4,7,8,512]{4,3,2,1,0:T(8,128)(2,1)S(1)}, u32[]{:S(2)}, u32[]{:S(2)}) collective-permute-start(bf16[2,4,7,8,512]{4,3,2,1,0:T(8,128)(2,1)} %slice.18), channel_id=1, source_target_pairs={{0,8},{1,33},{2,10},{3,35},{4,12},{5,37},{6,14},{7,39},{8,16},{9,4... | collective-permute-start | bytes 1376264 | tf_op jit(solution)/shard_map/ppermute | solution.py:46
  54.1 12.2 %collective-permute-start.16 = (bf16[2,4,7,8,512]{4,3,2,1,0:T(8,128)(2,1)}, bf16[2,4,7,8,512]{4,3,2,1,0:T(8,128)(2,1)}, u32[]{:S(2)}, u32[]{:S(2)}) collective-permute-start(bf16[2,4,7,8,512]{4,3,2,1,0:T(8,128)(2,1)} %slice.19), channel_id=1, source_target_pairs={{0,24},{1,97},{2,26},{3,99},{4,28},{5,101},{6,30},{7,103},{8,0},{9... | collective-permute-start | bytes 1376264 | tf_op jit(solution)/shard_map/ppermute | solution.py:47
  57.7 11.9 %collective-permute-start.6 = (bf16[256,1024]{1,0:T(8,128)(2,1)}, bf16[256,1024]{1,0:T(8,128)(2,1)}, u32[]{:S(2)}, u32[]{:S(2)}) collective-permute-start(bf16[256,1024]{1,0:T(8,128)(2,1)} %shard_map.106.refs_3_), channel_id=1, source_target_pairs={{0,1},{1,0},{2,3},{3,2},{4,5},{5,4},{6,7},{7,6},{8,9},{9,8},{10,11... | collective-permute-start | bytes 1572872 | tf_op jit(solution)/shard_map/ppermute | solution.py:39
  62.0 7.7 %collective-permute-start.14 = (bf16[1024,256]{1,0:T(8,128)(2,1)}, bf16[1024,256]{1,0:T(8,128)(2,1)S(1)}, u32[]{:S(2)}, u32[]{:S(2)}) collective-permute-start(bf16[1024,256]{1,0:T(8,128)(2,1)} %bitcast.17.refs_5_), channel_id=1, source_target_pairs={{0,1},{1,0},{2,3},{3,2},{4,5},{5,4},{6,7},{7,6},{8,9},{9,8},{10,11... | collective-permute-start | bytes 1572872 | tf_op jit(solution)/shard_map/ppermute | solution.py:39
  65.2 4.4 %collective-permute-start.5 = (bf16[256,768]{1,0:T(8,128)(2,1)}, bf16[256,768]{1,0:T(8,128)(2,1)S(1)}, u32[]{:S(2)}, u32[]{:S(2)}) collective-permute-start(bf16[256,768]{1,0:T(8,128)(2,1)} %copy-done.20), channel_id=1, source_target_pairs={{0,1},{1,0},{2,3},{3,2},{4,5},{5,4},{6,7},{7,6},{8,9},{9,8},{10,11... | collective-permute-start | bytes 1179656 | tf_op jit(solution)/shard_map/ppermute | solution.py:39
  68.5 7.1 %collective-permute-start.18 = (bf16[2,512,256]{2,1,0:T(8,128)(2,1)S(1)}, bf16[2,512,256]{2,1,0:T(8,128)(2,1)S(1)}, u32[]{:S(2)}, u32[]{:S(2)}) collective-permute-start(bf16[2,512,256]{2,1,0:T(8,128)(2,1)S(1)} %get-tuple-element.31.refs_3_), channel_id=1, source_target_pairs={{0,1},{1,0},{2,3},{3,2},{4,5},{5,4},{6,7},{7,6},{8,9},{9,8},{10,11... | collective-permute-start | bytes 1572872 | tf_op jit(solution)/shard_map/ppermute | solution.py:39
  69.5 6.2 %collective-permute-start.19 = (bf16[2,256,512]{2,1,0:T(8,128)(2,1)S(1)}, bf16[2,256,512]{2,1,0:T(8,128)(2,1)S(1)}, u32[]{:S(2)}, u32[]{:S(2)}) collective-permute-start(bf16[2,256,512]{2,1,0:T(8,128)(2,1)S(1)} %get-tuple-element.32.refs_5_), channel_id=1, source_target_pairs={{0,1},{1,0},{2,3},{3,2},{4,5},{5,4},{6,7},{7,6},{8,9},{9,8},{10,11... | collective-permute-start | bytes 1572872 | tf_op jit(solution)/shard_map/ppermute | solution.py:39
  83.3 18.1 %all-to-all-start.1 = ((bf16[32,32,256]{2,1,0:T(8,128)(2,1)}), bf16[32,32,256]{2,1,0:T(8,128)(2,1)}, u32[]{:S(2)}, u32[]{:S(2)}) async-start(bf16[32,32,256]{2,1,0:T(8,128)(2,1)} %bitcast.33), calls=%async_computation.1 | async-start | bytes 1048576 | tf_op jit(solution)/shard_map/all_to_all | solution.py:331
  94.5 11.1 %collective-permute-start.22 = (bf16[2,256,512]{2,1,0:T(8,128)(2,1)}, bf16[2,256,512]{2,1,0:T(8,128)(2,1)S(1)}, u32[]{:S(2)}, u32[]{:S(2)}) collective-permute-start(bf16[2,256,512]{2,1,0:T(8,128)(2,1)} %get-tuple-element.39.refs_1_.refs_5_), channel_id=1, source_target_pairs={{0,1},{1,0},{2,3},{3,2},{4,5},{5,4},{6,7},{7,6},{8,9},{9,8},{10,11... | collective-permute-start | bytes 1572872 | tf_op jit(solution)/shard_map/ppermute | solution.py:39
  95.2 12.0 %collective-permute-start.21 = (bf16[2,512,256]{2,1,0:T(8,128)(2,1)}, bf16[2,512,256]{2,1,0:T(8,128)(2,1)}, u32[]{:S(2)}, u32[]{:S(2)}) collective-permute-start(bf16[2,512,256]{2,1,0:T(8,128)(2,1)} %get-tuple-element.38.refs_3_), channel_id=1, source_target_pairs={{0,1},{1,0},{2,3},{3,2},{4,5},{5,4},{6,7},{7,6},{8,9},{9,8},{10,11... | collective-permute-start | bytes 1572872 | tf_op jit(solution)/shard_map/ppermute | solution.py:39
  103.3 4.0 %collective-permute-start.20 = (bf16[256,1024]{1,0:T(8,128)(2,1)S(1)}, bf16[256,1024]{1,0:T(8,128)(2,1)S(1)}, u32[]{:S(2)}, u32[]{:S(2)}) collective-permute-start(bf16[256,1024]{1,0:T(8,128)(2,1)S(1)} %shard_map.112.refs_1_), channel_id=1, source_target_pairs={{0,1},{1,0},{2,3},{3,2},{4,5},{5,4},{6,7},{7,6},{8,9},{9,8},{10,11... | collective-permute-start | bytes 1572872 | tf_op jit(solution)/shard_map/ppermute | solution.py:39
  (25 other events, 188.3 us)

commit v8 on v6

--- a/solution.py
+++ b/solution.py
@@ -215,9 +215,11 @@
 
 def tail_first(
     meta, hid, hid_other, turned, turned_other, nodes, nodes_other, e_all, v_all, dst, mats_next, send,
-    e_new, v_new, rows, sender, held, sem,
+    e_out, v_out, rows, e_new, v_new, sender, held, sem,
 ):
     new_edges(hid, hid_other, turned, turned_other, e_all, e_new)
+    copies = [pltpu.make_async_copy(e_new, e_out, sem.at[4])]
+    copies[0].start()
 
     def body(sl, first):
         local = lambda i: dot((nodes, nodes_other)[i][0], v_all[:, sl])
@@ -225,24 +227,33 @@
         v_new[:, sl] = norm_add(msg, v_all[:, sl])
 
     chunks(v_new.shape[1], body)
+    copies.append(pltpu.make_async_copy(v_new, v_out, sem.at[5]))
+    copies[1].start()
     sender[...] = dot(mats_next[1], v_new[...]).astype(BF)
     select_rows(send, sender[...], rows, held, sem)
+    for copy in copies:
+        copy.wait()
 
 
 def tail_last(
     meta, hid, hid_other, turned, turned_other, nodes, nodes_other, e_all, v_all, dst, local,
-    e_out, v_out, e_new, sums,
+    e_out, v_out, e_new, sums, held, sem,
 ):
     new_edges(hid, hid_other, turned, turned_other, e_all, e_new)
     mine = pl.ds(pl.multiple_of(meta[4] * 64, 64), 64)
-    e_out[...] = e_new[mine, :]
+    copies = [pltpu.make_async_copy(e_new.at[mine, :], e_out, sem.at[0])]
+    copies[0].start()
 
     def body(sl, first):
         msg = node_message(first, sl, turned, turned_other, nodes, nodes_other, e_new, dst, lambda i: local[i, :, sl])
         sums[...] = msg
-        v_out[:, sl] = norm_add(msg, v_all[mine, sl], sums[mine, :])
+        held[:, sl] = norm_add(msg, v_all[mine, sl], sums[mine, :])
+        copies.append(pltpu.make_async_copy(held.at[:, sl], v_out.at[:, sl], sem.at[len(copies)]))
+        copies[-1].start()
 
     chunks(v_out.shape[1], body)
+    for copy in copies:
+        copy.wait()
 
 
 def edge_local(meta, v_all, e_all, mats, src, dst, part, sender, receiver):
@@ -330,9 +341,13 @@
     )
     e_new, v_new, rows = call(
         tail_first,
-        [((LATENT, m), BF), ((LATENT, n), BF), pltpu.HBM((m, HALF), BF)],
+        [pltpu.HBM((LATENT, m), BF), pltpu.HBM((LATENT, n), BF), pltpu.HBM((m, HALF), BF)],
         meta, hid, swap(hid), *tails[0], e_all, v_all, dst, mats[1], send,
-        scratch=[pltpu.VMEM((HALF, n), BF), pltpu.VMEM((m, HALF), BF), pltpu.SemaphoreType.DMA((4,))], flops=6 * big(LATENT, m),
+        scratch=[
+            pltpu.VMEM((LATENT, m), BF), pltpu.VMEM((LATENT, n), BF), pltpu.VMEM((HALF, n), BF),
+            pltpu.VMEM((m, HALF), BF), pltpu.SemaphoreType.DMA((6,)),
+        ],
+        flops=6 * big(LATENT, m),
     )
     far = exchange(rows)
     (part,) = call(
@@ -346,9 +361,9 @@
     )
     e_out, v_out = call(
         tail_last,
-        [((64, m), BF), ((64, n), BF)],
+        [pltpu.HBM((64, m), BF), pltpu.HBM((64, n), BF)],
         meta, hid, swap(hid), *tails[1], e_new, v_new, dst, local,
-        scratch=[pltpu.VMEM((LATENT, m), BF), pltpu.VMEM((LATENT, n // 2), F32)], flops=5 * big(LATENT, m),
+        scratch=[pltpu.VMEM((LATENT, m), BF), pltpu.VMEM((LATENT, n // 2), F32), pltpu.VMEM((64, n), BF), pltpu.SemaphoreType.DMA((3,))], flops=5 * big(LATENT, m),
     )
     return v_out, e_out
 

time: 113 us -> 114 us (level)
  no operation moved by 1% of the time
where the time goes in v8:
time: 114 us; the launch traced here: 113 us
  starting transfers between devices  56.2 us (49%)
  Pallas kernels  32.1 us (28%)
  waiting for transfers between devices  20.8 us (18%)
  local copies, waits for them, and re-layouts  3.03 us (3%)
    pallas_call x11, Pallas kernels, call(): pl.pallas_call(body, out_shape=[o if isinstance(o, pl.MemoryRef) else jax...  32.1 us
    all_to_all x2, starting transfers between devices, exchange(): lax.all_to_all(rows.reshape(32, SLOTS, HALF), 'dom', 0, 0, tiled=True)  16.4 us
    ppermute x9, starting transfers between devices, swap(): return lax.ppermute(x, 'ch', CORE)  12.8 us
    ppermute x3, starting transfers between devices, shards(): lax.ppermute(piece, 'ch', z_shift(s))  11.4 us
    ppermute x2, waiting for transfers between devices, ring_gather(): nxt = lax.ppermute(x, axis, perm(3))  7.2 us
    all_to_all x2, waiting for transfers between devices, exchange(): lax.all_to_all(rows.reshape(32, SLOTS, HALF), 'dom', 0, 0, tiled=True)  6.15 us
    ppermute x2, starting transfers between devices, ring_gather(): nxt = lax.ppermute(x, axis, perm(3))  4.1 us
    ppermute x2, starting transfers between devices, ring_gather(): far_b = lax.ppermute(nxt[half:], axis, perm(3))  3.74 us
  transfers between devices with their start and end apart: 25, of which 7 were waited for; matrix products, arithmetic and copies ran while one was open for 1% of the time, Pallas kernels for 15%

profile of v8, /device:TPU:1, one launch (start us, length us, event | category | flops | bytes accessed | tf_op | source)
XLA Modules:
  0.0 113.4 jit_solution(7450239170119517445)
XLA Ops:
  0.7 1.6 %shard_map.104 = (bf16[7,8,512]{2,1,0:T(8,128)(2,1)S(1)}, bf16[64,1792]{1,0:T(8,128)(2,1)S(1)}) custom-call(s32[5]{0:T(128)S(1)} %stack.53.refs_0_, bf16[2,3,64,512]{3,2,1,0:T(8,128)(2,1)} %bitcast.38, bf16[2,64,512]{2,1,0:T(8,128)(2,1)} %refs_2_.1, bf16[2,2,64,512]{3,2,1,0:T(8,128)(2,1)} %bitcast.39, bf16[2,64,512]{2,1,0:T(8,128)(2,1)} %refs_4_.1, ...), custom_call_target="tpu_custom_call" | custom-call | bytes 1146900 | tf_op jit(solution)/shard_map/pallas_call | solution.py:85
  2.4 7.8 %collective-permute-start = (bf16[7,8,512]{2,1,0:T(8,128)(2,1)S(1)}, bf16[7,8,512]{2,1,0:T(8,128)(2,1)S(1)}, u32[]{:S(2)}, u32[]{:S(2)}) collective-permute-start(bf16[7,8,512]{2,1,0:T(8,128)(2,1)S(1)} %get-tuple-element.24), channel_id=1, source_target_pairs={{0,4},{1,5},{2,6},{3,7},{4,0},{5,1},{6,2},{7,3},{8,12},{9,13},{10,... | collective-permute-start | bytes 172040 | tf_op jit(solution)/shard_map/ppermute | solution.py:300
  11.4 2.4 %collective-permute-start.8 = (bf16[7,8,512]{2,1,0:T(8,128)(2,1)S(1)}, bf16[7,8,512]{2,1,0:T(8,128)(2,1)S(1)}, u32[]{:S(2)}, u32[]{:S(2)}) collective-permute-start(bf16[7,8,512]{2,1,0:T(8,128)(2,1)S(1)} %get-tuple-element.24), channel_id=1, source_target_pairs={{0,6},{1,7},{2,0},{3,1},{4,2},{5,3},{6,4},{7,5},{8,14},{9,15},{10,... | collective-permute-start | bytes 172040 | tf_op jit(solution)/shard_map/ppermute | solution.py:300
  13.8 2.6 %collective-permute-start.1 = (bf16[64,1792]{1,0:T(8,128)(2,1)S(1)}, bf16[64,1792]{1,0:T(8,128)(2,1)S(1)}, u32[]{:S(2)}, u32[]{:S(2)}) collective-permute-start(bf16[64,1792]{1,0:T(8,128)(2,1)S(1)} %get-tuple-element.25.refs_1_), channel_id=1, source_target_pairs={{0,6},{1,7},{2,0},{3,1},{4,2},{5,3},{6,4},{7,5},{8,14},{9,15},{10,... | collective-permute-start | bytes 688136 | tf_op jit(solution)/shard_map/ppermute | solution.py:45
  16.4 2.6 %collective-permute-start.9 = (bf16[4,7,8,512]{3,2,1,0:T(8,128)(2,1)S(1)}, bf16[4,7,8,512]{3,2,1,0:T(8,128)(2,1)S(1)}, u32[]{:S(2)}, u32[]{:S(2)}) collective-permute-start(bf16[4,7,8,512]{3,2,1,0:T(8,128)(2,1)S(1)} %pad_maximum_fusion.1), channel_id=1, source_target_pairs={{0,96},{1,25},{2,98},{3,27},{4,100},{5,29},{6,102},{7,31},{8,104},... | collective-permute-start | bytes 688136 | tf_op jit(solution)/shard_map/ppermute | solution.py:304
  20.1 7.2 %collective-permute-done.1.refs_2_ = bf16[64,1792]{1,0:T(8,128)(2,1)S(1)} collective-permute-done((bf16[64,1792]{1,0:T(8,128)(2,1)S(1)}, bf16[64,1792]{1,0:T(8,128)(2,1)S(1)}, u32[]{:S(2)}, u32[]{:S(2)}) %collective-permute-start.1) | collective-permute-done | bytes 229408 | tf_op jit(solution)/shard_map/ppermute | solution.py:45
  29.6 1.5 %collective-permute-start.12 = (bf16[4,4,7,8,512]{4,3,2,1,0:T(8,128)(2,1)S(1)}, bf16[4,4,7,8,512]{4,3,2,1,0:T(8,128)(2,1)S(1)}, u32[]{:S(2)}, u32[]{:S(2)}) collective-permute-start(bf16[4,4,7,8,512]{4,3,2,1,0:T(8,128)(2,1)S(1)} %pad_maximum_fusion.refs_1_), channel_id=1, source_target_pairs={{0,24},{1,97},{2,26},{3,99},{4,28},{5,101},{6,30},{7,103},{8,0},{9... | collective-permute-start | bytes 2752520 | tf_op jit(solution)/shard_map/ppermute | solution.py:45
  32.6 2.3 %collective-permute-start.4 = (bf16[32,1792]{1,0:T(8,128)(2,1)S(1)}, bf16[32,1792]{1,0:T(8,128)(2,1)S(1)}, u32[]{:S(2)}, u32[]{:S(2)}) collective-permute-start(bf16[32,1792]{1,0:T(8,128)(2,1)S(1)} %slice.17), channel_id=1, source_target_pairs={{0,6},{1,7},{2,0},{3,1},{4,2},{5,3},{6,4},{7,5},{8,14},{9,15},{10,... | collective-permute-start | bytes 344072 | tf_op jit(solution)/shard_map/ppermute | solution.py:47
  34.9 2.1 %collective-permute-done.3.refs_3_ = bf16[32,1792]{1,0:T(8,128)(2,1)S(1)} collective-permute-done((bf16[32,1792]{1,0:T(8,128)(2,1)S(1)}, bf16[32,1792]{1,0:T(8,128)(2,1)S(1)}, u32[]{:S(2)}, u32[]{:S(2)}) %collective-permute-start.3) | collective-permute-done | bytes 114720 | tf_op jit(solution)/shard_map/ppermute | solution.py:46
  37.0 2.1 %collective-permute-done.4.refs_4_ = bf16[32,1792]{1,0:T(8,128)(2,1)S(1)} collective-permute-done((bf16[32,1792]{1,0:T(8,128)(2,1)S(1)}, bf16[32,1792]{1,0:T(8,128)(2,1)S(1)}, u32[]{:S(2)}, u32[]{:S(2)}) %collective-permute-start.4) | collective-permute-done | bytes 114720 | tf_op jit(solution)/shard_map/ppermute | solution.py:47
  39.1 2.0 %shard_map.105 = (bf16[256,768]{1,0:T(8,128)(2,1)S(1)}, bf16[1024,256]{1,0:T(8,128)(2,1)}) custom-call(s32[5]{0:T(128)S(1)} %stack.53.refs_0_, bf16[64,1792]{1,0:T(8,128)(2,1)S(1)} %get-tuple-element.25.refs_1_, bf16[64,1792]{1,0:T(8,128)(2,1)S(1)} %collective-permute-done.1.refs_2_, bf16[32,1792]{1,0:T(8,128)(2,1)S(1)} %collective-permute-done.3.refs_3_, ...), custom_call_target="tpu_custom_call" | custom-call | flops 402653184 | bytes 921620 | tf_op jit(solution)/shard_map/pallas_call | solution.py:85
  42.4 8.7 %all-to-all-start = ((bf16[32,32,256]{2,1,0:T(8,128)(2,1)}), bf16[32,32,256]{2,1,0:T(8,128)(2,1)S(1)}, u32[]{:S(2)}, u32[]{:S(2)}) async-start(bf16[32,32,256]{2,1,0:T(8,128)(2,1)} %bitcast.36), calls=%async_computation | async-start | bytes 1048576 | tf_op jit(solution)/shard_map/all_to_all | solution.py:316
  56.9 4.2 %collective-permute-start.6 = (bf16[256,1024]{1,0:T(8,128)(2,1)}, bf16[256,1024]{1,0:T(8,128)(2,1)}, u32[]{:S(2)}, u32[]{:S(2)}) collective-permute-start(bf16[256,1024]{1,0:T(8,128)(2,1)} %shard_map.106.refs_3_), channel_id=1, source_target_pairs={{0,1},{1,0},{2,3},{3,2},{4,5},{5,4},{6,7},{7,6},{8,9},{9,8},{10,11... | collective-permute-start | bytes 1572872 | tf_op jit(solution)/shard_map/ppermute | solution.py:39
  61.2 3.9 %collective-permute-start.14 = (bf16[1024,256]{1,0:T(8,128)(2,1)S(1)}, bf16[1024,256]{1,0:T(8,128)(2,1)S(1)}, u32[]{:S(2)}, u32[]{:S(2)}) collective-permute-start(bf16[1024,256]{1,0:T(8,128)(2,1)S(1)} %bitcast.23), channel_id=1, source_target_pairs={{0,1},{1,0},{2,3},{3,2},{4,5},{5,4},{6,7},{7,6},{8,9},{9,8},{10,11... | collective-permute-start | bytes 1572872 | tf_op jit(solution)/shard_map/ppermute | solution.py:39
  66.3 1.6 %shard_map.107 = (bf16[3,256,512]{2,1,0:T(8,128)(2,1)S(1)}, bf16[2,256,512]{2,1,0:T(8,128)(2,1)S(1)}, bf16[2,512,256]{2,1,0:T(8,128)(2,1)S(1)}) custom-call(s32[5]{0:T(128)S(1)} %stack.53.refs_0_, bf16[4,4,7,8,512]{4,3,2,1,0:T(8,128)(2,1)S(1)} %pad_maximum_fusion.refs_1_, bf16[4,4,7,8,512]{4,3,2,1,0:T(8,128)(2,1)S(1)} %collective-permute-done.12.refs_2_, ...), custom_call_target="tpu_custom_call" | custom-call | flops 1610612736 | bytes 3670036 | tf_op jit(solution)/shard_map/pallas_call | solution.py:85
  69.2 4.0 %shard_map.108 = (bf16[512,768]{1,0:T(8,128)(2,1)S(1)}, bf16[512,1024]{1,0:T(8,128)(2,1)S(1)}, bf16[256,1024]{1,0:T(8,128)(2,1)S(1)}) custom-call(s32[5]{0:T(128)S(1)} %stack.53.refs_0_, bf16[256,768]{1,0:T(8,128)(2,1)S(1)} %copy-done.14, bf16[256,768]{1,0:T(8,128)(2,1)S(1)} %collective-permute-done.5.refs_2_, bf16[256,1024]{1,0:T(8,128)(2,1)} %shard_map.106.refs_3_, ...), custom_call_target="tpu_custom_call" | custom-call | flops 1879048192 | bytes 3678228 | tf_op jit(solution)/shard_map/pallas_call | solution.py:85
  73.7 2.4 %shard_map.109 = (bf16[3,256,512]{2,1,0:T(8,128)(2,1)S(1)}, bf16[2,256,512]{2,1,0:T(8,128)(2,1)}, bf16[2,512,256]{2,1,0:T(8,128)(2,1)}) custom-call(s32[5]{0:T(128)S(1)} %stack.53.refs_0_, bf16[4,4,7,8,512]{4,3,2,1,0:T(8,128)(2,1)S(1)} %pad_maximum_fusion.refs_1_, bf16[4,4,7,8,512]{4,3,2,1,0:T(8,128)(2,1)S(1)} %collective-permute-done.12.refs_2_, ...), custom_call_target="tpu_custom_call" | custom-call | bytes 3670036 | tf_op jit(solution)/shard_map/pallas_call | solution.py:85
  76.1 7.4 %shard_map.110 = (bf16[512,1024]{1,0:T(8,128)(2,1)}, bf16[512,768]{1,0:T(8,128)(2,1)}, bf16[1024,256]{1,0:T(8,128)(2,1)}) custom-call(s32[5]{0:T(128)S(1)} %stack.53.refs_0_, bf16[256,1024]{1,0:T(8,128)(2,1)S(1)} %get-tuple-element.31.refs_1_, bf16[256,1024]{1,0:T(8,128)(2,1)S(1)} %collective-permute-done.17.refs_2_, ...), custom_call_target="tpu_custom_call" | custom-call | flops 3221225472 | bytes 5775380 | tf_op jit(solution)/shard_map/pallas_call | solution.py:85
  83.5 7.7 %all-to-all-start.1 = ((bf16[32,32,256]{2,1,0:T(8,128)(2,1)}), bf16[32,32,256]{2,1,0:T(8,128)(2,1)S(1)}, u32[]{:S(2)}, u32[]{:S(2)}) async-start(bf16[32,32,256]{2,1,0:T(8,128)(2,1)} %bitcast.37), calls=%async_computation.1 | async-start | bytes 1048576 | tf_op jit(solution)/shard_map/all_to_all | solution.py:316
  93.3 2.3 %shard_map.111.refs_1_ = f32[256,1024]{1,0:T(8,128)S(1)} custom-call(s32[5]{0:T(128)S(1)} %stack.53.refs_0_, bf16[512,768]{1,0:T(8,128)(2,1)S(1)} %copy-done, bf16[512,1024]{1,0:T(8,128)(2,1)S(1)} %copy-done.1, bf16[3,256,512]{2,1,0:T(8,128)(2,1)S(1)} %get-tuple-element.36.refs_10_.refs_3_, s32[1,1024]{1,0:T(1,128)S(1)} %bitcast.27, s32[1,1024]{1,0:T(1,128)S(1)} %bitcast.31), custom_call_target="tpu_custom_call" | custom-call | flops 805306368 | bytes 2629652 | tf_op jit(solution)/shard_map/pallas_call | solution.py:85
  95.6 6.1 %all-to-all-done.1 = bf16[32,32,256]{2,1,0:T(8,128)(2,1)S(1)} async-done(((bf16[32,32,256]{2,1,0:T(8,128)(2,1)}), bf16[32,32,256]{2,1,0:T(8,128)(2,1)S(1)}, u32[]{:S(2)}, u32[]{:S(2)}) %all-to-all-start.1) | async-done | bytes 524320 | tf_op jit(solution)/shard_map/all_to_all | solution.py:316
  103.0 2.1 %collective-permute-start.20 = (bf16[256,1024]{1,0:T(8,128)(2,1)S(1)}, bf16[256,1024]{1,0:T(8,128)(2,1)S(1)}, u32[]{:S(2)}, u32[]{:S(2)}) collective-permute-start(bf16[256,1024]{1,0:T(8,128)(2,1)S(1)} %shard_map.112.refs_1_), channel_id=1, source_target_pairs={{0,1},{1,0},{2,3},{3,2},{4,5},{5,4},{6,7},{7,6},{8,9},{9,8},{10,11... | collective-permute-start | bytes 1572872 | tf_op jit(solution)/shard_map/ppermute | solution.py:39
  105.1 1.8 %shard_map.113.refs_10_ = f32[2,256,768]{2,1,0:T(8,128)S(1)} custom-call(s32[5]{0:T(128)S(1)} %stack.53.refs_0_, bf16[2,256,512]{2,1,0:T(8,128)(2,1)} %get-tuple-element.41.refs_1_.refs_5_, bf16[2,256,512]{2,1,0:T(8,128)(2,1)} %collective-permute-done.22.refs_2_.refs_6_, bf16[512,768]{1,0:T(8,128)(2,1)S(1)} %copy-done), custom_call_target="tpu_custom_call" | custom-call | flops 402653184 | bytes 1835028 | tf_op jit(solution)/shard_map/pallas_call | solution.py:85
  107.0 6.3 %shard_map.114 = (bf16[64,1024]{1,0:T(8,128)(2,1)}, bf16[64,768]{1,0:T(8,128)(2,1)}) custom-call(s32[5]{0:T(128)S(1)} %stack.53.refs_0_, bf16[256,1024]{1,0:T(8,128)(2,1)S(1)} %shard_map.112.refs_1_, bf16[256,1024]{1,0:T(8,128)(2,1)S(1)} %collective-permute-done.20.refs_2_, bf16[2,512,256]{2,1,0:T(8,128)(2,1)} %get-tuple-element.40.refs_3_, ...), custom_call_target="tpu_custom_call" | custom-call | flops 2684354560 | bytes 6557716 | tf_op jit(solution)/shard_map/pallas_call | solution.py:85
  (76 shorter events, 19.6 us)
Async XLA Ops:
  2.4 11.4 %collective-permute-start = (bf16[7,8,512]{2,1,0:T(8,128)(2,1)S(1)}, bf16[7,8,512]{2,1,0:T(8,128)(2,1)S(1)}, u32[]{:S(2)}, u32[]{:S(2)}) collective-permute-start(bf16[7,8,512]{2,1,0:T(8,128)(2,1)S(1)} %get-tuple-element.24), channel_id=1, source_target_pairs={{0,4},{1,5},{2,6},{3,7},{4,0},{5,1},{6,2},{7,3},{8,12},{9,13},{10,... | collective-permute-start | bytes 172040 | tf_op jit(solution)/shard_map/ppermute | solution.py:300
  10.2 6.2 %collective-permute-start.7 = (bf16[7,8,512]{2,1,0:T(8,128)(2,1)S(1)}, bf16[7,8,512]{2,1,0:T(8,128)(2,1)S(1)}, u32[]{:S(2)}, u32[]{:S(2)}) collective-permute-start(bf16[7,8,512]{2,1,0:T(8,128)(2,1)S(1)} %get-tuple-element.24), channel_id=1, source_target_pairs={{0,2},{1,3},{2,4},{3,5},{4,6},{5,7},{6,0},{7,1},{8,10},{9,11},{10,... | collective-permute-start | bytes 172040 | tf_op jit(solution)/shard_map/ppermute | solution.py:300
  11.4 5.0 %collective-permute-start.8 = (bf16[7,8,512]{2,1,0:T(8,128)(2,1)S(1)}, bf16[7,8,512]{2,1,0:T(8,128)(2,1)S(1)}, u32[]{:S(2)}, u32[]{:S(2)}) collective-permute-start(bf16[7,8,512]{2,1,0:T(8,128)(2,1)S(1)} %get-tuple-element.24), channel_id=1, source_target_pairs={{0,6},{1,7},{2,0},{3,1},{4,2},{5,3},{6,4},{7,5},{8,14},{9,15},{10,... | collective-permute-start | bytes 172040 | tf_op jit(solution)/shard_map/ppermute | solution.py:300
  13.8 13.5 %collective-permute-start.1 = (bf16[64,1792]{1,0:T(8,128)(2,1)S(1)}, bf16[64,1792]{1,0:T(8,128)(2,1)S(1)}, u32[]{:S(2)}, u32[]{:S(2)}) collective-permute-start(bf16[64,1792]{1,0:T(8,128)(2,1)S(1)} %get-tuple-element.25.refs_1_), channel_id=1, source_target_pairs={{0,6},{1,7},{2,0},{3,1},{4,2},{5,3},{6,4},{7,5},{8,14},{9,15},{10,... | collective-permute-start | bytes 688136 | tf_op jit(solution)/shard_map/ppermute | solution.py:45
  16.4 11.8 %collective-permute-start.2 = (bf16[64,1792]{1,0:T(8,128)(2,1)S(1)}, bf16[64,1792]{1,0:T(8,128)(2,1)S(1)}, u32[]{:S(2)}, u32[]{:S(2)}) collective-permute-start(bf16[64,1792]{1,0:T(8,128)(2,1)S(1)} %get-tuple-element.25.refs_1_), channel_id=1, source_target_pairs={{0,2},{1,3},{2,4},{3,5},{4,6},{5,7},{6,0},{7,1},{8,10},{9,11},{10,... | collective-permute-start | bytes 688136 | tf_op jit(solution)/shard_map/ppermute | solution.py:44
  16.4 11.7 %collective-permute-start.9 = (bf16[4,7,8,512]{3,2,1,0:T(8,128)(2,1)S(1)}, bf16[4,7,8,512]{3,2,1,0:T(8,128)(2,1)S(1)}, u32[]{:S(2)}, u32[]{:S(2)}) collective-permute-start(bf16[4,7,8,512]{3,2,1,0:T(8,128)(2,1)S(1)} %pad_maximum_fusion.1), channel_id=1, source_target_pairs={{0,96},{1,25},{2,98},{3,27},{4,100},{5,29},{6,102},{7,31},{8,104},... | collective-permute-start | bytes 688136 | tf_op jit(solution)/shard_map/ppermute | solution.py:304
  19.0 9.2 %collective-permute-start.10 = (bf16[4,7,8,512]{3,2,1,0:T(8,128)(2,1)S(1)}, bf16[4,7,8,512]{3,2,1,0:T(8,128)(2,1)S(1)}, u32[]{:S(2)}, u32[]{:S(2)}) collective-permute-start(bf16[4,7,8,512]{3,2,1,0:T(8,128)(2,1)S(1)} %pad_maximum_fusion.1), channel_id=1, source_target_pairs={{0,64},{1,17},{2,66},{3,19},{4,68},{5,21},{6,70},{7,23},{8,72},{9,... | collective-permute-start | bytes 688136 | tf_op jit(solution)/shard_map/ppermute | solution.py:304
  19.5 8.7 %collective-permute-start.11 = (bf16[4,7,8,512]{3,2,1,0:T(8,128)(2,1)S(1)}, bf16[4,7,8,512]{3,2,1,0:T(8,128)(2,1)S(1)}, u32[]{:S(2)}, u32[]{:S(2)}) collective-permute-start(bf16[4,7,8,512]{3,2,1,0:T(8,128)(2,1)S(1)} %pad_maximum_fusion.1), channel_id=1, source_target_pairs={{0,32},{1,9},{2,34},{3,11},{4,36},{5,13},{6,38},{7,15},{8,40},{9,1... | collective-permute-start | bytes 688136 | tf_op jit(solution)/shard_map/ppermute | solution.py:304
  28.3 14.1 %collective-permute-start.13 = (bf16[4,4,7,8,512]{4,3,2,1,0:T(8,128)(2,1)S(1)}, bf16[4,4,7,8,512]{4,3,2,1,0:T(8,128)(2,1)S(1)}, u32[]{:S(2)}, u32[]{:S(2)}) collective-permute-start(bf16[4,4,7,8,512]{4,3,2,1,0:T(8,128)(2,1)S(1)} %pad_maximum_fusion.refs_1_), channel_id=1, source_target_pairs={{0,8},{1,33},{2,10},{3,35},{4,12},{5,37},{6,14},{7,39},{8,16},{9,4... | collective-permute-start | bytes 2752520 | tf_op jit(solution)/shard_map/ppermute | solution.py:44
  29.6 12.8 %collective-permute-start.12 = (bf16[4,4,7,8,512]{4,3,2,1,0:T(8,128)(2,1)S(1)}, bf16[4,4,7,8,512]{4,3,2,1,0:T(8,128)(2,1)S(1)}, u32[]{:S(2)}, u32[]{:S(2)}) collective-permute-start(bf16[4,4,7,8,512]{4,3,2,1,0:T(8,128)(2,1)S(1)} %pad_maximum_fusion.refs_1_), channel_id=1, source_target_pairs={{0,24},{1,97},{2,26},{3,99},{4,28},{5,101},{6,30},{7,103},{8,0},{9... | collective-permute-start | bytes 2752520 | tf_op jit(solution)/shard_map/ppermute | solution.py:45
  31.1 5.8 %collective-permute-start.3 = (bf16[32,1792]{1,0:T(8,128)(2,1)S(1)}, bf16[32,1792]{1,0:T(8,128)(2,1)S(1)}, u32[]{:S(2)}, u32[]{:S(2)}) collective-permute-start(bf16[32,1792]{1,0:T(8,128)(2,1)S(1)} %slice.16), channel_id=1, source_target_pairs={{0,2},{1,3},{2,4},{3,5},{4,6},{5,7},{6,0},{7,1},{8,10},{9,11},{10,... | collective-permute-start | bytes 344072 | tf_op jit(solution)/shard_map/ppermute | solution.py:46
  32.6 6.5 %collective-permute-start.4 = (bf16[32,1792]{1,0:T(8,128)(2,1)S(1)}, bf16[32,1792]{1,0:T(8,128)(2,1)S(1)}, u32[]{:S(2)}, u32[]{:S(2)}) collective-permute-start(bf16[32,1792]{1,0:T(8,128)(2,1)S(1)} %slice.17), channel_id=1, source_target_pairs={{0,6},{1,7},{2,0},{3,1},{4,2},{5,3},{6,4},{7,5},{8,14},{9,15},{10,... | collective-permute-start | bytes 344072 | tf_op jit(solution)/shard_map/ppermute | solution.py:47
  42.4 18.7 %all-to-all-start = ((bf16[32,32,256]{2,1,0:T(8,128)(2,1)}), bf16[32,32,256]{2,1,0:T(8,128)(2,1)S(1)}, u32[]{:S(2)}, u32[]{:S(2)}) async-start(bf16[32,32,256]{2,1,0:T(8,128)(2,1)} %bitcast.36), calls=%async_computation | async-start | bytes 1048576 | tf_op jit(solution)/shard_map/all_to_all | solution.py:316
  52.0 14.2 %collective-permute-start.15 = (bf16[2,4,7,8,512]{4,3,2,1,0:T(8,128)(2,1)}, bf16[2,4,7,8,512]{4,3,2,1,0:T(8,128)(2,1)}, u32[]{:S(2)}, u32[]{:S(2)}) collective-permute-start(bf16[2,4,7,8,512]{4,3,2,1,0:T(8,128)(2,1)} %slice.18), channel_id=1, source_target_pairs={{0,8},{1,33},{2,10},{3,35},{4,12},{5,37},{6,14},{7,39},{8,16},{9,4... | collective-permute-start | bytes 1376264 | tf_op jit(solution)/shard_map/ppermute | solution.py:46
  54.1 12.2 %collective-permute-start.16 = (bf16[2,4,7,8,512]{4,3,2,1,0:T(8,128)(2,1)}, bf16[2,4,7,8,512]{4,3,2,1,0:T(8,128)(2,1)}, u32[]{:S(2)}, u32[]{:S(2)}) collective-permute-start(bf16[2,4,7,8,512]{4,3,2,1,0:T(8,128)(2,1)} %slice.19), channel_id=1, source_target_pairs={{0,24},{1,97},{2,26},{3,99},{4,28},{5,101},{6,30},{7,103},{8,0},{9... | collective-permute-start | bytes 1376264 | tf_op jit(solution)/shard_map/ppermute | solution.py:47
  56.9 12.2 %collective-permute-start.6 = (bf16[256,1024]{1,0:T(8,128)(2,1)}, bf16[256,1024]{1,0:T(8,128)(2,1)}, u32[]{:S(2)}, u32[]{:S(2)}) collective-permute-start(bf16[256,1024]{1,0:T(8,128)(2,1)} %shard_map.106.refs_3_), channel_id=1, source_target_pairs={{0,1},{1,0},{2,3},{3,2},{4,5},{5,4},{6,7},{7,6},{8,9},{9,8},{10,11... | collective-permute-start | bytes 1572872 | tf_op jit(solution)/shard_map/ppermute | solution.py:39
  61.2 8.0 %collective-permute-start.14 = (bf16[1024,256]{1,0:T(8,128)(2,1)S(1)}, bf16[1024,256]{1,0:T(8,128)(2,1)S(1)}, u32[]{:S(2)}, u32[]{:S(2)}) collective-permute-start(bf16[1024,256]{1,0:T(8,128)(2,1)S(1)} %bitcast.23), channel_id=1, source_target_pairs={{0,1},{1,0},{2,3},{3,2},{4,5},{5,4},{6,7},{7,6},{8,9},{9,8},{10,11... | collective-permute-start | bytes 1572872 | tf_op jit(solution)/shard_map/ppermute | solution.py:39
  65.1 4.1 %collective-permute-start.5 = (bf16[256,768]{1,0:T(8,128)(2,1)}, bf16[256,768]{1,0:T(8,128)(2,1)S(1)}, u32[]{:S(2)}, u32[]{:S(2)}) collective-permute-start(bf16[256,768]{1,0:T(8,128)(2,1)} %copy-done.13), channel_id=1, source_target_pairs={{0,1},{1,0},{2,3},{3,2},{4,5},{5,4},{6,7},{7,6},{8,9},{9,8},{10,11... | collective-permute-start | bytes 1179656 | tf_op jit(solution)/shard_map/ppermute | solution.py:39
  67.9 8.2 %collective-permute-start.18 = (bf16[2,512,256]{2,1,0:T(8,128)(2,1)S(1)}, bf16[2,512,256]{2,1,0:T(8,128)(2,1)S(1)}, u32[]{:S(2)}, u32[]{:S(2)}) collective-permute-start(bf16[2,512,256]{2,1,0:T(8,128)(2,1)S(1)} %get-tuple-element.32.refs_3_), channel_id=1, source_target_pairs={{0,1},{1,0},{2,3},{3,2},{4,5},{5,4},{6,7},{7,6},{8,9},{9,8},{10,11... | collective-permute-start | bytes 1572872 | tf_op jit(solution)/shard_map/ppermute | solution.py:39
  69.0 7.1 %collective-permute-start.19 = (bf16[2,256,512]{2,1,0:T(8,128)(2,1)S(1)}, bf16[2,256,512]{2,1,0:T(8,128)(2,1)S(1)}, u32[]{:S(2)}, u32[]{:S(2)}) collective-permute-start(bf16[2,256,512]{2,1,0:T(8,128)(2,1)S(1)} %get-tuple-element.33.refs_5_), channel_id=1, source_target_pairs={{0,1},{1,0},{2,3},{3,2},{4,5},{5,4},{6,7},{7,6},{8,9},{9,8},{10,11... | collective-permute-start | bytes 1572872 | tf_op jit(solution)/shard_map/ppermute | solution.py:39
  83.5 18.2 %all-to-all-start.1 = ((bf16[32,32,256]{2,1,0:T(8,128)(2,1)}), bf16[32,32,256]{2,1,0:T(8,128)(2,1)S(1)}, u32[]{:S(2)}, u32[]{:S(2)}) async-start(bf16[32,32,256]{2,1,0:T(8,128)(2,1)} %bitcast.37), calls=%async_computation.1 | async-start | bytes 1048576 | tf_op jit(solution)/shard_map/all_to_all | solution.py:316
  91.2 13.9 %collective-permute-start.22 = (bf16[2,256,512]{2,1,0:T(8,128)(2,1)}, bf16[2,256,512]{2,1,0:T(8,128)(2,1)}, u32[]{:S(2)}, u32[]{:S(2)}) collective-permute-start(bf16[2,256,512]{2,1,0:T(8,128)(2,1)} %get-tuple-element.41.refs_1_.refs_5_), channel_id=1, source_target_pairs={{0,1},{1,0},{2,3},{3,2},{4,5},{5,4},{6,7},{7,6},{8,9},{9,8},{10,11... | collective-permute-start | bytes 1572872 | tf_op jit(solution)/shard_map/ppermute | solution.py:39
  91.9 15.0 %collective-permute-start.21 = (bf16[2,512,256]{2,1,0:T(8,128)(2,1)}, bf16[2,512,256]{2,1,0:T(8,128)(2,1)}, u32[]{:S(2)}, u32[]{:S(2)}) collective-permute-start(bf16[2,512,256]{2,1,0:T(8,128)(2,1)} %get-tuple-element.40.refs_3_), channel_id=1, source_target_pairs={{0,1},{1,0},{2,3},{3,2},{4,5},{5,4},{6,7},{7,6},{8,9},{9,8},{10,11... | collective-permute-start | bytes 1572872 | tf_op jit(solution)/shard_map/ppermute | solution.py:39
  103.0 3.9 %collective-permute-start.20 = (bf16[256,1024]{1,0:T(8,128)(2,1)S(1)}, bf16[256,1024]{1,0:T(8,128)(2,1)S(1)}, u32[]{:S(2)}, u32[]{:S(2)}) collective-permute-start(bf16[256,1024]{1,0:T(8,128)(2,1)S(1)} %shard_map.112.refs_1_), channel_id=1, source_target_pairs={{0,1},{1,0},{2,3},{3,2},{4,5},{5,4},{6,7},{7,6},{8,9},{9,8},{10,11... | collective-permute-start | bytes 1572872 | tf_op jit(solution)/shard_map/ppermute | solution.py:39
  (17 other events, 144.7 us)

commit v9 on v6

--- a/solution.py
+++ b/solution.py
@@ -294,7 +294,8 @@
     quarters = [wz, nxt, far, prev]
     quarters[0] = lax.optimization_barrier((wz, parts[1], parts[4]))[0]
     one = jnp.stack(quarters)
-    w_parts = ring_gather(one, ("dom", "ch"), lambda s: ring(2, s))
+    w_prev = lax.ppermute(one, ("dom", "ch"), ring(2, 1))
+    w_next = lax.ppermute(one, ("dom", "ch"), ring(2, 3))
 
     v_half, rows = call(
         send_first, [((HALF, n), BF), pltpu.HBM((m, HALF), BF)], meta, *parts, send,
@@ -304,7 +305,11 @@
     def exchange(rows):
         return lax.all_to_all(rows.reshape(32, SLOTS, HALF), "dom", 0, 0, tiled=True).reshape(-1, HALF)
 
-    halo = exchange(lax.optimization_barrier((rows, w_parts[1], w_parts[4]))[0])
+    rows, half_a, half_b = lax.optimization_barrier((rows, w_prev[:2], w_next[2:]))
+    halo = exchange(rows)
+    far_a = lax.ppermute(half_a, ("dom", "ch"), ring(2, 1))
+    far_b = lax.ppermute(half_b, ("dom", "ch"), ring(2, 3))
+    w_parts = (one, w_next, far_a, far_b, w_prev)
     v_other = swap(v_half)
     (e_half,) = call(gather_edges, [((HALF, m), BF)], meta, *parts)
     e_other = swap(e_half)

time: 113 us -> 113 us (level)
  local copies, waits for them, and re-layouts: 2.93 us -> 7.98 us
  starting transfers between devices: 56 us -> 52.3 us
  waiting for transfers between devices: 20.9 us -> 19.1 us
    ppermute x0 -> x4, starting transfers between devices: none -> 5.58 us  [the longest x1 1.53 us: shards(): w_next = lax.ppermute(one, ('dom', 'ch'), ring(2, 3))]
    unnamed x30, local copies, waits for them, and re-layouts: 1.19 us -> 6.23 us
    all_to_all x2, starting transfers between devices: 16.3 us -> 14 us  [exchange(): lax.all_to_all(rows.reshape(32, SLOTS, HALF), 'dom', 0, 0, tiled=True)]
    slice x0 -> x2, local copies, waits for them, and re-layouts: none -> 1.65 us  [the longest x1 0.83 us: shards(): w_prev[:2]]
    ppermute x2 -> x1, starting transfers between devices: 4.1 us -> 2.57 us  [ring_gather(): nxt = lax.ppermute(x, axis, perm(3))]
    ppermute x9, starting transfers between devices: 12.8 us -> 11.4 us  [swap(): return lax.ppermute(x, 'ch', CORE)]
    ppermute x2 -> x1, starting transfers between devices: 3.74 us -> 2.3 us  [ring_gather(): far_b = lax.ppermute(nxt[half:], axis, perm(3))]
    ppermute x2 -> x1, starting transfers between devices: 1.31 us -> 0.01 us  [ring_gather(): prev = lax.ppermute(x, axis, perm(1))]
  transfers between devices with their start and end apart: 25 -> 25, of which waited for: 7 -> 6; matrix products, arithmetic and copies ran while one was open for 1% -> 1% of each run, Pallas kernels for 15% -> 15%
where the time goes in v9:
time: 113 us; the launch traced here: 112 us
  starting transfers between devices  52.3 us (46%)
  Pallas kernels  31.5 us (28%)
  waiting for transfers between devices  19.1 us (17%)
  local copies, waits for them, and re-layouts  7.98 us (7%)
    pallas_call x11, Pallas kernels, call(): pl.pallas_call(body, out_shape=[o if isinstance(o, pl.MemoryRef) else jax...  31.5 us
    all_to_all x2, starting transfers between devices, exchange(): lax.all_to_all(rows.reshape(32, SLOTS, HALF), 'dom', 0, 0, tiled=True)  14 us
    ppermute x3, starting transfers between devices, shards(): lax.ppermute(piece, 'ch', z_shift(s))  11.4 us
    ppermute x9, starting transfers between devices, swap(): return lax.ppermute(x, 'ch', CORE)  11.4 us
    ppermute x1, waiting for transfers between devices, ring_gather(): nxt = lax.ppermute(x, axis, perm(3))  7.19 us
    all_to_all x2, waiting for transfers between devices, exchange(): lax.all_to_all(rows.reshape(32, SLOTS, HALF), 'dom', 0, 0, tiled=True)  6.25 us
    unnamed x30, local copies, waits for them, and re-layouts  6.23 us
    ppermute x3, starting transfers between devices, shards(): lax.ppermute(wz, ('dom', 'ch'), ring(1, s))  3.68 us
  transfers between devices with their start and end apart: 25, of which 6 were waited for; matrix products, arithmetic and copies ran while one was open for 1% of the time, Pallas kernels for 15%

profile of v9, /device:TPU:1, one launch (start us, length us, event | category | flops | bytes accessed | tf_op | source)
XLA Modules:
  0.0 112.0 jit_solution(361066481036250864)
XLA Ops:
  0.7 1.6 %shard_map.104 = (bf16[7,8,512]{2,1,0:T(8,128)(2,1)S(1)}, bf16[64,1792]{1,0:T(8,128)(2,1)S(1)}) custom-call(s32[5]{0:T(128)S(1)} %stack.53.refs_0_, bf16[2,3,64,512]{3,2,1,0:T(8,128)(2,1)} %bitcast.38, bf16[2,64,512]{2,1,0:T(8,128)(2,1)} %refs_2_.1, bf16[2,2,64,512]{3,2,1,0:T(8,128)(2,1)} %bitcast.39, bf16[2,64,512]{2,1,0:T(8,128)(2,1)} %refs_4_.1, ...), custom_call_target="tpu_custom_call" | custom-call | bytes 1146900 | tf_op jit(solution)/shard_map/pallas_call | solution.py:85
  2.4 7.8 %collective-permute-start = (bf16[7,8,512]{2,1,0:T(8,128)(2,1)S(1)}, bf16[7,8,512]{2,1,0:T(8,128)(2,1)S(1)}, u32[]{:S(2)}, u32[]{:S(2)}) collective-permute-start(bf16[7,8,512]{2,1,0:T(8,128)(2,1)S(1)} %get-tuple-element.26), channel_id=1, source_target_pairs={{0,4},{1,5},{2,6},{3,7},{4,0},{5,1},{6,2},{7,3},{8,12},{9,13},{10,... | collective-permute-start | bytes 172040 | tf_op jit(solution)/shard_map/ppermute | solution.py:289
  11.4 2.4 %collective-permute-start.8 = (bf16[7,8,512]{2,1,0:T(8,128)(2,1)S(1)}, bf16[7,8,512]{2,1,0:T(8,128)(2,1)S(1)}, u32[]{:S(2)}, u32[]{:S(2)}) collective-permute-start(bf16[7,8,512]{2,1,0:T(8,128)(2,1)S(1)} %get-tuple-element.26), channel_id=1, source_target_pairs={{0,6},{1,7},{2,0},{3,1},{4,2},{5,3},{6,4},{7,5},{8,14},{9,15},{10,... | collective-permute-start | bytes 172040 | tf_op jit(solution)/shard_map/ppermute | solution.py:289
  13.8 2.6 %collective-permute-start.1 = (bf16[64,1792]{1,0:T(8,128)(2,1)S(1)}, bf16[64,1792]{1,0:T(8,128)(2,1)S(1)}, u32[]{:S(2)}, u32[]{:S(2)}) collective-permute-start(bf16[64,1792]{1,0:T(8,128)(2,1)S(1)} %get-tuple-element.27.refs_1_), channel_id=1, source_target_pairs={{0,6},{1,7},{2,0},{3,1},{4,2},{5,3},{6,4},{7,5},{8,14},{9,15},{10,... | collective-permute-start | bytes 688136 | tf_op jit(solution)/shard_map/ppermute | solution.py:45
  16.4 2.6 %collective-permute-start.9 = (bf16[4,7,8,512]{3,2,1,0:T(8,128)(2,1)S(1)}, bf16[4,7,8,512]{3,2,1,0:T(8,128)(2,1)S(1)}, u32[]{:S(2)}, u32[]{:S(2)}) collective-permute-start(bf16[4,7,8,512]{3,2,1,0:T(8,128)(2,1)S(1)} %pad_maximum_fusion.1), channel_id=1, source_target_pairs={{0,96},{1,25},{2,98},{3,27},{4,100},{5,29},{6,102},{7,31},{8,104},... | collective-permute-start | bytes 688136 | tf_op jit(solution)/shard_map/ppermute | solution.py:293
  20.1 7.2 %collective-permute-done.1.refs_2_ = bf16[64,1792]{1,0:T(8,128)(2,1)S(1)} collective-permute-done((bf16[64,1792]{1,0:T(8,128)(2,1)S(1)}, bf16[64,1792]{1,0:T(8,128)(2,1)S(1)}, u32[]{:S(2)}, u32[]{:S(2)}) %collective-permute-start.1) | collective-permute-done | bytes 229408 | tf_op jit(solution)/shard_map/ppermute | solution.py:45
  32.6 2.3 %collective-permute-start.4 = (bf16[32,1792]{1,0:T(8,128)(2,1)S(1)}, bf16[32,1792]{1,0:T(8,128)(2,1)S(1)}, u32[]{:S(2)}, u32[]{:S(2)}) collective-permute-start(bf16[32,1792]{1,0:T(8,128)(2,1)S(1)} %slice.17), channel_id=1, source_target_pairs={{0,6},{1,7},{2,0},{3,1},{4,2},{5,3},{6,4},{7,5},{8,14},{9,15},{10,... | collective-permute-start | bytes 344072 | tf_op jit(solution)/shard_map/ppermute | solution.py:47
  34.9 2.1 %collective-permute-done.3.refs_3_ = bf16[32,1792]{1,0:T(8,128)(2,1)S(1)} collective-permute-done((bf16[32,1792]{1,0:T(8,128)(2,1)S(1)}, bf16[32,1792]{1,0:T(8,128)(2,1)S(1)}, u32[]{:S(2)}, u32[]{:S(2)}) %collective-permute-start.3) | collective-permute-done | bytes 114720 | tf_op jit(solution)/shard_map/ppermute | solution.py:46
  37.0 2.1 %collective-permute-done.4.refs_4_ = bf16[32,1792]{1,0:T(8,128)(2,1)S(1)} collective-permute-done((bf16[32,1792]{1,0:T(8,128)(2,1)S(1)}, bf16[32,1792]{1,0:T(8,128)(2,1)S(1)}, u32[]{:S(2)}, u32[]{:S(2)}) %collective-permute-start.4) | collective-permute-done | bytes 114720 | tf_op jit(solution)/shard_map/ppermute | solution.py:47
  39.1 2.0 %shard_map.105 = (bf16[256,768]{1,0:T(8,128)(2,1)S(1)}, bf16[1024,256]{1,0:T(8,128)(2,1)}) custom-call(s32[5]{0:T(128)S(1)} %stack.53.refs_0_, bf16[64,1792]{1,0:T(8,128)(2,1)S(1)} %get-tuple-element.27.refs_1_, bf16[64,1792]{1,0:T(8,128)(2,1)S(1)} %collective-permute-done.1.refs_2_, bf16[32,1792]{1,0:T(8,128)(2,1)S(1)} %collective-permute-done.3.refs_3_, ...), custom_call_target="tpu_custom_call" | custom-call | flops 402653184 | bytes 921620 | tf_op jit(solution)/shard_map/pallas_call | solution.py:85
  44.1 7.8 %all-to-all-start = ((bf16[32,32,256]{2,1,0:T(8,128)(2,1)}), bf16[32,32,256]{2,1,0:T(8,128)(2,1)S(1)}, u32[]{:S(2)}, u32[]{:S(2)}) async-start(bf16[32,32,256]{2,1,0:T(8,128)(2,1)} %bitcast.36), calls=%async_computation | async-start | bytes 1048576 | tf_op jit(solution)/shard_map/all_to_all | solution.py:306
  59.8 4.2 %collective-permute-start.6 = (bf16[256,1024]{1,0:T(8,128)(2,1)}, bf16[256,1024]{1,0:T(8,128)(2,1)}, u32[]{:S(2)}, u32[]{:S(2)}) collective-permute-start(bf16[256,1024]{1,0:T(8,128)(2,1)} %shard_map.106.refs_3_), channel_id=1, source_target_pairs={{0,1},{1,0},{2,3},{3,2},{4,5},{5,4},{6,7},{7,6},{8,9},{9,8},{10,11... | collective-permute-start | bytes 1572872 | tf_op jit(solution)/shard_map/ppermute | solution.py:39
  64.0 1.9 %collective-permute-start.14 = (bf16[1024,256]{1,0:T(8,128)(2,1)S(1)}, bf16[1024,256]{1,0:T(8,128)(2,1)S(1)}, u32[]{:S(2)}, u32[]{:S(2)}) collective-permute-start(bf16[1024,256]{1,0:T(8,128)(2,1)S(1)} %bitcast.23), channel_id=1, source_target_pairs={{0,1},{1,0},{2,3},{3,2},{4,5},{5,4},{6,7},{7,6},{8,9},{9,8},{10,11... | collective-permute-start | bytes 1572872 | tf_op jit(solution)/shard_map/ppermute | solution.py:39
  66.5 1.6 %shard_map.107 = (bf16[3,256,512]{2,1,0:T(8,128)(2,1)S(1)}, bf16[2,256,512]{2,1,0:T(8,128)(2,1)S(1)}, bf16[2,512,256]{2,1,0:T(8,128)(2,1)S(1)}) custom-call(s32[5]{0:T(128)S(1)} %stack.53.refs_0_, bf16[4,4,7,8,512]{4,3,2,1,0:T(8,128)(2,1)S(1)} %pad_maximum_fusion.refs_1_, bf16[4,4,7,8,512]{4,3,2,1,0:T(8,128)(2,1)S(1)} %collective-permute-done.13.refs_2_, ...), custom_call_target="tpu_custom_call" | custom-call | flops 1610612736 | bytes 3670036 | tf_op jit(solution)/shard_map/pallas_call | solution.py:85
  68.1 1.7 %collective-permute-start.18 = (bf16[2,512,256]{2,1,0:T(8,128)(2,1)S(1)}, bf16[2,512,256]{2,1,0:T(8,128)(2,1)S(1)}, u32[]{:S(2)}, u32[]{:S(2)}) collective-permute-start(bf16[2,512,256]{2,1,0:T(8,128)(2,1)S(1)} %get-tuple-element.36.refs_3_), channel_id=1, source_target_pairs={{0,1},{1,0},{2,3},{3,2},{4,5},{5,4},{6,7},{7,6},{8,9},{9,8},{10,11... | collective-permute-start | bytes 1572872 | tf_op jit(solution)/shard_map/ppermute | solution.py:39
  70.0 4.0 %shard_map.108 = (bf16[512,768]{1,0:T(8,128)(2,1)S(1)}, bf16[512,1024]{1,0:T(8,128)(2,1)S(1)}, bf16[256,1024]{1,0:T(8,128)(2,1)S(1)}) custom-call(s32[5]{0:T(128)S(1)} %stack.53.refs_0_, bf16[256,768]{1,0:T(8,128)(2,1)S(1)} %copy-done.13, bf16[256,768]{1,0:T(8,128)(2,1)S(1)} %collective-permute-done.5.refs_2_, bf16[256,1024]{1,0:T(8,128)(2,1)} %shard_map.106.refs_3_, ...), custom_call_target="tpu_custom_call" | custom-call | flops 1879048192 | bytes 3678228 | tf_op jit(solution)/shard_map/pallas_call | solution.py:85
  74.5 2.4 %shard_map.109 = (bf16[3,256,512]{2,1,0:T(8,128)(2,1)S(1)}, bf16[2,256,512]{2,1,0:T(8,128)(2,1)}, bf16[2,512,256]{2,1,0:T(8,128)(2,1)}) custom-call(s32[5]{0:T(128)S(1)} %stack.53.refs_0_, bf16[4,4,7,8,512]{4,3,2,1,0:T(8,128)(2,1)S(1)} %pad_maximum_fusion.refs_1_, bf16[4,4,7,8,512]{4,3,2,1,0:T(8,128)(2,1)S(1)} %collective-permute-done.13.refs_2_, ...), custom_call_target="tpu_custom_call" | custom-call | bytes 3670036 | tf_op jit(solution)/shard_map/pallas_call | solution.py:85
  76.9 6.9 %shard_map.110 = (bf16[512,1024]{1,0:T(8,128)(2,1)S(1)}, bf16[512,768]{1,0:T(8,128)(2,1)S(1)}, bf16[1024,256]{1,0:T(8,128)(2,1)}) custom-call(s32[5]{0:T(128)S(1)} %stack.53.refs_0_, bf16[256,1024]{1,0:T(8,128)(2,1)S(1)} %get-tuple-element.35.refs_1_, bf16[256,1024]{1,0:T(8,128)(2,1)S(1)} %collective-permute-done.17.refs_2_, ...), custom_call_target="tpu_custom_call" | custom-call | flops 3221225472 | bytes 5775380 | tf_op jit(solution)/shard_map/pallas_call | solution.py:85
  83.8 6.2 %all-to-all-start.1 = ((bf16[32,32,256]{2,1,0:T(8,128)(2,1)}), bf16[32,32,256]{2,1,0:T(8,128)(2,1)S(1)}, u32[]{:S(2)}, u32[]{:S(2)}) async-start(bf16[32,32,256]{2,1,0:T(8,128)(2,1)} %bitcast.37), calls=%async_computation.1 | async-start | bytes 1048576 | tf_op jit(solution)/shard_map/all_to_all | solution.py:306
  92.0 2.3 %shard_map.111.refs_1_ = f32[256,1024]{1,0:T(8,128)S(1)} custom-call(s32[5]{0:T(128)S(1)} %stack.53.refs_0_, bf16[512,768]{1,0:T(8,128)(2,1)S(1)} %get-tuple-element.41.refs_1_.refs_3_.refs_8_, bf16[512,1024]{1,0:T(8,128)(2,1)S(1)} %get-tuple-element.42.refs_2_.refs_7_, bf16[3,256,512]{2,1,0:T(8,128)(2,1)S(1)} %copy-done.1, s32[1,1024]{1,0:T(1,128)S(1)} %bitcast.27, ...), custom_call_target="tpu_custom_call" | custom-call | flops 805306368 | bytes 2629652 | tf_op jit(solution)/shard_map/pallas_call | solution.py:85
  94.3 6.2 %all-to-all-done.1 = bf16[32,32,256]{2,1,0:T(8,128)(2,1)S(1)} async-done(((bf16[32,32,256]{2,1,0:T(8,128)(2,1)}), bf16[32,32,256]{2,1,0:T(8,128)(2,1)S(1)}, u32[]{:S(2)}, u32[]{:S(2)}) %all-to-all-start.1) | async-done | bytes 524320 | tf_op jit(solution)/shard_map/all_to_all | solution.py:306
  101.8 2.1 %collective-permute-start.20 = (bf16[256,1024]{1,0:T(8,128)(2,1)S(1)}, bf16[256,1024]{1,0:T(8,128)(2,1)S(1)}, u32[]{:S(2)}, u32[]{:S(2)}) collective-permute-start(bf16[256,1024]{1,0:T(8,128)(2,1)S(1)} %shard_map.112.refs_1_), channel_id=1, source_target_pairs={{0,1},{1,0},{2,3},{3,2},{4,5},{5,4},{6,7},{7,6},{8,9},{9,8},{10,11... | collective-permute-start | bytes 1572872 | tf_op jit(solution)/shard_map/ppermute | solution.py:39
  103.9 1.8 %shard_map.113.refs_10_ = f32[2,256,768]{2,1,0:T(8,128)S(1)} custom-call(s32[5]{0:T(128)S(1)} %stack.53.refs_0_, bf16[2,256,512]{2,1,0:T(8,128)(2,1)} %get-tuple-element.45.refs_1_.refs_5_, bf16[2,256,512]{2,1,0:T(8,128)(2,1)} %collective-permute-done.22.refs_2_.refs_6_, bf16[512,768]{1,0:T(8,128)(2,1)S(1)} %get-tuple-element.41.refs_1_.refs_3_.refs_8_), custom_call_target="tpu_custom_call" | custom-call | flops 402653184 | bytes 1835028 | tf_op jit(solution)/shard_map/pallas_call | solution.py:85
  105.7 6.2 %shard_map.114 = (bf16[64,1024]{1,0:T(8,128)(2,1)}, bf16[64,768]{1,0:T(8,128)(2,1)}) custom-call(s32[5]{0:T(128)S(1)} %stack.53.refs_0_, bf16[256,1024]{1,0:T(8,128)(2,1)S(1)} %shard_map.112.refs_1_, bf16[256,1024]{1,0:T(8,128)(2,1)S(1)} %collective-permute-done.20.refs_2_, bf16[2,512,256]{2,1,0:T(8,128)(2,1)} %get-tuple-element.44.refs_3_, ...), custom_call_target="tpu_custom_call" | custom-call | flops 2684354560 | bytes 6557716 | tf_op jit(solution)/shard_map/pallas_call | solution.py:85
  (74 shorter events, 23.1 us)
Async XLA Ops:
  2.4 11.4 %collective-permute-start = (bf16[7,8,512]{2,1,0:T(8,128)(2,1)S(1)}, bf16[7,8,512]{2,1,0:T(8,128)(2,1)S(1)}, u32[]{:S(2)}, u32[]{:S(2)}) collective-permute-start(bf16[7,8,512]{2,1,0:T(8,128)(2,1)S(1)} %get-tuple-element.26), channel_id=1, source_target_pairs={{0,4},{1,5},{2,6},{3,7},{4,0},{5,1},{6,2},{7,3},{8,12},{9,13},{10,... | collective-permute-start | bytes 172040 | tf_op jit(solution)/shard_map/ppermute | solution.py:289
  10.2 6.2 %collective-permute-start.7 = (bf16[7,8,512]{2,1,0:T(8,128)(2,1)S(1)}, bf16[7,8,512]{2,1,0:T(8,128)(2,1)S(1)}, u32[]{:S(2)}, u32[]{:S(2)}) collective-permute-start(bf16[7,8,512]{2,1,0:T(8,128)(2,1)S(1)} %get-tuple-element.26), channel_id=1, source_target_pairs={{0,2},{1,3},{2,4},{3,5},{4,6},{5,7},{6,0},{7,1},{8,10},{9,11},{10,... | collective-permute-start | bytes 172040 | tf_op jit(solution)/shard_map/ppermute | solution.py:289
  11.4 5.0 %collective-permute-start.8 = (bf16[7,8,512]{2,1,0:T(8,128)(2,1)S(1)}, bf16[7,8,512]{2,1,0:T(8,128)(2,1)S(1)}, u32[]{:S(2)}, u32[]{:S(2)}) collective-permute-start(bf16[7,8,512]{2,1,0:T(8,128)(2,1)S(1)} %get-tuple-element.26), channel_id=1, source_target_pairs={{0,6},{1,7},{2,0},{3,1},{4,2},{5,3},{6,4},{7,5},{8,14},{9,15},{10,... | collective-permute-start | bytes 172040 | tf_op jit(solution)/shard_map/ppermute | solution.py:289
  13.8 13.5 %collective-permute-start.1 = (bf16[64,1792]{1,0:T(8,128)(2,1)S(1)}, bf16[64,1792]{1,0:T(8,128)(2,1)S(1)}, u32[]{:S(2)}, u32[]{:S(2)}) collective-permute-start(bf16[64,1792]{1,0:T(8,128)(2,1)S(1)} %get-tuple-element.27.refs_1_), channel_id=1, source_target_pairs={{0,6},{1,7},{2,0},{3,1},{4,2},{5,3},{6,4},{7,5},{8,14},{9,15},{10,... | collective-permute-start | bytes 688136 | tf_op jit(solution)/shard_map/ppermute | solution.py:45
  16.4 11.8 %collective-permute-start.2 = (bf16[64,1792]{1,0:T(8,128)(2,1)S(1)}, bf16[64,1792]{1,0:T(8,128)(2,1)S(1)}, u32[]{:S(2)}, u32[]{:S(2)}) collective-permute-start(bf16[64,1792]{1,0:T(8,128)(2,1)S(1)} %get-tuple-element.27.refs_1_), channel_id=1, source_target_pairs={{0,2},{1,3},{2,4},{3,5},{4,6},{5,7},{6,0},{7,1},{8,10},{9,11},{10,... | collective-permute-start | bytes 688136 | tf_op jit(solution)/shard_map/ppermute | solution.py:44
  16.4 11.7 %collective-permute-start.9 = (bf16[4,7,8,512]{3,2,1,0:T(8,128)(2,1)S(1)}, bf16[4,7,8,512]{3,2,1,0:T(8,128)(2,1)S(1)}, u32[]{:S(2)}, u32[]{:S(2)}) collective-permute-start(bf16[4,7,8,512]{3,2,1,0:T(8,128)(2,1)S(1)} %pad_maximum_fusion.1), channel_id=1, source_target_pairs={{0,96},{1,25},{2,98},{3,27},{4,100},{5,29},{6,102},{7,31},{8,104},... | collective-permute-start | bytes 688136 | tf_op jit(solution)/shard_map/ppermute | solution.py:293
  19.0 9.2 %collective-permute-start.10 = (bf16[4,7,8,512]{3,2,1,0:T(8,128)(2,1)S(1)}, bf16[4,7,8,512]{3,2,1,0:T(8,128)(2,1)S(1)}, u32[]{:S(2)}, u32[]{:S(2)}) collective-permute-start(bf16[4,7,8,512]{3,2,1,0:T(8,128)(2,1)S(1)} %pad_maximum_fusion.1), channel_id=1, source_target_pairs={{0,64},{1,17},{2,66},{3,19},{4,68},{5,21},{6,70},{7,23},{8,72},{9,... | collective-permute-start | bytes 688136 | tf_op jit(solution)/shard_map/ppermute | solution.py:293
  19.5 8.7 %collective-permute-start.11 = (bf16[4,7,8,512]{3,2,1,0:T(8,128)(2,1)S(1)}, bf16[4,7,8,512]{3,2,1,0:T(8,128)(2,1)S(1)}, u32[]{:S(2)}, u32[]{:S(2)}) collective-permute-start(bf16[4,7,8,512]{3,2,1,0:T(8,128)(2,1)S(1)} %pad_maximum_fusion.1), channel_id=1, source_target_pairs={{0,32},{1,9},{2,34},{3,11},{4,36},{5,13},{6,38},{7,15},{8,40},{9,1... | collective-permute-start | bytes 688136 | tf_op jit(solution)/shard_map/ppermute | solution.py:293
  28.3 14.2 %collective-permute-start.12 = (bf16[4,4,7,8,512]{4,3,2,1,0:T(8,128)(2,1)S(1)}, bf16[4,4,7,8,512]{4,3,2,1,0:T(8,128)(2,1)S(1)}, u32[]{:S(2)}, u32[]{:S(2)}) collective-permute-start(bf16[4,4,7,8,512]{4,3,2,1,0:T(8,128)(2,1)S(1)} %pad_maximum_fusion.refs_1_), channel_id=1, source_target_pairs={{0,8},{1,33},{2,10},{3,35},{4,12},{5,37},{6,14},{7,39},{8,16},{9,4... | collective-permute-start | bytes 2752520 | tf_op jit(solution)/shard_map/ppermute | solution.py:297
  29.6 13.7 %collective-permute-start.13 = (bf16[4,4,7,8,512]{4,3,2,1,0:T(8,128)(2,1)S(1)}, bf16[4,4,7,8,512]{4,3,2,1,0:T(8,128)(2,1)S(1)}, u32[]{:S(2)}, u32[]{:S(2)}) collective-permute-start(bf16[4,4,7,8,512]{4,3,2,1,0:T(8,128)(2,1)S(1)} %pad_maximum_fusion.refs_1_), channel_id=1, source_target_pairs={{0,24},{1,97},{2,26},{3,99},{4,28},{5,101},{6,30},{7,103},{8,0},{9... | collective-permute-start | bytes 2752520 | tf_op jit(solution)/shard_map/ppermute | solution.py:298
  31.1 5.8 %collective-permute-start.3 = (bf16[32,1792]{1,0:T(8,128)(2,1)S(1)}, bf16[32,1792]{1,0:T(8,128)(2,1)S(1)}, u32[]{:S(2)}, u32[]{:S(2)}) collective-permute-start(bf16[32,1792]{1,0:T(8,128)(2,1)S(1)} %slice.16), channel_id=1, source_target_pairs={{0,2},{1,3},{2,4},{3,5},{4,6},{5,7},{6,0},{7,1},{8,10},{9,11},{10,... | collective-permute-start | bytes 344072 | tf_op jit(solution)/shard_map/ppermute | solution.py:46
  32.6 6.5 %collective-permute-start.4 = (bf16[32,1792]{1,0:T(8,128)(2,1)S(1)}, bf16[32,1792]{1,0:T(8,128)(2,1)S(1)}, u32[]{:S(2)}, u32[]{:S(2)}) collective-permute-start(bf16[32,1792]{1,0:T(8,128)(2,1)S(1)} %slice.17), channel_id=1, source_target_pairs={{0,6},{1,7},{2,0},{3,1},{4,2},{5,3},{6,4},{7,5},{8,14},{9,15},{10,... | collective-permute-start | bytes 344072 | tf_op jit(solution)/shard_map/ppermute | solution.py:47
  44.1 19.8 %all-to-all-start = ((bf16[32,32,256]{2,1,0:T(8,128)(2,1)}), bf16[32,32,256]{2,1,0:T(8,128)(2,1)S(1)}, u32[]{:S(2)}, u32[]{:S(2)}) async-start(bf16[32,32,256]{2,1,0:T(8,128)(2,1)} %bitcast.36), calls=%async_computation | async-start | bytes 1048576 | tf_op jit(solution)/shard_map/all_to_all | solution.py:306
  52.0 14.5 %collective-permute-start.15 = (bf16[2,4,7,8,512]{4,3,2,1,0:T(8,128)(2,1)}, bf16[2,4,7,8,512]{4,3,2,1,0:T(8,128)(2,1)}, u32[]{:S(2)}, u32[]{:S(2)}) collective-permute-start(bf16[2,4,7,8,512]{4,3,2,1,0:T(8,128)(2,1)} %slice.18), channel_id=1, source_target_pairs={{0,8},{1,33},{2,10},{3,35},{4,12},{5,37},{6,14},{7,39},{8,16},{9,4... | collective-permute-start | bytes 1376264 | tf_op jit(solution)/shard_map/ppermute | solution.py:310
  53.3 13.2 %collective-permute-start.16 = (bf16[2,4,7,8,512]{4,3,2,1,0:T(8,128)(2,1)}, bf16[2,4,7,8,512]{4,3,2,1,0:T(8,128)(2,1)}, u32[]{:S(2)}, u32[]{:S(2)}) collective-permute-start(bf16[2,4,7,8,512]{4,3,2,1,0:T(8,128)(2,1)} %slice.19), channel_id=1, source_target_pairs={{0,24},{1,97},{2,26},{3,99},{4,28},{5,101},{6,30},{7,103},{8,0},{9... | collective-permute-start | bytes 1376264 | tf_op jit(solution)/shard_map/ppermute | solution.py:311
  59.8 10.2 %collective-permute-start.6 = (bf16[256,1024]{1,0:T(8,128)(2,1)}, bf16[256,1024]{1,0:T(8,128)(2,1)}, u32[]{:S(2)}, u32[]{:S(2)}) collective-permute-start(bf16[256,1024]{1,0:T(8,128)(2,1)} %shard_map.106.refs_3_), channel_id=1, source_target_pairs={{0,1},{1,0},{2,3},{3,2},{4,5},{5,4},{6,7},{7,6},{8,9},{9,8},{10,11... | collective-permute-start | bytes 1572872 | tf_op jit(solution)/shard_map/ppermute | solution.py:39
  64.0 5.9 %collective-permute-start.14 = (bf16[1024,256]{1,0:T(8,128)(2,1)S(1)}, bf16[1024,256]{1,0:T(8,128)(2,1)S(1)}, u32[]{:S(2)}, u32[]{:S(2)}) collective-permute-start(bf16[1024,256]{1,0:T(8,128)(2,1)S(1)} %bitcast.23), channel_id=1, source_target_pairs={{0,1},{1,0},{2,3},{3,2},{4,5},{5,4},{6,7},{7,6},{8,9},{9,8},{10,11... | collective-permute-start | bytes 1572872 | tf_op jit(solution)/shard_map/ppermute | solution.py:39
  65.9 4.1 %collective-permute-start.5 = (bf16[256,768]{1,0:T(8,128)(2,1)}, bf16[256,768]{1,0:T(8,128)(2,1)S(1)}, u32[]{:S(2)}, u32[]{:S(2)}) collective-permute-start(bf16[256,768]{1,0:T(8,128)(2,1)} %copy-done.12), channel_id=1, source_target_pairs={{0,1},{1,0},{2,3},{3,2},{4,5},{5,4},{6,7},{7,6},{8,9},{9,8},{10,11... | collective-permute-start | bytes 1179656 | tf_op jit(solution)/shard_map/ppermute | solution.py:39
  68.1 8.8 %collective-permute-start.18 = (bf16[2,512,256]{2,1,0:T(8,128)(2,1)S(1)}, bf16[2,512,256]{2,1,0:T(8,128)(2,1)S(1)}, u32[]{:S(2)}, u32[]{:S(2)}) collective-permute-start(bf16[2,512,256]{2,1,0:T(8,128)(2,1)S(1)} %get-tuple-element.36.refs_3_), channel_id=1, source_target_pairs={{0,1},{1,0},{2,3},{3,2},{4,5},{5,4},{6,7},{7,6},{8,9},{9,8},{10,11... | collective-permute-start | bytes 1572872 | tf_op jit(solution)/shard_map/ppermute | solution.py:39
  69.8 7.1 %collective-permute-start.19 = (bf16[2,256,512]{2,1,0:T(8,128)(2,1)S(1)}, bf16[2,256,512]{2,1,0:T(8,128)(2,1)S(1)}, u32[]{:S(2)}, u32[]{:S(2)}) collective-permute-start(bf16[2,256,512]{2,1,0:T(8,128)(2,1)S(1)} %get-tuple-element.37.refs_5_), channel_id=1, source_target_pairs={{0,1},{1,0},{2,3},{3,2},{4,5},{5,4},{6,7},{7,6},{8,9},{9,8},{10,11... | collective-permute-start | bytes 1572872 | tf_op jit(solution)/shard_map/ppermute | solution.py:39
  83.8 16.7 %all-to-all-start.1 = ((bf16[32,32,256]{2,1,0:T(8,128)(2,1)}), bf16[32,32,256]{2,1,0:T(8,128)(2,1)S(1)}, u32[]{:S(2)}, u32[]{:S(2)}) async-start(bf16[32,32,256]{2,1,0:T(8,128)(2,1)} %bitcast.37), calls=%async_computation.1 | async-start | bytes 1048576 | tf_op jit(solution)/shard_map/all_to_all | solution.py:306
  90.0 13.9 %collective-permute-start.22 = (bf16[2,256,512]{2,1,0:T(8,128)(2,1)}, bf16[2,256,512]{2,1,0:T(8,128)(2,1)}, u32[]{:S(2)}, u32[]{:S(2)}) collective-permute-start(bf16[2,256,512]{2,1,0:T(8,128)(2,1)} %get-tuple-element.45.refs_1_.refs_5_), channel_id=1, source_target_pairs={{0,1},{1,0},{2,3},{3,2},{4,5},{5,4},{6,7},{7,6},{8,9},{9,8},{10,11... | collective-permute-start | bytes 1572872 | tf_op jit(solution)/shard_map/ppermute | solution.py:39
  90.7 15.0 %collective-permute-start.21 = (bf16[2,512,256]{2,1,0:T(8,128)(2,1)}, bf16[2,512,256]{2,1,0:T(8,128)(2,1)}, u32[]{:S(2)}, u32[]{:S(2)}) collective-permute-start(bf16[2,512,256]{2,1,0:T(8,128)(2,1)} %get-tuple-element.44.refs_3_), channel_id=1, source_target_pairs={{0,1},{1,0},{2,3},{3,2},{4,5},{5,4},{6,7},{7,6},{8,9},{9,8},{10,11... | collective-permute-start | bytes 1572872 | tf_op jit(solution)/shard_map/ppermute | solution.py:39
  101.8 3.9 %collective-permute-start.20 = (bf16[256,1024]{1,0:T(8,128)(2,1)S(1)}, bf16[256,1024]{1,0:T(8,128)(2,1)S(1)}, u32[]{:S(2)}, u32[]{:S(2)}) collective-permute-start(bf16[256,1024]{1,0:T(8,128)(2,1)S(1)} %shard_map.112.refs_1_), channel_id=1, source_target_pairs={{0,1},{1,0},{2,3},{3,2},{4,5},{5,4},{6,7},{7,6},{8,9},{9,8},{10,11... | collective-permute-start | bytes 1572872 | tf_op jit(solution)/shard_map/ppermute | solution.py:39
  (16 other events, 118.7 us)

commit v10 on v8

--- a/solution.py
+++ b/solution.py
@@ -305,7 +305,8 @@
     quarters = [wz, nxt, far, prev]
     quarters[0] = lax.optimization_barrier((wz, parts[1], parts[4]))[0]
     one = jnp.stack(quarters)
-    w_parts = ring_gather(one, ("dom", "ch"), lambda s: ring(2, s))
+    w_prev = lax.ppermute(one, ("dom", "ch"), ring(2, 1))
+    w_next = lax.ppermute(one, ("dom", "ch"), ring(2, 3))
 
     v_half, rows = call(
         send_first, [((HALF, n), BF), pltpu.HBM((m, HALF), BF)], meta, *parts, send,
@@ -315,7 +316,11 @@
     def exchange(rows):
         return lax.all_to_all(rows.reshape(32, SLOTS, HALF), "dom", 0, 0, tiled=True).reshape(-1, HALF)
 
-    halo = exchange(lax.optimization_barrier((rows, w_parts[1], w_parts[4]))[0])
+    rows, half_a, half_b = lax.optimization_barrier((rows, w_prev[:2], w_next[2:]))
+    halo = exchange(rows)
+    far_a = lax.ppermute(half_a, ("dom", "ch"), ring(2, 1))
+    far_b = lax.ppermute(half_b, ("dom", "ch"), ring(2, 3))
+    w_parts = (one, w_next, far_a, far_b, w_prev)
     v_other = swap(v_half)
     (e_half,) = call(gather_edges, [((HALF, m), BF)], meta, *parts)
     e_other = swap(e_half)

time: 114 us -> 113 us (level)
  local copies, waits for them, and re-layouts: 3.03 us -> 8.05 us
  starting transfers between devices: 56.2 us -> 52.5 us
  waiting for transfers between devices: 20.8 us -> 19 us
    ppermute x0 -> x4, starting transfers between devices: none -> 5.58 us  [the longest x1 1.53 us: shards(): w_next = lax.ppermute(one, ('dom', 'ch'), ring(2, 3))]
    unnamed x32, local copies, waits for them, and re-layouts: 1.29 us -> 6.31 us
    all_to_all x2, starting transfers between devices: 16.4 us -> 14.1 us  [exchange(): lax.all_to_all(rows.reshape(32, SLOTS, HALF), 'dom', 0, 0, tiled=True)]
    slice x0 -> x2, local copies, waits for them, and re-layouts: none -> 1.64 us  [the longest x1 0.82 us: shards(): w_next[2:]]
    ppermute x2 -> x1, starting transfers between devices: 4.1 us -> 2.57 us  [ring_gather(): nxt = lax.ppermute(x, axis, perm(3))]
    ppermute x9, starting transfers between devices: 12.8 us -> 11.3 us  [swap(): return lax.ppermute(x, 'ch', CORE)]
    ppermute x2 -> x1, starting transfers between devices: 3.74 us -> 2.3 us  [ring_gather(): far_b = lax.ppermute(nxt[half:], axis, perm(3))]
    ppermute x2 -> x1, starting transfers between devices: 1.31 us -> 0.01 us  [ring_gather(): prev = lax.ppermute(x, axis, perm(1))]
  transfers between devices with their start and end apart: 25 -> 25, of which waited for: 7 -> 6; matrix products, arithmetic and copies ran while one was open for 1% -> 1% of each run, Pallas kernels for 15% -> 15%
where the time goes in v10:
time: 113 us
  starting transfers between devices  52.5 us (46%)
  Pallas kernels  32.1 us (28%)
  waiting for transfers between devices  19 us (17%)
  local copies, waits for them, and re-layouts  8.05 us (7%)
    pallas_call x11, Pallas kernels, call(): pl.pallas_call(body, out_shape=[o if isinstance(o, pl.MemoryRef) else jax...  32.1 us
    all_to_all x2, starting transfers between devices, exchange(): lax.all_to_all(rows.reshape(32, SLOTS, HALF), 'dom', 0, 0, tiled=True)  14.1 us
    ppermute x3, starting transfers between devices, shards(): lax.ppermute(piece, 'ch', z_shift(s))  11.4 us
    ppermute x9, starting transfers between devices, swap(): return lax.ppermute(x, 'ch', CORE)  11.3 us
    ppermute x1, waiting for transfers between devices, ring_gather(): nxt = lax.ppermute(x, axis, perm(3))  7.19 us
    unnamed x32, local copies, waits for them, and re-layouts  6.31 us
    all_to_all x2, waiting for transfers between devices, exchange(): lax.all_to_all(rows.reshape(32, SLOTS, HALF), 'dom', 0, 0, tiled=True)  6.15 us
    ppermute x3, starting transfers between devices, shards(): lax.ppermute(wz, ('dom', 'ch'), ring(1, s))  3.68 us
  transfers between devices with their start and end apart: 25, of which 6 were waited for; matrix products, arithmetic and copies ran while one was open for 1% of the time, Pallas kernels for 15%

profile of v10, /device:TPU:1, one launch (start us, length us, event | category | flops | bytes accessed | tf_op | source)
XLA Modules:
  0.0 112.8 jit_solution(4053656462772303623)
XLA Ops:
  0.7 1.6 %shard_map.104 = (bf16[7,8,512]{2,1,0:T(8,128)(2,1)S(1)}, bf16[64,1792]{1,0:T(8,128)(2,1)S(1)}) custom-call(s32[5]{0:T(128)S(1)} %stack.53.refs_0_, bf16[2,3,64,512]{3,2,1,0:T(8,128)(2,1)} %bitcast.38, bf16[2,64,512]{2,1,0:T(8,128)(2,1)} %refs_2_.1, bf16[2,2,64,512]{3,2,1,0:T(8,128)(2,1)} %bitcast.39, bf16[2,64,512]{2,1,0:T(8,128)(2,1)} %refs_4_.1, ...), custom_call_target="tpu_custom_call" | custom-call | bytes 1146900 | tf_op jit(solution)/shard_map/pallas_call | solution.py:85
  2.4 7.8 %collective-permute-start = (bf16[7,8,512]{2,1,0:T(8,128)(2,1)S(1)}, bf16[7,8,512]{2,1,0:T(8,128)(2,1)S(1)}, u32[]{:S(2)}, u32[]{:S(2)}) collective-permute-start(bf16[7,8,512]{2,1,0:T(8,128)(2,1)S(1)} %get-tuple-element.26), channel_id=1, source_target_pairs={{0,4},{1,5},{2,6},{3,7},{4,0},{5,1},{6,2},{7,3},{8,12},{9,13},{10,... | collective-permute-start | bytes 172040 | tf_op jit(solution)/shard_map/ppermute | solution.py:300
  11.4 2.4 %collective-permute-start.8 = (bf16[7,8,512]{2,1,0:T(8,128)(2,1)S(1)}, bf16[7,8,512]{2,1,0:T(8,128)(2,1)S(1)}, u32[]{:S(2)}, u32[]{:S(2)}) collective-permute-start(bf16[7,8,512]{2,1,0:T(8,128)(2,1)S(1)} %get-tuple-element.26), channel_id=1, source_target_pairs={{0,6},{1,7},{2,0},{3,1},{4,2},{5,3},{6,4},{7,5},{8,14},{9,15},{10,... | collective-permute-start | bytes 172040 | tf_op jit(solution)/shard_map/ppermute | solution.py:300
  13.8 2.6 %collective-permute-start.1 = (bf16[64,1792]{1,0:T(8,128)(2,1)S(1)}, bf16[64,1792]{1,0:T(8,128)(2,1)S(1)}, u32[]{:S(2)}, u32[]{:S(2)}) collective-permute-start(bf16[64,1792]{1,0:T(8,128)(2,1)S(1)} %get-tuple-element.27.refs_1_), channel_id=1, source_target_pairs={{0,6},{1,7},{2,0},{3,1},{4,2},{5,3},{6,4},{7,5},{8,14},{9,15},{10,... | collective-permute-start | bytes 688136 | tf_op jit(solution)/shard_map/ppermute | solution.py:45
  16.4 2.6 %collective-permute-start.9 = (bf16[4,7,8,512]{3,2,1,0:T(8,128)(2,1)S(1)}, bf16[4,7,8,512]{3,2,1,0:T(8,128)(2,1)S(1)}, u32[]{:S(2)}, u32[]{:S(2)}) collective-permute-start(bf16[4,7,8,512]{3,2,1,0:T(8,128)(2,1)S(1)} %pad_maximum_fusion.1), channel_id=1, source_target_pairs={{0,96},{1,25},{2,98},{3,27},{4,100},{5,29},{6,102},{7,31},{8,104},... | collective-permute-start | bytes 688136 | tf_op jit(solution)/shard_map/ppermute | solution.py:304
  20.1 7.2 %collective-permute-done.1.refs_2_ = bf16[64,1792]{1,0:T(8,128)(2,1)S(1)} collective-permute-done((bf16[64,1792]{1,0:T(8,128)(2,1)S(1)}, bf16[64,1792]{1,0:T(8,128)(2,1)S(1)}, u32[]{:S(2)}, u32[]{:S(2)}) %collective-permute-start.1) | collective-permute-done | bytes 229408 | tf_op jit(solution)/shard_map/ppermute | solution.py:45
  32.6 2.3 %collective-permute-start.4 = (bf16[32,1792]{1,0:T(8,128)(2,1)S(1)}, bf16[32,1792]{1,0:T(8,128)(2,1)S(1)}, u32[]{:S(2)}, u32[]{:S(2)}) collective-permute-start(bf16[32,1792]{1,0:T(8,128)(2,1)S(1)} %slice.17), channel_id=1, source_target_pairs={{0,6},{1,7},{2,0},{3,1},{4,2},{5,3},{6,4},{7,5},{8,14},{9,15},{10,... | collective-permute-start | bytes 344072 | tf_op jit(solution)/shard_map/ppermute | solution.py:47
  34.9 2.1 %collective-permute-done.3.refs_3_ = bf16[32,1792]{1,0:T(8,128)(2,1)S(1)} collective-permute-done((bf16[32,1792]{1,0:T(8,128)(2,1)S(1)}, bf16[32,1792]{1,0:T(8,128)(2,1)S(1)}, u32[]{:S(2)}, u32[]{:S(2)}) %collective-permute-start.3) | collective-permute-done | bytes 114720 | tf_op jit(solution)/shard_map/ppermute | solution.py:46
  37.0 2.1 %collective-permute-done.4.refs_4_ = bf16[32,1792]{1,0:T(8,128)(2,1)S(1)} collective-permute-done((bf16[32,1792]{1,0:T(8,128)(2,1)S(1)}, bf16[32,1792]{1,0:T(8,128)(2,1)S(1)}, u32[]{:S(2)}, u32[]{:S(2)}) %collective-permute-start.4) | collective-permute-done | bytes 114720 | tf_op jit(solution)/shard_map/ppermute | solution.py:47
  39.1 2.0 %shard_map.105 = (bf16[256,768]{1,0:T(8,128)(2,1)S(1)}, bf16[1024,256]{1,0:T(8,128)(2,1)}) custom-call(s32[5]{0:T(128)S(1)} %stack.53.refs_0_, bf16[64,1792]{1,0:T(8,128)(2,1)S(1)} %get-tuple-element.27.refs_1_, bf16[64,1792]{1,0:T(8,128)(2,1)S(1)} %collective-permute-done.1.refs_2_, bf16[32,1792]{1,0:T(8,128)(2,1)S(1)} %collective-permute-done.3.refs_3_, ...), custom_call_target="tpu_custom_call" | custom-call | flops 402653184 | bytes 921620 | tf_op jit(solution)/shard_map/pallas_call | solution.py:85
  44.1 7.8 %all-to-all-start = ((bf16[32,32,256]{2,1,0:T(8,128)(2,1)}), bf16[32,32,256]{2,1,0:T(8,128)(2,1)S(1)}, u32[]{:S(2)}, u32[]{:S(2)}) async-start(bf16[32,32,256]{2,1,0:T(8,128)(2,1)} %bitcast.36), calls=%async_computation | async-start | bytes 1048576 | tf_op jit(solution)/shard_map/all_to_all | solution.py:317
  59.8 4.2 %collective-permute-start.6 = (bf16[256,1024]{1,0:T(8,128)(2,1)}, bf16[256,1024]{1,0:T(8,128)(2,1)}, u32[]{:S(2)}, u32[]{:S(2)}) collective-permute-start(bf16[256,1024]{1,0:T(8,128)(2,1)} %shard_map.106.refs_3_), channel_id=1, source_target_pairs={{0,1},{1,0},{2,3},{3,2},{4,5},{5,4},{6,7},{7,6},{8,9},{9,8},{10,11... | collective-permute-start | bytes 1572872 | tf_op jit(solution)/shard_map/ppermute | solution.py:39
  64.0 1.8 %collective-permute-start.14 = (bf16[1024,256]{1,0:T(8,128)(2,1)S(1)}, bf16[1024,256]{1,0:T(8,128)(2,1)S(1)}, u32[]{:S(2)}, u32[]{:S(2)}) collective-permute-start(bf16[1024,256]{1,0:T(8,128)(2,1)S(1)} %bitcast.23), channel_id=1, source_target_pairs={{0,1},{1,0},{2,3},{3,2},{4,5},{5,4},{6,7},{7,6},{8,9},{9,8},{10,11... | collective-permute-start | bytes 1572872 | tf_op jit(solution)/shard_map/ppermute | solution.py:39
  66.5 1.6 %shard_map.107 = (bf16[3,256,512]{2,1,0:T(8,128)(2,1)S(1)}, bf16[2,256,512]{2,1,0:T(8,128)(2,1)S(1)}, bf16[2,512,256]{2,1,0:T(8,128)(2,1)S(1)}) custom-call(s32[5]{0:T(128)S(1)} %stack.53.refs_0_, bf16[4,4,7,8,512]{4,3,2,1,0:T(8,128)(2,1)S(1)} %pad_maximum_fusion.refs_1_, bf16[4,4,7,8,512]{4,3,2,1,0:T(8,128)(2,1)S(1)} %collective-permute-done.13.refs_2_, ...), custom_call_target="tpu_custom_call" | custom-call | flops 1610612736 | bytes 3670036 | tf_op jit(solution)/shard_map/pallas_call | solution.py:85
  68.1 1.7 %collective-permute-start.18 = (bf16[2,512,256]{2,1,0:T(8,128)(2,1)S(1)}, bf16[2,512,256]{2,1,0:T(8,128)(2,1)S(1)}, u32[]{:S(2)}, u32[]{:S(2)}) collective-permute-start(bf16[2,512,256]{2,1,0:T(8,128)(2,1)S(1)} %get-tuple-element.36.refs_3_), channel_id=1, source_target_pairs={{0,1},{1,0},{2,3},{3,2},{4,5},{5,4},{6,7},{7,6},{8,9},{9,8},{10,11... | collective-permute-start | bytes 1572872 | tf_op jit(solution)/shard_map/ppermute | solution.py:39
  70.0 4.0 %shard_map.108 = (bf16[512,768]{1,0:T(8,128)(2,1)S(1)}, bf16[512,1024]{1,0:T(8,128)(2,1)S(1)}, bf16[256,1024]{1,0:T(8,128)(2,1)S(1)}) custom-call(s32[5]{0:T(128)S(1)} %stack.53.refs_0_, bf16[256,768]{1,0:T(8,128)(2,1)S(1)} %copy-done.14, bf16[256,768]{1,0:T(8,128)(2,1)S(1)} %collective-permute-done.5.refs_2_, bf16[256,1024]{1,0:T(8,128)(2,1)} %shard_map.106.refs_3_, ...), custom_call_target="tpu_custom_call" | custom-call | flops 1879048192 | bytes 3678228 | tf_op jit(solution)/shard_map/pallas_call | solution.py:85
  74.5 2.4 %shard_map.109 = (bf16[3,256,512]{2,1,0:T(8,128)(2,1)S(1)}, bf16[2,256,512]{2,1,0:T(8,128)(2,1)}, bf16[2,512,256]{2,1,0:T(8,128)(2,1)}) custom-call(s32[5]{0:T(128)S(1)} %stack.53.refs_0_, bf16[4,4,7,8,512]{4,3,2,1,0:T(8,128)(2,1)S(1)} %pad_maximum_fusion.refs_1_, bf16[4,4,7,8,512]{4,3,2,1,0:T(8,128)(2,1)S(1)} %collective-permute-done.13.refs_2_, ...), custom_call_target="tpu_custom_call" | custom-call | bytes 3670036 | tf_op jit(solution)/shard_map/pallas_call | solution.py:85
  76.9 7.4 %shard_map.110 = (bf16[512,1024]{1,0:T(8,128)(2,1)}, bf16[512,768]{1,0:T(8,128)(2,1)}, bf16[1024,256]{1,0:T(8,128)(2,1)}) custom-call(s32[5]{0:T(128)S(1)} %stack.53.refs_0_, bf16[256,1024]{1,0:T(8,128)(2,1)S(1)} %get-tuple-element.35.refs_1_, bf16[256,1024]{1,0:T(8,128)(2,1)S(1)} %collective-permute-done.17.refs_2_, ...), custom_call_target="tpu_custom_call" | custom-call | flops 3221225472 | bytes 5775380 | tf_op jit(solution)/shard_map/pallas_call | solution.py:85
  84.3 6.3 %all-to-all-start.1 = ((bf16[32,32,256]{2,1,0:T(8,128)(2,1)}), bf16[32,32,256]{2,1,0:T(8,128)(2,1)S(1)}, u32[]{:S(2)}, u32[]{:S(2)}) async-start(bf16[32,32,256]{2,1,0:T(8,128)(2,1)} %bitcast.37), calls=%async_computation.1 | async-start | bytes 1048576 | tf_op jit(solution)/shard_map/all_to_all | solution.py:317
  92.7 2.3 %shard_map.111.refs_1_ = f32[256,1024]{1,0:T(8,128)S(1)} custom-call(s32[5]{0:T(128)S(1)} %stack.53.refs_0_, bf16[512,768]{1,0:T(8,128)(2,1)S(1)} %copy-done, bf16[512,1024]{1,0:T(8,128)(2,1)S(1)} %copy-done.1, bf16[3,256,512]{2,1,0:T(8,128)(2,1)S(1)} %get-tuple-element.40.refs_10_.refs_3_, s32[1,1024]{1,0:T(1,128)S(1)} %bitcast.27, s32[1,1024]{1,0:T(1,128)S(1)} %bitcast.31), custom_call_target="tpu_custom_call" | custom-call | flops 805306368 | bytes 2629652 | tf_op jit(solution)/shard_map/pallas_call | solution.py:85
  95.0 6.1 %all-to-all-done.1 = bf16[32,32,256]{2,1,0:T(8,128)(2,1)S(1)} async-done(((bf16[32,32,256]{2,1,0:T(8,128)(2,1)}), bf16[32,32,256]{2,1,0:T(8,128)(2,1)S(1)}, u32[]{:S(2)}, u32[]{:S(2)}) %all-to-all-start.1) | async-done | bytes 524320 | tf_op jit(solution)/shard_map/all_to_all | solution.py:317
  102.5 2.1 %collective-permute-start.20 = (bf16[256,1024]{1,0:T(8,128)(2,1)S(1)}, bf16[256,1024]{1,0:T(8,128)(2,1)S(1)}, u32[]{:S(2)}, u32[]{:S(2)}) collective-permute-start(bf16[256,1024]{1,0:T(8,128)(2,1)S(1)} %shard_map.112.refs_1_), channel_id=1, source_target_pairs={{0,1},{1,0},{2,3},{3,2},{4,5},{5,4},{6,7},{7,6},{8,9},{9,8},{10,11... | collective-permute-start | bytes 1572872 | tf_op jit(solution)/shard_map/ppermute | solution.py:39
  104.6 1.8 %shard_map.113.refs_10_ = f32[2,256,768]{2,1,0:T(8,128)S(1)} custom-call(s32[5]{0:T(128)S(1)} %stack.53.refs_0_, bf16[2,256,512]{2,1,0:T(8,128)(2,1)} %get-tuple-element.45.refs_1_.refs_5_, bf16[2,256,512]{2,1,0:T(8,128)(2,1)} %collective-permute-done.22.refs_2_.refs_6_, bf16[512,768]{1,0:T(8,128)(2,1)S(1)} %copy-done), custom_call_target="tpu_custom_call" | custom-call | flops 402653184 | bytes 1835028 | tf_op jit(solution)/shard_map/pallas_call | solution.py:85
  106.4 6.3 %shard_map.114 = (bf16[64,1024]{1,0:T(8,128)(2,1)}, bf16[64,768]{1,0:T(8,128)(2,1)}) custom-call(s32[5]{0:T(128)S(1)} %stack.53.refs_0_, bf16[256,1024]{1,0:T(8,128)(2,1)S(1)} %shard_map.112.refs_1_, bf16[256,1024]{1,0:T(8,128)(2,1)S(1)} %collective-permute-done.20.refs_2_, bf16[2,512,256]{2,1,0:T(8,128)(2,1)} %get-tuple-element.44.refs_3_, ...), custom_call_target="tpu_custom_call" | custom-call | flops 2684354560 | bytes 6557716 | tf_op jit(solution)/shard_map/pallas_call | solution.py:85
  (76 shorter events, 23.2 us)
Async XLA Ops:
  2.4 11.4 %collective-permute-start = (bf16[7,8,512]{2,1,0:T(8,128)(2,1)S(1)}, bf16[7,8,512]{2,1,0:T(8,128)(2,1)S(1)}, u32[]{:S(2)}, u32[]{:S(2)}) collective-permute-start(bf16[7,8,512]{2,1,0:T(8,128)(2,1)S(1)} %get-tuple-element.26), channel_id=1, source_target_pairs={{0,4},{1,5},{2,6},{3,7},{4,0},{5,1},{6,2},{7,3},{8,12},{9,13},{10,... | collective-permute-start | bytes 172040 | tf_op jit(solution)/shard_map/ppermute | solution.py:300
  10.2 6.2 %collective-permute-start.7 = (bf16[7,8,512]{2,1,0:T(8,128)(2,1)S(1)}, bf16[7,8,512]{2,1,0:T(8,128)(2,1)S(1)}, u32[]{:S(2)}, u32[]{:S(2)}) collective-permute-start(bf16[7,8,512]{2,1,0:T(8,128)(2,1)S(1)} %get-tuple-element.26), channel_id=1, source_target_pairs={{0,2},{1,3},{2,4},{3,5},{4,6},{5,7},{6,0},{7,1},{8,10},{9,11},{10,... | collective-permute-start | bytes 172040 | tf_op jit(solution)/shard_map/ppermute | solution.py:300
  11.4 5.0 %collective-permute-start.8 = (bf16[7,8,512]{2,1,0:T(8,128)(2,1)S(1)}, bf16[7,8,512]{2,1,0:T(8,128)(2,1)S(1)}, u32[]{:S(2)}, u32[]{:S(2)}) collective-permute-start(bf16[7,8,512]{2,1,0:T(8,128)(2,1)S(1)} %get-tuple-element.26), channel_id=1, source_target_pairs={{0,6},{1,7},{2,0},{3,1},{4,2},{5,3},{6,4},{7,5},{8,14},{9,15},{10,... | collective-permute-start | bytes 172040 | tf_op jit(solution)/shard_map/ppermute | solution.py:300
  13.8 13.5 %collective-permute-start.1 = (bf16[64,1792]{1,0:T(8,128)(2,1)S(1)}, bf16[64,1792]{1,0:T(8,128)(2,1)S(1)}, u32[]{:S(2)}, u32[]{:S(2)}) collective-permute-start(bf16[64,1792]{1,0:T(8,128)(2,1)S(1)} %get-tuple-element.27.refs_1_), channel_id=1, source_target_pairs={{0,6},{1,7},{2,0},{3,1},{4,2},{5,3},{6,4},{7,5},{8,14},{9,15},{10,... | collective-permute-start | bytes 688136 | tf_op jit(solution)/shard_map/ppermute | solution.py:45
  16.4 11.8 %collective-permute-start.2 = (bf16[64,1792]{1,0:T(8,128)(2,1)S(1)}, bf16[64,1792]{1,0:T(8,128)(2,1)S(1)}, u32[]{:S(2)}, u32[]{:S(2)}) collective-permute-start(bf16[64,1792]{1,0:T(8,128)(2,1)S(1)} %get-tuple-element.27.refs_1_), channel_id=1, source_target_pairs={{0,2},{1,3},{2,4},{3,5},{4,6},{5,7},{6,0},{7,1},{8,10},{9,11},{10,... | collective-permute-start | bytes 688136 | tf_op jit(solution)/shard_map/ppermute | solution.py:44
  16.4 11.7 %collective-permute-start.9 = (bf16[4,7,8,512]{3,2,1,0:T(8,128)(2,1)S(1)}, bf16[4,7,8,512]{3,2,1,0:T(8,128)(2,1)S(1)}, u32[]{:S(2)}, u32[]{:S(2)}) collective-permute-start(bf16[4,7,8,512]{3,2,1,0:T(8,128)(2,1)S(1)} %pad_maximum_fusion.1), channel_id=1, source_target_pairs={{0,96},{1,25},{2,98},{3,27},{4,100},{5,29},{6,102},{7,31},{8,104},... | collective-permute-start | bytes 688136 | tf_op jit(solution)/shard_map/ppermute | solution.py:304
  19.0 9.2 %collective-permute-start.10 = (bf16[4,7,8,512]{3,2,1,0:T(8,128)(2,1)S(1)}, bf16[4,7,8,512]{3,2,1,0:T(8,128)(2,1)S(1)}, u32[]{:S(2)}, u32[]{:S(2)}) collective-permute-start(bf16[4,7,8,512]{3,2,1,0:T(8,128)(2,1)S(1)} %pad_maximum_fusion.1), channel_id=1, source_target_pairs={{0,64},{1,17},{2,66},{3,19},{4,68},{5,21},{6,70},{7,23},{8,72},{9,... | collective-permute-start | bytes 688136 | tf_op jit(solution)/shard_map/ppermute | solution.py:304
  19.5 8.7 %collective-permute-start.11 = (bf16[4,7,8,512]{3,2,1,0:T(8,128)(2,1)S(1)}, bf16[4,7,8,512]{3,2,1,0:T(8,128)(2,1)S(1)}, u32[]{:S(2)}, u32[]{:S(2)}) collective-permute-start(bf16[4,7,8,512]{3,2,1,0:T(8,128)(2,1)S(1)} %pad_maximum_fusion.1), channel_id=1, source_target_pairs={{0,32},{1,9},{2,34},{3,11},{4,36},{5,13},{6,38},{7,15},{8,40},{9,1... | collective-permute-start | bytes 688136 | tf_op jit(solution)/shard_map/ppermute | solution.py:304
  28.3 14.2 %collective-permute-start.12 = (bf16[4,4,7,8,512]{4,3,2,1,0:T(8,128)(2,1)S(1)}, bf16[4,4,7,8,512]{4,3,2,1,0:T(8,128)(2,1)S(1)}, u32[]{:S(2)}, u32[]{:S(2)}) collective-permute-start(bf16[4,4,7,8,512]{4,3,2,1,0:T(8,128)(2,1)S(1)} %pad_maximum_fusion.refs_1_), channel_id=1, source_target_pairs={{0,8},{1,33},{2,10},{3,35},{4,12},{5,37},{6,14},{7,39},{8,16},{9,4... | collective-permute-start | bytes 2752520 | tf_op jit(solution)/shard_map/ppermute | solution.py:308
  29.6 13.7 %collective-permute-start.13 = (bf16[4,4,7,8,512]{4,3,2,1,0:T(8,128)(2,1)S(1)}, bf16[4,4,7,8,512]{4,3,2,1,0:T(8,128)(2,1)S(1)}, u32[]{:S(2)}, u32[]{:S(2)}) collective-permute-start(bf16[4,4,7,8,512]{4,3,2,1,0:T(8,128)(2,1)S(1)} %pad_maximum_fusion.refs_1_), channel_id=1, source_target_pairs={{0,24},{1,97},{2,26},{3,99},{4,28},{5,101},{6,30},{7,103},{8,0},{9... | collective-permute-start | bytes 2752520 | tf_op jit(solution)/shard_map/ppermute | solution.py:309
  31.1 5.8 %collective-permute-start.3 = (bf16[32,1792]{1,0:T(8,128)(2,1)S(1)}, bf16[32,1792]{1,0:T(8,128)(2,1)S(1)}, u32[]{:S(2)}, u32[]{:S(2)}) collective-permute-start(bf16[32,1792]{1,0:T(8,128)(2,1)S(1)} %slice.16), channel_id=1, source_target_pairs={{0,2},{1,3},{2,4},{3,5},{4,6},{5,7},{6,0},{7,1},{8,10},{9,11},{10,... | collective-permute-start | bytes 344072 | tf_op jit(solution)/shard_map/ppermute | solution.py:46
  32.6 6.5 %collective-permute-start.4 = (bf16[32,1792]{1,0:T(8,128)(2,1)S(1)}, bf16[32,1792]{1,0:T(8,128)(2,1)S(1)}, u32[]{:S(2)}, u32[]{:S(2)}) collective-permute-start(bf16[32,1792]{1,0:T(8,128)(2,1)S(1)} %slice.17), channel_id=1, source_target_pairs={{0,6},{1,7},{2,0},{3,1},{4,2},{5,3},{6,4},{7,5},{8,14},{9,15},{10,... | collective-permute-start | bytes 344072 | tf_op jit(solution)/shard_map/ppermute | solution.py:47
  44.1 19.9 %all-to-all-start = ((bf16[32,32,256]{2,1,0:T(8,128)(2,1)}), bf16[32,32,256]{2,1,0:T(8,128)(2,1)S(1)}, u32[]{:S(2)}, u32[]{:S(2)}) async-start(bf16[32,32,256]{2,1,0:T(8,128)(2,1)} %bitcast.36), calls=%async_computation | async-start | bytes 1048576 | tf_op jit(solution)/shard_map/all_to_all | solution.py:317
  52.0 14.5 %collective-permute-start.15 = (bf16[2,4,7,8,512]{4,3,2,1,0:T(8,128)(2,1)}, bf16[2,4,7,8,512]{4,3,2,1,0:T(8,128)(2,1)}, u32[]{:S(2)}, u32[]{:S(2)}) collective-permute-start(bf16[2,4,7,8,512]{4,3,2,1,0:T(8,128)(2,1)} %slice.18), channel_id=1, source_target_pairs={{0,8},{1,33},{2,10},{3,35},{4,12},{5,37},{6,14},{7,39},{8,16},{9,4... | collective-permute-start | bytes 1376264 | tf_op jit(solution)/shard_map/ppermute | solution.py:321
  53.3 13.2 %collective-permute-start.16 = (bf16[2,4,7,8,512]{4,3,2,1,0:T(8,128)(2,1)}, bf16[2,4,7,8,512]{4,3,2,1,0:T(8,128)(2,1)}, u32[]{:S(2)}, u32[]{:S(2)}) collective-permute-start(bf16[2,4,7,8,512]{4,3,2,1,0:T(8,128)(2,1)} %slice.19), channel_id=1, source_target_pairs={{0,24},{1,97},{2,26},{3,99},{4,28},{5,101},{6,30},{7,103},{8,0},{9... | collective-permute-start | bytes 1376264 | tf_op jit(solution)/shard_map/ppermute | solution.py:322
  59.8 10.1 %collective-permute-start.6 = (bf16[256,1024]{1,0:T(8,128)(2,1)}, bf16[256,1024]{1,0:T(8,128)(2,1)}, u32[]{:S(2)}, u32[]{:S(2)}) collective-permute-start(bf16[256,1024]{1,0:T(8,128)(2,1)} %shard_map.106.refs_3_), channel_id=1, source_target_pairs={{0,1},{1,0},{2,3},{3,2},{4,5},{5,4},{6,7},{7,6},{8,9},{9,8},{10,11... | collective-permute-start | bytes 1572872 | tf_op jit(solution)/shard_map/ppermute | solution.py:39
  64.0 5.9 %collective-permute-start.14 = (bf16[1024,256]{1,0:T(8,128)(2,1)S(1)}, bf16[1024,256]{1,0:T(8,128)(2,1)S(1)}, u32[]{:S(2)}, u32[]{:S(2)}) collective-permute-start(bf16[1024,256]{1,0:T(8,128)(2,1)S(1)} %bitcast.23), channel_id=1, source_target_pairs={{0,1},{1,0},{2,3},{3,2},{4,5},{5,4},{6,7},{7,6},{8,9},{9,8},{10,11... | collective-permute-start | bytes 1572872 | tf_op jit(solution)/shard_map/ppermute | solution.py:39
  65.9 4.1 %collective-permute-start.5 = (bf16[256,768]{1,0:T(8,128)(2,1)}, bf16[256,768]{1,0:T(8,128)(2,1)S(1)}, u32[]{:S(2)}, u32[]{:S(2)}) collective-permute-start(bf16[256,768]{1,0:T(8,128)(2,1)} %copy-done.13), channel_id=1, source_target_pairs={{0,1},{1,0},{2,3},{3,2},{4,5},{5,4},{6,7},{7,6},{8,9},{9,8},{10,11... | collective-permute-start | bytes 1179656 | tf_op jit(solution)/shard_map/ppermute | solution.py:39
  68.1 8.8 %collective-permute-start.18 = (bf16[2,512,256]{2,1,0:T(8,128)(2,1)S(1)}, bf16[2,512,256]{2,1,0:T(8,128)(2,1)S(1)}, u32[]{:S(2)}, u32[]{:S(2)}) collective-permute-start(bf16[2,512,256]{2,1,0:T(8,128)(2,1)S(1)} %get-tuple-element.36.refs_3_), channel_id=1, source_target_pairs={{0,1},{1,0},{2,3},{3,2},{4,5},{5,4},{6,7},{7,6},{8,9},{9,8},{10,11... | collective-permute-start | bytes 1572872 | tf_op jit(solution)/shard_map/ppermute | solution.py:39
  69.8 7.1 %collective-permute-start.19 = (bf16[2,256,512]{2,1,0:T(8,128)(2,1)S(1)}, bf16[2,256,512]{2,1,0:T(8,128)(2,1)S(1)}, u32[]{:S(2)}, u32[]{:S(2)}) collective-permute-start(bf16[2,256,512]{2,1,0:T(8,128)(2,1)S(1)} %get-tuple-element.37.refs_5_), channel_id=1, source_target_pairs={{0,1},{1,0},{2,3},{3,2},{4,5},{5,4},{6,7},{7,6},{8,9},{9,8},{10,11... | collective-permute-start | bytes 1572872 | tf_op jit(solution)/shard_map/ppermute | solution.py:39
  84.3 16.8 %all-to-all-start.1 = ((bf16[32,32,256]{2,1,0:T(8,128)(2,1)}), bf16[32,32,256]{2,1,0:T(8,128)(2,1)S(1)}, u32[]{:S(2)}, u32[]{:S(2)}) async-start(bf16[32,32,256]{2,1,0:T(8,128)(2,1)} %bitcast.37), calls=%async_computation.1 | async-start | bytes 1048576 | tf_op jit(solution)/shard_map/all_to_all | solution.py:317
  90.7 13.9 %collective-permute-start.22 = (bf16[2,256,512]{2,1,0:T(8,128)(2,1)}, bf16[2,256,512]{2,1,0:T(8,128)(2,1)}, u32[]{:S(2)}, u32[]{:S(2)}) collective-permute-start(bf16[2,256,512]{2,1,0:T(8,128)(2,1)} %get-tuple-element.45.refs_1_.refs_5_), channel_id=1, source_target_pairs={{0,1},{1,0},{2,3},{3,2},{4,5},{5,4},{6,7},{7,6},{8,9},{9,8},{10,11... | collective-permute-start | bytes 1572872 | tf_op jit(solution)/shard_map/ppermute | solution.py:39
  91.3 15.0 %collective-permute-start.21 = (bf16[2,512,256]{2,1,0:T(8,128)(2,1)}, bf16[2,512,256]{2,1,0:T(8,128)(2,1)}, u32[]{:S(2)}, u32[]{:S(2)}) collective-permute-start(bf16[2,512,256]{2,1,0:T(8,128)(2,1)} %get-tuple-element.44.refs_3_), channel_id=1, source_target_pairs={{0,1},{1,0},{2,3},{3,2},{4,5},{5,4},{6,7},{7,6},{8,9},{9,8},{10,11... | collective-permute-start | bytes 1572872 | tf_op jit(solution)/shard_map/ppermute | solution.py:39
  102.5 3.9 %collective-permute-start.20 = (bf16[256,1024]{1,0:T(8,128)(2,1)S(1)}, bf16[256,1024]{1,0:T(8,128)(2,1)S(1)}, u32[]{:S(2)}, u32[]{:S(2)}) collective-permute-start(bf16[256,1024]{1,0:T(8,128)(2,1)S(1)} %shard_map.112.refs_1_), channel_id=1, source_target_pairs={{0,1},{1,0},{2,3},{3,2},{4,5},{5,4},{6,7},{7,6},{8,9},{9,8},{10,11... | collective-permute-start | bytes 1572872 | tf_op jit(solution)/shard_map/ppermute | solution.py:39
  (17 other events, 122.9 us)
